TPU v7x, 32 devices: a whole 2x2x4 slice. The times are simulated.
32 devices in a mesh: seq: 16 (over z, y, x), tp: 2 (over core).
Axes of the slice: x: 2, y: 2, z: 4, core: 2. Of those that a mesh axis runs over, the one named last changes fastest.
Arguments:
- tokens: bfloat16 [2048, 2048], P('seq'), may hold values from -6 to 6
- attn_gain: float32 [2048], replicated, may hold values from 0.1 to 1.9
- mlp_gain: float32 [2048], replicated, may hold values from 0.1 to 1.9
- w_query: float32 [2048, 2048], P('seq', 'tp'), may hold values from -0.70710678 to 0.70710678
- w_key: float32 [2048, 2048], P('seq', 'tp'), may hold values from -0.70710678 to 0.70710678
- w_value: float32 [2048, 2048], P('seq', 'tp'), may hold values from -0.125 to 0.125
- w_out: float32 [2048, 2048], P('tp', 'seq'), may hold values from -0.125 to 0.125
- sink_logits: float32 [16], P('tp'), may hold values from 8 to 16
- router: float32 [2048, 16], P('seq'), may hold values from -0.25 to 0.25
- expert_gate: float32 [16, 2048, 1024], P(None, 'seq', 'tp'), may hold values from -0.125 to 0.125
- expert_up: float32 [16, 2048, 1024], P(None, 'seq', 'tp'), may hold values from -0.125 to 0.125
- expert_down: float32 [16, 2048, 1024], P(None, 'seq', 'tp'), may hold values from -0.1875 to 0.1875
- layout_map: int32 [16], replicated, may hold values from 0 to 15, each once
- real_lengths: int32 [2], replicated, may hold values from 256 to 1088, as said below
- routes: int32 [2048, 8], P('seq'), may hold values from 0 to 15, all different within a row; in each aligned block of 128 rows (0 to 127, 128 to 255, ...) at most 72 rows name the same one
Outputs:
- layer_out: bfloat16 [2048, 2048], P('seq', 'tp')
Inputs may be any that keep to these rules, and one draw needn't show every extreme that they name: Prompt p has real tokens in the first real_lengths[p] of its slots and padding after them; each length is at least 256; the last prompt has no padding. `routes`: each row names 8 different experts; among the rows of one device no expert is named more than 72 times, and in some device some expert exactly 72 times. `layout_map`: each trainer expert is held by exactly one server expert number.
All inputs are finite; a program needn't handle non-finite values.
Results may differ from a plain program's by a relative error of at most 0.0075.
The roundings to bfloat16 on the way count: a program that leaves them out, or rounds other values in their place, can miss the bound.
Values may be sent and summed in bfloat16 or wider, within the bound.
No kernel may reach another device: no remote copies, remote signals or barrier semaphores. Data moves between devices by JAX's collectives and lax.ppermute only.
A program may use at most 128 MiB of HBM per device.

v0:
```python
import jax
import jax.numpy as jnp
from jax import lax
from jax.sharding import PartitionSpec as P

HEAD = 128
HALF_WIN = 2048


EPSILON = 1e-05
ROPE_BASE = 50000.0
MASKED = -1e30


def from_behind(value, axis, steps):
    count = lax.axis_size(axis)
    first, last = (max(0, -steps), min(count, count - steps))
    return lax.ppermute(value, axis, [(source, source + steps) for source in range(first, last)])


def rms_scale(row_values, gain_vector):
    mean_square = jnp.mean(row_values * row_values, axis=-1, keepdims=True)
    return row_values * lax.rsqrt(mean_square + EPSILON) * gain_vector


def rotate(head_block, positions):
    half_dim = head_block.shape[-1] // 2
    frequency = ROPE_BASE ** (-jnp.arange(half_dim, dtype=jnp.float32) / half_dim)
    angles = positions[:, None, None] * frequency[None, None, :]
    cosine = jnp.cos(angles)
    sine_part = jnp.sin(angles)
    first_half = head_block[..., :half_dim]
    second_half = head_block[..., half_dim:]
    return jnp.concatenate(
        [
            first_half * cosine - second_half * sine_part,
            second_half * cosine + first_half * sine_part,
        ],
        axis=-1,
    )


def length_of(prompt, real_lengths):
    one_hot = prompt[:, None] == jnp.arange(real_lengths.shape[0], dtype=jnp.int32)[None, :]
    return jnp.sum(jnp.where(one_hot, real_lengths[None, :], 0), axis=1)


def prompt_split(slot_ids, slot_len, stagger, prompt_count):
    prompt = jnp.minimum((slot_ids + stagger) // slot_len, prompt_count - 1)
    start = jnp.maximum(prompt * slot_len - stagger, 0)
    return (prompt, slot_ids - start)


def key_rules(query_ids, key_ids, slot_len, stagger, total_slots, real_lengths):
    prompt_count = real_lengths.shape[0]
    key_prompt, key_pos = prompt_split(key_ids, slot_len, stagger, prompt_count)
    query_prompt = prompt_split(query_ids, slot_len, stagger, prompt_count)[0]
    inside = (key_ids >= 0) & (key_ids < total_slots)
    key_live = inside & (key_pos < length_of(key_prompt, real_lengths))
    same_prompt = query_prompt[:, None] == key_prompt[None, :]
    nearby = jnp.abs(query_ids[:, None] - key_ids[None, :]) < HALF_WIN
    return same_prompt & nearby & key_live[None, :]


def attend(softmax_state, query_rows, key_rows, value_rows, allowed):
    running_max, denominator, accumulated = softmax_state
    scores = jnp.einsum(
        "tge,kge->gtk", query_rows, key_rows, preferred_element_type=jnp.float32
    ) * HEAD ** (-0.5)
    scores = jnp.where(allowed[None], scores, MASKED)
    new_max = jnp.maximum(running_max, jnp.max(scores, axis=2))
    rescale = jnp.exp(running_max - new_max)
    weight_tensors = jnp.exp(scores - new_max[:, :, None])
    denominator = denominator * rescale + jnp.sum(weight_tensors, axis=2)
    accumulated = accumulated * rescale[:, :, None] + jnp.einsum(
        "ytz,zyb->ytb",
        weight_tensors,
        value_rows.astype(jnp.float32),
        precision=lax.Precision.HIGHEST,
    )
    return (new_max, denominator, accumulated)


def shards(
    tokens,
    attn_gain,
    mlp_gain,
    w_query,
    w_key,
    w_value,
    w_out,
    sink_logits,
    router,
    expert_gate,
    expert_up,
    expert_down,
    layout_map,
    real_lengths,
    routes,
):
    token_count, model_width = tokens.shape
    seq_count = lax.axis_size("seq")
    tp_count = lax.axis_size("tp")
    expert_count = router.shape[1]
    route_count = routes.shape[1]
    head_count = sink_logits.shape[0]
    proj_width = head_count * HEAD
    col_share = model_width // tp_count
    total_slots = token_count * seq_count
    prompt_count = real_lengths.shape[0]
    slot_len = total_slots // prompt_count
    stagger = token_count // 2
    capacity = max(2, min(token_count, 9 * token_count * route_count // (8 * expert_count)))
    seq_place = lax.axis_index("seq")
    tp_place = lax.axis_index("tp")
    offsets = jnp.arange(token_count, dtype=jnp.int32)
    token_index = seq_place * token_count + offsets
    prompt, position = prompt_split(token_index, slot_len, stagger, prompt_count)
    valid_token = position < length_of(prompt, real_lengths)
    normed = rms_scale(tokens.astype(jnp.float32), attn_gain).astype(jnp.bfloat16)
    stack_local = jnp.concatenate([w_query, w_key, w_value], axis=1).astype(jnp.bfloat16)
    router_local = router.astype(jnp.bfloat16)
    stack_piece = lax.all_gather(stack_local, "seq", axis=0, tiled=True)
    router_piece = lax.all_gather(router_local, "seq", axis=0, tiled=True)
    product = jnp.dot(normed, stack_piece, preferred_element_type=jnp.float32)
    router_full = router_piece
    product, router_full = (product, router_full)
    rotary_positions = position.astype(jnp.float32)
    query_rows = rotate(
        product[:, :proj_width].reshape(token_count, head_count, HEAD), rotary_positions
    ).astype(jnp.bfloat16)
    key_rows = rotate(
        product[:, proj_width : 2 * proj_width].reshape(token_count, head_count, HEAD),
        rotary_positions,
    ).astype(jnp.bfloat16)
    value_rows = (
        product[:, 2 * proj_width :].astype(jnp.bfloat16).reshape(token_count, head_count, HEAD)
    )
    softmax_state = (
        jnp.broadcast_to(sink_logits[:, None], (head_count, token_count)),
        jnp.ones((head_count, token_count), jnp.float32),
        jnp.zeros((head_count, token_count, HEAD), jnp.float32),
    )
    softmax_state = attend(
        softmax_state,
        query_rows,
        key_rows,
        value_rows,
        key_rules(token_index, token_index, slot_len, stagger, total_slots, real_lengths),
    )
    own_pair = jnp.stack([key_rows, value_rows])

    def one_turn(turn_index, loop_carry):
        loop_state, from_below, from_above = loop_carry
        from_below = from_behind(from_below, "seq", 1)
        from_above = from_behind(from_above, "seq", -1)
        reach_rows = (turn_index + 1) * token_count
        key_ids = jnp.concatenate([token_index - reach_rows, token_index + reach_rows])
        neighbours = jnp.concatenate([from_below, from_above], axis=1)
        allowed = key_rules(token_index, key_ids, slot_len, stagger, total_slots, real_lengths)
        loop_state = attend(loop_state, query_rows, neighbours[0], neighbours[1], allowed)
        return (loop_state, from_below, from_above)

    softmax_state, from_below, from_above = lax.fori_loop(
        0, HALF_WIN // token_count, one_turn, (softmax_state, own_pair, own_pair)
    )
    running_max, denominator, accumulated = softmax_state
    attention_result = (
        jnp.transpose(accumulated / denominator[:, :, None], (1, 0, 2))
        .reshape(token_count, proj_width)
        .astype(jnp.bfloat16)
    )
    partial_out = jnp.dot(
        attention_result,
        lax.all_gather(w_out.astype(jnp.bfloat16), "seq", axis=1, tiled=True),
        preferred_element_type=jnp.float32,
    )
    mixed_full = lax.psum(partial_out, "tp")
    full_rows = tokens.astype(jnp.float32) + mixed_full
    outgoing = rms_scale(full_rows, mlp_gain).astype(jnp.bfloat16)
    logits = jnp.dot(outgoing, router_full, preferred_element_type=jnp.float32)
    residual = lax.dynamic_slice_in_dim(full_rows, tp_place * col_share, col_share, 1)
    expert_ids = jnp.arange(expert_count, dtype=jnp.int32)
    chosen = routes[:, :, None] == expert_ids[None, None, :]
    route_logits = jnp.sum(jnp.where(chosen, logits[:, None, :], 0.0), axis=2)
    route_weight = jax.nn.softmax(route_logits, axis=1) * valid_token[:, None]
    flat_routes = routes.reshape(-1)
    live_route = jnp.repeat(valid_token, route_count)
    one_hot = ((flat_routes[:, None] == expert_ids[None, :]) & live_route[:, None]).astype(
        jnp.int32
    )
    rank_within = jnp.sum((jnp.cumsum(one_hot, axis=0) - one_hot) * one_hot, axis=1)
    slot_index = flat_routes * capacity + rank_within
    target_slot = jnp.where(live_route, slot_index, expert_count * capacity)
    owner_row = jnp.repeat(offsets, route_count) + 1
    source_row = (
        jnp.zeros((expert_count * capacity,), jnp.int32).at[target_slot].set(owner_row, mode="drop")
    )
    buffer = jnp.where(
        (source_row > 0)[:, None],
        outgoing[jnp.maximum(source_row - 1, 0)],
        jnp.zeros((), jnp.bfloat16),
    )
    buffer = buffer.reshape(expert_count, capacity, outgoing.shape[1])
    trainer = jnp.concatenate([expert_gate, expert_up, expert_down], axis=2).astype(jnp.bfloat16)
    ordered = jnp.take(trainer, layout_map, axis=0)
    server = lax.all_to_all(ordered, "seq", split_axis=0, concat_axis=1, tiled=True)
    hidden_share = expert_gate.shape[2]
    local_experts = server.shape[0]
    full_block = lax.all_to_all(buffer, "seq", split_axis=0, concat_axis=0, tiled=True)
    item_count = full_block.shape[1]
    grouped = full_block.reshape(seq_count, local_experts, item_count, model_width)
    gate_up = jnp.einsum(
        "sacd,adf->sacf",
        grouped,
        server[:, :, : 2 * hidden_share],
        preferred_element_type=jnp.float32,
    )
    hidden_state = (jax.nn.silu(gate_up[..., :hidden_share]) * gate_up[..., hidden_share:]).astype(
        jnp.bfloat16
    )
    partial_rows = jnp.einsum(
        "sacf,adf->sacd",
        hidden_state,
        server[:, :, 2 * hidden_share :],
        preferred_element_type=jnp.float32,
    )
    partial_rows = lax.optimization_barrier(partial_rows.astype(jnp.bfloat16)).astype(jnp.float32)
    summed = lax.psum_scatter(
        partial_rows.astype(jnp.bfloat16), "tp", scatter_dimension=3, tiled=True
    )
    returned = lax.all_to_all(
        summed.reshape(seq_count * local_experts, item_count, col_share),
        "seq",
        split_axis=0,
        concat_axis=0,
        tiled=True,
    )
    picked = returned.reshape(expert_count * capacity, col_share)[
        jnp.where(live_route, slot_index, 0)
    ]
    picked = picked.reshape(token_count, route_count, col_share)
    expert_mix = jnp.sum(route_weight[:, :, None] * picked.astype(jnp.float32), axis=1)
    return (residual + expert_mix).astype(jnp.bfloat16)


def solution(mesh):
    placed = (
        P("seq", None),
        P(),
        P(),
        P("seq", "tp"),
        P("seq", "tp"),
        P("seq", "tp"),
        P("tp", "seq"),
        P("tp"),
        P("seq", None),
        P(None, "seq", "tp"),
        P(None, "seq", "tp"),
        P(None, "seq", "tp"),
        P(),
        P(),
        P("seq", None),
    )
    return jax.shard_map(
        shards, mesh=mesh, in_specs=placed, out_specs=P("seq", "tp"), check_vma=False
    )
```

profile of v0, /device:TPU:0, one launch (start us, length us, event | category | flops | bytes accessed | tf_op | source)
XLA Modules:
  0.0 1061.8 jit_solution(7470347210897196199)
XLA Ops:
  10.8 2.6 convert.46
  14.5 1.9 copy-done.3
  17.1 5.7 pad_maximum_fusion
  22.7 6.6 gather_fusion
  29.3 6.1 broadcast_select_fusion
  35.4 8.3 all-to-all-start
  46.3 4.5 reduce-window.6
  51.7 223.1 %all-gather.3.cloned.1.call-done = bf16[2048,3072]{1,0:T(8,128)(2,1)} async-done(((bf16[128,3072]{1,0:T(8,128)(2,1)}), bf16[2048,3072]{1,0:T(8,128)(2,1)}) %all-gather.3.cloned.1.call-update) | async-done | bytes 12582928 | tf_op jit(solution)/shard_map/all_gather | solution.py:123
  274.8 6.5 fusion.21
  284.2 489.6 %while.25 = (s32[]{:T(128)}, f32[8,128]{1,0:T(8,128)S(1)}, f32[8,128]{1,0:T(8,128)S(1)}, f32[8,128,128]{2,1,0:T(8,128)S(1)}, bf16[2,128,8,128]{3,1,2,0:T(8,128)(...) while((s32[]{:T(128)}, f32[8,128]{1,0:T(8,128)S(1)}, ...), condition=%wide.region_8.9_spmd.clone, body=%wide.region_4.8_spmd.clone.sunk | while | flops 471806848 | bytes 14038749 | solution.py:164
  285.5 4.6 collective-permute-start
  290.4 24.8 %collective-permute-done = bf16[2,128,8,128]{3,1,2,0:T(8,128)(2,1)S(1)} collective-permute-done((bf16[2,128,8,128]{3,1,2,0:T(8,128)(2,1)S(1)}, bf16[2,128,8,128]{3,1,2,0:T(8,128)(2,1)S(1)}, u32[]{:S(2)}, u32[]{:S(2)}) %collective-permute-start) | collective-permute-done | bytes 524320 | tf_op jit(solution)/shard_map/while/body/eval_jaxpr/ppermute | solution.py:18
  317.1 1.3 collective-permute-start.1
  318.4 5.0 collective-permute-start
  323.8 14.7 %collective-permute-done = bf16[2,128,8,128]{3,1,2,0:T(8,128)(2,1)S(1)} collective-permute-done((bf16[2,128,8,128]{3,1,2,0:T(8,128)(2,1)S(1)}, bf16[2,128,8,128]{3,1,2,0:T(8,128)(2,1)S(1)}, u32[]{:S(2)}, u32[]{:S(2)}) %collective-permute-start) | collective-permute-done | bytes 524320 | tf_op jit(solution)/shard_map/while/body/eval_jaxpr/ppermute | solution.py:18
  341.8 7.3 collective-permute-start
  349.4 20.9 %collective-permute-done = bf16[2,128,8,128]{3,1,2,0:T(8,128)(2,1)S(1)} collective-permute-done((bf16[2,128,8,128]{3,1,2,0:T(8,128)(2,1)S(1)}, bf16[2,128,8,128]{3,1,2,0:T(8,128)(2,1)S(1)}, u32[]{:S(2)}, u32[]{:S(2)}) %collective-permute-start) | collective-permute-done | bytes 524320 | tf_op jit(solution)/shard_map/while/body/eval_jaxpr/ppermute | solution.py:18
  373.5 10.2 collective-permute-start
  384.0 32.2 %collective-permute-done = bf16[2,128,8,128]{3,1,2,0:T(8,128)(2,1)S(1)} collective-permute-done((bf16[2,128,8,128]{3,1,2,0:T(8,128)(2,1)S(1)}, bf16[2,128,8,128]{3,1,2,0:T(8,128)(2,1)S(1)}, u32[]{:S(2)}, u32[]{:S(2)}) %collective-permute-start) | collective-permute-done | bytes 524320 | tf_op jit(solution)/shard_map/while/body/eval_jaxpr/ppermute | solution.py:18
  419.4 5.0 collective-permute-start
  424.8 26.8 %collective-permute-done = bf16[2,128,8,128]{3,1,2,0:T(8,128)(2,1)S(1)} collective-permute-done((bf16[2,128,8,128]{3,1,2,0:T(8,128)(2,1)S(1)}, bf16[2,128,8,128]{3,1,2,0:T(8,128)(2,1)S(1)}, u32[]{:S(2)}, u32[]{:S(2)}) %collective-permute-start) | collective-permute-done | bytes 524320 | tf_op jit(solution)/shard_map/while/body/eval_jaxpr/ppermute | solution.py:18
  453.5 1.3 collective-permute-start.1
  454.8 5.0 collective-permute-start
  460.2 22.1 %collective-permute-done = bf16[2,128,8,128]{3,1,2,0:T(8,128)(2,1)S(1)} collective-permute-done((bf16[2,128,8,128]{3,1,2,0:T(8,128)(2,1)S(1)}, bf16[2,128,8,128]{3,1,2,0:T(8,128)(2,1)S(1)}, u32[]{:S(2)}, u32[]{:S(2)}) %collective-permute-start) | collective-permute-done | bytes 524320 | tf_op jit(solution)/shard_map/while/body/eval_jaxpr/ppermute | solution.py:18
  485.4 5.0 collective-permute-start
  490.8 21.4 %collective-permute-done = bf16[2,128,8,128]{3,1,2,0:T(8,128)(2,1)S(1)} collective-permute-done((bf16[2,128,8,128]{3,1,2,0:T(8,128)(2,1)S(1)}, bf16[2,128,8,128]{3,1,2,0:T(8,128)(2,1)S(1)}, u32[]{:S(2)}, u32[]{:S(2)}) %collective-permute-start) | collective-permute-done | bytes 524320 | tf_op jit(solution)/shard_map/while/body/eval_jaxpr/ppermute | solution.py:18
  515.4 5.0 collective-permute-start
  520.8 22.1 %collective-permute-done = bf16[2,128,8,128]{3,1,2,0:T(8,128)(2,1)S(1)} collective-permute-done((bf16[2,128,8,128]{3,1,2,0:T(8,128)(2,1)S(1)}, bf16[2,128,8,128]{3,1,2,0:T(8,128)(2,1)S(1)}, u32[]{:S(2)}, u32[]{:S(2)}) %collective-permute-start) | collective-permute-done | bytes 524320 | tf_op jit(solution)/shard_map/while/body/eval_jaxpr/ppermute | solution.py:18
  544.7 1.3 collective-permute-start.1
  546.0 5.0 collective-permute-start
  551.4 21.3 %collective-permute-done = bf16[2,128,8,128]{3,1,2,0:T(8,128)(2,1)S(1)} collective-permute-done((bf16[2,128,8,128]{3,1,2,0:T(8,128)(2,1)S(1)}, bf16[2,128,8,128]{3,1,2,0:T(8,128)(2,1)S(1)}, u32[]{:S(2)}, u32[]{:S(2)}) %collective-permute-start) | collective-permute-done | bytes 524320 | tf_op jit(solution)/shard_map/while/body/eval_jaxpr/ppermute | solution.py:18
  574.6 1.3 collective-permute-start.1
  575.9 5.0 collective-permute-start
  581.3 20.2 %collective-permute-done = bf16[2,128,8,128]{3,1,2,0:T(8,128)(2,1)S(1)} collective-permute-done((bf16[2,128,8,128]{3,1,2,0:T(8,128)(2,1)S(1)}, bf16[2,128,8,128]{3,1,2,0:T(8,128)(2,1)S(1)}, u32[]{:S(2)}, u32[]{:S(2)}) %collective-permute-start) | collective-permute-done | bytes 524320 | tf_op jit(solution)/shard_map/while/body/eval_jaxpr/ppermute | solution.py:18
  604.8 5.0 collective-permute-start
  610.2 21.9 %collective-permute-done = bf16[2,128,8,128]{3,1,2,0:T(8,128)(2,1)S(1)} collective-permute-done((bf16[2,128,8,128]{3,1,2,0:T(8,128)(2,1)S(1)}, bf16[2,128,8,128]{3,1,2,0:T(8,128)(2,1)S(1)}, u32[]{:S(2)}, u32[]{:S(2)}) %collective-permute-start) | collective-permute-done | bytes 524320 | tf_op jit(solution)/shard_map/while/body/eval_jaxpr/ppermute | solution.py:18
  635.3 5.0 collective-permute-start
  640.7 21.3 %collective-permute-done = bf16[2,128,8,128]{3,1,2,0:T(8,128)(2,1)S(1)} collective-permute-done((bf16[2,128,8,128]{3,1,2,0:T(8,128)(2,1)S(1)}, bf16[2,128,8,128]{3,1,2,0:T(8,128)(2,1)S(1)}, u32[]{:S(2)}, u32[]{:S(2)}) %collective-permute-start) | collective-permute-done | bytes 524320 | tf_op jit(solution)/shard_map/while/body/eval_jaxpr/ppermute | solution.py:18
  663.9 1.3 collective-permute-start.1
  665.2 5.0 collective-permute-start
  670.6 20.3 %collective-permute-done = bf16[2,128,8,128]{3,1,2,0:T(8,128)(2,1)S(1)} collective-permute-done((bf16[2,128,8,128]{3,1,2,0:T(8,128)(2,1)S(1)}, bf16[2,128,8,128]{3,1,2,0:T(8,128)(2,1)S(1)}, u32[]{:S(2)}, u32[]{:S(2)}) %collective-permute-start) | collective-permute-done | bytes 524320 | tf_op jit(solution)/shard_map/while/body/eval_jaxpr/ppermute | solution.py:18
  692.8 1.3 collective-permute-start.1
  694.1 5.0 collective-permute-start
  699.4 22.0 %collective-permute-done = bf16[2,128,8,128]{3,1,2,0:T(8,128)(2,1)S(1)} collective-permute-done((bf16[2,128,8,128]{3,1,2,0:T(8,128)(2,1)S(1)}, bf16[2,128,8,128]{3,1,2,0:T(8,128)(2,1)S(1)}, u32[]{:S(2)}, u32[]{:S(2)}) %collective-permute-start) | collective-permute-done | bytes 524320 | tf_op jit(solution)/shard_map/while/body/eval_jaxpr/ppermute | solution.py:18
  724.7 5.0 collective-permute-start
  730.1 22.2 %collective-permute-done = bf16[2,128,8,128]{3,1,2,0:T(8,128)(2,1)S(1)} collective-permute-done((bf16[2,128,8,128]{3,1,2,0:T(8,128)(2,1)S(1)}, bf16[2,128,8,128]{3,1,2,0:T(8,128)(2,1)S(1)}, u32[]{:S(2)}, u32[]{:S(2)}) %collective-permute-start) | collective-permute-done | bytes 524320 | tf_op jit(solution)/shard_map/while/body/eval_jaxpr/ppermute | solution.py:18
  754.2 1.3 collective-permute-start.1
  755.5 5.0 collective-permute-start
  760.9 11.0 %collective-permute-done = bf16[2,128,8,128]{3,1,2,0:T(8,128)(2,1)S(1)} collective-permute-done((bf16[2,128,8,128]{3,1,2,0:T(8,128)(2,1)S(1)}, bf16[2,128,8,128]{3,1,2,0:T(8,128)(2,1)S(1)}, u32[]{:S(2)}, u32[]{:S(2)}) %collective-permute-start) | collective-permute-done | bytes 524320 | tf_op jit(solution)/shard_map/while/body/eval_jaxpr/ppermute | solution.py:18
  774.1 3.9 fusion.69
  778.3 4.3 scatter_custom_fusion
  782.7 30.6 %all-reduce.2.cloned.1.call-done = f32[128,2048]{1,0:T(8,128)} async-done(((f32[128,2048]{1,0:T(8,128)}), f32[128,2048]{1,0:T(8,128)}) %all-reduce.2.cloned.1.call-update) | async-done | bytes 1048592 | tf_op jit(solution)/shard_map/psum | solution.py:178
  813.3 1.4 multiply_reduce_fusion
  815.9 6.0 gather_fusion.1
  822.0 4.9 broadcast_select_fusion.1
  826.8 112.2 %all_to_all.22 = bf16[16,72,2048]{2,1,0:T(8,128)(2,1)S(1)} all-to-all(bf16[16,72,2048]{2,1,0:T(8,128)(2,1)} %broadcast_select_fusion.1), channel_id=1, replica_groups=mesh['seq'=16,'tp'=2] {'seq'}, dimensions={0} | all-to-all | bytes 9437184 | tf_op jit(solution)/shard_map/all_to_all | solution.py:210
  939.0 7.3 fusion.14
  946.3 5.9 convert_bitcast_fusion
  952.2 11.2 %reduce-scatter.2.cloned.1.call-done = bf16[16,1,72,1024]{3,2,0,1:T(8,128)(2,1)} async-done(((bf16[16,1,72,2048]{3,2,0,1:T(8,128)(2,1)}), bf16[16,1,72,1024]{3,2,0,1:T(8,128)(2,1)}) %reduce-scatter.2.cloned.1.call-update) | async-done | bytes 2359312 | tf_op jit(solution)/shard_map/reduce_scatter | solution.py:229
  963.4 6.8 all-to-all-start.2
  970.2 74.5 %all_gather.11 = bf16[2048,16]{0,1:T(8,128)(2,1)S(1)} all-gather(bf16[128,16]{0,1:T(8,128)(2,1)S(1)} %convert_element_type.94), channel_id=1, replica_groups=mesh['seq'=16,'tp'=2] {'seq'}, dimensions={0}, use_global_device_ids=true | all-gather | bytes 69632 | tf_op jit(solution)/shard_map/all_gather | solution.py:124
  1045.1 5.4 gather_fusion.2
  1050.5 2.9 fusion.12
  1053.4 1.8 add_convert_fusion
  (391 shorter events, 59.9 us)
Async XLA Ops:
  6.5 268.2 %all-gather.3.cloned.1.call-start = ((), (), s32[]{:S(2)}) async-start(), calls=%async_computation.4 | async-start | bytes 13369344 | tf_op jit(solution)/shard_map/all_gather | solution.py:123
  10.8 3.5 copy-start.2
  14.2 2.2 copy-start.3
  16.4 0.7 copy-start.11
  35.4 8.4 copy-start.4
  35.4 9.4 copy-start.7
  35.4 9.9 copy-start.6
  35.4 10.3 copy-start.1
  35.4 239.4 %copy-start.5 = (f32[2048]{0:T(1024)S(1)}, f32[2048]{0:T(1024)}, u32[]{:S(2)}) copy-start(f32[2048]{0:T(1024)} %param.18) | copy-start | bytes 24580
  35.4 791.4 %all-to-all-start = ((bf16[16,128,1536]{2,1,0:T(8,128)(2,1)}), bf16[16,128,1536]{2,1,0:T(8,128)(2,1)}, u32[]{:S(2)}, u32[]{:S(2)}) async-start(bf16[16,128,1536]{2,1,0:T(8,128)(2,1)} %broadcast_select_fusion), calls=%async_computation | async-start | bytes 12582912 | tf_op jit(solution)/shard_map/all_to_all | solution.py:207
  43.7 730.4 %all-gather.5.cloned.1.call-start = ((), (), s32[]{:S(2)}) async-start(), calls=%async_computation.5 | async-start | bytes 4456448 | tf_op jit(solution)/shard_map/all_gather | solution.py:175
  44.5 768.8 %all-reduce.2.cloned.1.call-start = ((), (), s32[]{:S(2)}) async-start(), calls=%async_computation.6 | async-start | bytes 2097152 | tf_op jit(solution)/shard_map/psum | solution.py:178
  281.8 1.3 copy-start.10
  284.2 31.1 %collective-permute-start.1 = (bf16[2,128,8,128]{3,1,2,0:T(8,128)(2,1)S(1)}, bf16[2,128,8,128]{3,1,2,0:T(8,128)(2,1)S(1)}, u32[]{:S(2)}, u32[]{:S(2)}) collective-permute-start(bf16[2,128,8,128]{3,1,2,0:T(8,128)(2,1)S(1)} %get-tuple-element.428), channel_id=1, source_target_pairs={{2,0},{4,2},{6,4},{8,6},{10,8},{12,10},{14,12},{16,14},{18,16},{20... | collective-permute-start | bytes 1572872 | tf_op jit(solution)/shard_map/while/body/eval_jaxpr/ppermute | solution.py:18
  285.5 29.7 %collective-permute-start = (bf16[2,128,8,128]{3,1,2,0:T(8,128)(2,1)S(1)}, bf16[2,128,8,128]{3,1,2,0:T(8,128)(2,1)S(1)}, u32[]{:S(2)}, u32[]{:S(2)}) collective-permute-start(bf16[2,128,8,128]{3,1,2,0:T(8,128)(2,1)S(1)} %get-tuple-element.427), channel_id=1, source_target_pairs={{0,2},{2,4},{4,6},{6,8},{8,10},{10,12},{12,14},{14,16},{16,18},{18... | collective-permute-start | bytes 1572872 | tf_op jit(solution)/shard_map/while/body/eval_jaxpr/ppermute | solution.py:18
  317.1 21.5 %collective-permute-start.1 = (bf16[2,128,8,128]{3,1,2,0:T(8,128)(2,1)S(1)}, bf16[2,128,8,128]{3,1,2,0:T(8,128)(2,1)S(1)}, u32[]{:S(2)}, u32[]{:S(2)}) collective-permute-start(bf16[2,128,8,128]{3,1,2,0:T(8,128)(2,1)S(1)} %get-tuple-element.428), channel_id=1, source_target_pairs={{2,0},{4,2},{6,4},{8,6},{10,8},{12,10},{14,12},{16,14},{18,16},{20... | collective-permute-start | bytes 1572872 | tf_op jit(solution)/shard_map/while/body/eval_jaxpr/ppermute | solution.py:18
  318.4 20.1 %collective-permute-start = (bf16[2,128,8,128]{3,1,2,0:T(8,128)(2,1)S(1)}, bf16[2,128,8,128]{3,1,2,0:T(8,128)(2,1)S(1)}, u32[]{:S(2)}, u32[]{:S(2)}) collective-permute-start(bf16[2,128,8,128]{3,1,2,0:T(8,128)(2,1)S(1)} %get-tuple-element.427), channel_id=1, source_target_pairs={{0,2},{2,4},{4,6},{6,8},{8,10},{10,12},{12,14},{14,16},{16,18},{18... | collective-permute-start | bytes 1572872 | tf_op jit(solution)/shard_map/while/body/eval_jaxpr/ppermute | solution.py:18
  340.5 29.9 %collective-permute-start.1 = (bf16[2,128,8,128]{3,1,2,0:T(8,128)(2,1)S(1)}, bf16[2,128,8,128]{3,1,2,0:T(8,128)(2,1)S(1)}, u32[]{:S(2)}, u32[]{:S(2)}) collective-permute-start(bf16[2,128,8,128]{3,1,2,0:T(8,128)(2,1)S(1)} %get-tuple-element.428), channel_id=1, source_target_pairs={{2,0},{4,2},{6,4},{8,6},{10,8},{12,10},{14,12},{16,14},{18,16},{20... | collective-permute-start | bytes 1572872 | tf_op jit(solution)/shard_map/while/body/eval_jaxpr/ppermute | solution.py:18
  341.8 28.5 %collective-permute-start = (bf16[2,128,8,128]{3,1,2,0:T(8,128)(2,1)S(1)}, bf16[2,128,8,128]{3,1,2,0:T(8,128)(2,1)S(1)}, u32[]{:S(2)}, u32[]{:S(2)}) collective-permute-start(bf16[2,128,8,128]{3,1,2,0:T(8,128)(2,1)S(1)} %get-tuple-element.427), channel_id=1, source_target_pairs={{0,2},{2,4},{4,6},{6,8},{8,10},{10,12},{12,14},{14,16},{16,18},{18... | collective-permute-start | bytes 1572872 | tf_op jit(solution)/shard_map/while/body/eval_jaxpr/ppermute | solution.py:18
  372.2 44.0 %collective-permute-start.1 = (bf16[2,128,8,128]{3,1,2,0:T(8,128)(2,1)S(1)}, bf16[2,128,8,128]{3,1,2,0:T(8,128)(2,1)S(1)}, u32[]{:S(2)}, u32[]{:S(2)}) collective-permute-start(bf16[2,128,8,128]{3,1,2,0:T(8,128)(2,1)S(1)} %get-tuple-element.428), channel_id=1, source_target_pairs={{2,0},{4,2},{6,4},{8,6},{10,8},{12,10},{14,12},{16,14},{18,16},{20... | collective-permute-start | bytes 1572872 | tf_op jit(solution)/shard_map/while/body/eval_jaxpr/ppermute | solution.py:18
  373.5 42.7 %collective-permute-start = (bf16[2,128,8,128]{3,1,2,0:T(8,128)(2,1)S(1)}, bf16[2,128,8,128]{3,1,2,0:T(8,128)(2,1)S(1)}, u32[]{:S(2)}, u32[]{:S(2)}) collective-permute-start(bf16[2,128,8,128]{3,1,2,0:T(8,128)(2,1)S(1)} %get-tuple-element.427), channel_id=1, source_target_pairs={{0,2},{2,4},{4,6},{6,8},{8,10},{10,12},{12,14},{14,16},{16,18},{18... | collective-permute-start | bytes 1572872 | tf_op jit(solution)/shard_map/while/body/eval_jaxpr/ppermute | solution.py:18
  418.1 33.5 %collective-permute-start.1 = (bf16[2,128,8,128]{3,1,2,0:T(8,128)(2,1)S(1)}, bf16[2,128,8,128]{3,1,2,0:T(8,128)(2,1)S(1)}, u32[]{:S(2)}, u32[]{:S(2)}) collective-permute-start(bf16[2,128,8,128]{3,1,2,0:T(8,128)(2,1)S(1)} %get-tuple-element.428), channel_id=1, source_target_pairs={{2,0},{4,2},{6,4},{8,6},{10,8},{12,10},{14,12},{16,14},{18,16},{20... | collective-permute-start | bytes 1572872 | tf_op jit(solution)/shard_map/while/body/eval_jaxpr/ppermute | solution.py:18
  419.4 32.1 %collective-permute-start = (bf16[2,128,8,128]{3,1,2,0:T(8,128)(2,1)S(1)}, bf16[2,128,8,128]{3,1,2,0:T(8,128)(2,1)S(1)}, u32[]{:S(2)}, u32[]{:S(2)}) collective-permute-start(bf16[2,128,8,128]{3,1,2,0:T(8,128)(2,1)S(1)} %get-tuple-element.427), channel_id=1, source_target_pairs={{0,2},{2,4},{4,6},{6,8},{8,10},{10,12},{12,14},{14,16},{16,18},{18... | collective-permute-start | bytes 1572872 | tf_op jit(solution)/shard_map/while/body/eval_jaxpr/ppermute | solution.py:18
  453.5 28.8 %collective-permute-start.1 = (bf16[2,128,8,128]{3,1,2,0:T(8,128)(2,1)S(1)}, bf16[2,128,8,128]{3,1,2,0:T(8,128)(2,1)S(1)}, u32[]{:S(2)}, u32[]{:S(2)}) collective-permute-start(bf16[2,128,8,128]{3,1,2,0:T(8,128)(2,1)S(1)} %get-tuple-element.428), channel_id=1, source_target_pairs={{2,0},{4,2},{6,4},{8,6},{10,8},{12,10},{14,12},{16,14},{18,16},{20... | collective-permute-start | bytes 1572872 | tf_op jit(solution)/shard_map/while/body/eval_jaxpr/ppermute | solution.py:18
  454.8 27.4 %collective-permute-start = (bf16[2,128,8,128]{3,1,2,0:T(8,128)(2,1)S(1)}, bf16[2,128,8,128]{3,1,2,0:T(8,128)(2,1)S(1)}, u32[]{:S(2)}, u32[]{:S(2)}) collective-permute-start(bf16[2,128,8,128]{3,1,2,0:T(8,128)(2,1)S(1)} %get-tuple-element.427), channel_id=1, source_target_pairs={{0,2},{2,4},{4,6},{6,8},{8,10},{10,12},{12,14},{14,16},{16,18},{18... | collective-permute-start | bytes 1572872 | tf_op jit(solution)/shard_map/while/body/eval_jaxpr/ppermute | solution.py:18
  484.1 28.1 %collective-permute-start.1 = (bf16[2,128,8,128]{3,1,2,0:T(8,128)(2,1)S(1)}, bf16[2,128,8,128]{3,1,2,0:T(8,128)(2,1)S(1)}, u32[]{:S(2)}, u32[]{:S(2)}) collective-permute-start(bf16[2,128,8,128]{3,1,2,0:T(8,128)(2,1)S(1)} %get-tuple-element.428), channel_id=1, source_target_pairs={{2,0},{4,2},{6,4},{8,6},{10,8},{12,10},{14,12},{16,14},{18,16},{20... | collective-permute-start | bytes 1572872 | tf_op jit(solution)/shard_map/while/body/eval_jaxpr/ppermute | solution.py:18
  485.4 26.8 %collective-permute-start = (bf16[2,128,8,128]{3,1,2,0:T(8,128)(2,1)S(1)}, bf16[2,128,8,128]{3,1,2,0:T(8,128)(2,1)S(1)}, u32[]{:S(2)}, u32[]{:S(2)}) collective-permute-start(bf16[2,128,8,128]{3,1,2,0:T(8,128)(2,1)S(1)} %get-tuple-element.427), channel_id=1, source_target_pairs={{0,2},{2,4},{4,6},{6,8},{8,10},{10,12},{12,14},{14,16},{16,18},{18... | collective-permute-start | bytes 1572872 | tf_op jit(solution)/shard_map/while/body/eval_jaxpr/ppermute | solution.py:18
  514.1 28.8 %collective-permute-start.1 = (bf16[2,128,8,128]{3,1,2,0:T(8,128)(2,1)S(1)}, bf16[2,128,8,128]{3,1,2,0:T(8,128)(2,1)S(1)}, u32[]{:S(2)}, u32[]{:S(2)}) collective-permute-start(bf16[2,128,8,128]{3,1,2,0:T(8,128)(2,1)S(1)} %get-tuple-element.428), channel_id=1, source_target_pairs={{2,0},{4,2},{6,4},{8,6},{10,8},{12,10},{14,12},{16,14},{18,16},{20... | collective-permute-start | bytes 1572872 | tf_op jit(solution)/shard_map/while/body/eval_jaxpr/ppermute | solution.py:18
  515.4 27.4 %collective-permute-start = (bf16[2,128,8,128]{3,1,2,0:T(8,128)(2,1)S(1)}, bf16[2,128,8,128]{3,1,2,0:T(8,128)(2,1)S(1)}, u32[]{:S(2)}, u32[]{:S(2)}) collective-permute-start(bf16[2,128,8,128]{3,1,2,0:T(8,128)(2,1)S(1)} %get-tuple-element.427), channel_id=1, source_target_pairs={{0,2},{2,4},{4,6},{6,8},{8,10},{10,12},{12,14},{14,16},{16,18},{18... | collective-permute-start | bytes 1572872 | tf_op jit(solution)/shard_map/while/body/eval_jaxpr/ppermute | solution.py:18
  544.7 28.0 %collective-permute-start.1 = (bf16[2,128,8,128]{3,1,2,0:T(8,128)(2,1)S(1)}, bf16[2,128,8,128]{3,1,2,0:T(8,128)(2,1)S(1)}, u32[]{:S(2)}, u32[]{:S(2)}) collective-permute-start(bf16[2,128,8,128]{3,1,2,0:T(8,128)(2,1)S(1)} %get-tuple-element.428), channel_id=1, source_target_pairs={{2,0},{4,2},{6,4},{8,6},{10,8},{12,10},{14,12},{16,14},{18,16},{20... | collective-permute-start | bytes 1572872 | tf_op jit(solution)/shard_map/while/body/eval_jaxpr/ppermute | solution.py:18
  546.0 26.7 %collective-permute-start = (bf16[2,128,8,128]{3,1,2,0:T(8,128)(2,1)S(1)}, bf16[2,128,8,128]{3,1,2,0:T(8,128)(2,1)S(1)}, u32[]{:S(2)}, u32[]{:S(2)}) collective-permute-start(bf16[2,128,8,128]{3,1,2,0:T(8,128)(2,1)S(1)} %get-tuple-element.427), channel_id=1, source_target_pairs={{0,2},{2,4},{4,6},{6,8},{8,10},{10,12},{12,14},{14,16},{16,18},{18... | collective-permute-start | bytes 1572872 | tf_op jit(solution)/shard_map/while/body/eval_jaxpr/ppermute | solution.py:18
  574.6 27.0 %collective-permute-start.1 = (bf16[2,128,8,128]{3,1,2,0:T(8,128)(2,1)S(1)}, bf16[2,128,8,128]{3,1,2,0:T(8,128)(2,1)S(1)}, u32[]{:S(2)}, u32[]{:S(2)}) collective-permute-start(bf16[2,128,8,128]{3,1,2,0:T(8,128)(2,1)S(1)} %get-tuple-element.428), channel_id=1, source_target_pairs={{2,0},{4,2},{6,4},{8,6},{10,8},{12,10},{14,12},{16,14},{18,16},{20... | collective-permute-start | bytes 1572872 | tf_op jit(solution)/shard_map/while/body/eval_jaxpr/ppermute | solution.py:18
  575.9 25.6 %collective-permute-start = (bf16[2,128,8,128]{3,1,2,0:T(8,128)(2,1)S(1)}, bf16[2,128,8,128]{3,1,2,0:T(8,128)(2,1)S(1)}, u32[]{:S(2)}, u32[]{:S(2)}) collective-permute-start(bf16[2,128,8,128]{3,1,2,0:T(8,128)(2,1)S(1)} %get-tuple-element.427), channel_id=1, source_target_pairs={{0,2},{2,4},{4,6},{6,8},{8,10},{10,12},{12,14},{14,16},{16,18},{18... | collective-permute-start | bytes 1572872 | tf_op jit(solution)/shard_map/while/body/eval_jaxpr/ppermute | solution.py:18
  603.5 28.7 %collective-permute-start.1 = (bf16[2,128,8,128]{3,1,2,0:T(8,128)(2,1)S(1)}, bf16[2,128,8,128]{3,1,2,0:T(8,128)(2,1)S(1)}, u32[]{:S(2)}, u32[]{:S(2)}) collective-permute-start(bf16[2,128,8,128]{3,1,2,0:T(8,128)(2,1)S(1)} %get-tuple-element.428), channel_id=1, source_target_pairs={{2,0},{4,2},{6,4},{8,6},{10,8},{12,10},{14,12},{16,14},{18,16},{20... | collective-permute-start | bytes 1572872 | tf_op jit(solution)/shard_map/while/body/eval_jaxpr/ppermute | solution.py:18
  604.8 27.3 %collective-permute-start = (bf16[2,128,8,128]{3,1,2,0:T(8,128)(2,1)S(1)}, bf16[2,128,8,128]{3,1,2,0:T(8,128)(2,1)S(1)}, u32[]{:S(2)}, u32[]{:S(2)}) collective-permute-start(bf16[2,128,8,128]{3,1,2,0:T(8,128)(2,1)S(1)} %get-tuple-element.427), channel_id=1, source_target_pairs={{0,2},{2,4},{4,6},{6,8},{8,10},{10,12},{12,14},{14,16},{16,18},{18... | collective-permute-start | bytes 1572872 | tf_op jit(solution)/shard_map/while/body/eval_jaxpr/ppermute | solution.py:18
  634.0 28.0 %collective-permute-start.1 = (bf16[2,128,8,128]{3,1,2,0:T(8,128)(2,1)S(1)}, bf16[2,128,8,128]{3,1,2,0:T(8,128)(2,1)S(1)}, u32[]{:S(2)}, u32[]{:S(2)}) collective-permute-start(bf16[2,128,8,128]{3,1,2,0:T(8,128)(2,1)S(1)} %get-tuple-element.428), channel_id=1, source_target_pairs={{2,0},{4,2},{6,4},{8,6},{10,8},{12,10},{14,12},{16,14},{18,16},{20... | collective-permute-start | bytes 1572872 | tf_op jit(solution)/shard_map/while/body/eval_jaxpr/ppermute | solution.py:18
  635.3 26.7 %collective-permute-start = (bf16[2,128,8,128]{3,1,2,0:T(8,128)(2,1)S(1)}, bf16[2,128,8,128]{3,1,2,0:T(8,128)(2,1)S(1)}, u32[]{:S(2)}, u32[]{:S(2)}) collective-permute-start(bf16[2,128,8,128]{3,1,2,0:T(8,128)(2,1)S(1)} %get-tuple-element.427), channel_id=1, source_target_pairs={{0,2},{2,4},{4,6},{6,8},{8,10},{10,12},{12,14},{14,16},{16,18},{18... | collective-permute-start | bytes 1572872 | tf_op jit(solution)/shard_map/while/body/eval_jaxpr/ppermute | solution.py:18
  663.9 27.0 %collective-permute-start.1 = (bf16[2,128,8,128]{3,1,2,0:T(8,128)(2,1)S(1)}, bf16[2,128,8,128]{3,1,2,0:T(8,128)(2,1)S(1)}, u32[]{:S(2)}, u32[]{:S(2)}) collective-permute-start(bf16[2,128,8,128]{3,1,2,0:T(8,128)(2,1)S(1)} %get-tuple-element.428), channel_id=1, source_target_pairs={{2,0},{4,2},{6,4},{8,6},{10,8},{12,10},{14,12},{16,14},{18,16},{20... | collective-permute-start | bytes 1572872 | tf_op jit(solution)/shard_map/while/body/eval_jaxpr/ppermute | solution.py:18
  665.2 25.6 %collective-permute-start = (bf16[2,128,8,128]{3,1,2,0:T(8,128)(2,1)S(1)}, bf16[2,128,8,128]{3,1,2,0:T(8,128)(2,1)S(1)}, u32[]{:S(2)}, u32[]{:S(2)}) collective-permute-start(bf16[2,128,8,128]{3,1,2,0:T(8,128)(2,1)S(1)} %get-tuple-element.427), channel_id=1, source_target_pairs={{0,2},{2,4},{4,6},{6,8},{8,10},{10,12},{12,14},{14,16},{16,18},{18... | collective-permute-start | bytes 1572872 | tf_op jit(solution)/shard_map/while/body/eval_jaxpr/ppermute | solution.py:18
  692.8 28.7 %collective-permute-start.1 = (bf16[2,128,8,128]{3,1,2,0:T(8,128)(2,1)S(1)}, bf16[2,128,8,128]{3,1,2,0:T(8,128)(2,1)S(1)}, u32[]{:S(2)}, u32[]{:S(2)}) collective-permute-start(bf16[2,128,8,128]{3,1,2,0:T(8,128)(2,1)S(1)} %get-tuple-element.428), channel_id=1, source_target_pairs={{2,0},{4,2},{6,4},{8,6},{10,8},{12,10},{14,12},{16,14},{18,16},{20... | collective-permute-start | bytes 1572872 | tf_op jit(solution)/shard_map/while/body/eval_jaxpr/ppermute | solution.py:18
  694.1 27.4 %collective-permute-start = (bf16[2,128,8,128]{3,1,2,0:T(8,128)(2,1)S(1)}, bf16[2,128,8,128]{3,1,2,0:T(8,128)(2,1)S(1)}, u32[]{:S(2)}, u32[]{:S(2)}) collective-permute-start(bf16[2,128,8,128]{3,1,2,0:T(8,128)(2,1)S(1)} %get-tuple-element.427), channel_id=1, source_target_pairs={{0,2},{2,4},{4,6},{6,8},{8,10},{10,12},{12,14},{14,16},{16,18},{18... | collective-permute-start | bytes 1572872 | tf_op jit(solution)/shard_map/while/body/eval_jaxpr/ppermute | solution.py:18
  723.4 29.0 %collective-permute-start.1 = (bf16[2,128,8,128]{3,1,2,0:T(8,128)(2,1)S(1)}, bf16[2,128,8,128]{3,1,2,0:T(8,128)(2,1)S(1)}, u32[]{:S(2)}, u32[]{:S(2)}) collective-permute-start(bf16[2,128,8,128]{3,1,2,0:T(8,128)(2,1)S(1)} %get-tuple-element.428), channel_id=1, source_target_pairs={{2,0},{4,2},{6,4},{8,6},{10,8},{12,10},{14,12},{16,14},{18,16},{20... | collective-permute-start | bytes 1572872 | tf_op jit(solution)/shard_map/while/body/eval_jaxpr/ppermute | solution.py:18
  724.7 27.6 %collective-permute-start = (bf16[2,128,8,128]{3,1,2,0:T(8,128)(2,1)S(1)}, bf16[2,128,8,128]{3,1,2,0:T(8,128)(2,1)S(1)}, u32[]{:S(2)}, u32[]{:S(2)}) collective-permute-start(bf16[2,128,8,128]{3,1,2,0:T(8,128)(2,1)S(1)} %get-tuple-element.427), channel_id=1, source_target_pairs={{0,2},{2,4},{4,6},{6,8},{8,10},{10,12},{12,14},{14,16},{16,18},{18... | collective-permute-start | bytes 1572872 | tf_op jit(solution)/shard_map/while/body/eval_jaxpr/ppermute | solution.py:18
  754.2 17.8 %collective-permute-start.1 = (bf16[2,128,8,128]{3,1,2,0:T(8,128)(2,1)S(1)}, bf16[2,128,8,128]{3,1,2,0:T(8,128)(2,1)S(1)}, u32[]{:S(2)}, u32[]{:S(2)}) collective-permute-start(bf16[2,128,8,128]{3,1,2,0:T(8,128)(2,1)S(1)} %get-tuple-element.428), channel_id=1, source_target_pairs={{2,0},{4,2},{6,4},{8,6},{10,8},{12,10},{14,12},{16,14},{18,16},{20... | collective-permute-start | bytes 1572872 | tf_op jit(solution)/shard_map/while/body/eval_jaxpr/ppermute | solution.py:18
  755.5 16.4 %collective-permute-start = (bf16[2,128,8,128]{3,1,2,0:T(8,128)(2,1)S(1)}, bf16[2,128,8,128]{3,1,2,0:T(8,128)(2,1)S(1)}, u32[]{:S(2)}, u32[]{:S(2)}) collective-permute-start(bf16[2,128,8,128]{3,1,2,0:T(8,128)(2,1)S(1)} %get-tuple-element.427), channel_id=1, source_target_pairs={{0,2},{2,4},{4,6},{6,8},{8,10},{10,12},{12,14},{14,16},{16,18},{18... | collective-permute-start | bytes 1572872 | tf_op jit(solution)/shard_map/while/body/eval_jaxpr/ppermute | solution.py:18
  774.1 41.7 %copy-start.8 = (f32[2048]{0:T(1024)S(1)}, f32[2048]{0:T(1024)}, u32[]{:S(2)}) copy-start(f32[2048]{0:T(1024)} %param.19) | copy-start | bytes 24580
  778.1 185.3 %reduce-scatter.2.cloned.1.call-start = ((), (), s32[]{:S(2)}) async-start(), calls=%async_computation.7 | async-start | bytes 7077888 | tf_op jit(solution)/shard_map/reduce_scatter | solution.py:229
  814.8 1.0 copy-start
  952.2 18.0 %copy-start.9 = (f32[128,16]{0,1:T(8,128)S(1)}, f32[128,16]{0,1:T(8,128)}, u32[]{:S(2)}) copy-start(f32[128,16]{0,1:T(8,128)} %param.25) | copy-start | bytes 24580
  963.4 81.8 %all-to-all-start.2 = ((bf16[16,72,1024]{2,1,0:T(8,128)(2,1)}), bf16[16,72,1024]{2,1,0:T(8,128)(2,1)S(1)}, u32[]{:S(2)}, u32[]{:S(2)}) async-start(bf16[16,72,1024]{2,1,0:T(8,128)(2,1)} %bitcast.102), calls=%async_computation.3 | async-start | bytes 4718592 | tf_op jit(solution)/shard_map/all_to_all | solution.py:232
Sparse Core Ops, SparseCore 0:
  10.9 263.8 all-gather.2
  277.5 148.5 all-gather.4
  778.2 35.0 all-reduce.1
  952.3 10.9 reduce-scatter.1
where the time goes:
time: 1070 us; the launch traced here: 1060 us
  waiting for transfers between devices  610 us (57%)
  blocking collectives  187 us (17%)
  starting transfers between devices  124 us (12%)
  matrix products  48.1 us (4%)
  other arithmetic  45.3 us (4%)
  local copies, waits for them, and re-layouts  32.1 us (3%)
  between operations  13.6 us (1%)
    ppermute x32, waiting for transfers between devices, from_behind(): lax.ppermute(value, axis, [(source, source + steps) for source in range(f...  345 us
    all_gather x1, waiting for transfers between devices, shards(): stack_piece = lax.all_gather(stack_local, 'seq', axis=0, tiled=True)  223 us
    all_to_all x1, blocking collectives, shards(): lax.all_to_all(buffer, 'seq', split_axis=0, concat_axis=0, tiled=True)  112 us
    ppermute x32, starting transfers between devices, from_behind(): lax.ppermute(value, axis, [(source, source + steps) for source in range(f...  108 us
    all_gather x1, blocking collectives, shards(): router_piece = lax.all_gather(router_local, 'seq', axis=0, tiled=True)  74.5 us
    psum x1, waiting for transfers between devices, shards(): mixed_full = lax.psum(partial_out, 'tp')  30.6 us
  transfers between devices with their start and end apart: 38, of which 19 were waited for; matrix products, arithmetic and copies ran while one was open for 9% of the time, Pallas kernels for 0%

commit v1 on v0

v1 whole, which is shorter than its diff:
```python
import jax
import jax.numpy as jnp
from jax import lax
from jax.experimental import pallas as pl
from jax.experimental.pallas import tpu as pltpu
from jax.sharding import PartitionSpec as P

HEAD = 128
HALF_WIN = 2048


EPSILON = 1e-05
ROPE_BASE = 50000.0
MASKED = -1e30


def from_behind(value, axis, steps):
    count = lax.axis_size(axis)
    first, last = (max(0, -steps), min(count, count - steps))
    return lax.ppermute(value, axis, [(source, source + steps) for source in range(first, last)])


def from_turned(value, axis, turn):
    count = lax.axis_size(axis)
    return lax.ppermute(value, axis, [((place + turn) % count, place) for place in range(count)])


def rms_scale(row_values, gain_vector):
    mean_square = jnp.mean(row_values * row_values, axis=-1, keepdims=True)
    return row_values * lax.rsqrt(mean_square + EPSILON) * gain_vector


def rotate(rows, cosine, sine_part):
    half_dim = rows.shape[-1] // 2
    first_half = rows[:, :half_dim]
    second_half = rows[:, half_dim:]
    return jnp.concatenate(
        [
            first_half * cosine - second_half * sine_part,
            second_half * cosine + first_half * sine_part,
        ],
        axis=-1,
    )


def length_of(prompt, real_lengths):
    one_hot = prompt[:, None] == jnp.arange(real_lengths.shape[0], dtype=jnp.int32)[None, :]
    return jnp.sum(jnp.where(one_hot, real_lengths[None, :], 0), axis=1)


def prompt_split(slot_ids, slot_len, stagger, prompt_count):
    prompt = jnp.minimum((slot_ids + stagger) // slot_len, prompt_count - 1)
    start = jnp.maximum(prompt * slot_len - stagger, 0)
    return (prompt, slot_ids - start)


def key_rules(query_ids, key_ids, slot_len, stagger, total_slots, real_lengths):
    prompt_count = real_lengths.shape[0]
    key_prompt, key_pos = prompt_split(key_ids, slot_len, stagger, prompt_count)
    query_prompt = prompt_split(query_ids, slot_len, stagger, prompt_count)[0]
    inside = (key_ids >= 0) & (key_ids < total_slots)
    key_live = inside & (key_pos < length_of(key_prompt, real_lengths))
    same_prompt = query_prompt[:, None] == key_prompt[None, :]
    nearby = jnp.abs(query_ids[:, None] - key_ids[None, :]) < HALF_WIN
    return same_prompt & nearby & key_live[None, :]


def parts_of(values, count):
    rest = values
    pieces = []
    for _ in range(count):
        piece = lax.reduce_precision(rest, 8, 7)
        rest = rest - piece
        pieces.append(piece.astype(jnp.bfloat16))
    return pieces


def attend(softmax_state, query_rows, key_rows, value_rows, allowed):
    running_max, denominator, accumulated = softmax_state
    scores = lax.dot_general(
        query_rows, key_rows, (((1,), (1,)), ((), ())), preferred_element_type=jnp.float32
    ) * HEAD ** (-0.5)
    scores = jnp.where(allowed, scores, MASKED)
    new_max = jnp.maximum(running_max, jnp.max(scores, axis=1, keepdims=True))
    rescale = jnp.exp(running_max - new_max)
    weight_tensors = jnp.exp(scores - new_max)
    denominator = denominator * rescale + jnp.sum(weight_tensors, axis=1, keepdims=True)
    high, low = parts_of(weight_tensors, 2)
    accumulated = (
        accumulated * rescale
        + jnp.dot(high, value_rows, preferred_element_type=jnp.float32)
        + jnp.dot(low, value_rows, preferred_element_type=jnp.float32)
    )
    return (new_max, denominator, accumulated)


def order_body(order_ref, gate_ref, up_ref, down_ref, both_ref, last_ref):
    width = gate_ref.shape[2]
    both_ref[0, :, :width] = gate_ref[0].astype(jnp.bfloat16)
    both_ref[0, :, width:] = up_ref[0].astype(jnp.bfloat16)
    last_ref[0] = down_ref[0].astype(jnp.bfloat16)


def order_experts(layout_map, gate, up, down):
    count, rows, width = gate.shape
    source = pl.BlockSpec((1, rows, width), lambda place, order: (order[place], 0, 0))
    return pl.pallas_call(
        order_body,
        grid_spec=pltpu.PrefetchScalarGridSpec(
            num_scalar_prefetch=1,
            grid=(count,),
            in_specs=[source, source, source],
            out_specs=[
                pl.BlockSpec((1, rows, 2 * width), lambda place, order: (place, 0, 0)),
                pl.BlockSpec((1, rows, width), lambda place, order: (place, 0, 0)),
            ],
        ),
        out_shape=[
            jax.ShapeDtypeStruct((count, rows, 2 * width), jnp.bfloat16),
            jax.ShapeDtypeStruct((count, rows, width), jnp.bfloat16),
        ],
        name="order_experts",
    )(layout_map, gate, up, down)


def shards(
    tokens,
    attn_gain,
    mlp_gain,
    w_query,
    w_key,
    w_value,
    w_out,
    sink_logits,
    router,
    expert_gate,
    expert_up,
    expert_down,
    layout_map,
    real_lengths,
    routes,
):
    token_count, model_width = tokens.shape
    seq_count = lax.axis_size("seq")
    tp_count = lax.axis_size("tp")
    expert_count = router.shape[1]
    route_count = routes.shape[1]
    head_count = sink_logits.shape[0]
    col_share = model_width // tp_count
    total_slots = token_count * seq_count
    prompt_count = real_lengths.shape[0]
    slot_len = total_slots // prompt_count
    stagger = token_count // 2
    capacity = max(2, min(token_count, 9 * token_count * route_count // (8 * expert_count)))
    part_count = seq_count // head_count
    part_slots = head_count * token_count
    local_experts = expert_count // seq_count
    seq_place = lax.axis_index("seq")
    tp_place = lax.axis_index("tp")
    part = seq_place // head_count
    head = seq_place % head_count
    groups = [[first + k for k in range(head_count)] for first in range(0, seq_count, head_count)]

    def tp_blocks(value):
        return [value] + [from_turned(value, "tp", turn) for turn in range(1, tp_count)]

    def tp_rows(weights, turn):
        block = (tp_place + turn) % tp_count
        return lax.dynamic_slice_in_dim(weights, block * col_share, col_share, 0)

    offsets = jnp.arange(token_count, dtype=jnp.int32)
    token_index = seq_place * token_count + offsets
    prompt, position = prompt_split(token_index, slot_len, stagger, prompt_count)
    valid_token = position < length_of(prompt, real_lengths)

    normed = rms_scale(tokens.astype(jnp.float32), attn_gain).astype(jnp.bfloat16)
    share = lax.dynamic_slice_in_dim(normed, tp_place * col_share, col_share, 1)
    part_rows = lax.all_to_all(
        jnp.broadcast_to(share[None], (head_count, token_count, col_share)),
        "seq",
        split_axis=0,
        concat_axis=0,
        tiled=True,
        axis_index_groups=groups,
    ).reshape(part_slots, col_share)
    by_head = jnp.concatenate(
        [
            w.reshape(token_rows, head_count, HEAD).transpose(1, 0, 2)
            for w in (w_query, w_key, w_value)
            for token_rows in (w.shape[0],)
        ],
        axis=2,
    ).astype(jnp.bfloat16)
    head_weights = lax.all_to_all(
        jnp.broadcast_to(by_head[None], (part_count, *by_head.shape)).reshape(
            seq_count, *by_head.shape[1:]
        ),
        "seq",
        split_axis=0,
        concat_axis=0,
        tiled=True,
    ).reshape(model_width, 3 * HEAD)
    out_weights = lax.all_gather(w_out.astype(jnp.bfloat16), "seq", axis=1, tiled=True)
    router_full = lax.all_gather(router.astype(jnp.bfloat16), "seq", axis=0, tiled=True)

    both, last = order_experts(layout_map, expert_gate, expert_up, expert_down)
    both, last, head_weights, part_rows = lax.optimization_barrier(
        (both, last, head_weights, part_rows)
    )

    def to_owner(blocks):
        taken = lax.all_to_all(blocks, "seq", split_axis=0, concat_axis=0, tiled=True)
        taken = taken.reshape(seq_count, local_experts, *blocks.shape[1:])
        return jnp.swapaxes(taken, 0, 1).reshape(local_experts, -1, blocks.shape[2])

    server_both = to_owner(both)
    server_down = to_owner(last)

    product = sum(
        jnp.dot(rows, tp_rows(head_weights, turn), preferred_element_type=jnp.float32)
        for turn, rows in enumerate(tp_blocks(part_rows))
    )
    part_ids = part * part_slots + jnp.arange(part_slots, dtype=jnp.int32)
    part_positions = prompt_split(part_ids, slot_len, stagger, prompt_count)[1]
    half_dim = HEAD // 2
    frequency = ROPE_BASE ** (-jnp.arange(half_dim, dtype=jnp.float32) / half_dim)
    angles = part_positions.astype(jnp.float32)[:, None] * frequency[None, :]
    cosine = jnp.cos(angles)
    sine_part = jnp.sin(angles)
    query_rows = rotate(product[:, :HEAD], cosine, sine_part).astype(jnp.bfloat16)
    key_rows = rotate(product[:, HEAD : 2 * HEAD], cosine, sine_part).astype(jnp.bfloat16)
    value_rows = product[:, 2 * HEAD :].astype(jnp.bfloat16)
    sink = lax.dynamic_slice_in_dim(sink_logits, head, 1, 0)

    def start_state(row_count):
        return (
            jnp.broadcast_to(sink[:, None], (row_count, 1)),
            jnp.ones((row_count, 1), jnp.float32),
            jnp.zeros((row_count, HEAD), jnp.float32),
        )

    if part_count == prompt_count:
        rows = jnp.concatenate([query_rows, key_rows, value_rows], axis=1)
        edge = from_behind(rows[part_slots - stagger :], "seq", head_count)
        rows = jnp.concatenate([edge, rows], axis=0)
        row_ids = part * part_slots - stagger + jnp.arange(part_slots + stagger, dtype=jnp.int32)
        allowed = key_rules(row_ids, row_ids, slot_len, stagger, total_slots, real_lengths)
        _, denominator, accumulated = attend(
            start_state(part_slots + stagger),
            rows[:, :HEAD],
            rows[:, HEAD : 2 * HEAD],
            rows[:, 2 * HEAD :],
            allowed,
        )
        mixed = (accumulated / denominator).astype(jnp.bfloat16)
        edge_back = from_behind(mixed[:stagger], "seq", -head_count)
        tail = jnp.where(part < part_count - 1, edge_back, mixed[part_slots:])
        mixed = jnp.concatenate([mixed[stagger:part_slots], tail], axis=0)
    else:
        softmax_state = attend(
            start_state(part_slots),
            query_rows,
            key_rows,
            value_rows,
            key_rules(part_ids, part_ids, slot_len, stagger, total_slots, real_lengths),
        )
        from_below = from_above = jnp.concatenate([key_rows, value_rows], axis=1)
        for turn in range(1, min(part_count - 1, -(-HALF_WIN // part_slots)) + 1):
            from_below = from_behind(from_below, "seq", head_count)
            from_above = from_behind(from_above, "seq", -head_count)
            reach = turn * part_slots
            key_ids = jnp.concatenate([part_ids - reach, part_ids + reach])
            pair = jnp.concatenate([from_below, from_above], axis=0)
            softmax_state = attend(
                softmax_state,
                query_rows,
                pair[:, :HEAD],
                pair[:, HEAD:],
                key_rules(part_ids, key_ids, slot_len, stagger, total_slots, real_lengths),
            )
        _, denominator, accumulated = softmax_state
        mixed = (accumulated / denominator).astype(jnp.bfloat16)
    attention_result = lax.all_to_all(
        mixed.reshape(head_count, token_count, HEAD),
        "seq",
        split_axis=0,
        concat_axis=0,
        tiled=True,
        axis_index_groups=groups,
    )
    attention_result = jnp.swapaxes(attention_result, 0, 1).reshape(token_count, head_count * HEAD)
    partial_out = jnp.dot(attention_result, out_weights, preferred_element_type=jnp.float32)
    if tp_count == 2:
        mixed_full = partial_out + from_turned(partial_out, "tp", 1)
    else:
        mixed_full = lax.psum(partial_out, "tp")
    full_rows = tokens.astype(jnp.float32) + mixed_full
    outgoing = rms_scale(full_rows, mlp_gain).astype(jnp.bfloat16)
    logits = jnp.dot(outgoing, router_full, preferred_element_type=jnp.float32)
    residual = lax.dynamic_slice_in_dim(full_rows, tp_place * col_share, col_share, 1)
    outgoing_share = lax.dynamic_slice_in_dim(outgoing, tp_place * col_share, col_share, 1)

    expert_ids = jnp.arange(expert_count, dtype=jnp.int32)
    chosen = jnp.any(routes[:, :, None] == expert_ids[None, None, :], axis=1)
    live = chosen & valid_token[:, None]
    earlier = (offsets[:, None] > offsets[None, :]).astype(jnp.bfloat16)
    rank_within = jnp.dot(earlier, live.astype(jnp.bfloat16), preferred_element_type=jnp.float32)
    rank_within = jnp.where(live, rank_within, -1.0)
    columns = jnp.arange(expert_count * capacity, dtype=jnp.int32)
    spread = (columns[None, :] // capacity == expert_ids[:, None]).astype(jnp.bfloat16)
    wanted = (columns % capacity).astype(jnp.float32)
    placed = (
        jnp.dot(rank_within.astype(jnp.bfloat16), spread, preferred_element_type=jnp.float32)
        == wanted[None, :]
    )
    buffer = lax.dot_general(
        placed.astype(jnp.bfloat16),
        outgoing_share,
        (((0,), (0,)), ((), ())),
        preferred_element_type=jnp.float32,
    ).astype(jnp.bfloat16)
    block_rows = local_experts * capacity
    received = lax.all_to_all(
        buffer.reshape(seq_count, block_rows, col_share),
        "seq",
        split_axis=0,
        concat_axis=0,
        tiled=True,
    )
    received = jnp.swapaxes(
        received.reshape(seq_count, local_experts, capacity, col_share), 0, 1
    ).reshape(local_experts, seq_count * capacity, col_share)
    hidden_share = expert_gate.shape[2]
    gate_up = sum(
        jnp.einsum(
            "acd,adf->acf",
            rows,
            lax.dynamic_slice_in_dim(
                server_both, (tp_place + turn) % tp_count * col_share, col_share, 1
            ),
            preferred_element_type=jnp.float32,
        )
        for turn, rows in enumerate(tp_blocks(received))
    )
    hidden_state = (jax.nn.silu(gate_up[..., :hidden_share]) * gate_up[..., hidden_share:]).astype(
        jnp.bfloat16
    )

    def down_columns(block):
        return jnp.einsum(
            "acf,adf->acd",
            hidden_state,
            lax.dynamic_slice_in_dim(server_down, block * col_share, col_share, 1),
            preferred_element_type=jnp.float32,
        ).astype(jnp.bfloat16)

    summed = 0.0
    sent = []
    for turn in range(1, tp_count):
        sent.append(from_turned(down_columns((tp_place - turn) % tp_count), "tp", turn))
    own = lax.optimization_barrier(down_columns(tp_place))
    summed = sum([piece.astype(jnp.float32) for piece in sent], own.astype(jnp.float32))
    summed = jnp.swapaxes(
        summed.astype(jnp.bfloat16).reshape(local_experts, seq_count, capacity, col_share), 0, 1
    ).reshape(seq_count, block_rows, col_share)
    returned = lax.all_to_all(
        summed, "seq", split_axis=0, concat_axis=0, tiled=True
    ).reshape(expert_count * capacity, col_share)

    route_logits = jnp.where(chosen, logits, -jnp.inf)
    route_exp = jnp.exp(route_logits - jnp.max(route_logits, axis=1, keepdims=True))
    route_weight = route_exp / jnp.sum(route_exp, axis=1, keepdims=True)
    route_weight = route_weight * valid_token[:, None]
    weight_parts = parts_of(route_weight, 3)
    stacked = jnp.concatenate(
        [
            jnp.where(
                placed, jnp.dot(piece, spread, preferred_element_type=jnp.float32), 0.0
            ).astype(jnp.bfloat16)
            for piece in weight_parts
        ],
        axis=0,
    )
    mixes = jnp.dot(stacked, returned, preferred_element_type=jnp.float32)
    expert_mix = sum(
        mixes[k * token_count : (k + 1) * token_count] for k in range(len(weight_parts))
    )
    return (residual + expert_mix).astype(jnp.bfloat16)


def solution(mesh):
    placed = (
        P("seq", None),
        P(),
        P(),
        P("seq", "tp"),
        P("seq", "tp"),
        P("seq", "tp"),
        P("tp", "seq"),
        P("tp"),
        P("seq", None),
        P(None, "seq", "tp"),
        P(None, "seq", "tp"),
        P(None, "seq", "tp"),
        P(),
        P(),
        P("seq", None),
    )
    return jax.shard_map(
        shards, mesh=mesh, in_specs=placed, out_specs=P("seq", "tp"), check_vma=False
    )
```

time: 1070 us -> 484 us (0.45)
  waiting for transfers between devices: 610 us -> 190 us
  starting transfers between devices: 124 us -> 40.3 us
  other arithmetic: 45.3 us -> 16.7 us
  local copies, waits for them, and re-layouts: 32.1 us -> 5.07 us
  blocking collectives: 187 us -> 167 us
  matrix products: 48.1 us -> 32.9 us
  Pallas kernels: 0 us -> 13 us
    ppermute x32 -> x2, waiting for transfers between devices: 345 us -> 7.06 us  [from_behind(): lax.ppermute(value, axis, [(source, source + steps) for source in range(f...]
    all_gather x1 -> x0, waiting for transfers between devices: 223 us -> none  [shards(): stack_piece = lax.all_gather(stack_local, 'seq', axis=0, tiled=True)]
    ppermute x32 -> x2, starting transfers between devices: 108 us -> 4.96 us  [from_behind(): lax.ppermute(value, axis, [(source, source + steps) for source in range(f...]
    all_gather x1, waiting for transfers between devices: 0.02 us -> 96.6 us  [shards(): lax.all_gather(w_out.astype(jnp.bfloat16), 'seq', axis=1, tiled=True)]
    all_to_all x2 -> x5, waiting for transfers between devices: 0.01 us -> 81.9 us  [the longest x2 35.6 us: to_owner(): lax.all_to_all(blocks, 'seq', split_axis=0, concat_axis=0, tiled=True)]
    psum x1 -> x0, waiting for transfers between devices: 30.6 us -> none  [shards(): mixed_full = lax.psum(partial_out, 'tp')]
    all_to_all x2 -> x5, starting transfers between devices: 15.1 us -> 35.1 us  [the longest x1 9.83 us: shards(): lax.all_to_all(summed, 'seq', split_axis=0, concat_axis=0, tiled=True)]
    all_to_all x1 -> x2, blocking collectives: 112 us -> 93.1 us  [the longest x1 75.2 us: shards(): lax.all_to_all(buffer.reshape(seq_count, block_rows, col_share), 'seq', s...]
  transfers between devices with their start and end apart: 38 -> 12, of which waited for: 19 -> 11; matrix products, arithmetic and copies ran while one was open for 9% -> 8% of each run, Pallas kernels for 0% -> 3%
where the time goes in v1:
time: 484 us; the launch traced here: 480 us
  waiting for transfers between devices  190 us (39%)
  blocking collectives  167 us (35%)
  starting transfers between devices  40.3 us (8%)
  matrix products  32.9 us (7%)
  other arithmetic  16.7 us (3%)
  between operations  14.1 us (3%)
  Pallas kernels  13 us (3%)
  local copies, waits for them, and re-layouts  5.07 us (1%)
    all_gather x1, waiting for transfers between devices, shards(): lax.all_gather(w_out.astype(jnp.bfloat16), 'seq', axis=1, tiled=True)  96.6 us
    all_to_all x1, blocking collectives, shards(): lax.all_to_all(buffer.reshape(seq_count, block_rows, col_share), 'seq', s...  75.2 us
    all_gather x1, blocking collectives, shards(): lax.all_gather(router.astype(jnp.bfloat16), 'seq', axis=0, tiled=True)  74 us
    all_to_all x2, waiting for transfers between devices, to_owner(): lax.all_to_all(blocks, 'seq', split_axis=0, concat_axis=0, tiled=True)  35.6 us
    all_to_all x1, waiting for transfers between devices, shards(): lax.all_to_all(jnp.broadcast_to(by_head[None], (part_count, *by_head.shap...  33.7 us
    all_to_all x1, blocking collectives, shards(): lax.all_to_all(mixed.reshape(head_count, token_count, HEAD), 'seq', split...  17.9 us
    pallas_call x1, Pallas kernels, order_experts(): pl.pallas_call(order_body, grid_spec=pltpu.PrefetchScalarGridSpec(num_sca...  13 us
    all_to_all x1, waiting for transfers between devices, shards(): lax.all_to_all(jnp.broadcast_to(share[None], (head_count, token_count, co...  12.6 us
  transfers between devices with their start and end apart: 12, of which 11 were waited for; matrix products, arithmetic and copies ran while one was open for 8% of the time, Pallas kernels for 3%

profile of v1, /device:TPU:0, one launch (start us, length us, event | category | flops | bytes accessed | tf_op | source)
XLA Modules:
  0.0 479.6 jit_solution(689247995225189317)
XLA Ops:
  6.5 1.1 convert_bitcast_fusion
  7.7 1.1 convert_bitcast_fusion.1
  9.0 0.1 pad_maximum_fusion
  9.1 0.1 copy.21
  9.2 1.4 broadcast_in_dim.53
  10.6 8.4 %all-to-all-start = ((bf16[16,128,384]{2,1,0:T(8,128)(2,1)}), bf16[16,128,384]{2,1,0:T(8,128)(2,1)S(1)}, u32[]{:S(2)}, u32[]{:S(2)}) async-start(bf16[16,128,384]{2,1,0:T(8,128)(2,1)} %bitcast.4), calls=%async_computation | async-start | bytes 3145728 | tf_op jit(solution)/shard_map/all_to_all | solution.py:194
  19.2 0.2 multiply_reduce_fusion.1
  19.4 0.1 fusion.43
  19.6 33.7 %all-to-all-done = bf16[16,128,384]{2,1,0:T(8,128)(2,1)S(1)} async-done(((bf16[16,128,384]{2,1,0:T(8,128)(2,1)}), bf16[16,128,384]{2,1,0:T(8,128)(2,1)S(1)}, u32[]{:S(2)}, u32[]{:S(2)}) %all-to-all-start) | async-done | bytes 1572896 | tf_op jit(solution)/shard_map/all_to_all | solution.py:194
  53.3 1.6 broadcast_in_dim.54
  54.9 7.5 %all-to-all-start.1 = ((bf16[8,128,1024]{2,1,0:T(8,128)(2,1)}), bf16[8,128,1024]{2,1,0:T(8,128)(2,1)}, u32[]{:S(2)}, u32[]{:S(2)}) async-start(bf16[8,128,1024]{2,1,0:T(8,128)(2,1)} %broadcast_in_dim.54), calls=%async_computation.1 | async-start | bytes 4194304 | tf_op jit(solution)/shard_map/all_to_all | solution.py:178
  62.4 13.0 %order_experts.1 = (bf16[16,128,1024]{2,1,0:T(8,128)(2,1)}, bf16[16,128,512]{2,1,0:T(8,128)(2,1)}) custom-call(s32[16]{0:T(128)} %order_ref.1, f32[16,128,512]{2,1,0:T(8,128)} %gate_ref.1, f32[16,128,512]{2,1,0:T(8,128)} %up_ref.1, f32[16,128,512]{2,1,0:T(8,128)} %down_ref.1), custom_call_target="tpu_custom_call" | custom-call | tf_op jit(solution)/shard_map/order_experts/pallas_call | solution.py:107
  75.4 12.6 %all-to-all-done.1 = bf16[8,128,1024]{2,1,0:T(8,128)(2,1)} async-done(((bf16[8,128,1024]{2,1,0:T(8,128)(2,1)}), bf16[8,128,1024]{2,1,0:T(8,128)(2,1)}, u32[]{:S(2)}, u32[]{:S(2)}) %all-to-all-start.1) | async-done | bytes 2097184 | tf_op jit(solution)/shard_map/all_to_all | solution.py:178
  88.0 0.7 convert_element_type.116
  88.9 2.6 fusion.38
  91.5 0.9 collective-permute-done
  92.5 2.6 convolution_add_fusion.1
  95.1 1.1 fusion.69
  96.2 1.1 fusion.68
  97.4 1.1 fusion.67
  98.5 1.1 fusion.66
  99.8 3.7 collective-permute-start.1
  103.5 0.6 dynamic_slice.30
  104.2 1.5 collective-permute-done.1
  105.7 2.7 fusion.127
  108.4 0.6 broadcast_maximum_fusion
  109.0 0.7 fusion.5
  109.7 0.6 fusion.98
  110.4 1.2 fusion.11
  111.6 1.2 fusion.16
  112.9 1.3 collective-permute-start.2
  114.2 5.5 %collective-permute-done.2 = bf16[64,128]{1,0:T(8,128)(2,1)S(1)} collective-permute-done((bf16[64,128]{1,0:T(8,128)(2,1)S(1)}, bf16[64,128]{1,0:T(8,128)(2,1)S(1)}, u32[]{:S(2)}, u32[]{:S(2)}) %collective-permute-start.2) | collective-permute-done | bytes 16416 | tf_op jit(solution)/shard_map/ppermute | solution.py:20
  119.8 0.2 copy.22
  119.9 17.9 %all_to_all.35 = bf16[8,128,128]{1,2,0:T(8,128)(2,1)S(1)} all-to-all(bf16[8,128,128]{1,2,0:T(8,128)(2,1)S(1)} %copy.22), channel_id=1, replica_groups={{0,2,4,6,8,10,12,14},{16,18,20,22,24,26,28,30},{1,3,5,7,9,11,13,15},{17..., dimensions={0} | all-to-all | bytes 524288 | tf_op jit(solution)/shard_map/all_to_all | solution.py:283
  137.8 4.6 all-to-all-start.4
  142.4 96.6 %all-gather.2.cloned.1.call-done = bf16[1024,2048]{1,0:T(8,128)(2,1)} async-done(((bf16[1024,128]{1,0:T(8,128)(2,1)}), bf16[1024,2048]{1,0:T(8,128)(2,1)}) %all-gather.2.cloned.1.call-update) | async-done | bytes 4194320 | tf_op jit(solution)/shard_map/all_gather | solution.py:203
  239.0 2.9 fusion.129
  242.2 0.5 fusion.126
  242.7 0.4 convolution_compare_fusion
  243.2 1.6 collective-permute-done.3
  244.8 1.5 multiply_reduce_fusion
  246.3 0.2 multiply_convert_fusion
  246.5 0.8 copy-done.1
  247.3 0.8 convolution_convert_fusion.2
  248.1 4.2 all-to-all-done.4
  252.3 75.2 %all_to_all.36 = bf16[16,72,1024]{2,1,0:T(8,128)(2,1)} all-to-all(bf16[16,72,1024]{2,1,0:T(8,128)(2,1)S(1)} %bitcast.65), channel_id=1, replica_groups=mesh['seq'=16,'tp'=2] {'seq'}, dimensions={0} | all-to-all | bytes 4718592 | tf_op jit(solution)/shard_map/all_to_all | solution.py:323
  327.6 4.8 all-to-all-start.5
  332.5 4.2 fusion.20
  336.7 0.4 collective-permute-done.4
  337.1 4.9 %add_bitcast_fusion = f32[1,1152,1024]{2,1,0:T(8,128)S(1)} fusion(f32[1152,1024]{1,0:T(8,128)S(1)} %fusion.20, bf16[1,1152,1024]{2,1,0:T(8,128)(2,1)} %collective-permute-done.4, bf16[1,2048,1024]{2,1,0:T(8,128)(2,1)} %bitcast.12, s32[]{:T(128)S(6)} %select_n.160), kind=kOutput, calls=%fused_computation.11 | convolution fusion | flops 2417098752 | bytes 13893636 | tf_op jit(solution)/shard_map/acd,adf->acf/dot_general | solution.py:335
  342.0 0.8 fusion.17
  342.8 31.4 %all-to-all-done.5 = bf16[16,128,512]{2,1,0:T(8,128)(2,1)} async-done(((bf16[16,128,512]{2,1,0:T(8,128)(2,1)}), bf16[16,128,512]{2,1,0:T(8,128)(2,1)}, u32[]{:S(2)}, u32[]{:S(2)}) %all-to-all-start.5) | async-done | bytes 2097184 | tf_op jit(solution)/shard_map/all_to_all | solution.py:212
  374.2 2.6 fusion.7
  377.0 2.7 fusion.6
  379.6 1.9 collective-permute-done.5
  381.5 2.5 add_convert_fusion
  384.0 9.8 %all-to-all-start.6 = ((bf16[16,72,1024]{2,1,0:T(8,128)(2,1)}), bf16[16,72,1024]{2,1,0:T(8,128)(2,1)}, u32[]{:S(2)}, u32[]{:S(2)}) async-start(bf16[16,72,1024]{2,1,0:T(8,128)(2,1)} %bitcast.24), calls=%async_computation.6 | async-start | bytes 4718592 | tf_op jit(solution)/shard_map/all_to_all | solution.py:366
  393.9 74.0 %all_gather.7 = bf16[2048,16]{0,1:T(8,128)(2,1)S(1)} all-gather(bf16[128,16]{0,1:T(8,128)(2,1)S(1)} %convert_element_type.120), channel_id=1, replica_groups=mesh['seq'=16,'tp'=2] {'seq'}, dimensions={0}, use_global_device_ids=true | all-gather | bytes 69632 | tf_op jit(solution)/shard_map/all_gather | solution.py:204
  467.9 0.3 fusion.128
  468.2 0.3 fusion.15
  468.5 0.3 fusion.14
  468.8 0.3 fusion.13
  469.1 2.8 fusion.31
  471.9 0.9 fusion.41
  (65 shorter events, 1.1 us)
Async XLA Ops:
  6.5 2.3 copy-start.4
  9.2 9.9 %copy-start = (bf16[128,2048]{1,0:T(8,128)(2,1)S(1)}, bf16[128,2048]{1,0:T(8,128)(2,1)}, u32[]{:S(2)}) copy-start(bf16[128,2048]{1,0:T(8,128)(2,1)} %param.15) | copy-start | bytes 1572868
  10.6 8.6 %copy-start.14 = (f32[2048]{0:T(1024)S(1)}, f32[2048]{0:T(1024)}, u32[]{:S(2)}) copy-start(f32[2048]{0:T(1024)} %param.16) | copy-start | bytes 24580
  10.6 42.6 %all-to-all-start = ((bf16[16,128,384]{2,1,0:T(8,128)(2,1)}), bf16[16,128,384]{2,1,0:T(8,128)(2,1)S(1)}, u32[]{:S(2)}, u32[]{:S(2)}) async-start(bf16[16,128,384]{2,1,0:T(8,128)(2,1)} %bitcast.4), calls=%async_computation | async-start | bytes 3145728 | tf_op jit(solution)/shard_map/all_to_all | solution.py:194
  54.9 33.1 %all-to-all-start.1 = ((bf16[8,128,1024]{2,1,0:T(8,128)(2,1)}), bf16[8,128,1024]{2,1,0:T(8,128)(2,1)}, u32[]{:S(2)}, u32[]{:S(2)}) async-start(bf16[8,128,1024]{2,1,0:T(8,128)(2,1)} %broadcast_in_dim.54), calls=%async_computation.1 | async-start | bytes 4194304 | tf_op jit(solution)/shard_map/all_to_all | solution.py:178
  62.3 25.6 %copy-start.5 = (f32[1024,128]{1,0:T(8,128)S(1)}, f32[1024,128]{1,0:T(8,128)}, u32[]{:S(2)}) copy-start(f32[1024,128]{1,0:T(8,128)} %param.21) | copy-start | bytes 1572868
  62.3 26.5 %copy-start.15 = (s32[2]{0:T(128)S(1)}, s32[2]{0:T(128)}, u32[]{:S(2)}) copy-start(s32[2]{0:T(128)} %param.28) | copy-start | bytes 28
  62.3 176.6 %all-gather.2.cloned.1.call-start = ((), (), s32[]{:S(2)}) async-start(), calls=%async_computation.7 | async-start | bytes 4456448 | tf_op jit(solution)/shard_map/all_gather | solution.py:203
  88.0 4.5 collective-permute-start
  95.1 8.5 %copy-start.16 = (f32[8]{0:T(128)S(1)}, f32[8]{0:T(128)}, u32[]{:S(2)}) copy-start(f32[8]{0:T(128)} %param.22) | copy-start | bytes 100
  99.8 5.9 %collective-permute-start.1 = (bf16[64,384]{0,1:T(8,128)(2,1)S(1)}, bf16[64,384]{0,1:T(8,128)(2,1)S(1)}, u32[]{:S(2)}, u32[]{:S(2)}) collective-permute-start(bf16[64,384]{0,1:T(8,128)(2,1)S(1)} %slice.80), channel_id=1, source_target_pairs={{0,16},{2,18},{4,20},{6,22},{8,24},{10,26},{12,28},{14,30},{1,17},... | collective-permute-start | bytes 147464 | tf_op jit(solution)/shard_map/ppermute | solution.py:20
  112.9 6.9 %collective-permute-start.2 = (bf16[64,128]{1,0:T(8,128)(2,1)S(1)}, bf16[64,128]{1,0:T(8,128)(2,1)S(1)}, u32[]{:S(2)}, u32[]{:S(2)}) collective-permute-start(bf16[64,128]{1,0:T(8,128)(2,1)S(1)} %slice.86), channel_id=1, source_target_pairs={{16,0},{18,2},{20,4},{22,6},{24,8},{26,10},{28,12},{30,14},{17,1},... | collective-permute-start | bytes 49160 | tf_op jit(solution)/shard_map/ppermute | solution.py:20
  137.8 114.5 %all-to-all-start.4 = ((bf16[16,128,1024]{2,1,0:T(8,128)(2,1)}), bf16[16,128,1024]{2,1,0:T(8,128)(2,1)}, u32[]{:S(2)}, u32[]{:S(2)}) async-start(bf16[16,128,1024]{2,1,0:T(8,128)(2,1)} %get-tuple-element.15), calls=%async_computation.4 | async-start | bytes 8388608 | tf_op jit(solution)/shard_map/all_to_all | solution.py:212
  239.0 3.1 copy-start.13
  241.9 2.9 collective-permute-start.3
  242.1 4.2 copy-start.6
  242.1 4.3 copy-start.8
  242.1 4.2 copy-start.9
  246.5 0.8 copy-start.1
  327.6 4.8 %copy-start.3 = (bf16[16,72,1024]{2,1,0:T(8,128)(2,1)S(1)}, bf16[16,72,1024]{2,1,0:T(8,128)(2,1)}, u32[]{:S(2)}) copy-start(bf16[16,72,1024]{2,1,0:T(8,128)(2,1)} %all_to_all.36) | copy-start | bytes 7077892
  327.6 46.7 %all-to-all-start.5 = ((bf16[16,128,512]{2,1,0:T(8,128)(2,1)}), bf16[16,128,512]{2,1,0:T(8,128)(2,1)}, u32[]{:S(2)}, u32[]{:S(2)}) async-start(bf16[16,128,512]{2,1,0:T(8,128)(2,1)} %get-tuple-element.16), calls=%async_computation.5 | async-start | bytes 4194304 | tf_op jit(solution)/shard_map/all_to_all | solution.py:212
  332.4 4.7 collective-permute-start.4
  376.9 4.6 collective-permute-start.5
  384.0 9.9 %copy-start.11 = (f32[128,16]{0,1:T(8,128)S(1)}, f32[128,16]{0,1:T(8,128)}, u32[]{:S(2)}) copy-start(f32[128,16]{0,1:T(8,128)} %param.23) | copy-start | bytes 24580
  384.0 83.9 %copy-start.2 = (bf16[128,2048]{1,0:T(8,128)(2,1)S(1)}, bf16[128,2048]{1,0:T(8,128)(2,1)}, u32[]{:S(2)}) copy-start(bf16[128,2048]{1,0:T(8,128)(2,1)} %copy-done.1) | copy-start | bytes 1572868
  384.0 83.9 %copy-start.10 = (pred[128,16]{0,1:T(8,128)(4,1)S(1)}, pred[128,16]{0,1:T(8,128)(4,1)}, u32[]{:S(2)}) copy-start(pred[128,16]{0,1:T(8,128)(4,1)} %copy-done.9) | copy-start | bytes 6148
  384.0 84.2 %copy-start.7 = (s32[1152]{0:T(1024)S(1)}, s32[1152]{0:T(1024)}, u32[]{:S(2)}) copy-start(s32[1152]{0:T(1024)} %copy-done.6) | copy-start | bytes 13828
  384.0 84.2 %copy-start.12 = (f32[128]{0:T(128)S(1)}, f32[128]{0:T(128)}, u32[]{:S(2)}) copy-start(f32[128]{0:T(128)} %get-tuple-element.17) | copy-start | bytes 1540
  384.0 85.0 %all-to-all-start.6 = ((bf16[16,72,1024]{2,1,0:T(8,128)(2,1)}), bf16[16,72,1024]{2,1,0:T(8,128)(2,1)}, u32[]{:S(2)}, u32[]{:S(2)}) async-start(bf16[16,72,1024]{2,1,0:T(8,128)(2,1)} %bitcast.24), calls=%async_computation.6 | async-start | bytes 4718592 | tf_op jit(solution)/shard_map/all_to_all | solution.py:366
Sparse Core Ops, SparseCore 0:
  88.8 150.1 all-gather.1

commit v2 on v1

--- a/solution.py
+++ b/solution.py
@@ -23,6 +23,27 @@
 def from_turned(value, axis, turn):
     count = lax.axis_size(axis)
     return lax.ppermute(value, axis, [((place + turn) % count, place) for place in range(count)])
+
+
+def swapped(value, axis, mask):
+    count = lax.axis_size(axis)
+    return lax.ppermute(value, axis, [(place, place ^ mask) for place in range(count)])
+
+
+def doubled(value, masks, axis):
+    turns = [0]
+    for mask in masks:
+        value = jnp.concatenate([value, swapped(value, "seq", mask)], axis=axis)
+        turns = turns + [turn ^ mask for turn in turns]
+    return (value, turns)
+
+
+def masks_below(count, least=1):
+    masks = []
+    while count > least:
+        count //= 2
+        masks.append(count)
+    return masks
 
 
 def rms_scale(row_values, gain_vector):
@@ -159,7 +180,6 @@
     tp_place = lax.axis_index("tp")
     part = seq_place // head_count
     head = seq_place % head_count
-    groups = [[first + k for k in range(head_count)] for first in range(0, seq_count, head_count)]
 
     def tp_blocks(value):
         return [value] + [from_turned(value, "tp", turn) for turn in range(1, tp_count)]
@@ -169,25 +189,14 @@
         return lax.dynamic_slice_in_dim(weights, block * col_share, col_share, 0)
 
     offsets = jnp.arange(token_count, dtype=jnp.int32)
-    token_index = seq_place * token_count + offsets
-    prompt, position = prompt_split(token_index, slot_len, stagger, prompt_count)
-    valid_token = position < length_of(prompt, real_lengths)
-
-    normed = rms_scale(tokens.astype(jnp.float32), attn_gain).astype(jnp.bfloat16)
-    share = lax.dynamic_slice_in_dim(normed, tp_place * col_share, col_share, 1)
-    part_rows = lax.all_to_all(
-        jnp.broadcast_to(share[None], (head_count, token_count, col_share)),
-        "seq",
-        split_axis=0,
-        concat_axis=0,
-        tiled=True,
-        axis_index_groups=groups,
-    ).reshape(part_slots, col_share)
+    turns = jnp.arange(head_count, dtype=jnp.int32)
+    group_masks = masks_below(head_count)
+    part_masks = masks_below(seq_count, head_count)
+
     by_head = jnp.concatenate(
         [
-            w.reshape(token_rows, head_count, HEAD).transpose(1, 0, 2)
+            w.reshape(w.shape[0], head_count, HEAD).transpose(1, 0, 2)
             for w in (w_query, w_key, w_value)
-            for token_rows in (w.shape[0],)
         ],
         axis=2,
     ).astype(jnp.bfloat16)
@@ -200,13 +209,24 @@
         concat_axis=0,
         tiled=True,
     ).reshape(model_width, 3 * HEAD)
-    out_weights = lax.all_gather(w_out.astype(jnp.bfloat16), "seq", axis=1, tiled=True)
-    router_full = lax.all_gather(router.astype(jnp.bfloat16), "seq", axis=0, tiled=True)
+
+    normed = rms_scale(tokens.astype(jnp.float32), attn_gain).astype(jnp.bfloat16)
+    share = lax.dynamic_slice_in_dim(normed, tp_place * col_share, col_share, 1)
+    first_rows, first_turns = doubled(share[None], group_masks[:1], 0)
+    pieces = []
+    for piece, masks in (
+        (first_rows[:, :, : col_share // 2], group_masks[1:]),
+        (first_rows[:, :, col_share // 2 :], group_masks[1:][::-1]),
+    ):
+        rows, row_turns = doubled(piece, masks, 0)
+        known = []
+        for turn in row_turns:
+            known.extend([first ^ turn for first in first_turns])
+        pieces.append(jnp.concatenate([rows[known.index(m)] for m in range(head_count)], axis=0))
+    part_rows = jnp.concatenate(pieces, axis=1)
 
     both, last = order_experts(layout_map, expert_gate, expert_up, expert_down)
-    both, last, head_weights, part_rows = lax.optimization_barrier(
-        (both, last, head_weights, part_rows)
-    )
+    both, last, head_weights = lax.optimization_barrier((both, last, head_weights))
 
     def to_owner(blocks):
         taken = lax.all_to_all(blocks, "seq", split_axis=0, concat_axis=0, tiled=True)
@@ -216,11 +236,49 @@
     server_both = to_owner(both)
     server_down = to_owner(last)
 
+    out_local = jnp.concatenate([w_out, router.T], axis=0).astype(jnp.bfloat16)
+    out_all, out_turns = doubled(out_local, masks_below(seq_count), 1)
+    width = out_local.shape[1]
+    bits = len(out_turns).bit_length() - 1
+
+    def in_order(value):
+        blocks = []
+        for place in range(seq_count):
+            turn = seq_place ^ place
+            index = sum(((turn >> k) & 1) << (bits - 1 - k) for k in range(bits))
+            blocks.append(lax.dynamic_slice_in_dim(value, index * width, width, 1))
+        return jnp.concatenate(blocks, axis=1)
+
+    all_routes, part_turns = doubled(routes[None], part_masks, 0)
+    expert_ids = jnp.arange(expert_count, dtype=jnp.int32)
+    block_rows = local_experts * capacity
+    columns = jnp.arange(head_count * block_rows, dtype=jnp.int32)
+    column_owner = part * head_count + (head ^ (columns // block_rows))
+    column_expert = column_owner * local_experts + columns // capacity % local_experts
+    spread = (column_expert[None, :] == expert_ids[:, None]).astype(jnp.bfloat16)
+    wanted = (columns % capacity).astype(jnp.float32)
+    earlier = (offsets[:, None] > offsets[None, :]).astype(jnp.bfloat16)
+
+    def routing(turn, own_routes):
+        ids = (seq_place ^ turn) * token_count + offsets
+        prompt, position = prompt_split(ids, slot_len, stagger, prompt_count)
+        valid_token = position < length_of(prompt, real_lengths)
+        chosen = jnp.any(own_routes[:, :, None] == expert_ids[None, None, :], axis=1)
+        live = chosen & valid_token[:, None]
+        rank = jnp.dot(earlier, live.astype(jnp.bfloat16), preferred_element_type=jnp.float32)
+        rank = jnp.where(live, rank, -1.0).astype(jnp.bfloat16)
+        placed = jnp.dot(rank, spread, preferred_element_type=jnp.float32) == wanted[None, :]
+        return (chosen, valid_token, placed)
+
+    routings = [routing(turn, all_routes[k]) for k, turn in enumerate(part_turns)]
+    chosen, valid_token, _ = routings[0]
+
     product = sum(
         jnp.dot(rows, tp_rows(head_weights, turn), preferred_element_type=jnp.float32)
         for turn, rows in enumerate(tp_blocks(part_rows))
     )
-    part_ids = part * part_slots + jnp.arange(part_slots, dtype=jnp.int32)
+    part_ids = (part * head_count + (head ^ turns))[:, None] * token_count + offsets[None, :]
+    part_ids = part_ids.reshape(-1)
     part_positions = prompt_split(part_ids, slot_len, stagger, prompt_count)[1]
     half_dim = HEAD // 2
     frequency = ROPE_BASE ** (-jnp.arange(half_dim, dtype=jnp.float32) / half_dim)
@@ -241,9 +299,13 @@
 
     if part_count == prompt_count:
         rows = jnp.concatenate([query_rows, key_rows, value_rows], axis=1)
-        edge = from_behind(rows[part_slots - stagger :], "seq", head_count)
-        rows = jnp.concatenate([edge, rows], axis=0)
-        row_ids = part * part_slots - stagger + jnp.arange(part_slots + stagger, dtype=jnp.int32)
+        edge_start = (head ^ (head_count - 1)) * token_count + token_count - stagger
+        edge = from_behind(
+            lax.dynamic_slice_in_dim(rows, edge_start, stagger, 0), "seq", head_count
+        )
+        rows = jnp.concatenate([rows, edge], axis=0)
+        edge_ids = part * part_slots - stagger + jnp.arange(stagger, dtype=jnp.int32)
+        row_ids = jnp.concatenate([part_ids, edge_ids])
         allowed = key_rules(row_ids, row_ids, slot_len, stagger, total_slots, real_lengths)
         _, denominator, accumulated = attend(
             start_state(part_slots + stagger),
@@ -253,9 +315,12 @@
             allowed,
         )
         mixed = (accumulated / denominator).astype(jnp.bfloat16)
-        edge_back = from_behind(mixed[:stagger], "seq", -head_count)
-        tail = jnp.where(part < part_count - 1, edge_back, mixed[part_slots:])
-        mixed = jnp.concatenate([mixed[stagger:part_slots], tail], axis=0)
+        edge_back = from_behind(mixed[part_slots:], "seq", -head_count)
+        mixed = mixed[:part_slots]
+        kept = lax.dynamic_slice_in_dim(mixed, edge_start, stagger, 0)
+        mixed = lax.dynamic_update_slice_in_dim(
+            mixed, jnp.where(part < part_count - 1, edge_back, kept), edge_start, 0
+        )
     else:
         softmax_state = attend(
             start_state(part_slots),
@@ -280,56 +345,48 @@
             )
         _, denominator, accumulated = softmax_state
         mixed = (accumulated / denominator).astype(jnp.bfloat16)
-    attention_result = lax.all_to_all(
-        mixed.reshape(head_count, token_count, HEAD),
-        "seq",
-        split_axis=0,
-        concat_axis=0,
-        tiled=True,
-        axis_index_groups=groups,
-    )
-    attention_result = jnp.swapaxes(attention_result, 0, 1).reshape(token_count, head_count * HEAD)
-    partial_out = jnp.dot(attention_result, out_weights, preferred_element_type=jnp.float32)
+    blocks = mixed.reshape(head_count, token_count, HEAD)
+    heads = jnp.stack(
+        [blocks[0]] + [swapped(blocks[m], "seq", m) for m in range(1, head_count)]
+    )
+    attention_result = jnp.concatenate(
+        [lax.dynamic_index_in_dim(heads, head ^ h, 0, keepdims=False) for h in range(head_count)],
+        axis=1,
+    )
+    partial_out = jnp.dot(
+        attention_result, out_all[: head_count * HEAD], preferred_element_type=jnp.float32
+    )
     if tp_count == 2:
         mixed_full = partial_out + from_turned(partial_out, "tp", 1)
     else:
         mixed_full = lax.psum(partial_out, "tp")
-    full_rows = tokens.astype(jnp.float32) + mixed_full
+    full_rows = tokens.astype(jnp.float32) + in_order(mixed_full)
     outgoing = rms_scale(full_rows, mlp_gain).astype(jnp.bfloat16)
-    logits = jnp.dot(outgoing, router_full, preferred_element_type=jnp.float32)
     residual = lax.dynamic_slice_in_dim(full_rows, tp_place * col_share, col_share, 1)
     outgoing_share = lax.dynamic_slice_in_dim(outgoing, tp_place * col_share, col_share, 1)
 
-    expert_ids = jnp.arange(expert_count, dtype=jnp.int32)
-    chosen = jnp.any(routes[:, :, None] == expert_ids[None, None, :], axis=1)
-    live = chosen & valid_token[:, None]
-    earlier = (offsets[:, None] > offsets[None, :]).astype(jnp.bfloat16)
-    rank_within = jnp.dot(earlier, live.astype(jnp.bfloat16), preferred_element_type=jnp.float32)
-    rank_within = jnp.where(live, rank_within, -1.0)
-    columns = jnp.arange(expert_count * capacity, dtype=jnp.int32)
-    spread = (columns[None, :] // capacity == expert_ids[:, None]).astype(jnp.bfloat16)
-    wanted = (columns % capacity).astype(jnp.float32)
-    placed = (
-        jnp.dot(rank_within.astype(jnp.bfloat16), spread, preferred_element_type=jnp.float32)
-        == wanted[None, :]
-    )
-    buffer = lax.dot_general(
-        placed.astype(jnp.bfloat16),
-        outgoing_share,
-        (((0,), (0,)), ((), ())),
-        preferred_element_type=jnp.float32,
-    ).astype(jnp.bfloat16)
-    block_rows = local_experts * capacity
-    received = lax.all_to_all(
-        buffer.reshape(seq_count, block_rows, col_share),
-        "seq",
-        split_axis=0,
-        concat_axis=0,
-        tiled=True,
-    )
-    received = jnp.swapaxes(
-        received.reshape(seq_count, local_experts, capacity, col_share), 0, 1
-    ).reshape(local_experts, seq_count * capacity, col_share)
+    all_rows, _ = doubled(outgoing_share[None], part_masks, 0)
+    buffer = jnp.stack(
+        [
+            lax.dot_general(
+                placed.astype(jnp.bfloat16),
+                all_rows[k],
+                (((0,), (0,)), ((), ())),
+                preferred_element_type=jnp.float32,
+            )
+            .astype(jnp.bfloat16)
+            .reshape(head_count, block_rows, col_share)
+            for k, (_, _, placed) in enumerate(routings)
+        ],
+        axis=1,
+    )
+    received = jnp.stack(
+        [buffer[0]] + [swapped(buffer[m], "seq", m) for m in range(1, head_count)]
+    )
+    row_count = head_count * part_count * capacity
+    received = jnp.moveaxis(
+        received.reshape(head_count, part_count, local_experts, capacity, col_share), 2, 0
+    ).reshape(local_experts, row_count, col_share)
     hidden_share = expert_gate.shape[2]
     gate_up = sum(
         jnp.einsum(
@@ -354,38 +411,58 @@
             preferred_element_type=jnp.float32,
         ).astype(jnp.bfloat16)
 
-    summed = 0.0
-    sent = []
-    for turn in range(1, tp_count):
-        sent.append(from_turned(down_columns((tp_place - turn) % tp_count), "tp", turn))
+    sent = [
+        from_turned(down_columns((tp_place - turn) % tp_count), "tp", turn)
+        for turn in range(1, tp_count)
+    ]
     own = lax.optimization_barrier(down_columns(tp_place))
     summed = sum([piece.astype(jnp.float32) for piece in sent], own.astype(jnp.float32))
-    summed = jnp.swapaxes(
-        summed.astype(jnp.bfloat16).reshape(local_experts, seq_count, capacity, col_share), 0, 1
-    ).reshape(seq_count, block_rows, col_share)
-    returned = lax.all_to_all(
-        summed, "seq", split_axis=0, concat_axis=0, tiled=True
-    ).reshape(expert_count * capacity, col_share)
-
+    summed = jnp.moveaxis(
+        summed.astype(jnp.bfloat16).reshape(
+            local_experts, head_count, part_count, capacity, col_share
+        ),
+        0,
+        2,
+    ).reshape(head_count, part_count, block_rows, col_share)
+
+    logits = lax.dot_general(
+        outgoing,
+        in_order(out_all[head_count * HEAD :]),
+        (((1,), (1,)), ((), ())),
+        preferred_element_type=jnp.float32,
+    )
     route_logits = jnp.where(chosen, logits, -jnp.inf)
     route_exp = jnp.exp(route_logits - jnp.max(route_logits, axis=1, keepdims=True))
     route_weight = route_exp / jnp.sum(route_exp, axis=1, keepdims=True)
     route_weight = route_weight * valid_token[:, None]
-    weight_parts = parts_of(route_weight, 3)
-    stacked = jnp.concatenate(
-        [
-            jnp.where(
-                placed, jnp.dot(piece, spread, preferred_element_type=jnp.float32), 0.0
-            ).astype(jnp.bfloat16)
-            for piece in weight_parts
-        ],
-        axis=0,
-    )
-    mixes = jnp.dot(stacked, returned, preferred_element_type=jnp.float32)
-    expert_mix = sum(
-        mixes[k * token_count : (k + 1) * token_count] for k in range(len(weight_parts))
-    )
-    return (residual + expert_mix).astype(jnp.bfloat16)
+    all_weights, _ = doubled(route_weight[None], part_masks, 0)
+
+    def weighted(k, rows):
+        placed = routings[k][2]
+        stacked = jnp.concatenate(
+            [
+                jnp.where(
+                    placed, jnp.dot(piece, spread, preferred_element_type=jnp.float32), 0.0
+                ).astype(jnp.bfloat16)
+                for piece in parts_of(all_weights[k], 3)
+            ],
+            axis=0,
+        )
+        mixes = jnp.dot(stacked, rows, preferred_element_type=jnp.float32)
+        return sum(mixes[k * token_count : (k + 1) * token_count] for k in range(3))
+
+    def back(blocks):
+        return jnp.stack(
+            [blocks[0]] + [swapped(blocks[m], "seq", m) for m in range(1, head_count)]
+        )
+
+    others = back(summed[:, 1:])
+    expert_mix = 0.0
+    for k, turn in enumerate(part_turns[1:]):
+        mix = weighted(k + 1, others[:, k].reshape(-1, col_share))
+        expert_mix = expert_mix + swapped(mix, "seq", turn)
+    own_mix = weighted(0, back(summed[:, 0]).reshape(-1, col_share))
+    return (residual + (expert_mix + own_mix)).astype(jnp.bfloat16)
 
 
 def solution(mesh):

time: 484 us -> 432 us (0.89)
  blocking collectives: 167 us -> 0 us
  starting transfers between devices: 40.3 us -> 112 us
  waiting for transfers between devices: 190 us -> 234 us
  between operations: 14.1 us -> 1.44 us
  local copies, waits for them, and re-layouts: 5.07 us -> 16.2 us
    ppermute x0 -> x41, waiting for transfers between devices: none -> 201 us  [swapped(): lax.ppermute(value, axis, [(place, place ^ mask) for place in range(count)])]
    all_gather x1 -> x0, waiting for transfers between devices: 96.6 us -> none  [shards(): lax.all_gather(w_out.astype(jnp.bfloat16), 'seq', axis=1, tiled=True)]
    all_to_all x2 -> x0, blocking collectives: 93.1 us -> none  [the longest x1 75.2 us: shards(): lax.all_to_all(buffer.reshape(seq_count, block_rows, col_share), 'seq', s...]
    ppermute x0 -> x41, starting transfers between devices: none -> 87.1 us  [swapped(): lax.ppermute(value, axis, [(place, place ^ mask) for place in range(count)])]
    all_gather x1 -> x0, blocking collectives: 74 us -> none  [shards(): lax.all_gather(router.astype(jnp.bfloat16), 'seq', axis=0, tiled=True)]
    all_to_all x1, waiting for transfers between devices: 33.7 us -> 0.01 us  [shards(): lax.all_to_all(jnp.broadcast_to(by_head[None], (part_count, *by_head.shap...]
    all_to_all x2 -> x0, starting transfers between devices: 17.3 us -> none  [the longest x1 9.83 us: shards(): lax.all_to_all(summed, 'seq', split_axis=0, concat_axis=0, tiled=True)]
    all_to_all x2 -> x0, waiting for transfers between devices: 12.6 us -> none  [the longest x1 12.6 us: shards(): lax.all_to_all(jnp.broadcast_to(share[None], (head_count, token_count, co...]
  transfers between devices with their start and end apart: 12 -> 50, of which waited for: 11 -> 28; matrix products, arithmetic and copies ran while one was open for 8% -> 14% of each run, Pallas kernels for 3% -> 3%
where the time goes in v2:
time: 432 us; the launch traced here: 430 us
  waiting for transfers between devices  234 us (54%)
  starting transfers between devices  112 us (26%)
  matrix products  33 us (8%)
  other arithmetic  20.4 us (5%)
  local copies, waits for them, and re-layouts  16.2 us (4%)
  Pallas kernels  12.9 us (3%)
    ppermute x41, waiting for transfers between devices, swapped(): lax.ppermute(value, axis, [(place, place ^ mask) for place in range(count)])  201 us
    ppermute x41, starting transfers between devices, swapped(): lax.ppermute(value, axis, [(place, place ^ mask) for place in range(count)])  87.1 us
    all_to_all x2, waiting for transfers between devices, to_owner(): lax.all_to_all(blocks, 'seq', split_axis=0, concat_axis=0, tiled=True)  31.2 us
    all_to_all x2, starting transfers between devices, to_owner(): lax.all_to_all(blocks, 'seq', split_axis=0, concat_axis=0, tiled=True)  13.1 us
    pallas_call x1, Pallas kernels, order_experts(): pl.pallas_call(order_body, grid_spec=pltpu.PrefetchScalarGridSpec(num_sca...  12.9 us
    dot_general x2, matrix products, shards(): jnp.einsum('acd,adf->acf', rows, lax.dynamic_slice_in_dim(server_both, (t...  9.84 us
    unnamed x106, local copies, waits for them, and re-layouts  8.76 us
  transfers between devices with their start and end apart: 50, of which 28 were waited for; matrix products, arithmetic and copies ran while one was open for 14% of the time, Pallas kernels for 3%

profile of v2, /device:TPU:0, one launch (start us, length us, event | category | flops | bytes accessed | tf_op | source)
XLA Modules:
  0.0 430.5 jit_solution(7741834768039089163)
XLA Ops:
  2.8 4.0 collective-permute-start.15
  8.3 1.6 collective-permute-start
  10.3 10.4 %collective-permute-done = bf16[1,128,1024]{2,1,0:T(8,128)(2,1)S(1)} collective-permute-done((bf16[1,128,1024]{2,1,0:T(8,128)(2,1)S(1)}, bf16[1,128,1024]{2,1,0:T(8,128)(2,1)S(1)}, u32[]{:S(2)}, u32[]{:S(2)}) %collective-permute-start) | collective-permute-done | bytes 262176 | tf_op jit(solution)/shard_map/ppermute | solution.py:30
  20.8 1.6 collective-permute-start.3
  24.0 4.8 %all-to-all-start = ((bf16[16,128,384]{2,1,0:T(8,128)(2,1)}), bf16[16,128,384]{2,1,0:T(8,128)(2,1)}, u32[]{:S(2)}, u32[]{:S(2)}) async-start(bf16[16,128,384]{2,1,0:T(8,128)(2,1)} %bitcast.22), calls=%async_computation | async-start | bytes 3145728 | tf_op jit(solution)/shard_map/all_to_all | solution.py:203
  28.8 2.8 collective-permute-start.20
  31.7 1.5 collective-permute-start.1
  33.9 13.9 %collective-permute-done.1 = bf16[2,128,512]{2,1,0:T(8,128)(2,1)S(1)} collective-permute-done((bf16[2,128,512]{2,1,0:T(8,128)(2,1)S(1)}, bf16[2,128,512]{2,1,0:T(8,128)(2,1)S(1)}, u32[]{:S(2)}, u32[]{:S(2)}) %collective-permute-start.1) | collective-permute-done | bytes 262176 | tf_op jit(solution)/shard_map/ppermute | solution.py:30
  47.8 2.4 collective-permute-start.2
  50.2 12.8 %collective-permute-done.4 = bf16[4,128,512]{2,1,0:T(8,128)(2,1)S(1)} collective-permute-done((bf16[4,128,512]{2,1,0:T(8,128)(2,1)S(1)}, bf16[4,128,512]{2,1,0:T(8,128)(2,1)S(1)}, u32[]{:S(2)}, u32[]{:S(2)}) %collective-permute-start.4) | collective-permute-done | bytes 524320 | tf_op jit(solution)/shard_map/ppermute | solution.py:30
  63.0 3.6 collective-permute-done.2
  66.8 1.6 pad_maximum_fusion.1
  69.7 12.9 %order_experts.1 = (bf16[16,128,1024]{2,1,0:T(8,128)(2,1)}, bf16[16,128,512]{2,1,0:T(8,128)(2,1)}) custom-call(s32[16]{0:T(128)} %order_ref.1, f32[16,128,512]{2,1,0:T(8,128)} %gate_ref.1, f32[16,128,512]{2,1,0:T(8,128)} %up_ref.1, f32[16,128,512]{2,1,0:T(8,128)} %down_ref.1), custom_call_target="tpu_custom_call" | custom-call | tf_op jit(solution)/shard_map/order_experts/pallas_call | solution.py:128
  83.9 13.1 %collective-permute-done.16 = bf16[1040,256]{1,0:T(8,128)(2,1)S(1)} collective-permute-done((bf16[1040,256]{1,0:T(8,128)(2,1)S(1)}, bf16[1040,256]{1,0:T(8,128)(2,1)S(1)}, u32[]{:S(2)}, u32[]{:S(2)}) %collective-permute-start.16) | collective-permute-done | bytes 532512 | tf_op jit(solution)/shard_map/ppermute | solution.py:30
  99.4 2.9 fusion.37
  102.3 2.2 fusion.41
  109.3 5.7 %collective-permute-start.6 = (bf16[64,384]{0,1:T(8,128)(2,1)S(1)}, bf16[64,384]{0,1:T(8,128)(2,1)S(1)}, u32[]{:S(2)}, u32[]{:S(2)}) collective-permute-start(bf16[64,384]{0,1:T(8,128)(2,1)S(1)} %constant_dynamic-slice_fusion.16), channel_id=1, source_target_pairs={{0,16},{2,18},{4,20},{6,22},{8,24},{10,26},{12,28},{14,30},{1,17},... | collective-permute-start | bytes 147464 | tf_op jit(solution)/shard_map/ppermute | solution.py:20
  115.0 8.0 %collective-permute-done.17 = bf16[1040,512]{1,0:T(8,128)(2,1)S(1)} collective-permute-done((bf16[1040,512]{1,0:T(8,128)(2,1)}, bf16[1040,512]{1,0:T(8,128)(2,1)S(1)}, u32[]{:S(2)}, u32[]{:S(2)}) %collective-permute-start.17) | collective-permute-done | bytes 1064992 | tf_op jit(solution)/shard_map/ppermute | solution.py:30
  123.0 1.7 pad_maximum_fusion
  125.4 2.5 fusion.171
  134.7 7.1 %all-to-all-start.1 = ((bf16[16,128,1024]{2,1,0:T(8,128)(2,1)}), bf16[16,128,1024]{2,1,0:T(8,128)(2,1)}, u32[]{:S(2)}, u32[]{:S(2)}) async-start(bf16[16,128,1024]{2,1,0:T(8,128)(2,1)} %get-tuple-element.13), calls=%async_computation.1 | async-start | bytes 8388608 | tf_op jit(solution)/shard_map/all_to_all | solution.py:232
  141.8 1.9 collective-permute-start.8
  145.4 61.0 %collective-permute-done.8 = bf16[128,128]{1,0:T(8,128)(2,1)S(1)} collective-permute-done((bf16[128,128]{1,0:T(8,128)(2,1)S(1)}, bf16[128,128]{1,0:T(8,128)(2,1)S(1)}, u32[]{:S(2)}, u32[]{:S(2)}) %collective-permute-start.8) | collective-permute-done | bytes 32800 | tf_op jit(solution)/shard_map/ppermute | solution.py:30
  206.7 1.8 collective-permute-start.12
  208.5 2.8 collective-permute-start.13
  211.3 11.8 %collective-permute-start.14 = (bf16[128,128]{1,0:T(8,128)(2,1)S(1)}, bf16[128,128]{1,0:T(8,128)(2,1)S(1)}, u32[]{:S(2)}, u32[]{:S(2)}) collective-permute-start(bf16[128,128]{1,0:T(8,128)(2,1)S(1)} %get-tuple-element.47), channel_id=1, source_target_pairs={{0,14},{2,12},{4,10},{6,8},{8,6},{10,4},{12,2},{14,0},{16,30},{18,... | collective-permute-start | bytes 98312 | tf_op jit(solution)/shard_map/ppermute | solution.py:30
  225.7 3.2 constant_dynamic-update-slice_fusion.36
  228.9 2.9 fusion.5
  232.6 1.9 collective-permute-done.19
  235.6 8.5 %collective-permute-start.22 = (bf16[1,128,1024]{2,1,0:T(8,128)(2,1)S(1)}, bf16[1,128,1024]{2,1,0:T(8,128)(2,1)S(1)}, u32[]{:S(2)}, u32[]{:S(2)}) collective-permute-start(bf16[1,128,1024]{2,1,0:T(8,128)(2,1)S(1)} %dynamic-slice_bitcast_fusion), channel_id=1, source_target_pairs={{0,16},{2,18},{4,20},{6,22},{8,24},{10,26},{12,28},{14,30},{16,0},... | collective-permute-start | bytes 786440 | tf_op jit(solution)/shard_map/ppermute | solution.py:30
  244.8 9.1 %collective-permute-done.22 = bf16[1,128,1024]{2,1,0:T(8,128)(2,1)S(1)} collective-permute-done((bf16[1,128,1024]{2,1,0:T(8,128)(2,1)S(1)}, bf16[1,128,1024]{2,1,0:T(8,128)(2,1)S(1)}, u32[]{:S(2)}, u32[]{:S(2)}) %collective-permute-start.22) | collective-permute-done | bytes 262176 | tf_op jit(solution)/shard_map/ppermute | solution.py:30
  254.9 2.2 collective-permute-start.24
  258.8 1.9 collective-permute-start.27
  260.7 3.8 collective-permute-done.23
  266.4 5.3 %collective-permute-start.29 = (bf16[2,72,1024]{2,1,0:T(8,128)(2,1)S(1)}, bf16[2,72,1024]{2,1,0:T(8,128)(2,1)S(1)}, u32[]{:S(2)}, u32[]{:S(2)}) collective-permute-start(bf16[2,72,1024]{2,1,0:T(8,128)(2,1)S(1)} %get-tuple-element.36), channel_id=1, source_target_pairs={{0,14},{2,12},{4,10},{6,8},{8,6},{10,4},{12,2},{14,0},{16,30},{18,... | collective-permute-start | bytes 884744 | tf_op jit(solution)/shard_map/ppermute | solution.py:30
  272.4 3.0 collective-permute-done.25
  277.6 4.3 collective-permute-done.28
  282.5 4.9 %collective-permute-done.29 = bf16[2,72,1024]{2,1,0:T(8,128)(2,1)S(1)} collective-permute-done((bf16[2,72,1024]{2,1,0:T(8,128)(2,1)S(1)}, bf16[2,72,1024]{2,1,0:T(8,128)(2,1)S(1)}, u32[]{:S(2)}, u32[]{:S(2)}) %collective-permute-start.29) | collective-permute-done | bytes 294944 | tf_op jit(solution)/shard_map/ppermute | solution.py:30
  288.2 6.0 %all-to-all-start.2 = ((bf16[16,128,512]{2,1,0:T(8,128)(2,1)}), bf16[16,128,512]{2,1,0:T(8,128)(2,1)}, u32[]{:S(2)}, u32[]{:S(2)}) async-start(bf16[16,128,512]{2,1,0:T(8,128)(2,1)} %get-tuple-element.14), calls=%async_computation.2 | async-start | bytes 4194304 | tf_op jit(solution)/shard_map/all_to_all | solution.py:232
  295.4 4.9 %fusion.17 = f32[1152,1024]{1,0:T(8,128)S(1)} fusion(bf16[1,1152,1024]{2,1,0:T(8,128)(2,1)} %collective-permute-done.30, bf16[1,2048,1024]{2,1,0:T(8,128)(2,1)} %bitcast.64, s32[]{:T(128)S(6)} %select_n.276), kind=kOutput, calls=%fused_computation.41 | convolution fusion | flops 2415919104 | bytes 9175044 | tf_op jit(solution)/shard_map/acd,adf->acf/dot_general | solution.py:392
  300.3 4.9 %add_bitcast_fusion = f32[1,1152,1024]{2,1,0:T(8,128)S(1)} fusion(f32[1152,1024]{1,0:T(8,128)S(1)} %fusion.17, bf16[1152,1024]{1,0:T(8,128)(2,1)} %bitcast.63, bf16[1,2048,1024]{2,1,0:T(8,128)(2,1)} %bitcast.64, s32[]{:T(128)S(6)} %select_n.274), kind=kOutput, calls=%fused_computation.11 | convolution fusion | flops 2417098752 | bytes 13893636 | tf_op jit(solution)/shard_map/acd,adf->acf/dot_general | solution.py:392
  306.0 31.2 %all-to-all-done.2 = bf16[16,128,512]{2,1,0:T(8,128)(2,1)} async-done(((bf16[16,128,512]{2,1,0:T(8,128)(2,1)}), bf16[16,128,512]{2,1,0:T(8,128)(2,1)}, u32[]{:S(2)}, u32[]{:S(2)}) %all-to-all-start.2) | async-done | bytes 2097184 | tf_op jit(solution)/shard_map/all_to_all | solution.py:232
  337.2 2.6 fusion.9
  340.2 8.3 %collective-permute-start.21 = (f32[1,128,16]{1,2,0:T(8,128)S(1)}, f32[1,128,16]{1,2,0:T(8,128)S(1)}, u32[]{:S(2)}, u32[]{:S(2)}) collective-permute-start(f32[1,128,16]{1,2,0:T(8,128)S(1)} %fusion.168), channel_id=1, source_target_pairs={{0,16},{2,18},{4,20},{6,22},{8,24},{10,26},{12,28},{14,30},{16,0},... | collective-permute-start | bytes 24584 | tf_op jit(solution)/shard_map/ppermute | solution.py:30
  351.0 2.6 fusion.8
  355.0 1.6 collective-permute-start.40
  356.6 2.0 collective-permute-start.42
  358.5 1.9 collective-permute-start.43
  361.9 4.9 %collective-permute-done.32 = bf16[1,72,1024]{2,1,0:T(8,128)(2,1)S(1)} collective-permute-done((bf16[1,72,1024]{2,1,0:T(8,128)(2,1)S(1)}, bf16[1,72,1024]{2,1,0:T(8,128)(2,1)S(1)}, u32[]{:S(2)}, u32[]{:S(2)}) %collective-permute-start.32) | collective-permute-done | bytes 147488 | tf_op jit(solution)/shard_map/ppermute | solution.py:30
  367.2 4.8 %collective-permute-done.33 = bf16[1,72,1024]{2,1,0:T(8,128)(2,1)S(1)} collective-permute-done((bf16[1,72,1024]{2,1,0:T(8,128)(2,1)S(1)}, bf16[1,72,1024]{2,1,0:T(8,128)(2,1)S(1)}, u32[]{:S(2)}, u32[]{:S(2)}) %collective-permute-start.33) | collective-permute-done | bytes 147488 | tf_op jit(solution)/shard_map/ppermute | solution.py:30
  372.0 1.7 collective-permute-start.34
  373.7 4.3 %collective-permute-done.34 = bf16[1,72,1024]{2,1,0:T(8,128)(2,1)S(1)} collective-permute-done((bf16[1,72,1024]{2,1,0:T(8,128)(2,1)S(1)}, bf16[1,72,1024]{2,1,0:T(8,128)(2,1)S(1)}, u32[]{:S(2)}, u32[]{:S(2)}) %collective-permute-start.34) | collective-permute-done | bytes 147488 | tf_op jit(solution)/shard_map/ppermute | solution.py:30
  378.0 1.5 collective-permute-start.35
  379.5 4.9 %collective-permute-done.35 = bf16[1,72,1024]{2,1,0:T(8,128)(2,1)S(1)} collective-permute-done((bf16[1,72,1024]{2,1,0:T(8,128)(2,1)S(1)}, bf16[1,72,1024]{2,1,0:T(8,128)(2,1)S(1)}, u32[]{:S(2)}, u32[]{:S(2)}) %collective-permute-start.35) | collective-permute-done | bytes 147488 | tf_op jit(solution)/shard_map/ppermute | solution.py:30
  384.4 1.9 collective-permute-start.36
  386.3 5.6 %collective-permute-done.36 = bf16[1,72,1024]{2,1,0:T(8,128)(2,1)S(1)} collective-permute-done((bf16[1,72,1024]{2,1,0:T(8,128)(2,1)S(1)}, bf16[1,72,1024]{2,1,0:T(8,128)(2,1)S(1)}, u32[]{:S(2)}, u32[]{:S(2)}) %collective-permute-start.36) | collective-permute-done | bytes 147488 | tf_op jit(solution)/shard_map/ppermute | solution.py:30
  391.9 1.7 collective-permute-start.37
  393.6 4.9 %collective-permute-done.37 = bf16[1,72,1024]{2,1,0:T(8,128)(2,1)S(1)} collective-permute-done((bf16[1,72,1024]{2,1,0:T(8,128)(2,1)S(1)}, bf16[1,72,1024]{2,1,0:T(8,128)(2,1)S(1)}, u32[]{:S(2)}, u32[]{:S(2)}) %collective-permute-start.37) | collective-permute-done | bytes 147488 | tf_op jit(solution)/shard_map/ppermute | solution.py:30
  400.0 7.2 %collective-permute-done.38 = bf16[1,72,1024]{2,1,0:T(8,128)(2,1)S(1)} collective-permute-done((bf16[1,72,1024]{2,1,0:T(8,128)(2,1)S(1)}, bf16[1,72,1024]{2,1,0:T(8,128)(2,1)S(1)}, u32[]{:S(2)}, u32[]{:S(2)}) %collective-permute-start.38) | collective-permute-done | bytes 147488 | tf_op jit(solution)/shard_map/ppermute | solution.py:30
  410.7 2.6 collective-permute-start.46
  413.4 1.5 collective-permute-start.39
  415.0 2.1 collective-permute-done.45
  417.2 5.0 %collective-permute-done.46 = bf16[72,1024]{1,0:T(8,128)(2,1)S(1)} collective-permute-done((bf16[72,1024]{1,0:T(8,128)(2,1)S(1)}, bf16[72,1024]{1,0:T(8,128)(2,1)S(1)}, u32[]{:S(2)}, u32[]{:S(2)}) %collective-permute-start.46) | collective-permute-done | bytes 147488 | tf_op jit(solution)/shard_map/ppermute | solution.py:30
  423.0 6.6 %collective-permute-done.39 = f32[128,1024]{1,0:T(8,128)S(1)} collective-permute-done((f32[128,1024]{1,0:T(8,128)S(1)}, f32[128,1024]{1,0:T(8,128)S(1)}, u32[]{:S(2)}, u32[]{:S(2)}) %collective-permute-start.39) | collective-permute-done | bytes 524320 | tf_op jit(solution)/shard_map/ppermute | solution.py:30
  (241 shorter events, 54.4 us)
Async XLA Ops:
  0.0 8.0 %copy-start = (bf16[128,2048]{1,0:T(8,128)(2,1)S(1)}, bf16[128,2048]{1,0:T(8,128)(2,1)}, u32[]{:S(2)}) copy-start(bf16[128,2048]{1,0:T(8,128)(2,1)} %param.15) | copy-start | bytes 1572868
  0.0 8.2 %copy-start.11 = (f32[2048]{0:T(1024)S(1)}, f32[2048]{0:T(1024)}, u32[]{:S(2)}) copy-start(f32[2048]{0:T(1024)} %param.16) | copy-start | bytes 24580
  0.0 10.0 %copy-start.5 = (f32[128,1024]{1,0:T(8,128)S(1)}, f32[128,1024]{1,0:T(8,128)}, u32[]{:S(2)}) copy-start(f32[128,1024]{1,0:T(8,128)} %param.18) | copy-start | bytes 1572868
  1.2 8.9 %copy-start.6 = (f32[128,1024]{1,0:T(8,128)S(1)}, f32[128,1024]{1,0:T(8,128)}, u32[]{:S(2)}) copy-start(f32[128,1024]{1,0:T(8,128)} %param.19) | copy-start | bytes 1572868
  2.8 79.9 %collective-permute-start.15 = (bf16[1040,128]{1,0:T(8,128)(2,1)}, bf16[1040,128]{1,0:T(8,128)(2,1)S(1)}, u32[]{:S(2)}, u32[]{:S(2)}) collective-permute-start(bf16[1040,128]{1,0:T(8,128)(2,1)} %get-tuple-element.45), channel_id=1, source_target_pairs={{0,16},{2,18},{4,20},{6,22},{8,24},{10,26},{12,28},{14,30},{16,0},... | collective-permute-start | bytes 798728 | tf_op jit(solution)/shard_map/ppermute | solution.py:30
  8.2 2.0 copy-start.7
  8.3 12.4 %collective-permute-start = (bf16[1,128,1024]{2,1,0:T(8,128)(2,1)S(1)}, bf16[1,128,1024]{2,1,0:T(8,128)(2,1)S(1)}, u32[]{:S(2)}, u32[]{:S(2)}) collective-permute-start(bf16[1,128,1024]{2,1,0:T(8,128)(2,1)S(1)} %fusion.96), channel_id=1, source_target_pairs={{0,8},{2,10},{4,12},{6,14},{8,0},{10,2},{12,4},{14,6},{16,24},{18,... | collective-permute-start | bytes 786440 | tf_op jit(solution)/shard_map/ppermute | solution.py:30
  20.8 12.4 %collective-permute-start.3 = (bf16[2,128,512]{2,1,0:T(8,128)(2,1)S(1)}, bf16[2,128,512]{2,1,0:T(8,128)(2,1)S(1)}, u32[]{:S(2)}, u32[]{:S(2)}) collective-permute-start(bf16[2,128,512]{2,1,0:T(8,128)(2,1)S(1)} %get-tuple-element.44), channel_id=1, source_target_pairs={{0,2},{2,0},{4,6},{6,4},{8,10},{10,8},{12,14},{14,12},{16,18},{18,... | collective-permute-start | bytes 786440 | tf_op jit(solution)/shard_map/ppermute | solution.py:30
  22.6 6.2 %copy-start.9 = (s32[128,8]{0,1:T(8,128)S(1)}, s32[128,8]{0,1:T(8,128)}, u32[]{:S(2)}) copy-start(s32[128,8]{0,1:T(8,128)} %param.29) | copy-start | bytes 12292
  24.0 75.4 %all-to-all-start = ((bf16[16,128,384]{2,1,0:T(8,128)(2,1)}), bf16[16,128,384]{2,1,0:T(8,128)(2,1)}, u32[]{:S(2)}, u32[]{:S(2)}) async-start(bf16[16,128,384]{2,1,0:T(8,128)(2,1)} %bitcast.22), calls=%async_computation | async-start | bytes 3145728 | tf_op jit(solution)/shard_map/all_to_all | solution.py:203
  28.8 203.8 %collective-permute-start.20 = (s32[1,128,8]{1,2,0:T(8,128)S(1)}, s32[1,128,8]{1,2,0:T(8,128)S(1)}, u32[]{:S(2)}, u32[]{:S(2)}) collective-permute-start(s32[1,128,8]{1,2,0:T(8,128)S(1)} %bitcast.300), channel_id=1, source_target_pairs={{0,16},{2,18},{4,20},{6,22},{8,24},{10,26},{12,28},{14,30},{16,0},... | collective-permute-start | bytes 12296 | tf_op jit(solution)/shard_map/ppermute | solution.py:30
  31.7 16.1 %collective-permute-start.1 = (bf16[2,128,512]{2,1,0:T(8,128)(2,1)S(1)}, bf16[2,128,512]{2,1,0:T(8,128)(2,1)S(1)}, u32[]{:S(2)}, u32[]{:S(2)}) collective-permute-start(bf16[2,128,512]{2,1,0:T(8,128)(2,1)S(1)} %get-tuple-element.43), channel_id=1, source_target_pairs={{0,4},{2,6},{4,0},{6,2},{8,12},{10,14},{12,8},{14,10},{16,20},{18,... | collective-permute-start | bytes 786440 | tf_op jit(solution)/shard_map/ppermute | solution.py:30
  33.2 29.7 %collective-permute-start.4 = (bf16[4,128,512]{2,1,0:T(8,128)(2,1)S(1)}, bf16[4,128,512]{2,1,0:T(8,128)(2,1)S(1)}, u32[]{:S(2)}, u32[]{:S(2)}) collective-permute-start(bf16[4,128,512]{2,1,0:T(8,128)(2,1)S(1)} %pad_maximum_fusion.6), channel_id=1, source_target_pairs={{0,4},{2,6},{4,0},{6,2},{8,12},{10,14},{12,8},{14,10},{16,20},{18,... | collective-permute-start | bytes 1572872 | tf_op jit(solution)/shard_map/ppermute | solution.py:30
  47.8 18.8 %collective-permute-start.2 = (bf16[4,128,512]{2,1,0:T(8,128)(2,1)S(1)}, bf16[4,128,512]{2,1,0:T(8,128)(2,1)S(1)}, u32[]{:S(2)}, u32[]{:S(2)}) collective-permute-start(bf16[4,128,512]{2,1,0:T(8,128)(2,1)S(1)} %pad_maximum_fusion.5), channel_id=1, source_target_pairs={{0,2},{2,0},{4,6},{6,4},{8,10},{10,8},{12,14},{14,12},{16,18},{18,... | collective-permute-start | bytes 1572872 | tf_op jit(solution)/shard_map/ppermute | solution.py:30
  66.7 1.7 copy-start.1
  66.8 2.2 copy-start.10
  66.8 2.3 copy-start.12
  66.8 2.0 copy-start.3
  68.4 30.9 %collective-permute-start.5 = (bf16[1024,1024]{1,0:T(8,128)(2,1)}, bf16[1024,1024]{1,0:T(8,128)(2,1)}, u32[]{:S(2)}, u32[]{:S(2)}) collective-permute-start(bf16[1024,1024]{1,0:T(8,128)(2,1)} %pad_maximum_fusion.1), channel_id=1, source_target_pairs={{1,0},{0,1},{3,2},{2,3},{5,4},{4,5},{7,6},{6,7},{9,8},{8,9},{11,10... | collective-permute-start | bytes 6291464 | tf_op jit(solution)/shard_map/ppermute | solution.py:25
  82.8 14.2 %collective-permute-start.16 = (bf16[1040,256]{1,0:T(8,128)(2,1)S(1)}, bf16[1040,256]{1,0:T(8,128)(2,1)S(1)}, u32[]{:S(2)}, u32[]{:S(2)}) collective-permute-start(bf16[1040,256]{1,0:T(8,128)(2,1)S(1)} %pad_maximum_fusion.4), channel_id=1, source_target_pairs={{0,8},{2,10},{4,12},{6,14},{8,0},{10,2},{12,4},{14,6},{16,24},{18,... | collective-permute-start | bytes 1597448 | tf_op jit(solution)/shard_map/ppermute | solution.py:30
  98.0 24.9 %collective-permute-start.17 = (bf16[1040,512]{1,0:T(8,128)(2,1)}, bf16[1040,512]{1,0:T(8,128)(2,1)S(1)}, u32[]{:S(2)}, u32[]{:S(2)}) collective-permute-start(bf16[1040,512]{1,0:T(8,128)(2,1)} %pad_maximum_fusion.2), channel_id=1, source_target_pairs={{0,4},{2,6},{4,0},{6,2},{8,12},{10,14},{12,8},{14,10},{16,20},{18,... | collective-permute-start | bytes 3194888 | tf_op jit(solution)/shard_map/ppermute | solution.py:30
  99.4 3.0 copy-start.2
  99.4 3.0 copy-start.4
  109.3 16.1 %collective-permute-start.6 = (bf16[64,384]{0,1:T(8,128)(2,1)S(1)}, bf16[64,384]{0,1:T(8,128)(2,1)S(1)}, u32[]{:S(2)}, u32[]{:S(2)}) collective-permute-start(bf16[64,384]{0,1:T(8,128)(2,1)S(1)} %constant_dynamic-slice_fusion.16), channel_id=1, source_target_pairs={{0,16},{2,18},{4,20},{6,22},{8,24},{10,26},{12,28},{14,30},{1,17},... | collective-permute-start | bytes 147464 | tf_op jit(solution)/shard_map/ppermute | solution.py:20
  124.7 101.0 %collective-permute-start.18 = (bf16[1040,1024]{1,0:T(8,128)(2,1)}, bf16[1040,1024]{1,0:T(8,128)(2,1)}, u32[]{:S(2)}, u32[]{:S(2)}) collective-permute-start(bf16[1040,1024]{1,0:T(8,128)(2,1)} %pad_maximum_fusion), channel_id=1, source_target_pairs={{0,2},{2,0},{4,6},{6,4},{8,10},{10,8},{12,14},{14,12},{16,18},{18,... | collective-permute-start | bytes 6389768 | tf_op jit(solution)/shard_map/ppermute | solution.py:30
  132.3 9.5 %collective-permute-start.7 = (bf16[64,128]{1,0:T(8,128)(2,1)S(1)}, bf16[64,128]{1,0:T(8,128)(2,1)S(1)}, u32[]{:S(2)}, u32[]{:S(2)}) collective-permute-start(bf16[64,128]{1,0:T(8,128)(2,1)S(1)} %slice.363), channel_id=1, source_target_pairs={{16,0},{18,2},{20,4},{22,6},{24,8},{26,10},{28,12},{30,14},{17,1},... | collective-permute-start | bytes 49160 | tf_op jit(solution)/shard_map/ppermute | solution.py:20
  134.7 153.5 %all-to-all-start.1 = ((bf16[16,128,1024]{2,1,0:T(8,128)(2,1)}), bf16[16,128,1024]{2,1,0:T(8,128)(2,1)}, u32[]{:S(2)}, u32[]{:S(2)}) async-start(bf16[16,128,1024]{2,1,0:T(8,128)(2,1)} %get-tuple-element.13), calls=%async_computation.1 | async-start | bytes 8388608 | tf_op jit(solution)/shard_map/all_to_all | solution.py:232
  141.8 64.6 %collective-permute-start.8 = (bf16[128,128]{1,0:T(8,128)(2,1)S(1)}, bf16[128,128]{1,0:T(8,128)(2,1)S(1)}, u32[]{:S(2)}, u32[]{:S(2)}) collective-permute-start(bf16[128,128]{1,0:T(8,128)(2,1)S(1)} %get-tuple-element.53), channel_id=1, source_target_pairs={{0,2},{2,0},{4,6},{6,4},{8,10},{10,8},{12,14},{14,12},{16,18},{18,... | collective-permute-start | bytes 98312 | tf_op jit(solution)/shard_map/ppermute | solution.py:30
  143.8 62.9 %collective-permute-start.9 = (bf16[128,128]{1,0:T(8,128)(2,1)S(1)}, bf16[128,128]{1,0:T(8,128)(2,1)S(1)}, u32[]{:S(2)}, u32[]{:S(2)}) collective-permute-start(bf16[128,128]{1,0:T(8,128)(2,1)S(1)} %get-tuple-element.52), channel_id=1, source_target_pairs={{0,4},{2,6},{4,0},{6,2},{8,12},{10,14},{12,8},{14,10},{16,20},{18,... | collective-permute-start | bytes 98312 | tf_op jit(solution)/shard_map/ppermute | solution.py:30
  145.2 63.3 %collective-permute-start.10 = (bf16[128,128]{1,0:T(8,128)(2,1)S(1)}, bf16[128,128]{1,0:T(8,128)(2,1)S(1)}, u32[]{:S(2)}, u32[]{:S(2)}) collective-permute-start(bf16[128,128]{1,0:T(8,128)(2,1)S(1)} %get-tuple-element.51), channel_id=1, source_target_pairs={{0,6},{2,4},{4,2},{6,0},{8,14},{10,12},{12,10},{14,8},{16,22},{18,... | collective-permute-start | bytes 98312 | tf_op jit(solution)/shard_map/ppermute | solution.py:30
  206.4 4.9 %collective-permute-start.11 = (bf16[128,128]{1,0:T(8,128)(2,1)S(1)}, bf16[128,128]{1,0:T(8,128)(2,1)S(1)}, u32[]{:S(2)}, u32[]{:S(2)}) collective-permute-start(bf16[128,128]{1,0:T(8,128)(2,1)S(1)} %get-tuple-element.50), channel_id=1, source_target_pairs={{0,8},{2,10},{4,12},{6,14},{8,0},{10,2},{12,4},{14,6},{16,24},{18,... | collective-permute-start | bytes 98312 | tf_op jit(solution)/shard_map/ppermute | solution.py:30
  206.7 16.4 %collective-permute-start.12 = (bf16[128,128]{1,0:T(8,128)(2,1)S(1)}, bf16[128,128]{1,0:T(8,128)(2,1)S(1)}, u32[]{:S(2)}, u32[]{:S(2)}) collective-permute-start(bf16[128,128]{1,0:T(8,128)(2,1)S(1)} %get-tuple-element.49), channel_id=1, source_target_pairs={{0,10},{2,8},{4,14},{6,12},{8,2},{10,0},{12,6},{14,4},{16,26},{18,... | collective-permute-start | bytes 98312 | tf_op jit(solution)/shard_map/ppermute | solution.py:30
  208.5 15.9 %collective-permute-start.13 = (bf16[128,128]{1,0:T(8,128)(2,1)S(1)}, bf16[128,128]{1,0:T(8,128)(2,1)S(1)}, u32[]{:S(2)}, u32[]{:S(2)}) collective-permute-start(bf16[128,128]{1,0:T(8,128)(2,1)S(1)} %get-tuple-element.48), channel_id=1, source_target_pairs={{0,12},{2,14},{4,8},{6,10},{8,4},{10,6},{12,0},{14,2},{16,28},{18,... | collective-permute-start | bytes 98312 | tf_op jit(solution)/shard_map/ppermute | solution.py:30
  211.3 14.2 %collective-permute-start.14 = (bf16[128,128]{1,0:T(8,128)(2,1)S(1)}, bf16[128,128]{1,0:T(8,128)(2,1)S(1)}, u32[]{:S(2)}, u32[]{:S(2)}) collective-permute-start(bf16[128,128]{1,0:T(8,128)(2,1)S(1)} %get-tuple-element.47), channel_id=1, source_target_pairs={{0,14},{2,12},{4,10},{6,8},{8,6},{10,4},{12,2},{14,0},{16,30},{18,... | collective-permute-start | bytes 98312 | tf_op jit(solution)/shard_map/ppermute | solution.py:30
  231.8 2.7 collective-permute-start.19
  234.7 0.7 copy-start.8
  235.6 18.3 %collective-permute-start.22 = (bf16[1,128,1024]{2,1,0:T(8,128)(2,1)S(1)}, bf16[1,128,1024]{2,1,0:T(8,128)(2,1)S(1)}, u32[]{:S(2)}, u32[]{:S(2)}) collective-permute-start(bf16[1,128,1024]{2,1,0:T(8,128)(2,1)S(1)} %dynamic-slice_bitcast_fusion), channel_id=1, source_target_pairs={{0,16},{2,18},{4,20},{6,22},{8,24},{10,26},{12,28},{14,30},{16,0},... | collective-permute-start | bytes 786440 | tf_op jit(solution)/shard_map/ppermute | solution.py:30
  254.5 9.9 %collective-permute-start.23 = (bf16[2,72,1024]{2,1,0:T(8,128)(2,1)S(1)}, bf16[2,72,1024]{2,1,0:T(8,128)(2,1)S(1)}, u32[]{:S(2)}, u32[]{:S(2)}) collective-permute-start(bf16[2,72,1024]{2,1,0:T(8,128)(2,1)S(1)} %get-tuple-element.37), channel_id=1, source_target_pairs={{0,2},{2,0},{4,6},{6,4},{8,10},{10,8},{12,14},{14,12},{16,18},{18,... | collective-permute-start | bytes 884744 | tf_op jit(solution)/shard_map/ppermute | solution.py:30
  254.9 11.5 %collective-permute-start.24 = (bf16[2,72,1024]{2,1,0:T(8,128)(2,1)S(1)}, bf16[2,72,1024]{2,1,0:T(8,128)(2,1)S(1)}, u32[]{:S(2)}, u32[]{:S(2)}) collective-permute-start(bf16[2,72,1024]{2,1,0:T(8,128)(2,1)S(1)} %get-tuple-element.38), channel_id=1, source_target_pairs={{0,4},{2,6},{4,0},{6,2},{8,12},{10,14},{12,8},{14,10},{16,20},{18,... | collective-permute-start | bytes 884744 | tf_op jit(solution)/shard_map/ppermute | solution.py:30
  257.8 17.6 %collective-permute-start.25 = (bf16[2,72,1024]{2,1,0:T(8,128)(2,1)S(1)}, bf16[2,72,1024]{2,1,0:T(8,128)(2,1)S(1)}, u32[]{:S(2)}, u32[]{:S(2)}) collective-permute-start(bf16[2,72,1024]{2,1,0:T(8,128)(2,1)S(1)} %get-tuple-element.39), channel_id=1, source_target_pairs={{0,6},{2,4},{4,2},{6,0},{8,14},{10,12},{12,10},{14,8},{16,22},{18,... | collective-permute-start | bytes 884744 | tf_op jit(solution)/shard_map/ppermute | solution.py:30
  258.8 17.3 %collective-permute-start.26 = (bf16[2,72,1024]{2,1,0:T(8,128)(2,1)S(1)}, bf16[2,72,1024]{2,1,0:T(8,128)(2,1)S(1)}, u32[]{:S(2)}, u32[]{:S(2)}) collective-permute-start(bf16[2,72,1024]{2,1,0:T(8,128)(2,1)S(1)} %get-tuple-element.40), channel_id=1, source_target_pairs={{0,8},{2,10},{4,12},{6,14},{8,0},{10,2},{12,4},{14,6},{16,24},{18,... | collective-permute-start | bytes 884744 | tf_op jit(solution)/shard_map/ppermute | solution.py:30
  258.8 18.0 %collective-permute-start.27 = (bf16[2,72,1024]{2,1,0:T(8,128)(2,1)S(1)}, bf16[2,72,1024]{2,1,0:T(8,128)(2,1)S(1)}, u32[]{:S(2)}, u32[]{:S(2)}) collective-permute-start(bf16[2,72,1024]{2,1,0:T(8,128)(2,1)S(1)} %get-tuple-element.41), channel_id=1, source_target_pairs={{0,10},{2,8},{4,14},{6,12},{8,2},{10,0},{12,6},{14,4},{16,26},{18,... | collective-permute-start | bytes 884744 | tf_op jit(solution)/shard_map/ppermute | solution.py:30
  264.5 17.4 %collective-permute-start.28 = (bf16[2,72,1024]{2,1,0:T(8,128)(2,1)S(1)}, bf16[2,72,1024]{2,1,0:T(8,128)(2,1)S(1)}, u32[]{:S(2)}, u32[]{:S(2)}) collective-permute-start(bf16[2,72,1024]{2,1,0:T(8,128)(2,1)S(1)} %get-tuple-element.42), channel_id=1, source_target_pairs={{0,12},{2,14},{4,8},{6,10},{8,4},{10,6},{12,0},{14,2},{16,28},{18,... | collective-permute-start | bytes 884744 | tf_op jit(solution)/shard_map/ppermute | solution.py:30
  266.4 21.1 %collective-permute-start.29 = (bf16[2,72,1024]{2,1,0:T(8,128)(2,1)S(1)}, bf16[2,72,1024]{2,1,0:T(8,128)(2,1)S(1)}, u32[]{:S(2)}, u32[]{:S(2)}) collective-permute-start(bf16[2,72,1024]{2,1,0:T(8,128)(2,1)S(1)} %get-tuple-element.36), channel_id=1, source_target_pairs={{0,14},{2,12},{4,10},{6,8},{8,6},{10,4},{12,2},{14,0},{16,30},{18,... | collective-permute-start | bytes 884744 | tf_op jit(solution)/shard_map/ppermute | solution.py:30
  288.2 7.2 %collective-permute-start.30 = (bf16[1,1152,1024]{2,1,0:T(8,128)(2,1)}, bf16[1,1152,1024]{2,1,0:T(8,128)(2,1)}, u32[]{:S(2)}, u32[]{:S(2)}) collective-permute-start(bf16[1,1152,1024]{2,1,0:T(8,128)(2,1)} %bitcast.66), channel_id=1, source_target_pairs={{1,0},{0,1},{3,2},{2,3},{5,4},{4,5},{7,6},{6,7},{9,8},{8,9},{11,10... | collective-permute-start | bytes 7077896 | tf_op jit(solution)/shard_map/ppermute | solution.py:25
  288.2 49.0 %all-to-all-start.2 = ((bf16[16,128,512]{2,1,0:T(8,128)(2,1)}), bf16[16,128,512]{2,1,0:T(8,128)(2,1)}, u32[]{:S(2)}, u32[]{:S(2)}) async-start(bf16[16,128,512]{2,1,0:T(8,128)(2,1)} %get-tuple-element.14), calls=%async_computation.2 | async-start | bytes 4194304 | tf_op jit(solution)/shard_map/all_to_all | solution.py:232
  339.8 13.8 %collective-permute-start.31 = (bf16[1,1152,1024]{2,1,0:T(8,128)(2,1)S(1)}, bf16[1,1152,1024]{2,1,0:T(8,128)(2,1)S(1)}, u32[]{:S(2)}, u32[]{:S(2)}) collective-permute-start(bf16[1,1152,1024]{2,1,0:T(8,128)(2,1)S(1)} %fusion.9), channel_id=1, source_target_pairs={{1,0},{0,1},{3,2},{2,3},{5,4},{4,5},{7,6},{6,7},{9,8},{8,9},{11,10... | collective-permute-start | bytes 7077896 | tf_op jit(solution)/shard_map/ppermute | solution.py:25
  340.2 9.9 %collective-permute-start.21 = (f32[1,128,16]{1,2,0:T(8,128)S(1)}, f32[1,128,16]{1,2,0:T(8,128)S(1)}, u32[]{:S(2)}, u32[]{:S(2)}) collective-permute-start(f32[1,128,16]{1,2,0:T(8,128)S(1)} %fusion.168), channel_id=1, source_target_pairs={{0,16},{2,18},{4,20},{6,22},{8,24},{10,26},{12,28},{14,30},{16,0},... | collective-permute-start | bytes 24584 | tf_op jit(solution)/shard_map/ppermute | solution.py:30
  355.0 54.5 %collective-permute-start.40 = (bf16[72,1024]{1,0:T(8,128)(2,1)S(1)}, bf16[72,1024]{1,0:T(8,128)(2,1)S(1)}, u32[]{:S(2)}, u32[]{:S(2)}) collective-permute-start(bf16[72,1024]{1,0:T(8,128)(2,1)S(1)} %get-tuple-element.27), channel_id=1, source_target_pairs={{0,2},{2,0},{4,6},{6,4},{8,10},{10,8},{12,14},{14,12},{16,18},{18,... | collective-permute-start | bytes 442376 | tf_op jit(solution)/shard_map/ppermute | solution.py:30
  356.5 54.2 %collective-permute-start.41 = (bf16[72,1024]{1,0:T(8,128)(2,1)S(1)}, bf16[72,1024]{1,0:T(8,128)(2,1)S(1)}, u32[]{:S(2)}, u32[]{:S(2)}) collective-permute-start(bf16[72,1024]{1,0:T(8,128)(2,1)S(1)} %get-tuple-element.26), channel_id=1, source_target_pairs={{0,4},{2,6},{4,0},{6,2},{8,12},{10,14},{12,8},{14,10},{16,20},{18,... | collective-permute-start | bytes 442376 | tf_op jit(solution)/shard_map/ppermute | solution.py:30
  356.6 56.9 %collective-permute-start.42 = (bf16[72,1024]{1,0:T(8,128)(2,1)S(1)}, bf16[72,1024]{1,0:T(8,128)(2,1)S(1)}, u32[]{:S(2)}, u32[]{:S(2)}) collective-permute-start(bf16[72,1024]{1,0:T(8,128)(2,1)S(1)} %get-tuple-element.25), channel_id=1, source_target_pairs={{0,6},{2,4},{4,2},{6,0},{8,14},{10,12},{12,10},{14,8},{16,22},{18,... | collective-permute-start | bytes 442376 | tf_op jit(solution)/shard_map/ppermute | solution.py:30
  358.5 56.4 %collective-permute-start.43 = (bf16[72,1024]{1,0:T(8,128)(2,1)S(1)}, bf16[72,1024]{1,0:T(8,128)(2,1)S(1)}, u32[]{:S(2)}, u32[]{:S(2)}) collective-permute-start(bf16[72,1024]{1,0:T(8,128)(2,1)S(1)} %get-tuple-element.24), channel_id=1, source_target_pairs={{0,8},{2,10},{4,12},{6,14},{8,0},{10,2},{12,4},{14,6},{16,24},{18,... | collective-permute-start | bytes 442376 | tf_op jit(solution)/shard_map/ppermute | solution.py:30
  360.4 6.4 %collective-permute-start.32 = (bf16[1,72,1024]{2,1,0:T(8,128)(2,1)S(1)}, bf16[1,72,1024]{2,1,0:T(8,128)(2,1)S(1)}, u32[]{:S(2)}, u32[]{:S(2)}) collective-permute-start(bf16[1,72,1024]{2,1,0:T(8,128)(2,1)S(1)} %get-tuple-element.34), channel_id=1, source_target_pairs={{0,2},{2,0},{4,6},{6,4},{8,10},{10,8},{12,14},{14,12},{16,18},{18,... | collective-permute-start | bytes 442376 | tf_op jit(solution)/shard_map/ppermute | solution.py:30
  366.8 5.1 %collective-permute-start.33 = (bf16[1,72,1024]{2,1,0:T(8,128)(2,1)S(1)}, bf16[1,72,1024]{2,1,0:T(8,128)(2,1)S(1)}, u32[]{:S(2)}, u32[]{:S(2)}) collective-permute-start(bf16[1,72,1024]{2,1,0:T(8,128)(2,1)S(1)} %get-tuple-element.33), channel_id=1, source_target_pairs={{0,4},{2,6},{4,0},{6,2},{8,12},{10,14},{12,8},{14,10},{16,20},{18,... | collective-permute-start | bytes 442376 | tf_op jit(solution)/shard_map/ppermute | solution.py:30
  372.0 6.0 %collective-permute-start.34 = (bf16[1,72,1024]{2,1,0:T(8,128)(2,1)S(1)}, bf16[1,72,1024]{2,1,0:T(8,128)(2,1)S(1)}, u32[]{:S(2)}, u32[]{:S(2)}) collective-permute-start(bf16[1,72,1024]{2,1,0:T(8,128)(2,1)S(1)} %get-tuple-element.32), channel_id=1, source_target_pairs={{0,6},{2,4},{4,2},{6,0},{8,14},{10,12},{12,10},{14,8},{16,22},{18,... | collective-permute-start | bytes 442376 | tf_op jit(solution)/shard_map/ppermute | solution.py:30
  378.0 6.4 %collective-permute-start.35 = (bf16[1,72,1024]{2,1,0:T(8,128)(2,1)S(1)}, bf16[1,72,1024]{2,1,0:T(8,128)(2,1)S(1)}, u32[]{:S(2)}, u32[]{:S(2)}) collective-permute-start(bf16[1,72,1024]{2,1,0:T(8,128)(2,1)S(1)} %get-tuple-element.31), channel_id=1, source_target_pairs={{0,8},{2,10},{4,12},{6,14},{8,0},{10,2},{12,4},{14,6},{16,24},{18,... | collective-permute-start | bytes 442376 | tf_op jit(solution)/shard_map/ppermute | solution.py:30
  384.4 7.5 %collective-permute-start.36 = (bf16[1,72,1024]{2,1,0:T(8,128)(2,1)S(1)}, bf16[1,72,1024]{2,1,0:T(8,128)(2,1)S(1)}, u32[]{:S(2)}, u32[]{:S(2)}) collective-permute-start(bf16[1,72,1024]{2,1,0:T(8,128)(2,1)S(1)} %get-tuple-element.30), channel_id=1, source_target_pairs={{0,10},{2,8},{4,14},{6,12},{8,2},{10,0},{12,6},{14,4},{16,26},{18,... | collective-permute-start | bytes 442376 | tf_op jit(solution)/shard_map/ppermute | solution.py:30
  391.9 6.6 %collective-permute-start.37 = (bf16[1,72,1024]{2,1,0:T(8,128)(2,1)S(1)}, bf16[1,72,1024]{2,1,0:T(8,128)(2,1)S(1)}, u32[]{:S(2)}, u32[]{:S(2)}) collective-permute-start(bf16[1,72,1024]{2,1,0:T(8,128)(2,1)S(1)} %get-tuple-element.29), channel_id=1, source_target_pairs={{0,12},{2,14},{4,8},{6,10},{8,4},{10,6},{12,0},{14,2},{16,28},{18,... | collective-permute-start | bytes 442376 | tf_op jit(solution)/shard_map/ppermute | solution.py:30
  398.6 8.6 %collective-permute-start.38 = (bf16[1,72,1024]{2,1,0:T(8,128)(2,1)S(1)}, bf16[1,72,1024]{2,1,0:T(8,128)(2,1)S(1)}, u32[]{:S(2)}, u32[]{:S(2)}) collective-permute-start(bf16[1,72,1024]{2,1,0:T(8,128)(2,1)S(1)} %get-tuple-element.28), channel_id=1, source_target_pairs={{0,14},{2,12},{4,10},{6,8},{8,6},{10,4},{12,2},{14,0},{16,30},{18,... | collective-permute-start | bytes 442376 | tf_op jit(solution)/shard_map/ppermute | solution.py:30
  407.2 7.8 %collective-permute-start.44 = (bf16[72,1024]{1,0:T(8,128)(2,1)S(1)}, bf16[72,1024]{1,0:T(8,128)(2,1)S(1)}, u32[]{:S(2)}, u32[]{:S(2)}) collective-permute-start(bf16[72,1024]{1,0:T(8,128)(2,1)S(1)} %get-tuple-element.23), channel_id=1, source_target_pairs={{0,10},{2,8},{4,14},{6,12},{8,2},{10,0},{12,6},{14,4},{16,26},{18,... | collective-permute-start | bytes 442376 | tf_op jit(solution)/shard_map/ppermute | solution.py:30
  409.5 7.7 %collective-permute-start.45 = (bf16[72,1024]{1,0:T(8,128)(2,1)S(1)}, bf16[72,1024]{1,0:T(8,128)(2,1)S(1)}, u32[]{:S(2)}, u32[]{:S(2)}) collective-permute-start(bf16[72,1024]{1,0:T(8,128)(2,1)S(1)} %get-tuple-element.22), channel_id=1, source_target_pairs={{0,12},{2,14},{4,8},{6,10},{8,4},{10,6},{12,0},{14,2},{16,28},{18,... | collective-permute-start | bytes 442376 | tf_op jit(solution)/shard_map/ppermute | solution.py:30
  410.7 11.4 %collective-permute-start.46 = (bf16[72,1024]{1,0:T(8,128)(2,1)S(1)}, bf16[72,1024]{1,0:T(8,128)(2,1)S(1)}, u32[]{:S(2)}, u32[]{:S(2)}) collective-permute-start(bf16[72,1024]{1,0:T(8,128)(2,1)S(1)} %get-tuple-element.21), channel_id=1, source_target_pairs={{0,14},{2,12},{4,10},{6,8},{8,6},{10,4},{12,2},{14,0},{16,30},{18,... | collective-permute-start | bytes 442376 | tf_op jit(solution)/shard_map/ppermute | solution.py:30
  413.4 16.2 %collective-permute-start.39 = (f32[128,1024]{1,0:T(8,128)S(1)}, f32[128,1024]{1,0:T(8,128)S(1)}, u32[]{:S(2)}, u32[]{:S(2)}) collective-permute-start(f32[128,1024]{1,0:T(8,128)S(1)} %slice_add_fusion.2), channel_id=1, source_target_pairs={{0,16},{2,18},{4,20},{6,22},{8,24},{10,26},{12,28},{14,30},{16,0},... | collective-permute-start | bytes 1572872 | tf_op jit(solution)/shard_map/ppermute | solution.py:30

commit v3 on v2

--- a/solution.py
+++ b/solution.py
@@ -12,6 +12,7 @@
 EPSILON = 1e-05
 ROPE_BASE = 50000.0
 MASKED = -1e30
+SMALL = pl.CostEstimate(flops=1, bytes_accessed=1, transcendentals=1)
 
 
 def from_behind(value, axis, steps):
@@ -115,11 +116,10 @@
     return (new_max, denominator, accumulated)
 
 
-def order_body(order_ref, gate_ref, up_ref, down_ref, both_ref, last_ref):
+def order_body(order_ref, gate_ref, up_ref, down_ref, out_ref):
     width = gate_ref.shape[2]
-    both_ref[0, :, :width] = gate_ref[0].astype(jnp.bfloat16)
-    both_ref[0, :, width:] = up_ref[0].astype(jnp.bfloat16)
-    last_ref[0] = down_ref[0].astype(jnp.bfloat16)
+    for k, source in enumerate((gate_ref, up_ref, down_ref)):
+        out_ref[:, :, k * width : (k + 1) * width] = source[...].astype(jnp.bfloat16)
 
 
 def order_experts(layout_map, gate, up, down):
@@ -131,17 +131,154 @@
             num_scalar_prefetch=1,
             grid=(count,),
             in_specs=[source, source, source],
-            out_specs=[
-                pl.BlockSpec((1, rows, 2 * width), lambda place, order: (place, 0, 0)),
-                pl.BlockSpec((1, rows, width), lambda place, order: (place, 0, 0)),
-            ],
+            out_specs=pl.BlockSpec((1, rows, 3 * width), lambda place, order: (place, 0, 0)),
         ),
-        out_shape=[
-            jax.ShapeDtypeStruct((count, rows, 2 * width), jnp.bfloat16),
-            jax.ShapeDtypeStruct((count, rows, width), jnp.bfloat16),
-        ],
+        out_shape=jax.ShapeDtypeStruct((count, rows, 3 * width), jnp.bfloat16),
         name="order_experts",
     )(layout_map, gate, up, down)
+
+
+def pack_body(query_ref, key_ref, value_ref, out_ref):
+    out_ref[0, :, :HEAD] = query_ref[...].astype(jnp.bfloat16)
+    out_ref[0, :, HEAD : 2 * HEAD] = key_ref[...].astype(jnp.bfloat16)
+    out_ref[0, :, 2 * HEAD :] = value_ref[...].astype(jnp.bfloat16)
+
+
+def pack_heads(w_query, w_key, w_value, copies):
+    rows, width = w_query.shape
+    heads = width // HEAD
+    source = pl.BlockSpec((rows, HEAD), lambda place: (0, place % heads))
+    return pl.pallas_call(
+        pack_body,
+        grid=(copies * heads,),
+        in_specs=[source, source, source],
+        out_specs=pl.BlockSpec((1, rows, 3 * HEAD), lambda place: (place, 0, 0)),
+        out_shape=jax.ShapeDtypeStruct((copies * heads, rows, 3 * HEAD), jnp.bfloat16),
+        name="pack_heads",
+    )(w_query, w_key, w_value)
+
+
+def project_body(turn_count, share, start_ref, *refs):
+    rows, (weight_ref, cosine_ref, sine_ref, out_ref) = (refs[:turn_count], refs[turn_count:])
+    product = 0.0
+    for turn in range(turn_count):
+        first = pl.multiple_of(start_ref[turn], share)
+        product = product + jnp.dot(
+            rows[turn][...], weight_ref[pl.ds(first, share), :], preferred_element_type=jnp.float32
+        )
+    cosine, sine_part = (cosine_ref[...], sine_ref[...])
+    out_ref[:, :HEAD] = rotate(product[:, :HEAD], cosine, sine_part).astype(jnp.bfloat16)
+    out_ref[:, HEAD : 2 * HEAD] = rotate(
+        product[:, HEAD : 2 * HEAD], cosine, sine_part
+    ).astype(jnp.bfloat16)
+    out_ref[:, 2 * HEAD :] = product[:, 2 * HEAD :].astype(jnp.bfloat16)
+
+
+def project(starts, row_blocks, weights, cosine, sine_part):
+    row_count, share = row_blocks[0].shape
+    step = row_count // 4
+    whole = pl.BlockSpec(weights.shape, lambda place, starts: (0, 0))
+    angle = pl.BlockSpec((step, cosine.shape[1]), lambda place, starts: (place, 0))
+    return pl.pallas_call(
+        lambda *refs: project_body(len(row_blocks), share, *refs),
+        grid_spec=pltpu.PrefetchScalarGridSpec(
+            num_scalar_prefetch=1,
+            grid=(4,),
+            in_specs=[pl.BlockSpec((step, share), lambda place, starts: (place, 0))]
+            * len(row_blocks)
+            + [whole, angle, angle],
+            out_specs=pl.BlockSpec((step, weights.shape[1]), lambda place, starts: (place, 0)),
+        ),
+        out_shape=jax.ShapeDtypeStruct((row_count, weights.shape[1]), jnp.bfloat16),
+        compiler_params=pltpu.CompilerParams(vmem_limit_bytes=32 * 2**20),
+        cost_estimate=SMALL,
+        name="project",
+    )(starts, *row_blocks, weights, cosine, sine_part)
+
+
+def attend_body(sink_ref, query_prompt_ref, key_prompt_ref, query_ref, key_ref, value_ref, out_ref):
+    sink = sink_ref[0]
+    scores = lax.dot_general(
+        query_ref[...],
+        key_ref[...],
+        (((1,), (1,)), ((), ())),
+        preferred_element_type=jnp.float32,
+    ) * HEAD ** (-0.5)
+    scores = jnp.where(query_prompt_ref[...] == key_prompt_ref[...], scores, MASKED)
+    top = jnp.maximum(sink, jnp.max(scores, axis=1, keepdims=True))
+    weights = jnp.exp(scores - top)
+    denominator = jnp.exp(sink - top) + jnp.sum(weights, axis=1, keepdims=True)
+    high = weights.astype(jnp.bfloat16)
+    low = (weights - high.astype(jnp.float32)).astype(jnp.bfloat16)
+    values = value_ref[...]
+    mix = jnp.dot(high, values, preferred_element_type=jnp.float32) + jnp.dot(
+        low, values, preferred_element_type=jnp.float32
+    )
+    out_ref[...] = (mix / denominator).astype(jnp.bfloat16)
+
+
+def attend_once(sink, query_prompt, key_prompt, rows):
+    row_count = rows.shape[0]
+    steps = 4 if row_count % 64 == 0 else 1
+    step = row_count // steps
+    return pl.pallas_call(
+        attend_body,
+        grid=(steps,),
+        in_specs=[
+            pl.BlockSpec(memory_space=pltpu.SMEM),
+            pl.BlockSpec((step, 1), lambda place: (place, 0)),
+            pl.BlockSpec((1, row_count), lambda place: (0, 0)),
+            pl.BlockSpec((step, HEAD), lambda place: (place, 0)),
+            pl.BlockSpec((row_count, HEAD), lambda place: (0, 1)),
+            pl.BlockSpec((row_count, HEAD), lambda place: (0, 2)),
+        ],
+        out_specs=pl.BlockSpec((step, HEAD), lambda place: (place, 0)),
+        out_shape=jax.ShapeDtypeStruct((row_count, HEAD), jnp.bfloat16),
+        compiler_params=pltpu.CompilerParams(vmem_limit_bytes=32 * 2**20),
+        cost_estimate=SMALL,
+        name="attend_once",
+    )(sink, query_prompt[:, None], key_prompt[None, :], rows, rows, rows)
+
+
+def settle_body(part_count, width, place_ref, *refs):
+    pieces = refs[:part_count]
+    token_ref, gain_ref, router_ref, full_ref, outgoing_ref, logit_ref, router_all = refs[
+        part_count:
+    ]
+    count = full_ref.shape[1] // width
+    for place in range(count):
+        first = pl.multiple_of(place_ref[place] * width, width)
+        block = sum(piece[:, pl.ds(first, width)] for piece in pieces)
+        here = slice(place * width, (place + 1) * width)
+        full_ref[:, here] = token_ref[:, here].astype(jnp.float32) + block
+        router_all[:, here] = router_ref[:, pl.ds(first, width)]
+    outgoing = rms_scale(full_ref[...], gain_ref[...]).astype(jnp.bfloat16)
+    outgoing_ref[...] = outgoing
+    logit_ref[...] = lax.dot_general(
+        outgoing,
+        router_all[...],
+        (((1,), (1,)), ((), ())),
+        preferred_element_type=jnp.float32,
+    )
+
+
+def settle(places, pieces, tokens, gain, router, width):
+    rows, columns = tokens.shape
+    vmem = pl.BlockSpec(memory_space=pltpu.VMEM)
+    return pl.pallas_call(
+        lambda *refs: settle_body(len(pieces), width, *refs),
+        in_specs=[pl.BlockSpec(memory_space=pltpu.SMEM)] + [vmem] * (len(pieces) + 3),
+        out_specs=[vmem] * 3,
+        out_shape=[
+            jax.ShapeDtypeStruct((rows, columns), jnp.float32),
+            jax.ShapeDtypeStruct((rows, columns), jnp.bfloat16),
+            jax.ShapeDtypeStruct((rows, router.shape[0]), jnp.float32),
+        ],
+        scratch_shapes=[pltpu.VMEM(router.shape, jnp.bfloat16)],
+        compiler_params=pltpu.CompilerParams(vmem_limit_bytes=32 * 2**20),
+        cost_estimate=SMALL,
+        name="settle",
+    )(places, *pieces, tokens, gain[None, :], router)
 
 
 def shards(
@@ -184,26 +321,14 @@
     def tp_blocks(value):
         return [value] + [from_turned(value, "tp", turn) for turn in range(1, tp_count)]
 
-    def tp_rows(weights, turn):
-        block = (tp_place + turn) % tp_count
-        return lax.dynamic_slice_in_dim(weights, block * col_share, col_share, 0)
-
     offsets = jnp.arange(token_count, dtype=jnp.int32)
     turns = jnp.arange(head_count, dtype=jnp.int32)
     group_masks = masks_below(head_count)
+    groups = [[first + k for k in range(head_count)] for first in range(0, seq_count, head_count)]
     part_masks = masks_below(seq_count, head_count)
 
-    by_head = jnp.concatenate(
-        [
-            w.reshape(w.shape[0], head_count, HEAD).transpose(1, 0, 2)
-            for w in (w_query, w_key, w_value)
-        ],
-        axis=2,
-    ).astype(jnp.bfloat16)
     head_weights = lax.all_to_all(
-        jnp.broadcast_to(by_head[None], (part_count, *by_head.shape)).reshape(
-            seq_count, *by_head.shape[1:]
-        ),
+        pack_heads(w_query, w_key, w_value, part_count),
         "seq",
         split_axis=0,
         concat_axis=0,
@@ -225,29 +350,49 @@
         pieces.append(jnp.concatenate([rows[known.index(m)] for m in range(head_count)], axis=0))
     part_rows = jnp.concatenate(pieces, axis=1)
 
-    both, last = order_experts(layout_map, expert_gate, expert_up, expert_down)
-    both, last, head_weights = lax.optimization_barrier((both, last, head_weights))
+    own_blocks = order_experts(layout_map, expert_gate, expert_up, expert_down)
+    own_blocks, head_weights = lax.optimization_barrier((own_blocks, head_weights))
 
     def to_owner(blocks):
         taken = lax.all_to_all(blocks, "seq", split_axis=0, concat_axis=0, tiled=True)
         taken = taken.reshape(seq_count, local_experts, *blocks.shape[1:])
         return jnp.swapaxes(taken, 0, 1).reshape(local_experts, -1, blocks.shape[2])
 
-    server_both = to_owner(both)
-    server_down = to_owner(last)
+    server = to_owner(own_blocks)
 
     out_local = jnp.concatenate([w_out, router.T], axis=0).astype(jnp.bfloat16)
-    out_all, out_turns = doubled(out_local, masks_below(seq_count), 1)
     width = out_local.shape[1]
-    bits = len(out_turns).bit_length() - 1
-
-    def in_order(value):
-        blocks = []
-        for place in range(seq_count):
-            turn = seq_place ^ place
-            index = sum(((turn >> k) & 1) << (bits - 1 - k) for k in range(bits))
-            blocks.append(lax.dynamic_slice_in_dim(value, index * width, width, 1))
-        return jnp.concatenate(blocks, axis=1)
+    out_rows = out_local.shape[0] // 32 * 16
+    seq_masks = masks_below(seq_count)
+    bits = len(seq_masks)
+    out_some, out_turns = doubled(out_local, seq_masks[:-2], 1)
+    out_halves = []
+    for piece, (second, third) in (
+        (out_some[:out_rows], seq_masks[-2:]),
+        (out_some[out_rows:], seq_masks[-2:][::-1]),
+    ):
+        piece, _ = doubled(piece, [second], 1)
+        out_halves.append((piece, swapped(piece, "seq", third)))
+
+    def times_columns(rows, half, first_row, last_row):
+        own, other = (piece[first_row:last_row] for piece in out_halves[half])
+        value = jnp.concatenate(
+            [
+                jnp.dot(rows, piece, preferred_element_type=jnp.float32)
+                if rows is not None
+                else piece
+                for piece in (own, other)
+            ],
+            axis=1,
+        )
+        if half == 0:
+            return value
+        span = len(out_turns) * width
+        quarters = [value[:, k * span : (k + 1) * span] for k in range(4)]
+        return jnp.concatenate([quarters[k] for k in (0, 2, 1, 3)], axis=1)
+
+    turn_places = seq_place ^ jnp.arange(seq_count, dtype=jnp.int32)
+    out_places = sum(((turn_places >> k) & 1) << (bits - 1 - k) for k in range(bits))
 
     all_routes, part_turns = doubled(routes[None], part_masks, 0)
     expert_ids = jnp.arange(expert_count, dtype=jnp.int32)
@@ -273,10 +418,6 @@
     routings = [routing(turn, all_routes[k]) for k, turn in enumerate(part_turns)]
     chosen, valid_token, _ = routings[0]
 
-    product = sum(
-        jnp.dot(rows, tp_rows(head_weights, turn), preferred_element_type=jnp.float32)
-        for turn, rows in enumerate(tp_blocks(part_rows))
-    )
     part_ids = (part * head_count + (head ^ turns))[:, None] * token_count + offsets[None, :]
     part_ids = part_ids.reshape(-1)
     part_positions = prompt_split(part_ids, slot_len, stagger, prompt_count)[1]
@@ -285,9 +426,8 @@
     angles = part_positions.astype(jnp.float32)[:, None] * frequency[None, :]
     cosine = jnp.cos(angles)
     sine_part = jnp.sin(angles)
-    query_rows = rotate(product[:, :HEAD], cosine, sine_part).astype(jnp.bfloat16)
-    key_rows = rotate(product[:, HEAD : 2 * HEAD], cosine, sine_part).astype(jnp.bfloat16)
-    value_rows = product[:, 2 * HEAD :].astype(jnp.bfloat16)
+    starts = (tp_place + jnp.arange(tp_count, dtype=jnp.int32)) % tp_count * col_share
+    rows = project(starts, tp_blocks(part_rows), head_weights, cosine, sine_part)
     sink = lax.dynamic_slice_in_dim(sink_logits, head, 1, 0)
 
     def start_state(row_count):
@@ -297,24 +437,21 @@
             jnp.zeros((row_count, HEAD), jnp.float32),
         )
 
-    if part_count == prompt_count:
-        rows = jnp.concatenate([query_rows, key_rows, value_rows], axis=1)
+    if part_count == prompt_count and part_slots + stagger <= HALF_WIN:
         edge_start = (head ^ (head_count - 1)) * token_count + token_count - stagger
         edge = from_behind(
             lax.dynamic_slice_in_dim(rows, edge_start, stagger, 0), "seq", head_count
         )
-        rows = jnp.concatenate([rows, edge], axis=0)
         edge_ids = part * part_slots - stagger + jnp.arange(stagger, dtype=jnp.int32)
         row_ids = jnp.concatenate([part_ids, edge_ids])
-        allowed = key_rules(row_ids, row_ids, slot_len, stagger, total_slots, real_lengths)
-        _, denominator, accumulated = attend(
-            start_state(part_slots + stagger),
-            rows[:, :HEAD],
-            rows[:, HEAD : 2 * HEAD],
-            rows[:, 2 * HEAD :],
-            allowed,
-        )
-        mixed = (accumulated / denominator).astype(jnp.bfloat16)
+        row_prompt, row_position = prompt_split(row_ids, slot_len, stagger, prompt_count)
+        row_live = (row_ids >= 0) & (row_position < length_of(row_prompt, real_lengths))
+        mixed = attend_once(
+            sink,
+            row_prompt,
+            jnp.where(row_live, row_prompt, -1),
+            jnp.concatenate([rows, edge], axis=0),
+        )
         edge_back = from_behind(mixed[part_slots:], "seq", -head_count)
         mixed = mixed[:part_slots]
         kept = lax.dynamic_slice_in_dim(mixed, edge_start, stagger, 0)
@@ -322,6 +459,7 @@
             mixed, jnp.where(part < part_count - 1, edge_back, kept), edge_start, 0
         )
     else:
+        query_rows, key_rows, value_rows = (rows[:, k * HEAD : (k + 1) * HEAD] for k in range(3))
         softmax_state = attend(
             start_state(part_slots),
             query_rows,
@@ -353,17 +491,32 @@
         [lax.dynamic_index_in_dim(heads, head ^ h, 0, keepdims=False) for h in range(head_count)],
         axis=1,
     )
-    partial_out = jnp.dot(
-        attention_result, out_all[: head_count * HEAD], preferred_element_type=jnp.float32
+    proj_width = head_count * HEAD
+    partial_out = times_columns(attention_result[:, :out_rows], 0, 0, out_rows) + times_columns(
+        attention_result[:, out_rows:], 1, 0, proj_width - out_rows
     )
     if tp_count == 2:
-        mixed_full = partial_out + from_turned(partial_out, "tp", 1)
+        out_pieces = [partial_out, from_turned(partial_out, "tp", 1)]
     else:
-        mixed_full = lax.psum(partial_out, "tp")
-    full_rows = tokens.astype(jnp.float32) + in_order(mixed_full)
-    outgoing = rms_scale(full_rows, mlp_gain).astype(jnp.bfloat16)
+        out_pieces = [lax.psum(partial_out, "tp")]
+    router_rows = times_columns(None, 1, proj_width - out_rows, None)
+    if width % 128:
+
+        def in_order(value):
+            blocks = [
+                lax.dynamic_slice_in_dim(value, out_places[place] * width, width, 1)
+                for place in range(seq_count)
+            ]
+            return jnp.concatenate(blocks, axis=1)
+
+        out_pieces, router_rows = ([in_order(piece) for piece in out_pieces], in_order(router_rows))
+        out_places, width = (jnp.zeros((1,), jnp.int32), model_width)
+    full_rows, outgoing, logits = settle(
+        out_places, out_pieces, tokens, mlp_gain, router_rows, width
+    )
     residual = lax.dynamic_slice_in_dim(full_rows, tp_place * col_share, col_share, 1)
     outgoing_share = lax.dynamic_slice_in_dim(outgoing, tp_place * col_share, col_share, 1)
+
 
     all_rows, _ = doubled(outgoing_share[None], part_masks, 0)
     buffer = jnp.stack(
@@ -388,20 +541,27 @@
         received.reshape(head_count, part_count, local_experts, capacity, col_share), 2, 0
     ).reshape(local_experts, row_count, col_share)
     hidden_share = expert_gate.shape[2]
-    gate_up = sum(
-        jnp.einsum(
-            "acd,adf->acf",
-            rows,
-            lax.dynamic_slice_in_dim(
-                server_both, (tp_place + turn) % tp_count * col_share, col_share, 1
-            ),
-            preferred_element_type=jnp.float32,
-        )
-        for turn, rows in enumerate(tp_blocks(received))
+    row_blocks = tp_blocks(received)
+    gate_up = (
+        sum(
+            jnp.einsum(
+                "acd,adf->acf",
+                rows,
+                lax.dynamic_slice_in_dim(
+                    server[:, :, : 2 * hidden_share],
+                    (tp_place + turn) % tp_count * col_share,
+                    col_share,
+                    1,
+                ),
+                preferred_element_type=jnp.float32,
+            )
+            for turn, rows in enumerate(row_blocks)
+        )
     )
     hidden_state = (jax.nn.silu(gate_up[..., :hidden_share]) * gate_up[..., hidden_share:]).astype(
         jnp.bfloat16
     )
+    server_down = server[:, :, 2 * hidden_share :]
 
     def down_columns(block):
         return jnp.einsum(
@@ -425,12 +585,6 @@
         2,
     ).reshape(head_count, part_count, block_rows, col_share)
 
-    logits = lax.dot_general(
-        outgoing,
-        in_order(out_all[head_count * HEAD :]),
-        (((1,), (1,)), ((), ())),
-        preferred_element_type=jnp.float32,
-    )
     route_logits = jnp.where(chosen, logits, -jnp.inf)
     route_exp = jnp.exp(route_logits - jnp.max(route_logits, axis=1, keepdims=True))
     route_weight = route_exp / jnp.sum(route_exp, axis=1, keepdims=True)
@@ -452,16 +606,27 @@
         return sum(mixes[k * token_count : (k + 1) * token_count] for k in range(3))
 
     def back(blocks):
+        return lax.all_to_all(
+            blocks, "seq", split_axis=0, concat_axis=0, tiled=True, axis_index_groups=groups
+        )
+
+    def by_place(blocks):
         return jnp.stack(
-            [blocks[0]] + [swapped(blocks[m], "seq", m) for m in range(1, head_count)]
-        )
-
-    others = back(summed[:, 1:])
+            [
+                lax.dynamic_index_in_dim(blocks, head ^ place, 0, keepdims=False)
+                for place in range(head_count)
+            ]
+        )
+
+    summed = by_place(summed)
+    others, own_rows = summed[:, 1:], summed[:, :1]
+    others = back(others)
+    others, own_rows = lax.optimization_barrier((others, own_rows))
     expert_mix = 0.0
     for k, turn in enumerate(part_turns[1:]):
-        mix = weighted(k + 1, others[:, k].reshape(-1, col_share))
+        mix = weighted(k + 1, by_place(others[:, k]).reshape(-1, col_share))
         expert_mix = expert_mix + swapped(mix, "seq", turn)
-    own_mix = weighted(0, back(summed[:, 0]).reshape(-1, col_share))
+    own_mix = weighted(0, by_place(back(own_rows)[:, 0]).reshape(-1, col_share))
     return (residual + (expert_mix + own_mix)).astype(jnp.bfloat16)
 
 

time: 432 us -> 422 us (0.977)
  Pallas kernels: 12.9 us -> 36 us
  matrix products: 33 us -> 19.4 us
  waiting for transfers between devices: 234 us -> 221 us
    ppermute x41 -> x29, waiting for transfers between devices: 201 us -> 129 us  [swapped(): lax.ppermute(value, axis, [(place, place ^ mask) for place in range(count)])]
    ppermute x2, waiting for transfers between devices: 0.01 us -> 55.2 us  [from_behind(): lax.ppermute(value, axis, [(source, source + steps) for source in range(f...]
    all_to_all x1 -> x3, waiting for transfers between devices: 0.01 us -> 33.9 us  [the longest x2 33.9 us: back(): lax.all_to_all(blocks, 'seq', split_axis=0, concat_axis=0, tiled=True, ax...]
    all_to_all x2 -> x1, waiting for transfers between devices: 31.2 us -> 0.01 us  [to_owner(): lax.all_to_all(blocks, 'seq', split_axis=0, concat_axis=0, tiled=True)]
    pallas_call x0 -> x4, Pallas kernels: none -> 23.1 us  [the longest x1 9.43 us: pack_heads(): pl.pallas_call(pack_body, grid=(copies * heads,), in_specs=[source, sourc...]
    dot_general x9 -> x6, matrix products: 22.9 us -> 10.7 us  [the longest x2 7.06 us: shards(): jnp.einsum('acd,adf->acf', rows, lax.dynamic_slice_in_dim(server[:, :, :2...]
    all_to_all x1 -> x3, starting transfers between devices: 4.79 us -> 13.2 us  [the longest x2 7.28 us: back(): lax.all_to_all(blocks, 'seq', split_axis=0, concat_axis=0, tiled=True, ax...]
    slice x1 -> x9, local copies, waits for them, and re-layouts: 0.85 us -> 9.2 us  [the longest x1 2.63 us: shards(): server[:, :, :2 * hidden_share]]
  transfers between devices with their start and end apart: 50 -> 39, of which waited for: 28 -> 20; matrix products, arithmetic and copies ran while one was open for 14% -> 9% of each run, Pallas kernels for 3% -> 9%
where the time goes in v3:
time: 422 us; the launch traced here: 420 us
  waiting for transfers between devices  221 us (52%)
  starting transfers between devices  109 us (26%)
  Pallas kernels  36 us (9%)
  matrix products  19.4 us (5%)
  other arithmetic  18.5 us (4%)
  local copies, waits for them, and re-layouts  14.9 us (4%)
    ppermute x29, waiting for transfers between devices, swapped(): lax.ppermute(value, axis, [(place, place ^ mask) for place in range(count)])  129 us
    ppermute x29, starting transfers between devices, swapped(): lax.ppermute(value, axis, [(place, place ^ mask) for place in range(count)])  85.4 us
    ppermute x2, waiting for transfers between devices, from_behind(): lax.ppermute(value, axis, [(source, source + steps) for source in range(f...  55.2 us
    all_to_all x2, waiting for transfers between devices, back(): lax.all_to_all(blocks, 'seq', split_axis=0, concat_axis=0, tiled=True, ax...  33.9 us
    pallas_call x1, Pallas kernels, order_experts(): pl.pallas_call(order_body, grid_spec=pltpu.PrefetchScalarGridSpec(num_sca...  12.9 us
    pallas_call x1, Pallas kernels, pack_heads(): pl.pallas_call(pack_body, grid=(copies * heads,), in_specs=[source, sourc...  9.43 us
  transfers between devices with their start and end apart: 39, of which 20 were waited for; matrix products, arithmetic and copies ran while one was open for 9% of the time, Pallas kernels for 9%

profile of v3, /device:TPU:0, one launch (start us, length us, event | category | flops | bytes accessed | tf_op | source)
XLA Modules:
  0.0 419.8 jit_solution(14239177279177804437)
XLA Ops:
  0.0 4.0 collective-permute-start.22
  6.6 1.2 multiply_reduce_fusion
  8.1 1.9 collective-permute-start
  10.0 9.4 %pack_heads.1 = bf16[16,128,384]{2,1,0:T(8,128)(2,1)} custom-call(f32[128,1024]{1,0:T(8,128)} %query_ref.1, f32[128,1024]{1,0:T(8,128)} %key_ref.1, f32[128,1024]{1,0:T(8,128)} %value_ref.1), custom_call_target="tpu_custom_call" | custom-call | tf_op jit(solution)/shard_map/pack_heads/pallas_call | solution.py:151
  19.5 5.9 %all-to-all-start = ((bf16[16,128,384]{2,1,0:T(8,128)(2,1)}), bf16[16,128,384]{2,1,0:T(8,128)(2,1)}, u32[]{:S(2)}, u32[]{:S(2)}) async-start(bf16[16,128,384]{2,1,0:T(8,128)(2,1)} %pack_heads.1), calls=%async_computation | async-start | bytes 3145728 | tf_op jit(solution)/shard_map/all_to_all | solution.py:330
  26.2 1.9 collective-permute-start.1
  28.1 1.5 collective-permute-start.3
  29.7 13.6 %collective-permute-done.1 = bf16[2,128,512]{2,1,0:T(8,128)(2,1)S(1)} collective-permute-done((bf16[2,128,512]{2,1,0:T(8,128)(2,1)S(1)}, bf16[2,128,512]{2,1,0:T(8,128)(2,1)S(1)}, u32[]{:S(2)}, u32[]{:S(2)}) %collective-permute-start.1) | collective-permute-done | bytes 262176 | tf_op jit(solution)/shard_map/ppermute | solution.py:31
  43.3 2.2 collective-permute-start.2
  46.8 17.3 %collective-permute-done.2 = bf16[4,128,512]{2,1,0:T(8,128)(2,1)S(1)} collective-permute-done((bf16[4,128,512]{2,1,0:T(8,128)(2,1)S(1)}, bf16[4,128,512]{2,1,0:T(8,128)(2,1)S(1)}, u32[]{:S(2)}, u32[]{:S(2)}) %collective-permute-start.2) | collective-permute-done | bytes 524320 | tf_op jit(solution)/shard_map/ppermute | solution.py:31
  64.8 12.9 %order_experts.1 = bf16[16,128,1536]{2,1,0:T(8,128)(2,1)} custom-call(s32[16]{0:T(128)} %order_ref.1, f32[16,128,512]{2,1,0:T(8,128)} %gate_ref.1, f32[16,128,512]{2,1,0:T(8,128)} %up_ref.1, f32[16,128,512]{2,1,0:T(8,128)} %down_ref.1), custom_call_target="tpu_custom_call" | custom-call | tf_op jit(solution)/shard_map/order_experts/pallas_call | solution.py:128
  77.8 1.8 pad_maximum_fusion.5
  80.3 6.9 %all-to-all-start.1 = ((bf16[16,128,1536]{2,1,0:T(8,128)(2,1)}), bf16[16,128,1536]{2,1,0:T(8,128)(2,1)}, u32[]{:S(2)}, u32[]{:S(2)}) async-start(bf16[16,128,1536]{2,1,0:T(8,128)(2,1)} %order_experts.1), calls=%async_computation.1 | async-start | bytes 12582912 | tf_op jit(solution)/shard_map/all_to_all | solution.py:357
  87.2 31.1 %collective-permute-done.16 = bf16[1040,256]{1,0:T(8,128)(2,1)} collective-permute-done((bf16[1040,256]{1,0:T(8,128)(2,1)}, bf16[1040,256]{1,0:T(8,128)(2,1)}, u32[]{:S(2)}, u32[]{:S(2)}) %collective-permute-start.16) | collective-permute-done | bytes 532512 | tf_op jit(solution)/shard_map/ppermute | solution.py:31
  118.4 1.2 pad_maximum_fusion.2
  120.4 3.1 multiply_sine_fusion
  127.5 5.8 %project.1 = bf16[1024,384]{1,0:T(8,128)(2,1)S(1)} custom-call(s32[2]{0:T(128)S(1)} %fusion.145.refs_0_, bf16[1024,1024]{1,0:T(8,128)(2,1)S(1)} %pad_maximum_fusion.refs_1_, bf16[1024,1024]{1,0:T(8,128)(2,1)} %collective-permute-done.5.refs_2_, bf16[2048,384]{1,0:T(8,128)(2,1)} %bitcast.22.refs_3_, f32[1024,64]{1,0:T(8,128)S(1)} %copy-done.2, ...), custom_call_target="tpu_custom_call" | custom-call | flops 1 | bytes 1 | tf_op jit(solution)/shard_map/project/pallas_call | solution.py:182
  133.3 1.3 collective-permute-start.6
  134.6 18.1 %collective-permute-done.17 = bf16[512,512]{1,0:T(8,128)(2,1)} collective-permute-done((bf16[512,512]{1,0:T(8,128)(2,1)}, bf16[512,512]{1,0:T(8,128)(2,1)}, u32[]{:S(2)}, u32[]{:S(2)}) %collective-permute-start.17) | collective-permute-done | bytes 524320 | tf_op jit(solution)/shard_map/ppermute | solution.py:31
  152.7 1.3 pad_maximum_fusion.3
  154.1 40.8 %collective-permute-done.6 = bf16[64,384]{1,0:T(8,128)(2,1)S(1)} collective-permute-done((bf16[64,384]{1,0:T(8,128)(2,1)S(1)}, bf16[64,384]{1,0:T(8,128)(2,1)S(1)}, u32[]{:S(2)}, u32[]{:S(2)}) %collective-permute-start.6) | collective-permute-done | bytes 49184 | tf_op jit(solution)/shard_map/ppermute | solution.py:21
  194.9 5.3 %collective-permute-start.18 = (bf16[512,1024]{1,0:T(8,128)(2,1)S(1)}, bf16[512,1024]{1,0:T(8,128)(2,1)S(1)}, u32[]{:S(2)}, u32[]{:S(2)}) collective-permute-start(bf16[512,1024]{1,0:T(8,128)(2,1)S(1)} %pad_maximum_fusion.3), channel_id=1, source_target_pairs={{0,2},{2,0},{4,6},{6,4},{8,10},{10,8},{12,14},{14,12},{16,18},{18,... | collective-permute-start | bytes 3145736 | tf_op jit(solution)/shard_map/ppermute | solution.py:31
  200.2 6.7 %attend_once.1 = bf16[1088,128]{1,0:T(8,128)(2,1)S(1)} custom-call(f32[1]{0:T(128)} %dynamic_slice.161.sink_ref, s32[1088,1]{1,0:T(8,128)S(1)} %fusion.29.query_prompt_ref, s32[1,1088]{1,0:T(1,128)S(1)} %and_select_fusion.key_prompt_ref, bf16[1088,384]{1,0:T(8,128)(2,1)S(1)} %pad_maximum_fusion.4.query_ref.key_ref.value_ref, ...), custom_call_target="tpu_custom_call" | custom-call | flops 1 | bytes 1 | tf_op jit(solution)/shard_map/attend_once/pallas_call | solution.py:224
  206.9 1.5 collective-permute-start.7
  208.4 1.3 pad_maximum_fusion.1
  209.7 2.1 collective-permute-start.20
  211.8 14.4 %collective-permute-done.7 = bf16[64,128]{1,0:T(8,128)(2,1)S(1)} collective-permute-done((bf16[64,128]{1,0:T(8,128)(2,1)S(1)}, bf16[64,128]{1,0:T(8,128)(2,1)S(1)}, u32[]{:S(2)}, u32[]{:S(2)}) %collective-permute-start.7) | collective-permute-done | bytes 16416 | tf_op jit(solution)/shard_map/ppermute | solution.py:21
  226.3 1.3 collective-permute-start.8
  227.6 20.4 %collective-permute-start.14 = (bf16[128,128]{1,0:T(8,128)(2,1)S(1)}, bf16[128,128]{1,0:T(8,128)(2,1)S(1)}, u32[]{:S(2)}, u32[]{:S(2)}) collective-permute-start(bf16[128,128]{1,0:T(8,128)(2,1)S(1)} %get-tuple-element.48), channel_id=1, source_target_pairs={{0,14},{2,12},{4,10},{6,8},{8,6},{10,4},{12,2},{14,0},{16,30},{18,... | collective-permute-start | bytes 98312 | tf_op jit(solution)/shard_map/ppermute | solution.py:31
  247.9 3.6 collective-permute-start.9
  251.6 1.9 collective-permute-done.9
  253.5 1.9 collective-permute-start.10
  255.4 2.9 collective-permute-done.10
  258.3 17.3 %collective-permute-start.11 = (bf16[128,128]{1,0:T(8,128)(2,1)S(1)}, bf16[128,128]{1,0:T(8,128)(2,1)S(1)}, u32[]{:S(2)}, u32[]{:S(2)}) collective-permute-start(bf16[128,128]{1,0:T(8,128)(2,1)S(1)} %get-tuple-element.51), channel_id=1, source_target_pairs={{0,8},{2,10},{4,12},{6,14},{8,0},{10,2},{12,4},{14,6},{16,24},{18,... | collective-permute-start | bytes 98312 | tf_op jit(solution)/shard_map/ppermute | solution.py:31
  275.6 1.9 collective-permute-done.11
  277.5 2.1 collective-permute-start.12
  279.6 2.7 collective-permute-done.12
  282.3 1.7 collective-permute-start.13
  284.1 3.1 collective-permute-done.13
  287.2 1.5 fusion.96
  288.7 1.5 fusion.20
  294.2 1.2 settle.1
  296.4 3.3 collective-permute-start.24
  300.5 11.7 %collective-permute-done.24 = bf16[1,128,1024]{2,1,0:T(8,128)(2,1)S(1)} collective-permute-done((bf16[1,128,1024]{2,1,0:T(8,128)(2,1)S(1)}, bf16[1,128,1024]{2,1,0:T(8,128)(2,1)S(1)}, u32[]{:S(2)}, u32[]{:S(2)}) %collective-permute-start.24) | collective-permute-done | bytes 262176 | tf_op jit(solution)/shard_map/ppermute | solution.py:31
  314.2 2.5 collective-permute-start.31
  317.4 1.3 collective-permute-start.28
  318.7 10.5 %collective-permute-done.25 = bf16[2,72,1024]{2,1,0:T(8,128)(2,1)S(1)} collective-permute-done((bf16[2,72,1024]{2,1,0:T(8,128)(2,1)S(1)}, bf16[2,72,1024]{2,1,0:T(8,128)(2,1)S(1)}, u32[]{:S(2)}, u32[]{:S(2)}) %collective-permute-start.25) | collective-permute-done | bytes 294944 | tf_op jit(solution)/shard_map/ppermute | solution.py:31
  331.4 10.4 %collective-permute-done.27 = bf16[2,72,1024]{2,1,0:T(8,128)(2,1)S(1)} collective-permute-done((bf16[2,72,1024]{2,1,0:T(8,128)(2,1)S(1)}, bf16[2,72,1024]{2,1,0:T(8,128)(2,1)S(1)}, u32[]{:S(2)}, u32[]{:S(2)}) %collective-permute-start.27) | collective-permute-done | bytes 294944 | tf_op jit(solution)/shard_map/ppermute | solution.py:31
  341.9 2.6 collective-permute-done.30
  344.7 1.7 slice.330
  346.4 2.6 slice.327
  349.3 4.3 %fusion.3 = f32[1152,1024]{1,0:T(8,128)S(1)} fusion(bf16[1,1152,1024]{2,1,0:T(8,128)(2,1)} %collective-permute-done.32, bf16[1,2048,1024]{2,1,0:T(8,128)(2,1)S(1)} %slice.327, s32[]{:T(128)S(6)} %select_n.279), kind=kOutput, calls=%fused_computation.22 | convolution fusion | flops 2415919104 | bytes 9175044 | tf_op jit(solution)/shard_map/acd,adf->acf/dot_general | solution.py:547
  353.6 2.8 add_bitcast_fusion
  357.1 1.4 fusion.1
  358.9 1.7 fusion
  360.5 2.6 collective-permute-done.33
  363.2 1.1 add_convert_fusion
  364.6 1.6 fusion.161
  366.3 3.6 all-to-all-start.2
  370.4 3.1 collective-permute-start.23
  375.2 12.5 %all-to-all-done.2 = bf16[8,1,72,1024]{3,2,1,0:T(8,128)(2,1)S(1)} async-done(((bf16[8,1,72,1024]{3,2,1,0:T(8,128)(2,1)}), bf16[8,1,72,1024]{3,2,1,0:T(8,128)(2,1)S(1)}, u32[]{:S(2)}, u32[]{:S(2)}) %all-to-all-start.2) | async-done | bytes 1179680 | tf_op jit(solution)/shard_map/all_to_all | solution.py:609
  387.7 3.7 all-to-all-start.3
  393.4 2.7 collective-permute-start.34
  396.1 21.4 %all-to-all-done.3 = bf16[8,1,72,1024]{3,2,1,0:T(8,128)(2,1)S(1)} async-done(((bf16[8,1,72,1024]{3,2,1,0:T(8,128)(2,1)}), bf16[8,1,72,1024]{3,2,1,0:T(8,128)(2,1)S(1)}, u32[]{:S(2)}, u32[]{:S(2)}) %all-to-all-start.3) | async-done | bytes 1179680 | tf_op jit(solution)/shard_map/all_to_all | solution.py:609
  (184 shorter events, 29.7 us)
Async XLA Ops:
  0.0 7.8 %copy-start = (bf16[128,2048]{1,0:T(8,128)(2,1)S(1)}, bf16[128,2048]{1,0:T(8,128)(2,1)}, u32[]{:S(2)}) copy-start(bf16[128,2048]{1,0:T(8,128)(2,1)} %refs_3_.1) | copy-start | bytes 1572868
  0.0 8.0 %copy-start.8 = (f32[2048]{0:T(1024)S(1)}, f32[2048]{0:T(1024)}, u32[]{:S(2)}) copy-start(f32[2048]{0:T(1024)} %param.16) | copy-start | bytes 24580
  0.0 291.9 %collective-permute-start.22 = (s32[1,128,8]{1,2,0:T(8,128)}, s32[1,128,8]{1,2,0:T(8,128)S(1)}, u32[]{:S(2)}, u32[]{:S(2)}) collective-permute-start(s32[1,128,8]{1,2,0:T(8,128)} %bitcast.266), channel_id=1, source_target_pairs={{0,16},{2,18},{4,20},{6,22},{8,24},{10,26},{12,28},{14,30},{16,0},... | collective-permute-start | bytes 12296 | tf_op jit(solution)/shard_map/ppermute | solution.py:31
  6.5 71.2 %collective-permute-start.15 = (bf16[1040,128]{1,0:T(8,128)(2,1)}, bf16[1040,128]{1,0:T(8,128)(2,1)}, u32[]{:S(2)}, u32[]{:S(2)}) collective-permute-start(bf16[1040,128]{1,0:T(8,128)(2,1)} %pad_maximum_fusion.9), channel_id=1, source_target_pairs={{0,16},{2,18},{4,20},{6,22},{8,24},{10,26},{12,28},{14,30},{16,0},... | collective-permute-start | bytes 798728 | tf_op jit(solution)/shard_map/ppermute | solution.py:31
  8.1 18.0 %collective-permute-start = (bf16[1,128,1024]{2,1,0:T(8,128)(2,1)S(1)}, bf16[1,128,1024]{2,1,0:T(8,128)(2,1)S(1)}, u32[]{:S(2)}, u32[]{:S(2)}) collective-permute-start(bf16[1,128,1024]{2,1,0:T(8,128)(2,1)S(1)} %fusion.63), channel_id=1, source_target_pairs={{0,8},{2,10},{4,12},{6,14},{8,0},{10,2},{12,4},{14,6},{16,24},{18,... | collective-permute-start | bytes 786440 | tf_op jit(solution)/shard_map/ppermute | solution.py:31
  19.5 60.8 %all-to-all-start = ((bf16[16,128,384]{2,1,0:T(8,128)(2,1)}), bf16[16,128,384]{2,1,0:T(8,128)(2,1)}, u32[]{:S(2)}, u32[]{:S(2)}) async-start(bf16[16,128,384]{2,1,0:T(8,128)(2,1)} %pack_heads.1), calls=%async_computation | async-start | bytes 3145728 | tf_op jit(solution)/shard_map/all_to_all | solution.py:330
  25.5 20.1 %copy-start.7 = (s32[2]{0:T(128)S(1)}, s32[2]{0:T(128)}, u32[]{:S(2)}) copy-start(s32[2]{0:T(128)} %param.28) | copy-start | bytes 28
  26.2 17.1 %collective-permute-start.1 = (bf16[2,128,512]{2,1,0:T(8,128)(2,1)S(1)}, bf16[2,128,512]{2,1,0:T(8,128)(2,1)S(1)}, u32[]{:S(2)}, u32[]{:S(2)}) collective-permute-start(bf16[2,128,512]{2,1,0:T(8,128)(2,1)S(1)} %get-tuple-element.38), channel_id=1, source_target_pairs={{0,4},{2,6},{4,0},{6,2},{8,12},{10,14},{12,8},{14,10},{16,20},{18,... | collective-permute-start | bytes 786440 | tf_op jit(solution)/shard_map/ppermute | solution.py:31
  28.1 17.5 %collective-permute-start.3 = (bf16[2,128,512]{2,1,0:T(8,128)(2,1)S(1)}, bf16[2,128,512]{2,1,0:T(8,128)(2,1)S(1)}, u32[]{:S(2)}, u32[]{:S(2)}) collective-permute-start(bf16[2,128,512]{2,1,0:T(8,128)(2,1)S(1)} %get-tuple-element.39), channel_id=1, source_target_pairs={{0,2},{2,0},{4,6},{6,4},{8,10},{10,8},{12,14},{14,12},{16,18},{18,... | collective-permute-start | bytes 786440 | tf_op jit(solution)/shard_map/ppermute | solution.py:31
  43.3 20.7 %collective-permute-start.2 = (bf16[4,128,512]{2,1,0:T(8,128)(2,1)S(1)}, bf16[4,128,512]{2,1,0:T(8,128)(2,1)S(1)}, u32[]{:S(2)}, u32[]{:S(2)}) collective-permute-start(bf16[4,128,512]{2,1,0:T(8,128)(2,1)S(1)} %pad_maximum_fusion.6), channel_id=1, source_target_pairs={{0,2},{2,0},{4,6},{6,4},{8,10},{10,8},{12,14},{14,12},{16,18},{18,... | collective-permute-start | bytes 1572872 | tf_op jit(solution)/shard_map/ppermute | solution.py:31
  45.7 18.4 %collective-permute-start.4 = (bf16[4,128,512]{2,1,0:T(8,128)(2,1)S(1)}, bf16[4,128,512]{2,1,0:T(8,128)(2,1)S(1)}, u32[]{:S(2)}, u32[]{:S(2)}) collective-permute-start(bf16[4,128,512]{2,1,0:T(8,128)(2,1)S(1)} %pad_maximum_fusion.7), channel_id=1, source_target_pairs={{0,4},{2,6},{4,0},{6,2},{8,12},{10,14},{12,8},{14,10},{16,20},{18,... | collective-permute-start | bytes 1572872 | tf_op jit(solution)/shard_map/ppermute | solution.py:31
  64.6 60.8 %collective-permute-start.5 = (bf16[1024,1024]{1,0:T(8,128)(2,1)S(1)}, bf16[1024,1024]{1,0:T(8,128)(2,1)}, u32[]{:S(2)}, u32[]{:S(2)}) collective-permute-start(bf16[1024,1024]{1,0:T(8,128)(2,1)S(1)} %pad_maximum_fusion.refs_1_), channel_id=1, source_target_pairs={{1,0},{0,1},{3,2},{2,3},{5,4},{4,5},{7,6},{6,7},{9,8},{8,9},{11,10... | collective-permute-start | bytes 6291464 | tf_op jit(solution)/shard_map/ppermute | solution.py:26
  79.6 38.8 %collective-permute-start.16 = (bf16[1040,256]{1,0:T(8,128)(2,1)}, bf16[1040,256]{1,0:T(8,128)(2,1)}, u32[]{:S(2)}, u32[]{:S(2)}) collective-permute-start(bf16[1040,256]{1,0:T(8,128)(2,1)} %pad_maximum_fusion.5), channel_id=1, source_target_pairs={{0,8},{2,10},{4,12},{6,14},{8,0},{10,2},{12,4},{14,6},{16,24},{18,... | collective-permute-start | bytes 1597448 | tf_op jit(solution)/shard_map/ppermute | solution.py:31
  80.3 264.4 %all-to-all-start.1 = ((bf16[16,128,1536]{2,1,0:T(8,128)(2,1)}), bf16[16,128,1536]{2,1,0:T(8,128)(2,1)}, u32[]{:S(2)}, u32[]{:S(2)}) async-start(bf16[16,128,1536]{2,1,0:T(8,128)(2,1)} %order_experts.1), calls=%async_computation.1 | async-start | bytes 12582912 | tf_op jit(solution)/shard_map/all_to_all | solution.py:357
  119.6 5.2 %copy-start.10 = (f32[8]{0:T(128)S(1)}, f32[8]{0:T(128)}, u32[]{:S(2)}) copy-start(f32[8]{0:T(128)} %param.22) | copy-start | bytes 100
  120.4 32.3 %collective-permute-start.17 = (bf16[512,512]{1,0:T(8,128)(2,1)}, bf16[512,512]{1,0:T(8,128)(2,1)}, u32[]{:S(2)}, u32[]{:S(2)}) collective-permute-start(bf16[512,512]{1,0:T(8,128)(2,1)} %slice.301), channel_id=1, source_target_pairs={{0,4},{2,6},{4,0},{6,2},{8,12},{10,14},{12,8},{14,10},{16,20},{18,... | collective-permute-start | bytes 1572872 | tf_op jit(solution)/shard_map/ppermute | solution.py:31
  124.4 84.0 %collective-permute-start.19 = (bf16[528,512]{1,0:T(8,128)(2,1)}, bf16[528,512]{1,0:T(8,128)(2,1)}, u32[]{:S(2)}, u32[]{:S(2)}) collective-permute-start(bf16[528,512]{1,0:T(8,128)(2,1)} %slice.302), channel_id=1, source_target_pairs={{0,2},{2,0},{4,6},{6,4},{8,10},{10,8},{12,14},{14,12},{16,18},{18,... | collective-permute-start | bytes 1622024 | tf_op jit(solution)/shard_map/ppermute | solution.py:31
  125.4 1.0 copy-start.1
  126.4 1.0 copy-start.2
  133.3 61.5 %collective-permute-start.6 = (bf16[64,384]{1,0:T(8,128)(2,1)S(1)}, bf16[64,384]{1,0:T(8,128)(2,1)S(1)}, u32[]{:S(2)}, u32[]{:S(2)}) collective-permute-start(bf16[64,384]{1,0:T(8,128)(2,1)S(1)} %constant_dynamic-slice_fusion), channel_id=1, source_target_pairs={{0,16},{2,18},{4,20},{6,22},{8,24},{10,26},{12,28},{14,30},{1,17},... | collective-permute-start | bytes 147464 | tf_op jit(solution)/shard_map/ppermute | solution.py:21
  194.9 95.8 %collective-permute-start.18 = (bf16[512,1024]{1,0:T(8,128)(2,1)S(1)}, bf16[512,1024]{1,0:T(8,128)(2,1)S(1)}, u32[]{:S(2)}, u32[]{:S(2)}) collective-permute-start(bf16[512,1024]{1,0:T(8,128)(2,1)S(1)} %pad_maximum_fusion.3), channel_id=1, source_target_pairs={{0,2},{2,0},{4,6},{6,4},{8,10},{10,8},{12,14},{14,12},{16,18},{18,... | collective-permute-start | bytes 3145736 | tf_op jit(solution)/shard_map/ppermute | solution.py:31
  206.9 19.3 %collective-permute-start.7 = (bf16[64,128]{1,0:T(8,128)(2,1)S(1)}, bf16[64,128]{1,0:T(8,128)(2,1)S(1)}, u32[]{:S(2)}, u32[]{:S(2)}) collective-permute-start(bf16[64,128]{1,0:T(8,128)(2,1)S(1)} %slice.292), channel_id=1, source_target_pairs={{16,0},{18,2},{20,4},{22,6},{24,8},{26,10},{28,12},{30,14},{17,1},... | collective-permute-start | bytes 49160 | tf_op jit(solution)/shard_map/ppermute | solution.py:21
  209.7 80.6 %collective-permute-start.20 = (bf16[528,1024]{1,0:T(8,128)(2,1)S(1)}, bf16[528,1024]{1,0:T(8,128)(2,1)S(1)}, u32[]{:S(2)}, u32[]{:S(2)}) collective-permute-start(bf16[528,1024]{1,0:T(8,128)(2,1)S(1)} %pad_maximum_fusion.1), channel_id=1, source_target_pairs={{0,4},{2,6},{4,0},{6,2},{8,12},{10,14},{12,8},{14,10},{16,20},{18,... | collective-permute-start | bytes 3244040 | tf_op jit(solution)/shard_map/ppermute | solution.py:31
  226.3 21.7 %collective-permute-start.8 = (bf16[128,128]{1,0:T(8,128)(2,1)S(1)}, bf16[128,128]{1,0:T(8,128)(2,1)S(1)}, u32[]{:S(2)}, u32[]{:S(2)}) collective-permute-start(bf16[128,128]{1,0:T(8,128)(2,1)S(1)} %get-tuple-element.54), channel_id=1, source_target_pairs={{0,2},{2,0},{4,6},{6,4},{8,10},{10,8},{12,14},{14,12},{16,18},{18,... | collective-permute-start | bytes 98312 | tf_op jit(solution)/shard_map/ppermute | solution.py:31
  227.6 59.6 %collective-permute-start.14 = (bf16[128,128]{1,0:T(8,128)(2,1)S(1)}, bf16[128,128]{1,0:T(8,128)(2,1)S(1)}, u32[]{:S(2)}, u32[]{:S(2)}) collective-permute-start(bf16[128,128]{1,0:T(8,128)(2,1)S(1)} %get-tuple-element.48), channel_id=1, source_target_pairs={{0,14},{2,12},{4,10},{6,8},{8,6},{10,4},{12,2},{14,0},{16,30},{18,... | collective-permute-start | bytes 98312 | tf_op jit(solution)/shard_map/ppermute | solution.py:31
  247.9 5.5 %collective-permute-start.9 = (bf16[128,128]{1,0:T(8,128)(2,1)S(1)}, bf16[128,128]{1,0:T(8,128)(2,1)S(1)}, u32[]{:S(2)}, u32[]{:S(2)}) collective-permute-start(bf16[128,128]{1,0:T(8,128)(2,1)S(1)} %get-tuple-element.53), channel_id=1, source_target_pairs={{0,4},{2,6},{4,0},{6,2},{8,12},{10,14},{12,8},{14,10},{16,20},{18,... | collective-permute-start | bytes 98312 | tf_op jit(solution)/shard_map/ppermute | solution.py:31
  253.5 4.8 %collective-permute-start.10 = (bf16[128,128]{1,0:T(8,128)(2,1)S(1)}, bf16[128,128]{1,0:T(8,128)(2,1)S(1)}, u32[]{:S(2)}, u32[]{:S(2)}) collective-permute-start(bf16[128,128]{1,0:T(8,128)(2,1)S(1)} %get-tuple-element.52), channel_id=1, source_target_pairs={{0,6},{2,4},{4,2},{6,0},{8,14},{10,12},{12,10},{14,8},{16,22},{18,... | collective-permute-start | bytes 98312 | tf_op jit(solution)/shard_map/ppermute | solution.py:31
  258.3 19.2 %collective-permute-start.11 = (bf16[128,128]{1,0:T(8,128)(2,1)S(1)}, bf16[128,128]{1,0:T(8,128)(2,1)S(1)}, u32[]{:S(2)}, u32[]{:S(2)}) collective-permute-start(bf16[128,128]{1,0:T(8,128)(2,1)S(1)} %get-tuple-element.51), channel_id=1, source_target_pairs={{0,8},{2,10},{4,12},{6,14},{8,0},{10,2},{12,4},{14,6},{16,24},{18,... | collective-permute-start | bytes 98312 | tf_op jit(solution)/shard_map/ppermute | solution.py:31
  277.5 4.8 %collective-permute-start.12 = (bf16[128,128]{1,0:T(8,128)(2,1)S(1)}, bf16[128,128]{1,0:T(8,128)(2,1)S(1)}, u32[]{:S(2)}, u32[]{:S(2)}) collective-permute-start(bf16[128,128]{1,0:T(8,128)(2,1)S(1)} %get-tuple-element.50), channel_id=1, source_target_pairs={{0,10},{2,8},{4,14},{6,12},{8,2},{10,0},{12,6},{14,4},{16,26},{18,... | collective-permute-start | bytes 98312 | tf_op jit(solution)/shard_map/ppermute | solution.py:31
  282.3 4.8 %collective-permute-start.13 = (bf16[128,128]{1,0:T(8,128)(2,1)S(1)}, bf16[128,128]{1,0:T(8,128)(2,1)S(1)}, u32[]{:S(2)}, u32[]{:S(2)}) collective-permute-start(bf16[128,128]{1,0:T(8,128)(2,1)S(1)} %get-tuple-element.49), channel_id=1, source_target_pairs={{0,12},{2,14},{4,8},{6,10},{8,4},{10,6},{12,0},{14,2},{16,28},{18,... | collective-permute-start | bytes 98312 | tf_op jit(solution)/shard_map/ppermute | solution.py:31
  290.3 1.0 copy-start.9
  290.7 0.8 copy-start.6
  291.3 2.8 copy-start.5
  291.4 2.7 collective-permute-start.21
  295.4 1.0 copy-start.3
  296.4 15.9 %collective-permute-start.24 = (bf16[1,128,1024]{2,1,0:T(8,128)(2,1)S(1)}, bf16[1,128,1024]{2,1,0:T(8,128)(2,1)S(1)}, u32[]{:S(2)}, u32[]{:S(2)}) collective-permute-start(bf16[1,128,1024]{2,1,0:T(8,128)(2,1)S(1)} %dynamic-slice_bitcast_fusion), channel_id=1, source_target_pairs={{0,16},{2,18},{4,20},{6,22},{8,24},{10,26},{12,28},{14,30},{16,0},... | collective-permute-start | bytes 786440 | tf_op jit(solution)/shard_map/ppermute | solution.py:31
  312.9 16.3 %collective-permute-start.25 = (bf16[2,72,1024]{2,1,0:T(8,128)(2,1)S(1)}, bf16[2,72,1024]{2,1,0:T(8,128)(2,1)S(1)}, u32[]{:S(2)}, u32[]{:S(2)}) collective-permute-start(bf16[2,72,1024]{2,1,0:T(8,128)(2,1)S(1)} %get-tuple-element.26), channel_id=1, source_target_pairs={{0,2},{2,0},{4,6},{6,4},{8,10},{10,8},{12,14},{14,12},{16,18},{18,... | collective-permute-start | bytes 884744 | tf_op jit(solution)/shard_map/ppermute | solution.py:31
  313.6 17.5 %collective-permute-start.26 = (bf16[2,72,1024]{2,1,0:T(8,128)(2,1)S(1)}, bf16[2,72,1024]{2,1,0:T(8,128)(2,1)S(1)}, u32[]{:S(2)}, u32[]{:S(2)}) collective-permute-start(bf16[2,72,1024]{2,1,0:T(8,128)(2,1)S(1)} %get-tuple-element.27), channel_id=1, source_target_pairs={{0,4},{2,6},{4,0},{6,2},{8,12},{10,14},{12,8},{14,10},{16,20},{18,... | collective-permute-start | bytes 884744 | tf_op jit(solution)/shard_map/ppermute | solution.py:31
  314.2 30.3 %collective-permute-start.31 = (bf16[2,72,1024]{2,1,0:T(8,128)(2,1)S(1)}, bf16[2,72,1024]{2,1,0:T(8,128)(2,1)S(1)}, u32[]{:S(2)}, u32[]{:S(2)}) collective-permute-start(bf16[2,72,1024]{2,1,0:T(8,128)(2,1)S(1)} %get-tuple-element.25), channel_id=1, source_target_pairs={{0,14},{2,12},{4,10},{6,8},{8,6},{10,4},{12,2},{14,0},{16,30},{18,... | collective-permute-start | bytes 884744 | tf_op jit(solution)/shard_map/ppermute | solution.py:31
  316.7 25.0 %collective-permute-start.27 = (bf16[2,72,1024]{2,1,0:T(8,128)(2,1)S(1)}, bf16[2,72,1024]{2,1,0:T(8,128)(2,1)S(1)}, u32[]{:S(2)}, u32[]{:S(2)}) collective-permute-start(bf16[2,72,1024]{2,1,0:T(8,128)(2,1)S(1)} %get-tuple-element.28), channel_id=1, source_target_pairs={{0,6},{2,4},{4,2},{6,0},{8,14},{10,12},{12,10},{14,8},{16,22},{18,... | collective-permute-start | bytes 884744 | tf_op jit(solution)/shard_map/ppermute | solution.py:31
  317.4 24.4 %collective-permute-start.28 = (bf16[2,72,1024]{2,1,0:T(8,128)(2,1)S(1)}, bf16[2,72,1024]{2,1,0:T(8,128)(2,1)S(1)}, u32[]{:S(2)}, u32[]{:S(2)}) collective-permute-start(bf16[2,72,1024]{2,1,0:T(8,128)(2,1)S(1)} %get-tuple-element.29), channel_id=1, source_target_pairs={{0,8},{2,10},{4,12},{6,14},{8,0},{10,2},{12,4},{14,6},{16,24},{18,... | collective-permute-start | bytes 884744 | tf_op jit(solution)/shard_map/ppermute | solution.py:31
  329.2 12.7 %collective-permute-start.29 = (bf16[2,72,1024]{2,1,0:T(8,128)(2,1)S(1)}, bf16[2,72,1024]{2,1,0:T(8,128)(2,1)S(1)}, u32[]{:S(2)}, u32[]{:S(2)}) collective-permute-start(bf16[2,72,1024]{2,1,0:T(8,128)(2,1)S(1)} %get-tuple-element.30), channel_id=1, source_target_pairs={{0,10},{2,8},{4,14},{6,12},{8,2},{10,0},{12,6},{14,4},{16,26},{18,... | collective-permute-start | bytes 884744 | tf_op jit(solution)/shard_map/ppermute | solution.py:31
  331.1 13.4 %collective-permute-start.30 = (bf16[2,72,1024]{2,1,0:T(8,128)(2,1)S(1)}, bf16[2,72,1024]{2,1,0:T(8,128)(2,1)S(1)}, u32[]{:S(2)}, u32[]{:S(2)}) collective-permute-start(bf16[2,72,1024]{2,1,0:T(8,128)(2,1)S(1)} %get-tuple-element.31), channel_id=1, source_target_pairs={{0,12},{2,14},{4,8},{6,10},{8,4},{10,6},{12,0},{14,2},{16,28},{18,... | collective-permute-start | bytes 884744 | tf_op jit(solution)/shard_map/ppermute | solution.py:31
  344.5 4.7 %collective-permute-start.32 = (bf16[1,1152,1024]{2,1,0:T(8,128)(2,1)S(1)}, bf16[1,1152,1024]{2,1,0:T(8,128)(2,1)}, u32[]{:S(2)}, u32[]{:S(2)}) collective-permute-start(bf16[1,1152,1024]{2,1,0:T(8,128)(2,1)S(1)} %bitcast.262), channel_id=1, source_target_pairs={{1,0},{0,1},{3,2},{2,3},{5,4},{4,5},{7,6},{6,7},{9,8},{8,9},{11,10... | collective-permute-start | bytes 7077896 | tf_op jit(solution)/shard_map/ppermute | solution.py:26
  358.6 4.6 %collective-permute-start.33 = (bf16[1,1152,1024]{2,1,0:T(8,128)(2,1)S(1)}, bf16[1,1152,1024]{2,1,0:T(8,128)(2,1)S(1)}, u32[]{:S(2)}, u32[]{:S(2)}) collective-permute-start(bf16[1,1152,1024]{2,1,0:T(8,128)(2,1)S(1)} %fusion.1), channel_id=1, source_target_pairs={{1,0},{0,1},{3,2},{2,3},{5,4},{4,5},{7,6},{6,7},{9,8},{8,9},{11,10... | collective-permute-start | bytes 7077896 | tf_op jit(solution)/shard_map/ppermute | solution.py:26
  366.3 21.4 %all-to-all-start.2 = ((bf16[8,1,72,1024]{3,2,1,0:T(8,128)(2,1)}), bf16[8,1,72,1024]{3,2,1,0:T(8,128)(2,1)S(1)}, u32[]{:S(2)}, u32[]{:S(2)}) async-start(bf16[8,1,72,1024]{3,2,1,0:T(8,128)(2,1)} %get-tuple-element.24), calls=%async_computation.2 | async-start | bytes 2359296 | tf_op jit(solution)/shard_map/all_to_all | solution.py:609
  370.4 21.0 %collective-permute-start.23 = (f32[1,128,16]{2,1,0:T(8,128)S(1)}, f32[1,128,16]{2,1,0:T(8,128)S(1)}, u32[]{:S(2)}, u32[]{:S(2)}) collective-permute-start(f32[1,128,16]{2,1,0:T(8,128)S(1)} %fusion.159), channel_id=1, source_target_pairs={{0,16},{2,18},{4,20},{6,22},{8,24},{10,26},{12,28},{14,30},{16,0},... | collective-permute-start | bytes 24584 | tf_op jit(solution)/shard_map/ppermute | solution.py:31
  387.7 29.8 %all-to-all-start.3 = ((bf16[8,1,72,1024]{3,2,1,0:T(8,128)(2,1)}), bf16[8,1,72,1024]{3,2,1,0:T(8,128)(2,1)S(1)}, u32[]{:S(2)}, u32[]{:S(2)}) async-start(bf16[8,1,72,1024]{3,2,1,0:T(8,128)(2,1)} %get-tuple-element.18), calls=%async_computation.3 | async-start | bytes 2359296 | tf_op jit(solution)/shard_map/all_to_all | solution.py:609
  393.3 24.4 %copy-start.11 = (bf16[128,576]{0,1:T(8,128)(2,1)S(1)}, bf16[128,576]{0,1:T(8,128)(2,1)}, u32[]{:S(2)}) copy-start(bf16[128,576]{0,1:T(8,128)(2,1)} %fusion.16) | copy-start | bytes 442372
  393.4 25.1 %collective-permute-start.34 = (f32[128,1024]{1,0:T(8,128)S(1)}, f32[128,1024]{1,0:T(8,128)S(1)}, u32[]{:S(2)}, u32[]{:S(2)}) collective-permute-start(f32[128,1024]{1,0:T(8,128)S(1)} %slice_add_fusion.2), channel_id=1, source_target_pairs={{0,16},{2,18},{4,20},{6,22},{8,24},{10,26},{12,28},{14,30},{16,0},... | collective-permute-start | bytes 1572872 | tf_op jit(solution)/shard_map/ppermute | solution.py:31
  417.7 1.2 copy-start.4

commit v4 on v3

--- a/solution.py
+++ b/solution.py
@@ -139,21 +139,28 @@
 
 
 def pack_body(query_ref, key_ref, value_ref, out_ref):
-    out_ref[0, :, :HEAD] = query_ref[...].astype(jnp.bfloat16)
-    out_ref[0, :, HEAD : 2 * HEAD] = key_ref[...].astype(jnp.bfloat16)
-    out_ref[0, :, 2 * HEAD :] = value_ref[...].astype(jnp.bfloat16)
+    heads = query_ref.shape[1] // HEAD
+    for place in range(out_ref.shape[0]):
+        head = place % heads
+        for k, source in enumerate((query_ref, key_ref, value_ref)):
+            out_ref[place, :, k * HEAD : (k + 1) * HEAD] = source[
+                :, head * HEAD : (head + 1) * HEAD
+            ].astype(jnp.bfloat16)
 
 
 def pack_heads(w_query, w_key, w_value, copies):
     rows, width = w_query.shape
-    heads = width // HEAD
-    source = pl.BlockSpec((rows, HEAD), lambda place: (0, place % heads))
+    places = copies * (width // HEAD)
+    step = rows // 4 if rows % 64 == 0 else rows
+    source = pl.BlockSpec((step, width), lambda place: (place, 0))
     return pl.pallas_call(
         pack_body,
-        grid=(copies * heads,),
+        grid=(rows // step,),
         in_specs=[source, source, source],
-        out_specs=pl.BlockSpec((1, rows, 3 * HEAD), lambda place: (place, 0, 0)),
-        out_shape=jax.ShapeDtypeStruct((copies * heads, rows, 3 * HEAD), jnp.bfloat16),
+        out_specs=pl.BlockSpec((places, step, 3 * HEAD), lambda place: (0, place, 0)),
+        out_shape=jax.ShapeDtypeStruct((places, rows, 3 * HEAD), jnp.bfloat16),
+        compiler_params=pltpu.CompilerParams(vmem_limit_bytes=32 * 2**20),
+        cost_estimate=SMALL,
         name="pack_heads",
     )(w_query, w_key, w_value)
 
@@ -240,45 +247,81 @@
     )(sink, query_prompt[:, None], key_prompt[None, :], rows, rows, rows)
 
 
-def settle_body(part_count, width, place_ref, *refs):
-    pieces = refs[:part_count]
-    token_ref, gain_ref, router_ref, full_ref, outgoing_ref, logit_ref, router_all = refs[
-        part_count:
-    ]
-    count = full_ref.shape[1] // width
-    for place in range(count):
-        first = pl.multiple_of(place_ref[place] * width, width)
-        block = sum(piece[:, pl.ds(first, width)] for piece in pieces)
-        here = slice(place * width, (place + 1) * width)
-        full_ref[:, here] = token_ref[:, here].astype(jnp.float32) + block
-        router_all[:, here] = router_ref[:, pl.ds(first, width)]
-    outgoing = rms_scale(full_ref[...], gain_ref[...]).astype(jnp.bfloat16)
+def settle_body(piece_count, *refs):
+    pieces = refs[:piece_count]
+    token_ref, gain_ref, router_ref, full_ref, outgoing_ref, logit_ref = refs[piece_count:]
+    full = token_ref[...].astype(jnp.float32) + sum(piece[...] for piece in pieces)
+    full_ref[...] = full
+    outgoing = rms_scale(full, gain_ref[...]).astype(jnp.bfloat16)
     outgoing_ref[...] = outgoing
     logit_ref[...] = lax.dot_general(
         outgoing,
-        router_all[...],
+        router_ref[...],
         (((1,), (1,)), ((), ())),
         preferred_element_type=jnp.float32,
     )
 
 
-def settle(places, pieces, tokens, gain, router, width):
+def settle(pieces, tokens, gain, router):
     rows, columns = tokens.shape
     vmem = pl.BlockSpec(memory_space=pltpu.VMEM)
     return pl.pallas_call(
-        lambda *refs: settle_body(len(pieces), width, *refs),
-        in_specs=[pl.BlockSpec(memory_space=pltpu.SMEM)] + [vmem] * (len(pieces) + 3),
+        lambda *refs: settle_body(len(pieces), *refs),
+        in_specs=[vmem] * (len(pieces) + 3),
         out_specs=[vmem] * 3,
         out_shape=[
             jax.ShapeDtypeStruct((rows, columns), jnp.float32),
             jax.ShapeDtypeStruct((rows, columns), jnp.bfloat16),
             jax.ShapeDtypeStruct((rows, router.shape[0]), jnp.float32),
         ],
-        scratch_shapes=[pltpu.VMEM(router.shape, jnp.bfloat16)],
         compiler_params=pltpu.CompilerParams(vmem_limit_bytes=32 * 2**20),
         cost_estimate=SMALL,
         name="settle",
-    )(places, *pieces, tokens, gain[None, :], router)
+    )(*pieces, tokens, gain[None, :], router)
+
+
+def expert_body(turn_count, share, in_ref, out_ref, *refs):
+    rows, weight_ref, outs = (refs[:turn_count], refs[turn_count], refs[turn_count + 1 :])
+    hidden = weight_ref.shape[2] // 3
+    gate_up = 0.0
+    for turn in range(turn_count):
+        first = pl.multiple_of(in_ref[turn], share)
+        gate_up = gate_up + jnp.dot(
+            rows[turn][0],
+            weight_ref[0, pl.ds(first, share), : 2 * hidden],
+            preferred_element_type=jnp.float32,
+        )
+    gate, up = (gate_up[:, :hidden], gate_up[:, hidden:])
+    state = (gate / (1.0 + jnp.exp(-gate)) * up).astype(jnp.bfloat16)
+    for turn in range(turn_count):
+        first = pl.multiple_of(out_ref[turn], share)
+        outs[turn][0] = lax.dot_general(
+            state,
+            weight_ref[0, pl.ds(first, share), 2 * hidden :],
+            (((1,), (1,)), ((), ())),
+            preferred_element_type=jnp.float32,
+        ).astype(jnp.bfloat16)
+
+
+def experts(in_starts, out_starts, row_blocks, weights):
+    local_experts, row_count, share = row_blocks[0].shape
+    step = row_count // 2 if row_count % 32 == 0 else row_count
+    block = pl.BlockSpec((1, step, share), lambda e, place, a, b: (e, place, 0))
+    whole = pl.BlockSpec((1, *weights.shape[1:]), lambda e, place, a, b: (e, 0, 0))
+    count = len(row_blocks)
+    return pl.pallas_call(
+        lambda *refs: expert_body(count, share, *refs),
+        grid_spec=pltpu.PrefetchScalarGridSpec(
+            num_scalar_prefetch=2,
+            grid=(local_experts, row_count // step),
+            in_specs=[block] * count + [whole],
+            out_specs=[block] * count,
+        ),
+        out_shape=[jax.ShapeDtypeStruct(row_blocks[0].shape, jnp.bfloat16)] * count,
+        compiler_params=pltpu.CompilerParams(vmem_limit_bytes=52 * 2**20),
+        cost_estimate=SMALL,
+        name="experts",
+    )(in_starts, out_starts, *row_blocks, weights)
 
 
 def shards(
@@ -337,68 +380,39 @@
 
     normed = rms_scale(tokens.astype(jnp.float32), attn_gain).astype(jnp.bfloat16)
     share = lax.dynamic_slice_in_dim(normed, tp_place * col_share, col_share, 1)
+    own_blocks = order_experts(layout_map, expert_gate, expert_up, expert_down)
     first_rows, first_turns = doubled(share[None], group_masks[:1], 0)
     pieces = []
     for piece, masks in (
         (first_rows[:, :, : col_share // 2], group_masks[1:]),
         (first_rows[:, :, col_share // 2 :], group_masks[1:][::-1]),
     ):
-        rows, row_turns = doubled(piece, masks, 0)
-        known = []
-        for turn in row_turns:
-            known.extend([first ^ turn for first in first_turns])
-        pieces.append(jnp.concatenate([rows[known.index(m)] for m in range(head_count)], axis=0))
+        known = first_turns
+        for mask in masks:
+            if mask == masks[-1]:
+                piece, own_blocks = lax.optimization_barrier((piece, own_blocks))
+            piece = jnp.concatenate([piece, swapped(piece, "seq", mask)], axis=0)
+            known = known + [turn ^ mask for turn in known]
+        pieces.append(jnp.concatenate([piece[known.index(m)] for m in range(head_count)], axis=0))
     part_rows = jnp.concatenate(pieces, axis=1)
 
-    own_blocks = order_experts(layout_map, expert_gate, expert_up, expert_down)
-    own_blocks, head_weights = lax.optimization_barrier((own_blocks, head_weights))
-
-    def to_owner(blocks):
-        taken = lax.all_to_all(blocks, "seq", split_axis=0, concat_axis=0, tiled=True)
-        taken = taken.reshape(seq_count, local_experts, *blocks.shape[1:])
-        return jnp.swapaxes(taken, 0, 1).reshape(local_experts, -1, blocks.shape[2])
-
-    server = to_owner(own_blocks)
-
-    out_local = jnp.concatenate([w_out, router.T], axis=0).astype(jnp.bfloat16)
-    width = out_local.shape[1]
-    out_rows = out_local.shape[0] // 32 * 16
-    seq_masks = masks_below(seq_count)
-    bits = len(seq_masks)
-    out_some, out_turns = doubled(out_local, seq_masks[:-2], 1)
-    out_halves = []
-    for piece, (second, third) in (
-        (out_some[:out_rows], seq_masks[-2:]),
-        (out_some[out_rows:], seq_masks[-2:][::-1]),
-    ):
-        piece, _ = doubled(piece, [second], 1)
-        out_halves.append((piece, swapped(piece, "seq", third)))
-
-    def times_columns(rows, half, first_row, last_row):
-        own, other = (piece[first_row:last_row] for piece in out_halves[half])
-        value = jnp.concatenate(
+    out_all = lax.all_gather(
+        jnp.concatenate([w_out, router.T], axis=0).astype(jnp.bfloat16), "seq", axis=1, tiled=True
+    )
+
+    def by_place(blocks):
+        return jnp.stack(
             [
-                jnp.dot(rows, piece, preferred_element_type=jnp.float32)
-                if rows is not None
-                else piece
-                for piece in (own, other)
-            ],
-            axis=1,
-        )
-        if half == 0:
-            return value
-        span = len(out_turns) * width
-        quarters = [value[:, k * span : (k + 1) * span] for k in range(4)]
-        return jnp.concatenate([quarters[k] for k in (0, 2, 1, 3)], axis=1)
-
-    turn_places = seq_place ^ jnp.arange(seq_count, dtype=jnp.int32)
-    out_places = sum(((turn_places >> k) & 1) << (bits - 1 - k) for k in range(bits))
+                lax.dynamic_index_in_dim(blocks, head ^ place, 0, keepdims=False)
+                for place in range(head_count)
+            ]
+        )
 
     all_routes, part_turns = doubled(routes[None], part_masks, 0)
     expert_ids = jnp.arange(expert_count, dtype=jnp.int32)
     block_rows = local_experts * capacity
     columns = jnp.arange(head_count * block_rows, dtype=jnp.int32)
-    column_owner = part * head_count + (head ^ (columns // block_rows))
+    column_owner = part * head_count + columns // block_rows
     column_expert = column_owner * local_experts + columns // capacity % local_experts
     spread = (column_expert[None, :] == expert_ids[:, None]).astype(jnp.bfloat16)
     wanted = (columns % capacity).astype(jnp.float32)
@@ -483,37 +497,32 @@
             )
         _, denominator, accumulated = softmax_state
         mixed = (accumulated / denominator).astype(jnp.bfloat16)
-    blocks = mixed.reshape(head_count, token_count, HEAD)
-    heads = jnp.stack(
-        [blocks[0]] + [swapped(blocks[m], "seq", m) for m in range(1, head_count)]
-    )
-    attention_result = jnp.concatenate(
-        [lax.dynamic_index_in_dim(heads, head ^ h, 0, keepdims=False) for h in range(head_count)],
-        axis=1,
-    )
+    attention_result = lax.all_to_all(
+        by_place(mixed.reshape(head_count, token_count, HEAD)),
+        "seq",
+        split_axis=0,
+        concat_axis=0,
+        tiled=True,
+        axis_index_groups=groups,
+    )
+
+    attention_result, own_blocks = lax.optimization_barrier((attention_result, own_blocks))
+    server = lax.all_to_all(own_blocks, "seq", split_axis=0, concat_axis=0, tiled=True)
+    server = jnp.swapaxes(
+        server.reshape(seq_count, local_experts, *own_blocks.shape[1:]), 0, 1
+    ).reshape(local_experts, model_width, own_blocks.shape[2])
+
     proj_width = head_count * HEAD
-    partial_out = times_columns(attention_result[:, :out_rows], 0, 0, out_rows) + times_columns(
-        attention_result[:, out_rows:], 1, 0, proj_width - out_rows
+    partial_out = jnp.dot(
+        jnp.swapaxes(attention_result, 0, 1).reshape(token_count, proj_width),
+        out_all[:proj_width],
+        preferred_element_type=jnp.float32,
     )
     if tp_count == 2:
         out_pieces = [partial_out, from_turned(partial_out, "tp", 1)]
     else:
         out_pieces = [lax.psum(partial_out, "tp")]
-    router_rows = times_columns(None, 1, proj_width - out_rows, None)
-    if width % 128:
-
-        def in_order(value):
-            blocks = [
-                lax.dynamic_slice_in_dim(value, out_places[place] * width, width, 1)
-                for place in range(seq_count)
-            ]
-            return jnp.concatenate(blocks, axis=1)
-
-        out_pieces, router_rows = ([in_order(piece) for piece in out_pieces], in_order(router_rows))
-        out_places, width = (jnp.zeros((1,), jnp.int32), model_width)
-    full_rows, outgoing, logits = settle(
-        out_places, out_pieces, tokens, mlp_gain, router_rows, width
-    )
+    full_rows, outgoing, logits = settle(out_pieces, tokens, mlp_gain, out_all[proj_width:])
     residual = lax.dynamic_slice_in_dim(full_rows, tp_place * col_share, col_share, 1)
     outgoing_share = lax.dynamic_slice_in_dim(outgoing, tp_place * col_share, col_share, 1)
 
@@ -533,57 +542,31 @@
         ],
         axis=1,
     )
-    received = jnp.stack(
-        [buffer[0]] + [swapped(buffer[m], "seq", m) for m in range(1, head_count)]
-    )
-    row_count = head_count * part_count * capacity
-    received = jnp.moveaxis(
-        received.reshape(head_count, part_count, local_experts, capacity, col_share), 2, 0
-    ).reshape(local_experts, row_count, col_share)
-    hidden_share = expert_gate.shape[2]
-    row_blocks = tp_blocks(received)
-    gate_up = (
-        sum(
-            jnp.einsum(
-                "acd,adf->acf",
-                rows,
-                lax.dynamic_slice_in_dim(
-                    server[:, :, : 2 * hidden_share],
-                    (tp_place + turn) % tp_count * col_share,
-                    col_share,
-                    1,
-                ),
-                preferred_element_type=jnp.float32,
-            )
-            for turn, rows in enumerate(row_blocks)
-        )
-    )
-    hidden_state = (jax.nn.silu(gate_up[..., :hidden_share]) * gate_up[..., hidden_share:]).astype(
-        jnp.bfloat16
-    )
-    server_down = server[:, :, 2 * hidden_share :]
-
-    def down_columns(block):
-        return jnp.einsum(
-            "acf,adf->acd",
-            hidden_state,
-            lax.dynamic_slice_in_dim(server_down, block * col_share, col_share, 1),
-            preferred_element_type=jnp.float32,
-        ).astype(jnp.bfloat16)
-
-    sent = [
-        from_turned(down_columns((tp_place - turn) % tp_count), "tp", turn)
-        for turn in range(1, tp_count)
+    def to_mate(m):
+        block = lax.dynamic_index_in_dim(buffer, head ^ m, 0, keepdims=False)
+        return swapped(block, "seq", m) if m else block
+
+    received = by_place(jnp.stack([to_mate(m) for m in range(head_count)]))
+    received = received.reshape(head_count, part_count, local_experts, capacity, col_share)
+    turn_ids = jnp.arange(tp_count, dtype=jnp.int32)
+    in_starts = (tp_place + turn_ids) % tp_count * col_share
+    out_starts = (tp_place - turn_ids) % tp_count * col_share
+
+    halves = [
+        tp_blocks(jnp.moveaxis(rows, 2, 0).reshape(local_experts, -1, col_share))
+        for rows in (received[:, 1:], received[:, :1])
     ]
-    own = lax.optimization_barrier(down_columns(tp_place))
-    summed = sum([piece.astype(jnp.float32) for piece in sent], own.astype(jnp.float32))
-    summed = jnp.moveaxis(
-        summed.astype(jnp.bfloat16).reshape(
-            local_experts, head_count, part_count, capacity, col_share
-        ),
-        0,
-        2,
-    ).reshape(head_count, part_count, block_rows, col_share)
+    halves, server = lax.optimization_barrier((halves, server))
+
+    def through_experts(row_blocks, parts):
+        outs = experts(in_starts, out_starts, row_blocks, server)
+        outs = [outs[0]] + [from_turned(outs[k], "tp", k) for k in range(1, tp_count)]
+        summed = sum(piece.astype(jnp.float32) for piece in outs).astype(jnp.bfloat16)
+        summed = summed.reshape(local_experts, head_count, parts, capacity, col_share)
+        return jnp.moveaxis(summed, 0, 2).reshape(head_count, parts, block_rows, col_share)
+
+    others = through_experts(halves[0], part_count - 1)
+    own_rows = through_experts(halves[1], 1)
 
     route_logits = jnp.where(chosen, logits, -jnp.inf)
     route_exp = jnp.exp(route_logits - jnp.max(route_logits, axis=1, keepdims=True))
@@ -610,23 +593,13 @@
             blocks, "seq", split_axis=0, concat_axis=0, tiled=True, axis_index_groups=groups
         )
 
-    def by_place(blocks):
-        return jnp.stack(
-            [
-                lax.dynamic_index_in_dim(blocks, head ^ place, 0, keepdims=False)
-                for place in range(head_count)
-            ]
-        )
-
-    summed = by_place(summed)
-    others, own_rows = summed[:, 1:], summed[:, :1]
     others = back(others)
     others, own_rows = lax.optimization_barrier((others, own_rows))
     expert_mix = 0.0
     for k, turn in enumerate(part_turns[1:]):
-        mix = weighted(k + 1, by_place(others[:, k]).reshape(-1, col_share))
+        mix = weighted(k + 1, others[:, k].reshape(-1, col_share))
         expert_mix = expert_mix + swapped(mix, "seq", turn)
-    own_mix = weighted(0, by_place(back(own_rows)[:, 0]).reshape(-1, col_share))
+    own_mix = weighted(0, back(own_rows)[:, 0].reshape(-1, col_share))
     return (residual + (expert_mix + own_mix)).astype(jnp.bfloat16)
 
 

time: 422 us -> 410 us (0.972)
  starting transfers between devices: 109 us -> 58.2 us
  waiting for transfers between devices: 221 us -> 243 us
  blocking collectives: 0 us -> 17.4 us
  between operations: 1.12 us -> 14.3 us
  matrix products: 19.4 us -> 9.25 us
  Pallas kernels: 36 us -> 45.6 us
  local copies, waits for them, and re-layouts: 14.9 us -> 8.54 us
  other arithmetic: 18.5 us -> 12.5 us
    ppermute x29 -> x16, starting transfers between devices: 85.4 us -> 31.4 us  [swapped(): lax.ppermute(value, axis, [(place, place ^ mask) for place in range(count)])]
    ppermute x29 -> x16, waiting for transfers between devices: 129 us -> 176 us  [swapped(): lax.ppermute(value, axis, [(place, place ^ mask) for place in range(count)])]
    ppermute x2, waiting for transfers between devices: 55.2 us -> 9.31 us  [from_behind(): lax.ppermute(value, axis, [(source, source + steps) for source in range(f...]
    all_gather x0 -> x1, waiting for transfers between devices: none -> 45.6 us  [shards(): lax.all_gather(jnp.concatenate([w_out, router.T], axis=0).astype(jnp.bflo...]
    all_to_all x2, waiting for transfers between devices: 33.9 us -> 3.12 us  [back(): lax.all_to_all(blocks, 'seq', split_axis=0, concat_axis=0, tiled=True, ax...]
    all_to_all x0 -> x1, blocking collectives: none -> 17.4 us  [shards(): lax.all_to_all(by_place(mixed.reshape(head_count, token_count, HEAD)), 's...]
    dot_general x8 -> x1, matrix products: 13.8 us -> 2.99 us  [shards(): jnp.dot(jnp.swapaxes(attention_result, 0, 1).reshape(token_count, proj_wi...]
    pallas_call x2 -> x4, Pallas kernels: 10.6 us -> 20.1 us  [the longest x2 17.7 us: experts(): pl.pallas_call(lambda *refs: expert_body(count, share, *refs), grid_spec=...]
  transfers between devices with their start and end apart: 39 -> 29, of which waited for: 20 -> 20; matrix products, arithmetic and copies ran while one was open for 9% -> 5% of each run, Pallas kernels for 9% -> 9%
where the time goes in v4:
time: 410 us; the launch traced here: 409 us
  waiting for transfers between devices  243 us (59%)
  starting transfers between devices  58.2 us (14%)
  Pallas kernels  45.6 us (11%)
  blocking collectives  17.4 us (4%)
  between operations  14.3 us (3%)
  other arithmetic  12.5 us (3%)
  matrix products  9.25 us (2%)
  local copies, waits for them, and re-layouts  8.54 us (2%)
    ppermute x16, waiting for transfers between devices, swapped(): lax.ppermute(value, axis, [(place, place ^ mask) for place in range(count)])  176 us
    all_gather x1, waiting for transfers between devices, shards(): lax.all_gather(jnp.concatenate([w_out, router.T], axis=0).astype(jnp.bflo...  45.6 us
    ppermute x16, starting transfers between devices, swapped(): lax.ppermute(value, axis, [(place, place ^ mask) for place in range(count)])  31.4 us
    pallas_call x2, Pallas kernels, experts(): pl.pallas_call(lambda *refs: expert_body(count, share, *refs), grid_spec=...  17.7 us
    all_to_all x1, blocking collectives, shards(): lax.all_to_all(by_place(mixed.reshape(head_count, token_count, HEAD)), 's...  17.4 us
    pallas_call x1, Pallas kernels, order_experts(): pl.pallas_call(order_body, grid_spec=pltpu.PrefetchScalarGridSpec(num_sca...  13 us
    ppermute x2, waiting for transfers between devices, from_behind(): lax.ppermute(value, axis, [(source, source + steps) for source in range(f...  9.31 us
    ppermute x6, waiting for transfers between devices, from_turned(): lax.ppermute(value, axis, [((place + turn) % count, place) for place in r...  8.89 us
  transfers between devices with their start and end apart: 29, of which 20 were waited for; matrix products, arithmetic and copies ran while one was open for 5% of the time, Pallas kernels for 9%

profile of v4, /device:TPU:0, one launch (start us, length us, event | category | flops | bytes accessed | tf_op | source)
XLA Modules:
  0.0 408.7 jit_solution(15318306484690747781)
XLA Ops:
  6.5 1.3 convert_element_type.106
  7.8 1.2 multiply_reduce_fusion
  9.0 0.7 dynamic-slice
  9.9 3.1 collective-permute-start
  13.0 1.8 pack_heads.1
  14.8 6.0 %all-to-all-start = ((bf16[16,128,384]{2,1,0:T(8,128)(2,1)}), bf16[16,128,384]{2,1,0:T(8,128)(2,1)}, u32[]{:S(2)}, u32[]{:S(2)}) async-start(bf16[16,128,384]{2,1,0:T(8,128)(2,1)} %pack_heads.1), calls=%async_computation | async-start | bytes 3145728 | tf_op jit(solution)/shard_map/all_to_all | solution.py:373
  21.0 1.9 collective-permute-start.1
  23.0 0.7 pad_maximum_fusion.4
  23.7 1.5 collective-permute-start.3
  25.3 13.0 %order_experts.1 = bf16[16,128,1536]{2,1,0:T(8,128)(2,1)} custom-call(s32[16]{0:T(128)} %order_ref.1, f32[16,128,512]{2,1,0:T(8,128)} %gate_ref.1, f32[16,128,512]{2,1,0:T(8,128)} %up_ref.1, f32[16,128,512]{2,1,0:T(8,128)} %down_ref.1), custom_call_target="tpu_custom_call" | custom-call | tf_op jit(solution)/shard_map/order_experts/pallas_call | solution.py:128
  38.2 5.5 %collective-permute-done.1 = bf16[2,128,512]{2,1,0:T(8,128)(2,1)S(1)} collective-permute-done((bf16[2,128,512]{2,1,0:T(8,128)(2,1)S(1)}, bf16[2,128,512]{2,1,0:T(8,128)(2,1)S(1)}, u32[]{:S(2)}, u32[]{:S(2)}) %collective-permute-start.1) | collective-permute-done | bytes 262176 | tf_op jit(solution)/shard_map/ppermute | solution.py:31
  44.0 4.0 collective-permute-start.2
  48.0 11.3 %collective-permute-done.4 = bf16[4,128,512]{2,1,0:T(8,128)(2,1)S(1)} collective-permute-done((bf16[4,128,512]{2,1,0:T(8,128)(2,1)S(1)}, bf16[4,128,512]{2,1,0:T(8,128)(2,1)S(1)}, u32[]{:S(2)}, u32[]{:S(2)}) %collective-permute-start.4) | collective-permute-done | bytes 524320 | tf_op jit(solution)/shard_map/ppermute | solution.py:31
  59.4 2.8 collective-permute-done.2
  63.0 3.1 multiply_sine_fusion
  67.0 1.0 copy-done.1
  68.1 1.0 copy-done.2
  69.1 5.8 %project.1 = bf16[1024,384]{1,0:T(8,128)(2,1)S(1)} custom-call(s32[2]{0:T(128)S(1)} %fusion.111.refs_0_, bf16[1024,1024]{1,0:T(8,128)(2,1)S(1)} %pad_maximum_fusion.refs_1_, bf16[1024,1024]{1,0:T(8,128)(2,1)} %collective-permute-done.5.refs_2_, bf16[2048,384]{1,0:T(8,128)(2,1)} %bitcast.22.refs_3_, f32[1024,64]{1,0:T(8,128)S(1)} %copy-done.2, ...), custom_call_target="tpu_custom_call" | custom-call | flops 1 | bytes 1 | tf_op jit(solution)/shard_map/project/pallas_call | solution.py:189
  75.0 5.7 %collective-permute-start.6 = (bf16[64,384]{1,0:T(8,128)(2,1)S(1)}, bf16[64,384]{1,0:T(8,128)(2,1)S(1)}, u32[]{:S(2)}, u32[]{:S(2)}) collective-permute-start(bf16[64,384]{1,0:T(8,128)(2,1)S(1)} %constant_dynamic-slice_fusion.8), channel_id=1, source_target_pairs={{0,16},{2,18},{4,20},{6,22},{8,24},{10,26},{12,28},{14,30},{1,17},... | collective-permute-start | bytes 147464 | tf_op jit(solution)/shard_map/ppermute | solution.py:21
  80.8 0.6 dynamic_slice.92.sink_ref
  81.4 1.1 collective-permute-done.6
  82.5 6.7 %attend_once.1 = bf16[1088,128]{1,0:T(8,128)(2,1)S(1)} custom-call(f32[1]{0:T(128)} %dynamic_slice.92.sink_ref, s32[1088,1]{1,0:T(8,128)S(1)} %fusion.11.query_prompt_ref, s32[1,1088]{1,0:T(1,128)S(1)} %and_select_fusion.key_prompt_ref, bf16[1088,384]{1,0:T(8,128)(2,1)S(1)} %pad_maximum_fusion.1.query_ref.key_ref.value_ref, ...), custom_call_target="tpu_custom_call" | custom-call | flops 1 | bytes 1 | tf_op jit(solution)/shard_map/attend_once/pallas_call | solution.py:231
  89.2 1.3 collective-permute-start.7
  90.6 8.2 %collective-permute-done.7 = bf16[64,128]{1,0:T(8,128)(2,1)S(1)} collective-permute-done((bf16[64,128]{1,0:T(8,128)(2,1)S(1)}, bf16[64,128]{1,0:T(8,128)(2,1)S(1)}, u32[]{:S(2)}, u32[]{:S(2)}) %collective-permute-start.7) | collective-permute-done | bytes 16416 | tf_op jit(solution)/shard_map/ppermute | solution.py:21
  100.0 17.4 %all_to_all.25 = bf16[8,128,128]{1,2,0:T(8,128)(2,1)S(1)} all-to-all(bf16[8,128,128]{1,2,0:T(8,128)(2,1)S(1)} %constant_dynamic-update-slice_fusion), channel_id=1, replica_groups={{0,2,4,6,8,10,12,14},{16,18,20,22,24,26,28,30},{1,3,5,7,9,11,13,15},{17..., dimensions={0} | all-to-all | bytes 524288 | tf_op jit(solution)/shard_map/all_to_all | solution.py:500
  117.4 5.0 %all-to-all-start.2 = ((bf16[16,128,1536]{2,1,0:T(8,128)(2,1)}), bf16[16,128,1536]{2,1,0:T(8,128)(2,1)}, u32[]{:S(2)}, u32[]{:S(2)}) async-start(bf16[16,128,1536]{2,1,0:T(8,128)(2,1)} %order_experts.1), calls=%async_computation.2 | async-start | bytes 12582912 | tf_op jit(solution)/shard_map/all_to_all | solution.py:510
  122.4 2.6 collective-permute-start.9
  125.0 45.6 %all-gather.2.cloned.1.call-done = bf16[1040,2048]{1,0:T(8,128)(2,1)} async-done(((bf16[1040,128]{1,0:T(8,128)(2,1)}), bf16[1040,2048]{1,0:T(8,128)(2,1)}) %all-gather.2.cloned.1.call-update) | async-done | bytes 4259856 | tf_op jit(solution)/shard_map/all_gather | solution.py:399
  170.6 3.0 fusion.refs_0_
  174.2 91.7 %collective-permute-done.9 = s32[1,128,8]{1,2,0:T(8,128)S(1)} collective-permute-done((s32[1,128,8]{1,2,0:T(8,128)S(1)}, s32[1,128,8]{1,2,0:T(8,128)S(1)}, u32[]{:S(2)}, u32[]{:S(2)}) %collective-permute-start.9) | collective-permute-done | bytes 4128 | tf_op jit(solution)/shard_map/ppermute | solution.py:31
  265.9 0.8 slice.133.refs_4_
  266.8 0.6 settle.1
  267.4 1.0 copy-done.6
  268.9 0.5 convolution_convert_fusion.1
  269.3 12.4 %collective-permute-done.11 = bf16[1,128,1024]{2,1,0:T(8,128)(2,1)S(1)} collective-permute-done((bf16[1,128,1024]{2,1,0:T(8,128)(2,1)S(1)}, bf16[1,128,1024]{2,1,0:T(8,128)(2,1)S(1)}, u32[]{:S(2)}, u32[]{:S(2)}) %collective-permute-start.11) | collective-permute-done | bytes 262176 | tf_op jit(solution)/shard_map/ppermute | solution.py:31
  281.7 0.5 convolution_convert_fusion
  282.4 3.9 collective-permute-start.12
  286.3 1.6 collective-permute-start.14
  287.9 3.4 collective-permute-start.16
  291.3 3.7 collective-permute-done.12
  295.0 1.1 collective-permute-done.13
  296.1 4.3 %collective-permute-start.18 = (bf16[2,72,1024]{2,1,0:T(8,128)(2,1)S(1)}, bf16[2,72,1024]{2,1,0:T(8,128)(2,1)S(1)}, u32[]{:S(2)}, u32[]{:S(2)}) collective-permute-start(bf16[2,72,1024]{2,1,0:T(8,128)(2,1)S(1)} %get-tuple-element.51), channel_id=1, source_target_pairs={{0,14},{2,12},{4,10},{6,8},{8,6},{10,4},{12,2},{14,0},{16,30},{18,... | collective-permute-start | bytes 884744 | tf_op jit(solution)/shard_map/ppermute | solution.py:31
  300.4 6.8 %collective-permute-done.14 = bf16[2,72,1024]{2,1,0:T(8,128)(2,1)S(1)} collective-permute-done((bf16[2,72,1024]{2,1,0:T(8,128)(2,1)S(1)}, bf16[2,72,1024]{2,1,0:T(8,128)(2,1)S(1)}, u32[]{:S(2)}, u32[]{:S(2)}) %collective-permute-start.14) | collective-permute-done | bytes 294944 | tf_op jit(solution)/shard_map/ppermute | solution.py:31
  307.3 4.6 %collective-permute-done.17 = bf16[2,72,1024]{2,1,0:T(8,128)(2,1)S(1)} collective-permute-done((bf16[2,72,1024]{2,1,0:T(8,128)(2,1)S(1)}, bf16[2,72,1024]{2,1,0:T(8,128)(2,1)S(1)}, u32[]{:S(2)}, u32[]{:S(2)}) %collective-permute-start.17) | collective-permute-done | bytes 294944 | tf_op jit(solution)/shard_map/ppermute | solution.py:31
  311.9 5.1 %collective-permute-done.18 = bf16[2,72,1024]{2,1,0:T(8,128)(2,1)S(1)} collective-permute-done((bf16[2,72,1024]{2,1,0:T(8,128)(2,1)S(1)}, bf16[2,72,1024]{2,1,0:T(8,128)(2,1)S(1)}, u32[]{:S(2)}, u32[]{:S(2)}) %collective-permute-start.18) | collective-permute-done | bytes 294944 | tf_op jit(solution)/shard_map/ppermute | solution.py:31
  317.6 0.5 collective-permute-start.20
  318.1 3.2 collective-permute-done.19.refs_3_
  321.4 1.0 copy-done.11
  322.4 8.9 %experts.2 = (bf16[1,576,1024]{2,1,0:T(8,128)(2,1)S(1)}, bf16[1,576,1024]{2,1,0:T(8,128)(2,1)}) custom-call(s32[2]{0:T(128)S(1)} %fusion.111.refs_0_, s32[2]{0:T(128)S(1)} %fusion.112.refs_1_, bf16[1,576,1024]{2,1,0:T(8,128)(2,1)} %bitcast.141, bf16[1,576,1024]{2,1,0:T(8,128)(2,1)} %copy-done.11, bf16[1,2048,1536]{2,1,0:T(8,128)(2,1)} %bitcast.53.refs_4_), custom_call_target="tpu_custom_call" | custom-call | flops 1 | bytes 1 | tf_op jit(solution)/shard_map/experts/pallas_call | solution.py:312
  331.4 2.9 collective-permute-done.21
  334.3 1.5 add_convert_fusion.1
  335.8 3.6 all-to-all-start.3
  339.4 8.8 %experts.3 = (bf16[1,576,1024]{2,1,0:T(8,128)(2,1)S(1)}, bf16[1,576,1024]{2,1,0:T(8,128)(2,1)}) custom-call(s32[2]{0:T(128)S(1)} %fusion.111.refs_0_, s32[2]{0:T(128)S(1)} %fusion.112.refs_1_, bf16[1,576,1024]{2,1,0:T(8,128)(2,1)} %bitcast.139, bf16[1,576,1024]{2,1,0:T(8,128)(2,1)} %collective-permute-done.20.refs_3_, bf16[1,2048,1536]{2,1,0:T(8,128)(2,1)} %bitcast.53.refs_4_), custom_call_target="tpu_custom_call" | custom-call | flops 1 | bytes 1 | tf_op jit(solution)/shard_map/experts/pallas_call | solution.py:312
  348.8 2.5 collective-permute-done.22
  351.3 1.5 add_convert_fusion
  352.8 3.1 all-to-all-done.3
  355.9 4.2 %all-to-all-start.4 = ((bf16[8,1,72,1024]{3,2,1,0:T(8,128)(2,1)}), bf16[8,1,72,1024]{3,2,1,0:T(8,128)(2,1)}, u32[]{:S(2)}, u32[]{:S(2)}) async-start(bf16[8,1,72,1024]{3,2,1,0:T(8,128)(2,1)} %bitcast.58), calls=%async_computation.4 | async-start | bytes 2359296 | tf_op jit(solution)/shard_map/all_to_all | solution.py:592
  360.3 1.4 collective-permute-start.10
  362.0 11.8 %collective-permute-done.10 = f32[1,128,16]{2,1,0:T(8,128)S(1)} collective-permute-done((f32[1,128,16]{2,1,0:T(8,128)S(1)}, f32[1,128,16]{2,1,0:T(8,128)S(1)}, u32[]{:S(2)}, u32[]{:S(2)}) %collective-permute-start.10) | collective-permute-done | bytes 8224 | tf_op jit(solution)/shard_map/ppermute | solution.py:31
  374.7 0.8 fusion.18
  375.6 3.5 collective-permute-start.23
  379.7 2.1 fusion.24
  381.8 19.2 %collective-permute-done.23 = f32[128,1024]{1,0:T(8,128)S(1)} collective-permute-done((f32[128,1024]{1,0:T(8,128)S(1)}, f32[128,1024]{1,0:T(8,128)S(1)}, u32[]{:S(2)}, u32[]{:S(2)}) %collective-permute-start.23) | collective-permute-done | bytes 524320 | tf_op jit(solution)/shard_map/ppermute | solution.py:31
  401.0 0.9 fusion.15
  (152 shorter events, 8.1 us)
Async XLA Ops:
  6.5 6.4 %copy-start.3 = (f32[128,1024]{1,0:T(8,128)S(1)}, f32[128,1024]{1,0:T(8,128)}, u32[]{:S(2)}) copy-start(f32[128,1024]{1,0:T(8,128)} %query_ref.1) | copy-start | bytes 1572868
  6.5 6.4 %copy-start.4 = (f32[128,1024]{1,0:T(8,128)S(1)}, f32[128,1024]{1,0:T(8,128)}, u32[]{:S(2)}) copy-start(f32[128,1024]{1,0:T(8,128)} %key_ref.1) | copy-start | bytes 1572868
  6.5 6.4 %copy-start.5 = (f32[128,1024]{1,0:T(8,128)S(1)}, f32[128,1024]{1,0:T(8,128)}, u32[]{:S(2)}) copy-start(f32[128,1024]{1,0:T(8,128)} %value_ref.1) | copy-start | bytes 1572868
  9.9 11.0 %copy-start.12 = (f32[1024,128]{1,0:T(8,128)S(1)}, f32[1024,128]{1,0:T(8,128)}, u32[]{:S(2)}) copy-start(f32[1024,128]{1,0:T(8,128)} %param.21) | copy-start | bytes 1572868
  9.9 11.1 %collective-permute-start = (bf16[1,128,1024]{2,1,0:T(8,128)(2,1)S(1)}, bf16[1,128,1024]{2,1,0:T(8,128)(2,1)S(1)}, u32[]{:S(2)}, u32[]{:S(2)}) collective-permute-start(bf16[1,128,1024]{2,1,0:T(8,128)(2,1)S(1)} %fusion.47), channel_id=1, source_target_pairs={{0,8},{2,10},{4,12},{6,14},{8,0},{10,2},{12,4},{14,6},{16,24},{18,... | collective-permute-start | bytes 786440 | tf_op jit(solution)/shard_map/ppermute | solution.py:31
  14.8 6.1 %copy-start.13 = (f32[128,16]{0,1:T(8,128)S(1)}, f32[128,16]{0,1:T(8,128)}, u32[]{:S(2)}) copy-start(f32[128,16]{0,1:T(8,128)} %param.23) | copy-start | bytes 24580
  14.8 52.0 %all-to-all-start = ((bf16[16,128,384]{2,1,0:T(8,128)(2,1)}), bf16[16,128,384]{2,1,0:T(8,128)(2,1)}, u32[]{:S(2)}, u32[]{:S(2)}) async-start(bf16[16,128,384]{2,1,0:T(8,128)(2,1)} %pack_heads.1), calls=%async_computation | async-start | bytes 3145728 | tf_op jit(solution)/shard_map/all_to_all | solution.py:373
  20.8 149.7 %all-gather.2.cloned.1.call-start = ((), (), s32[]{:S(2)}) async-start(), calls=%async_computation.5 | async-start | bytes 4526080 | tf_op jit(solution)/shard_map/all_gather | solution.py:399
  21.0 22.7 %collective-permute-start.1 = (bf16[2,128,512]{2,1,0:T(8,128)(2,1)S(1)}, bf16[2,128,512]{2,1,0:T(8,128)(2,1)S(1)}, u32[]{:S(2)}, u32[]{:S(2)}) collective-permute-start(bf16[2,128,512]{2,1,0:T(8,128)(2,1)S(1)} %get-tuple-element.59), channel_id=1, source_target_pairs={{0,4},{2,6},{4,0},{6,2},{8,12},{10,14},{12,8},{14,10},{16,20},{18,... | collective-permute-start | bytes 786440 | tf_op jit(solution)/shard_map/ppermute | solution.py:31
  23.7 20.1 %collective-permute-start.3 = (bf16[2,128,512]{2,1,0:T(8,128)(2,1)S(1)}, bf16[2,128,512]{2,1,0:T(8,128)(2,1)S(1)}, u32[]{:S(2)}, u32[]{:S(2)}) collective-permute-start(bf16[2,128,512]{2,1,0:T(8,128)(2,1)S(1)} %get-tuple-element.60), channel_id=1, source_target_pairs={{0,2},{2,0},{4,6},{6,4},{8,10},{10,8},{12,14},{14,12},{16,18},{18,... | collective-permute-start | bytes 786440 | tf_op jit(solution)/shard_map/ppermute | solution.py:31
  43.9 15.4 %collective-permute-start.4 = (bf16[4,128,512]{2,1,0:T(8,128)(2,1)S(1)}, bf16[4,128,512]{2,1,0:T(8,128)(2,1)S(1)}, u32[]{:S(2)}, u32[]{:S(2)}) collective-permute-start(bf16[4,128,512]{2,1,0:T(8,128)(2,1)S(1)} %pad_maximum_fusion.3), channel_id=1, source_target_pairs={{0,4},{2,6},{4,0},{6,2},{8,12},{10,14},{12,8},{14,10},{16,20},{18,... | collective-permute-start | bytes 1572872 | tf_op jit(solution)/shard_map/ppermute | solution.py:31
  44.0 18.2 %collective-permute-start.2 = (bf16[4,128,512]{2,1,0:T(8,128)(2,1)S(1)}, bf16[4,128,512]{2,1,0:T(8,128)(2,1)S(1)}, u32[]{:S(2)}, u32[]{:S(2)}) collective-permute-start(bf16[4,128,512]{2,1,0:T(8,128)(2,1)S(1)} %pad_maximum_fusion.2), channel_id=1, source_target_pairs={{0,2},{2,0},{4,6},{6,4},{8,10},{10,8},{12,14},{14,12},{16,18},{18,... | collective-permute-start | bytes 1572872 | tf_op jit(solution)/shard_map/ppermute | solution.py:31
  62.4 3.9 copy-start.15
  62.7 4.4 %collective-permute-start.5 = (bf16[1024,1024]{1,0:T(8,128)(2,1)S(1)}, bf16[1024,1024]{1,0:T(8,128)(2,1)}, u32[]{:S(2)}, u32[]{:S(2)}) collective-permute-start(bf16[1024,1024]{1,0:T(8,128)(2,1)S(1)} %pad_maximum_fusion.refs_1_), channel_id=1, source_target_pairs={{1,0},{0,1},{3,2},{2,3},{5,4},{4,5},{7,6},{6,7},{9,8},{8,9},{11,10... | collective-permute-start | bytes 6291464 | tf_op jit(solution)/shard_map/ppermute | solution.py:26
  67.0 1.0 copy-start.1
  68.1 1.0 copy-start.2
  69.1 11.7 %copy-start.16 = (f32[8]{0:T(128)S(1)}, f32[8]{0:T(128)}, u32[]{:S(2)}) copy-start(f32[8]{0:T(128)} %param.22) | copy-start | bytes 100
  75.0 7.5 %collective-permute-start.6 = (bf16[64,384]{1,0:T(8,128)(2,1)S(1)}, bf16[64,384]{1,0:T(8,128)(2,1)S(1)}, u32[]{:S(2)}, u32[]{:S(2)}) collective-permute-start(bf16[64,384]{1,0:T(8,128)(2,1)S(1)} %constant_dynamic-slice_fusion.8), channel_id=1, source_target_pairs={{0,16},{2,18},{4,20},{6,22},{8,24},{10,26},{12,28},{14,30},{1,17},... | collective-permute-start | bytes 147464 | tf_op jit(solution)/shard_map/ppermute | solution.py:21
  89.2 9.6 %collective-permute-start.7 = (bf16[64,128]{1,0:T(8,128)(2,1)S(1)}, bf16[64,128]{1,0:T(8,128)(2,1)S(1)}, u32[]{:S(2)}, u32[]{:S(2)}) collective-permute-start(bf16[64,128]{1,0:T(8,128)(2,1)S(1)} %slice.131), channel_id=1, source_target_pairs={{16,0},{18,2},{20,4},{22,6},{24,8},{26,10},{28,12},{30,14},{17,1},... | collective-permute-start | bytes 49160 | tf_op jit(solution)/shard_map/ppermute | solution.py:21
  117.4 5.0 %copy-start.14 = (s32[128,8]{0,1:T(8,128)S(1)}, s32[128,8]{0,1:T(8,128)}, u32[]{:S(2)}) copy-start(s32[128,8]{0,1:T(8,128)} %param.29) | copy-start | bytes 12292
  117.4 204.9 %all-to-all-start.2 = ((bf16[16,128,1536]{2,1,0:T(8,128)(2,1)}), bf16[16,128,1536]{2,1,0:T(8,128)(2,1)}, u32[]{:S(2)}, u32[]{:S(2)}) async-start(bf16[16,128,1536]{2,1,0:T(8,128)(2,1)} %order_experts.1), calls=%async_computation.2 | async-start | bytes 12582912 | tf_op jit(solution)/shard_map/all_to_all | solution.py:510
  122.4 143.5 %collective-permute-start.9 = (s32[1,128,8]{1,2,0:T(8,128)S(1)}, s32[1,128,8]{1,2,0:T(8,128)S(1)}, u32[]{:S(2)}, u32[]{:S(2)}) collective-permute-start(s32[1,128,8]{1,2,0:T(8,128)S(1)} %bitcast.148), channel_id=1, source_target_pairs={{0,16},{2,18},{4,20},{6,22},{8,24},{10,26},{12,28},{14,30},{16,0},... | collective-permute-start | bytes 12296 | tf_op jit(solution)/shard_map/ppermute | solution.py:31
  170.6 96.2 %copy-start = (bf16[128,2048]{1,0:T(8,128)(2,1)S(1)}, bf16[128,2048]{1,0:T(8,128)(2,1)}, u32[]{:S(2)}) copy-start(bf16[128,2048]{1,0:T(8,128)(2,1)} %refs_2_.1) | copy-start | bytes 1572868
  170.6 96.2 %copy-start.8 = (f32[2048]{0:T(1024)S(1)}, f32[2048]{0:T(1024)}, u32[]{:S(2)}) copy-start(f32[2048]{0:T(1024)} %param.17) | copy-start | bytes 24580
  173.6 93.2 %collective-permute-start.8 = (f32[128,2048]{1,0:T(8,128)S(1)}, f32[128,2048]{1,0:T(8,128)S(1)}, u32[]{:S(2)}, u32[]{:S(2)}) collective-permute-start(f32[128,2048]{1,0:T(8,128)S(1)} %fusion.refs_0_), channel_id=1, source_target_pairs={{1,0},{0,1},{3,2},{2,3},{5,4},{4,5},{7,6},{6,7},{9,8},{8,9},{11,10... | collective-permute-start | bytes 3145736 | tf_op jit(solution)/shard_map/ppermute | solution.py:26
  267.4 1.0 copy-start.6
  268.4 13.3 %collective-permute-start.11 = (bf16[1,128,1024]{2,1,0:T(8,128)(2,1)S(1)}, bf16[1,128,1024]{2,1,0:T(8,128)(2,1)S(1)}, u32[]{:S(2)}, u32[]{:S(2)}) collective-permute-start(bf16[1,128,1024]{2,1,0:T(8,128)(2,1)S(1)} %dynamic-slice_bitcast_fusion), channel_id=1, source_target_pairs={{0,16},{2,18},{4,20},{6,22},{8,24},{10,26},{12,28},{14,30},{16,0},... | collective-permute-start | bytes 786440 | tf_op jit(solution)/shard_map/ppermute | solution.py:31
  282.4 12.6 %collective-permute-start.12 = (bf16[2,72,1024]{2,1,0:T(8,128)(2,1)S(1)}, bf16[2,72,1024]{2,1,0:T(8,128)(2,1)S(1)}, u32[]{:S(2)}, u32[]{:S(2)}) collective-permute-start(bf16[2,72,1024]{2,1,0:T(8,128)(2,1)S(1)} %get-tuple-element.53), channel_id=1, source_target_pairs={{0,2},{2,0},{4,6},{6,4},{8,10},{10,8},{12,14},{14,12},{16,18},{18,... | collective-permute-start | bytes 884744 | tf_op jit(solution)/shard_map/ppermute | solution.py:31
  286.2 9.9 %collective-permute-start.13 = (bf16[2,72,1024]{2,1,0:T(8,128)(2,1)S(1)}, bf16[2,72,1024]{2,1,0:T(8,128)(2,1)S(1)}, u32[]{:S(2)}, u32[]{:S(2)}) collective-permute-start(bf16[2,72,1024]{2,1,0:T(8,128)(2,1)S(1)} %get-tuple-element.54), channel_id=1, source_target_pairs={{0,4},{2,6},{4,0},{6,2},{8,12},{10,14},{12,8},{14,10},{16,20},{18,... | collective-permute-start | bytes 884744 | tf_op jit(solution)/shard_map/ppermute | solution.py:31
  286.3 20.9 %collective-permute-start.14 = (bf16[2,72,1024]{2,1,0:T(8,128)(2,1)S(1)}, bf16[2,72,1024]{2,1,0:T(8,128)(2,1)S(1)}, u32[]{:S(2)}, u32[]{:S(2)}) collective-permute-start(bf16[2,72,1024]{2,1,0:T(8,128)(2,1)S(1)} %get-tuple-element.55), channel_id=1, source_target_pairs={{0,6},{2,4},{4,2},{6,0},{8,14},{10,12},{12,10},{14,8},{16,22},{18,... | collective-permute-start | bytes 884744 | tf_op jit(solution)/shard_map/ppermute | solution.py:31
  287.9 19.3 %collective-permute-start.15 = (bf16[2,72,1024]{2,1,0:T(8,128)(2,1)S(1)}, bf16[2,72,1024]{2,1,0:T(8,128)(2,1)S(1)}, u32[]{:S(2)}, u32[]{:S(2)}) collective-permute-start(bf16[2,72,1024]{2,1,0:T(8,128)(2,1)S(1)} %get-tuple-element.56), channel_id=1, source_target_pairs={{0,8},{2,10},{4,12},{6,14},{8,0},{10,2},{12,4},{14,6},{16,24},{18,... | collective-permute-start | bytes 884744 | tf_op jit(solution)/shard_map/ppermute | solution.py:31
  287.9 19.4 %collective-permute-start.16 = (bf16[2,72,1024]{2,1,0:T(8,128)(2,1)S(1)}, bf16[2,72,1024]{2,1,0:T(8,128)(2,1)S(1)}, u32[]{:S(2)}, u32[]{:S(2)}) collective-permute-start(bf16[2,72,1024]{2,1,0:T(8,128)(2,1)S(1)} %get-tuple-element.58), channel_id=1, source_target_pairs={{0,10},{2,8},{4,14},{6,12},{8,2},{10,0},{12,6},{14,4},{16,26},{18,... | collective-permute-start | bytes 884744 | tf_op jit(solution)/shard_map/ppermute | solution.py:31
  295.0 16.9 %collective-permute-start.17 = (bf16[2,72,1024]{2,1,0:T(8,128)(2,1)S(1)}, bf16[2,72,1024]{2,1,0:T(8,128)(2,1)S(1)}, u32[]{:S(2)}, u32[]{:S(2)}) collective-permute-start(bf16[2,72,1024]{2,1,0:T(8,128)(2,1)S(1)} %get-tuple-element.57), channel_id=1, source_target_pairs={{0,12},{2,14},{4,8},{6,10},{8,4},{10,6},{12,0},{14,2},{16,28},{18,... | collective-permute-start | bytes 884744 | tf_op jit(solution)/shard_map/ppermute | solution.py:31
  296.1 20.9 %collective-permute-start.18 = (bf16[2,72,1024]{2,1,0:T(8,128)(2,1)S(1)}, bf16[2,72,1024]{2,1,0:T(8,128)(2,1)S(1)}, u32[]{:S(2)}, u32[]{:S(2)}) collective-permute-start(bf16[2,72,1024]{2,1,0:T(8,128)(2,1)S(1)} %get-tuple-element.51), channel_id=1, source_target_pairs={{0,14},{2,12},{4,10},{6,8},{8,6},{10,4},{12,2},{14,0},{16,30},{18,... | collective-permute-start | bytes 884744 | tf_op jit(solution)/shard_map/ppermute | solution.py:31
  317.5 4.9 %copy-start.10 = (bf16[8,1,1,72,1024]{4,3,0,2,1:T(8,128)(2,1)}, bf16[8,1,1,72,1024]{4,3,0,2,1:T(8,128)(2,1)S(1)}, u32[]{:S(2)}) copy-start(bf16[8,1,1,72,1024]{4,3,0,2,1:T(8,128)(2,1)S(1)} %get-tuple-element.50) | copy-start | bytes 3538948
  317.5 13.7 %copy-start.9 = (bf16[8,1,1,72,1024]{4,3,0,2,1:T(8,128)(2,1)}, bf16[8,1,1,72,1024]{4,3,0,2,1:T(8,128)(2,1)S(1)}, u32[]{:S(2)}) copy-start(bf16[8,1,1,72,1024]{4,3,0,2,1:T(8,128)(2,1)S(1)} %get-tuple-element.49) | copy-start | bytes 3538948
  317.5 3.8 collective-permute-start.19
  317.6 4.8 %collective-permute-start.20 = (bf16[1,576,1024]{2,1,0:T(8,128)(2,1)S(1)}, bf16[1,576,1024]{2,1,0:T(8,128)(2,1)}, u32[]{:S(2)}, u32[]{:S(2)}) collective-permute-start(bf16[1,576,1024]{2,1,0:T(8,128)(2,1)S(1)} %bitcast.138), channel_id=1, source_target_pairs={{1,0},{0,1},{3,2},{2,3},{5,4},{4,5},{7,6},{6,7},{9,8},{8,9},{11,10... | collective-permute-start | bytes 3538952 | tf_op jit(solution)/shard_map/ppermute | solution.py:26
  321.3 1.0 copy-start.11
  331.2 3.1 collective-permute-start.21
  335.8 20.1 %all-to-all-start.3 = ((bf16[8,1,72,1024]{3,2,1,0:T(8,128)(2,1)}), bf16[8,1,72,1024]{3,2,1,0:T(8,128)(2,1)S(1)}, u32[]{:S(2)}, u32[]{:S(2)}) async-start(bf16[8,1,72,1024]{3,2,1,0:T(8,128)(2,1)} %bitcast.55), calls=%async_computation.3 | async-start | bytes 2359296 | tf_op jit(solution)/shard_map/all_to_all | solution.py:592
  348.2 3.1 collective-permute-start.22
  355.9 23.8 %all-to-all-start.4 = ((bf16[8,1,72,1024]{3,2,1,0:T(8,128)(2,1)}), bf16[8,1,72,1024]{3,2,1,0:T(8,128)(2,1)}, u32[]{:S(2)}, u32[]{:S(2)}) async-start(bf16[8,1,72,1024]{3,2,1,0:T(8,128)(2,1)} %bitcast.58), calls=%async_computation.4 | async-start | bytes 2359296 | tf_op jit(solution)/shard_map/all_to_all | solution.py:592
  360.3 13.6 %collective-permute-start.10 = (f32[1,128,16]{2,1,0:T(8,128)S(1)}, f32[1,128,16]{2,1,0:T(8,128)S(1)}, u32[]{:S(2)}, u32[]{:S(2)}) collective-permute-start(f32[1,128,16]{2,1,0:T(8,128)S(1)} %fusion.123), channel_id=1, source_target_pairs={{0,16},{2,18},{4,20},{6,22},{8,24},{10,26},{12,28},{14,30},{16,0},... | collective-permute-start | bytes 24584 | tf_op jit(solution)/shard_map/ppermute | solution.py:31
  375.6 25.4 %collective-permute-start.23 = (f32[128,1024]{1,0:T(8,128)S(1)}, f32[128,1024]{1,0:T(8,128)S(1)}, u32[]{:S(2)}, u32[]{:S(2)}) collective-permute-start(f32[128,1024]{1,0:T(8,128)S(1)} %slice_add_fusion.2), channel_id=1, source_target_pairs={{0,16},{2,18},{4,20},{6,22},{8,24},{10,26},{12,28},{14,30},{16,0},... | collective-permute-start | bytes 1572872 | tf_op jit(solution)/shard_map/ppermute | solution.py:31
  379.4 21.6 %copy-start.7 = (f32[128,2048]{1,0:T(8,128)S(1)}, f32[128,2048]{1,0:T(8,128)}, u32[]{:S(2)}) copy-start(f32[128,2048]{1,0:T(8,128)} %copy-done.6) | copy-start | bytes 3145732
Sparse Core Ops, SparseCore 0:
  24.4 146.1 all-gather.1

commit v5 on v4

--- a/solution.py
+++ b/solution.py
@@ -116,24 +116,26 @@
     return (new_max, denominator, accumulated)
 
 
-def order_body(order_ref, gate_ref, up_ref, down_ref, out_ref):
-    width = gate_ref.shape[2]
-    for k, source in enumerate((gate_ref, up_ref, down_ref)):
-        out_ref[:, :, k * width : (k + 1) * width] = source[...].astype(jnp.bfloat16)
+def order_body(order_ref, gate_ref, up_ref, down_ref, gate_out, up_out, down_out):
+    gate_out[...] = gate_ref[...].astype(jnp.bfloat16)
+    up_out[...] = up_ref[...].astype(jnp.bfloat16)
+    down_out[...] = down_ref[...].astype(jnp.bfloat16)
 
 
 def order_experts(layout_map, gate, up, down):
     count, rows, width = gate.shape
     source = pl.BlockSpec((1, rows, width), lambda place, order: (order[place], 0, 0))
+    target = pl.BlockSpec((1, rows, width), lambda place, order: (place, 0, 0))
     return pl.pallas_call(
         order_body,
         grid_spec=pltpu.PrefetchScalarGridSpec(
             num_scalar_prefetch=1,
             grid=(count,),
             in_specs=[source, source, source],
-            out_specs=pl.BlockSpec((1, rows, 3 * width), lambda place, order: (place, 0, 0)),
+            out_specs=[target, target, target],
         ),
-        out_shape=jax.ShapeDtypeStruct((count, rows, 3 * width), jnp.bfloat16),
+        out_shape=[jax.ShapeDtypeStruct((count, rows, width), jnp.bfloat16)] * 3,
+        cost_estimate=SMALL,
         name="order_experts",
     )(layout_map, gate, up, down)
 
@@ -281,23 +283,24 @@
 
 
 def expert_body(turn_count, share, in_ref, out_ref, *refs):
-    rows, weight_ref, outs = (refs[:turn_count], refs[turn_count], refs[turn_count + 1 :])
-    hidden = weight_ref.shape[2] // 3
-    gate_up = 0.0
+    rows, (gate_ref, up_ref, down_ref), outs = (
+        refs[:turn_count],
+        refs[turn_count : turn_count + 3],
+        refs[turn_count + 3 :],
+    )
+    gate = up = 0.0
     for turn in range(turn_count):
-        first = pl.multiple_of(in_ref[turn], share)
-        gate_up = gate_up + jnp.dot(
-            rows[turn][0],
-            weight_ref[0, pl.ds(first, share), : 2 * hidden],
-            preferred_element_type=jnp.float32,
-        )
-    gate, up = (gate_up[:, :hidden], gate_up[:, hidden:])
+        here = pl.ds(pl.multiple_of(in_ref[turn], share), share)
+        gate = gate + jnp.dot(
+            rows[turn][0], gate_ref[0, here, :], preferred_element_type=jnp.float32
+        )
+        up = up + jnp.dot(rows[turn][0], up_ref[0, here, :], preferred_element_type=jnp.float32)
     state = (gate / (1.0 + jnp.exp(-gate)) * up).astype(jnp.bfloat16)
     for turn in range(turn_count):
-        first = pl.multiple_of(out_ref[turn], share)
+        here = pl.ds(pl.multiple_of(out_ref[turn], share), share)
         outs[turn][0] = lax.dot_general(
             state,
-            weight_ref[0, pl.ds(first, share), 2 * hidden :],
+            down_ref[0, here, :],
             (((1,), (1,)), ((), ())),
             preferred_element_type=jnp.float32,
         ).astype(jnp.bfloat16)
@@ -307,21 +310,21 @@
     local_experts, row_count, share = row_blocks[0].shape
     step = row_count // 2 if row_count % 32 == 0 else row_count
     block = pl.BlockSpec((1, step, share), lambda e, place, a, b: (e, place, 0))
-    whole = pl.BlockSpec((1, *weights.shape[1:]), lambda e, place, a, b: (e, 0, 0))
+    whole = pl.BlockSpec((1, *weights[0].shape[1:]), lambda e, place, a, b: (e, 0, 0))
     count = len(row_blocks)
     return pl.pallas_call(
         lambda *refs: expert_body(count, share, *refs),
         grid_spec=pltpu.PrefetchScalarGridSpec(
             num_scalar_prefetch=2,
             grid=(local_experts, row_count // step),
-            in_specs=[block] * count + [whole],
+            in_specs=[block] * count + [whole] * 3,
             out_specs=[block] * count,
         ),
         out_shape=[jax.ShapeDtypeStruct(row_blocks[0].shape, jnp.bfloat16)] * count,
         compiler_params=pltpu.CompilerParams(vmem_limit_bytes=52 * 2**20),
         cost_estimate=SMALL,
         name="experts",
-    )(in_starts, out_starts, *row_blocks, weights)
+    )(in_starts, out_starts, *row_blocks, *weights)
 
 
 def shards(
@@ -366,6 +369,7 @@
 
     offsets = jnp.arange(token_count, dtype=jnp.int32)
     turns = jnp.arange(head_count, dtype=jnp.int32)
+    aligned = part_count == prompt_count and part_slots + stagger <= HALF_WIN
     group_masks = masks_below(head_count)
     groups = [[first + k for k in range(head_count)] for first in range(0, seq_count, head_count)]
     part_masks = masks_below(seq_count, head_count)
@@ -380,8 +384,13 @@
 
     normed = rms_scale(tokens.astype(jnp.float32), attn_gain).astype(jnp.bfloat16)
     share = lax.dynamic_slice_in_dim(normed, tp_place * col_share, col_share, 1)
-    own_blocks = order_experts(layout_map, expert_gate, expert_up, expert_down)
+    all_routes, part_turns = doubled(routes[None], part_masks, 0)
+    if aligned:
+        edge = from_behind(share[token_count - stagger :], "seq", head_count)
+        edge = jnp.where(head == head_count - 1, edge, jnp.zeros((), jnp.bfloat16))
+    own_gate, own_up, own_down = order_experts(layout_map, expert_gate, expert_up, expert_down)
     first_rows, first_turns = doubled(share[None], group_masks[:1], 0)
+    first_rows, all_routes = lax.optimization_barrier((first_rows, all_routes))
     pieces = []
     for piece, masks in (
         (first_rows[:, :, : col_share // 2], group_masks[1:]),
@@ -390,11 +399,27 @@
         known = first_turns
         for mask in masks:
             if mask == masks[-1]:
-                piece, own_blocks = lax.optimization_barrier((piece, own_blocks))
+                piece, own_gate = lax.optimization_barrier((piece, own_gate))
             piece = jnp.concatenate([piece, swapped(piece, "seq", mask)], axis=0)
             known = known + [turn ^ mask for turn in known]
         pieces.append(jnp.concatenate([piece[known.index(m)] for m in range(head_count)], axis=0))
     part_rows = jnp.concatenate(pieces, axis=1)
+    part_ids = (part * head_count + (head ^ turns))[:, None] * token_count + offsets[None, :]
+    part_ids = part_ids.reshape(-1)
+    if aligned:
+        for mask in group_masks:
+            edge = edge + swapped(edge, "seq", mask)
+        part_rows = jnp.concatenate([part_rows, edge], axis=0)
+        edge_ids = part * part_slots - stagger + jnp.arange(stagger, dtype=jnp.int32)
+        part_ids = jnp.concatenate([part_ids, edge_ids])
+
+    def to_owner(blocks):
+        taken = lax.all_to_all(blocks, "seq", split_axis=0, concat_axis=0, tiled=True)
+        taken = taken.reshape(seq_count, local_experts, *blocks.shape[1:])
+        return jnp.swapaxes(taken, 0, 1).reshape(local_experts, model_width, blocks.shape[2])
+
+    own_gate, head_weights = lax.optimization_barrier((own_gate, head_weights))
+    server_gate = to_owner(own_gate)
 
     out_all = lax.all_gather(
         jnp.concatenate([w_out, router.T], axis=0).astype(jnp.bfloat16), "seq", axis=1, tiled=True
@@ -408,7 +433,6 @@
             ]
         )
 
-    all_routes, part_turns = doubled(routes[None], part_masks, 0)
     expert_ids = jnp.arange(expert_count, dtype=jnp.int32)
     block_rows = local_experts * capacity
     columns = jnp.arange(head_count * block_rows, dtype=jnp.int32)
@@ -432,8 +456,6 @@
     routings = [routing(turn, all_routes[k]) for k, turn in enumerate(part_turns)]
     chosen, valid_token, _ = routings[0]
 
-    part_ids = (part * head_count + (head ^ turns))[:, None] * token_count + offsets[None, :]
-    part_ids = part_ids.reshape(-1)
     part_positions = prompt_split(part_ids, slot_len, stagger, prompt_count)[1]
     half_dim = HEAD // 2
     frequency = ROPE_BASE ** (-jnp.arange(half_dim, dtype=jnp.float32) / half_dim)
@@ -451,27 +473,28 @@
             jnp.zeros((row_count, HEAD), jnp.float32),
         )
 
-    if part_count == prompt_count and part_slots + stagger <= HALF_WIN:
-        edge_start = (head ^ (head_count - 1)) * token_count + token_count - stagger
-        edge = from_behind(
-            lax.dynamic_slice_in_dim(rows, edge_start, stagger, 0), "seq", head_count
-        )
-        edge_ids = part * part_slots - stagger + jnp.arange(stagger, dtype=jnp.int32)
-        row_ids = jnp.concatenate([part_ids, edge_ids])
-        row_prompt, row_position = prompt_split(row_ids, slot_len, stagger, prompt_count)
-        row_live = (row_ids >= 0) & (row_position < length_of(row_prompt, real_lengths))
-        mixed = attend_once(
-            sink,
-            row_prompt,
-            jnp.where(row_live, row_prompt, -1),
-            jnp.concatenate([rows, edge], axis=0),
-        )
-        edge_back = from_behind(mixed[part_slots:], "seq", -head_count)
-        mixed = mixed[:part_slots]
-        kept = lax.dynamic_slice_in_dim(mixed, edge_start, stagger, 0)
-        mixed = lax.dynamic_update_slice_in_dim(
-            mixed, jnp.where(part < part_count - 1, edge_back, kept), edge_start, 0
-        )
+    if aligned:
+        row_prompt, row_position = prompt_split(part_ids, slot_len, stagger, prompt_count)
+        row_live = (part_ids >= 0) & (row_position < length_of(row_prompt, real_lengths))
+        mixed = attend_once(sink, row_prompt, jnp.where(row_live, row_prompt, -1), rows)
+        mixed, server_gate = lax.optimization_barrier((mixed, server_gate))
+        by_slot = by_place(mixed[:part_slots].reshape(head_count, token_count, HEAD))
+        by_slot = jnp.concatenate([mixed[part_slots:], by_slot.reshape(part_slots, HEAD)], axis=0)
+        by_slot = lax.dynamic_update_slice_in_dim(
+            jnp.zeros((stagger + total_slots, HEAD), jnp.bfloat16), by_slot, part * part_slots, 0
+        )[stagger:]
+        taken = lax.all_to_all(
+            by_slot.reshape(seq_count, token_count, HEAD),
+            "seq",
+            split_axis=0,
+            concat_axis=0,
+            tiled=True,
+        )
+        kept = lax.dynamic_slice_in_dim(taken, part * head_count, head_count, 0)
+        next_part = jnp.minimum(part + 1, part_count - 1)
+        moved = lax.dynamic_slice_in_dim(taken, next_part * head_count, head_count, 0)
+        is_moved = (head == head_count - 1) & (offsets >= token_count - stagger)
+        attention_result = jnp.where(is_moved[None, :, None], moved, kept)
     else:
         query_rows, key_rows, value_rows = (rows[:, k * HEAD : (k + 1) * HEAD] for k in range(3))
         softmax_state = attend(
@@ -497,20 +520,17 @@
             )
         _, denominator, accumulated = softmax_state
         mixed = (accumulated / denominator).astype(jnp.bfloat16)
-    attention_result = lax.all_to_all(
-        by_place(mixed.reshape(head_count, token_count, HEAD)),
-        "seq",
-        split_axis=0,
-        concat_axis=0,
-        tiled=True,
-        axis_index_groups=groups,
-    )
-
-    attention_result, own_blocks = lax.optimization_barrier((attention_result, own_blocks))
-    server = lax.all_to_all(own_blocks, "seq", split_axis=0, concat_axis=0, tiled=True)
-    server = jnp.swapaxes(
-        server.reshape(seq_count, local_experts, *own_blocks.shape[1:]), 0, 1
-    ).reshape(local_experts, model_width, own_blocks.shape[2])
+        mixed, server_gate = lax.optimization_barrier((mixed, server_gate))
+        attention_result = lax.all_to_all(
+            by_place(mixed.reshape(head_count, token_count, HEAD)),
+            "seq",
+            split_axis=0,
+            concat_axis=0,
+            tiled=True,
+            axis_index_groups=groups,
+        )
+    attention_result, own_up = lax.optimization_barrier((attention_result, own_up))
+    server_up = to_owner(own_up)
 
     proj_width = head_count * HEAD
     partial_out = jnp.dot(
@@ -527,7 +547,14 @@
     outgoing_share = lax.dynamic_slice_in_dim(outgoing, tp_place * col_share, col_share, 1)
 
 
+    route_logits = jnp.where(chosen, logits, -jnp.inf)
+    route_exp = jnp.exp(route_logits - jnp.max(route_logits, axis=1, keepdims=True))
+    route_weight = route_exp / jnp.sum(route_exp, axis=1, keepdims=True)
+    route_weight = route_weight * valid_token[:, None]
+    all_weights, _ = doubled(route_weight[None], part_masks, 0)
     all_rows, _ = doubled(outgoing_share[None], part_masks, 0)
+    all_rows, all_weights, own_down = lax.optimization_barrier((all_rows, all_weights, own_down))
+    server_down = to_owner(own_down)
     buffer = jnp.stack(
         [
             lax.dot_general(
@@ -556,6 +583,7 @@
         tp_blocks(jnp.moveaxis(rows, 2, 0).reshape(local_experts, -1, col_share))
         for rows in (received[:, 1:], received[:, :1])
     ]
+    server = (server_gate, server_up, server_down)
     halves, server = lax.optimization_barrier((halves, server))
 
     def through_experts(row_blocks, parts):
@@ -567,12 +595,6 @@
 
     others = through_experts(halves[0], part_count - 1)
     own_rows = through_experts(halves[1], 1)
-
-    route_logits = jnp.where(chosen, logits, -jnp.inf)
-    route_exp = jnp.exp(route_logits - jnp.max(route_logits, axis=1, keepdims=True))
-    route_weight = route_exp / jnp.sum(route_exp, axis=1, keepdims=True)
-    route_weight = route_weight * valid_token[:, None]
-    all_weights, _ = doubled(route_weight[None], part_masks, 0)
 
     def weighted(k, rows):
         placed = routings[k][2]
@@ -594,11 +616,11 @@
         )
 
     others = back(others)
-    others, own_rows = lax.optimization_barrier((others, own_rows))
-    expert_mix = 0.0
-    for k, turn in enumerate(part_turns[1:]):
-        mix = weighted(k + 1, others[:, k].reshape(-1, col_share))
-        expert_mix = expert_mix + swapped(mix, "seq", turn)
+    mixes = [
+        weighted(k, others[:, k - 1].reshape(-1, col_share)) for k in range(1, len(part_turns))
+    ]
+    mixes, own_rows = lax.optimization_barrier((mixes, own_rows))
+    expert_mix = sum(swapped(mix, "seq", turn) for mix, turn in zip(mixes, part_turns[1:]))
     own_mix = weighted(0, back(own_rows)[:, 0].reshape(-1, col_share))
     return (residual + (expert_mix + own_mix)).astype(jnp.bfloat16)
 

time: 410 us -> 415 us (1.012)
  waiting for transfers between devices: 243 us -> 216 us
  local copies, waits for them, and re-layouts: 8.54 us -> 34.4 us
  starting transfers between devices: 58.2 us -> 76.4 us
  blocking collectives: 17.4 us -> 0 us
    all_to_all x1 -> x4, waiting for transfers between devices: 0.01 us -> 62.1 us  [the longest x3 47.7 us: to_owner(): lax.all_to_all(blocks, 'seq', split_axis=0, concat_axis=0, tiled=True)]
    ppermute x16 -> x19, waiting for transfers between devices: 176 us -> 119 us  [swapped(): lax.ppermute(value, axis, [(place, place ^ mask) for place in range(count)])]
    all_gather x1, waiting for transfers between devices: 45.6 us -> 0.02 us  [shards(): lax.all_gather(jnp.concatenate([w_out, router.T], axis=0).astype(jnp.bflo...]
    all_to_all x1 -> x4, starting transfers between devices: 4.97 us -> 28.3 us  [the longest x3 15.4 us: to_owner(): lax.all_to_all(blocks, 'seq', split_axis=0, concat_axis=0, tiled=True)]
    all_to_all x2, waiting for transfers between devices: 3.12 us -> 24.6 us  [back(): lax.all_to_all(blocks, 'seq', split_axis=0, concat_axis=0, tiled=True, ax...]
    unnamed x76 -> x82, local copies, waits for them, and re-layouts: 5.67 us -> 27.1 us
    all_to_all x1 -> x0, blocking collectives: 17.4 us -> none  [shards(): lax.all_to_all(by_place(mixed.reshape(head_count, token_count, HEAD)), 's...]
    ppermute x2 -> x1, waiting for transfers between devices: 9.31 us -> 0.01 us  [from_behind(): lax.ppermute(value, axis, [(source, source + steps) for source in range(f...]
  transfers between devices with their start and end apart: 29 -> 34, of which waited for: 20 -> 21; matrix products, arithmetic and copies ran while one was open for 5% -> 12% of each run, Pallas kernels for 9% -> 9%
where the time goes in v5:
time: 415 us; the launch traced here: 413 us
  waiting for transfers between devices  216 us (52%)
  starting transfers between devices  76.4 us (18%)
  Pallas kernels  45 us (11%)
  local copies, waits for them, and re-layouts  34.4 us (8%)
  other arithmetic  15.3 us (4%)
  between operations  14.2 us (3%)
  matrix products  12.1 us (3%)
    ppermute x19, waiting for transfers between devices, swapped(): lax.ppermute(value, axis, [(place, place ^ mask) for place in range(count)])  119 us
    all_to_all x3, waiting for transfers between devices, to_owner(): lax.all_to_all(blocks, 'seq', split_axis=0, concat_axis=0, tiled=True)  47.7 us
    ppermute x19, starting transfers between devices, swapped(): lax.ppermute(value, axis, [(place, place ^ mask) for place in range(count)])  31.7 us
    unnamed x82, local copies, waits for them, and re-layouts  27.1 us
    all_to_all x2, waiting for transfers between devices, back(): lax.all_to_all(blocks, 'seq', split_axis=0, concat_axis=0, tiled=True, ax...  24.6 us
    pallas_call x2, Pallas kernels, experts(): pl.pallas_call(lambda *refs: expert_body(count, share, *refs), grid_spec=...  17.6 us
    all_to_all x3, starting transfers between devices, to_owner(): lax.all_to_all(blocks, 'seq', split_axis=0, concat_axis=0, tiled=True)  15.4 us
    all_to_all x1, waiting for transfers between devices, shards(): lax.all_to_all(by_slot.reshape(seq_count, token_count, HEAD), 'seq', spli...  14.4 us
  transfers between devices with their start and end apart: 34, of which 21 were waited for; matrix products, arithmetic and copies ran while one was open for 12% of the time, Pallas kernels for 9%

profile of v5, /device:TPU:0, one launch (start us, length us, event | category | flops | bytes accessed | tf_op | source)
XLA Modules:
  0.0 413.1 jit_solution(10318668935185874816)
XLA Ops:
  6.5 1.3 convert_element_type.106
  7.8 1.2 multiply_reduce_fusion
  9.9 3.1 collective-permute-start
  12.9 2.6 collective-permute-start.1
  15.7 2.4 collective-permute-start.6
  18.1 1.8 pack_heads.1
  19.9 4.0 all-to-all-start
  24.8 12.9 %order_experts.1 = (bf16[16,128,512]{2,1,0:T(8,128)(2,1)}, bf16[16,128,512]{2,1,0:T(8,128)(2,1)}, bf16[16,128,512]{2,1,0:T(8,128)(2,1)}) custom-call(s32[16]{0:T(128)} %order_ref.1, f32[16,128,512]{2,1,0:T(8,128)} %gate_ref.1, f32[16,128,512]{2,1,0:T(8,128)} %up_ref.1, f32[16,128,512]{2,1,0:T(8,128)} %down_ref.1), custom_call_target="tpu_custom_call" | custom-call | flops 1 | bytes 1 | tf_op jit(solution)/shard_map/order_experts/pallas_call | solution.py:129
  37.8 2.0 collective-permute-start.7
  39.9 1.5 collective-permute-start.2
  41.4 10.1 %collective-permute-done.7 = bf16[64,1024]{1,0:T(8,128)(2,1)S(1)} collective-permute-done((bf16[64,1024]{1,0:T(8,128)(2,1)S(1)}, bf16[64,1024]{1,0:T(8,128)(2,1)S(1)}, u32[]{:S(2)}, u32[]{:S(2)}) %collective-permute-start.7) | collective-permute-done | bytes 131104 | tf_op jit(solution)/shard_map/ppermute | solution.py:31
  51.5 1.7 collective-permute-start.8
  53.3 1.5 collective-permute-start.4
  54.7 3.6 collective-permute-done.8
  60.6 2.4 collective-permute-done.4
  63.1 1.8 collective-permute-start.5
  67.2 9.1 %collective-permute-done.3 = bf16[4,128,512]{2,1,0:T(8,128)(2,1)S(1)} collective-permute-done((bf16[4,128,512]{2,1,0:T(8,128)(2,1)S(1)}, bf16[4,128,512]{2,1,0:T(8,128)(2,1)S(1)}, u32[]{:S(2)}, u32[]{:S(2)}) %collective-permute-start.3) | collective-permute-done | bytes 524320 | tf_op jit(solution)/shard_map/ppermute | solution.py:31
  76.5 3.7 collective-permute-done.5
  81.6 5.7 %all-to-all-start.1 = ((bf16[16,128,512]{2,1,0:T(8,128)(2,1)}), bf16[16,128,512]{2,1,0:T(8,128)(2,1)}, u32[]{:S(2)}, u32[]{:S(2)}) async-start(bf16[16,128,512]{2,1,0:T(8,128)(2,1)} %get-tuple-element.46), calls=%async_computation.1 | async-start | bytes 4194304 | tf_op jit(solution)/shard_map/all_to_all | solution.py:417
  87.3 1.6 fusion.52
  91.1 1.6 fusion.51
  92.7 1.6 fusion.50
  94.2 1.6 pad_maximum_fusion.refs_1_
  98.1 2.0 multiply_sine_fusion
  100.3 5.4 %project.1.query_ref.key_ref.value_ref = bf16[1088,384]{1,0:T(8,128)(2,1)S(1)} custom-call(s32[2]{0:T(128)S(1)} %fusion.105.refs_0_, bf16[1088,1024]{1,0:T(8,128)(2,1)S(1)} %pad_maximum_fusion.refs_1_, bf16[1088,1024]{1,0:T(8,128)(2,1)} %collective-permute-done.10.refs_2_, bf16[2048,384]{1,0:T(8,128)(2,1)S(1)} %bitcast.150, ...), custom_call_target="tpu_custom_call" | custom-call | flops 1 | bytes 1 | tf_op jit(solution)/shard_map/project/pallas_call | solution.py:191
  106.8 6.7 %attend_once.1 = bf16[1088,128]{1,0:T(8,128)(2,1)S(1)} custom-call(f32[1]{0:T(128)} %dynamic_slice.92.sink_ref, s32[1088,1]{1,0:T(8,128)S(1)} %copy-done.3, s32[1,1088]{1,0:T(1,128)S(1)} %and_select_fusion.key_prompt_ref, bf16[1088,384]{1,0:T(8,128)(2,1)S(1)} %project.1.query_ref.key_ref.value_ref, bf16[1088,384]{1,0:T(8,128)(2,1)S(1)} %project.1.query_ref.key_ref.value_ref, ...), custom_call_target="tpu_custom_call" | custom-call | flops 1 | bytes 1 | tf_op jit(solution)/shard_map/attend_once/pallas_call | solution.py:233
  113.5 47.7 %all-to-all-done.1 = bf16[16,128,512]{2,1,0:T(8,128)(2,1)} async-done(((bf16[16,128,512]{2,1,0:T(8,128)(2,1)}), bf16[16,128,512]{2,1,0:T(8,128)(2,1)}, u32[]{:S(2)}, u32[]{:S(2)}) %all-to-all-start.1) | async-done | bytes 2097184 | tf_op jit(solution)/shard_map/all_to_all | solution.py:417
  162.4 12.9 %all-to-all-start.2 = ((bf16[16,128,128]{2,1,0:T(8,128)(2,1)}), bf16[16,128,128]{2,1,0:T(8,128)(2,1)S(1)}, u32[]{:S(2)}, u32[]{:S(2)}) async-start(bf16[16,128,128]{2,1,0:T(8,128)(2,1)} %bitcast.27), calls=%async_computation.2 | async-start | bytes 1048576 | tf_op jit(solution)/shard_map/all_to_all | solution.py:486
  175.4 14.4 %all-to-all-done.2 = bf16[16,128,128]{2,1,0:T(8,128)(2,1)S(1)} async-done(((bf16[16,128,128]{2,1,0:T(8,128)(2,1)}), bf16[16,128,128]{2,1,0:T(8,128)(2,1)S(1)}, u32[]{:S(2)}, u32[]{:S(2)}) %all-to-all-start.2) | async-done | bytes 524320 | tf_op jit(solution)/shard_map/all_to_all | solution.py:486
  189.8 4.6 %all-to-all-start.3 = ((bf16[16,128,512]{2,1,0:T(8,128)(2,1)}), bf16[16,128,512]{2,1,0:T(8,128)(2,1)}, u32[]{:S(2)}, u32[]{:S(2)}) async-start(bf16[16,128,512]{2,1,0:T(8,128)(2,1)} %get-tuple-element.58), calls=%async_computation.3 | async-start | bytes 4194304 | tf_op jit(solution)/shard_map/all_to_all | solution.py:417
  194.8 3.0 fusion.refs_0_
  199.3 1.2 collective-permute-done.11.refs_1_
  202.6 2.6 collective-permute-start.13
  206.0 44.4 %collective-permute-done.13 = f32[1,128,16]{2,1,0:T(8,128)S(1)} collective-permute-done((f32[1,128,16]{2,1,0:T(8,128)S(1)}, f32[1,128,16]{2,1,0:T(8,128)S(1)}, u32[]{:S(2)}, u32[]{:S(2)}) %collective-permute-start.13) | collective-permute-done | bytes 8224 | tf_op jit(solution)/shard_map/ppermute | solution.py:31
  250.5 4.5 %collective-permute-done.12 = bf16[1,128,1024]{2,1,0:T(8,128)(2,1)S(1)} collective-permute-done((bf16[1,128,1024]{2,1,0:T(8,128)(2,1)S(1)}, bf16[1,128,1024]{2,1,0:T(8,128)(2,1)S(1)}, u32[]{:S(2)}, u32[]{:S(2)}) %collective-permute-start.12) | collective-permute-done | bytes 262176 | tf_op jit(solution)/shard_map/ppermute | solution.py:31
  256.9 1.5 collective-permute-start.14
  258.4 2.1 collective-permute-start.15
  261.8 2.5 collective-permute-start.17
  264.3 8.9 %collective-permute-done.14 = bf16[2,72,1024]{2,1,0:T(8,128)(2,1)S(1)} collective-permute-done((bf16[2,72,1024]{2,1,0:T(8,128)(2,1)S(1)}, bf16[2,72,1024]{2,1,0:T(8,128)(2,1)S(1)}, u32[]{:S(2)}, u32[]{:S(2)}) %collective-permute-start.14) | collective-permute-done | bytes 294944 | tf_op jit(solution)/shard_map/ppermute | solution.py:31
  273.9 5.1 %all-to-all-start.4 = ((bf16[16,128,512]{2,1,0:T(8,128)(2,1)}), bf16[16,128,512]{2,1,0:T(8,128)(2,1)S(1)}, u32[]{:S(2)}, u32[]{:S(2)}) async-start(bf16[16,128,512]{2,1,0:T(8,128)(2,1)} %get-tuple-element.59), calls=%async_computation.4 | async-start | bytes 4194304 | tf_op jit(solution)/shard_map/all_to_all | solution.py:417
  279.0 1.7 bitcast_dynamic-update-slice_fusion.6
  280.7 3.7 collective-permute-start.20
  284.4 1.7 bitcast_dynamic-update-slice_fusion.5
  286.2 1.7 bitcast_dynamic-update-slice_fusion.4
  287.8 1.7 bitcast_dynamic-update-slice_fusion.3
  289.5 1.7 bitcast_dynamic-update-slice_fusion.2
  291.2 1.8 collective-permute-done.19
  293.0 1.7 bitcast_dynamic-update-slice_fusion.1
  294.8 29.9 %collective-permute-done.20 = bf16[2,72,1024]{2,1,0:T(8,128)(2,1)S(1)} collective-permute-done((bf16[2,72,1024]{2,1,0:T(8,128)(2,1)S(1)}, bf16[2,72,1024]{2,1,0:T(8,128)(2,1)S(1)}, u32[]{:S(2)}, u32[]{:S(2)}) %collective-permute-start.20) | collective-permute-done | bytes 294944 | tf_op jit(solution)/shard_map/ppermute | solution.py:31
  330.5 2.3 collective-permute-done.21.refs_3_
  334.6 1.4 copy-done.10
  336.0 8.8 %experts.2 = (bf16[1,576,1024]{2,1,0:T(8,128)(2,1)S(1)}, bf16[1,576,1024]{2,1,0:T(8,128)(2,1)}) custom-call(s32[2]{0:T(128)S(1)} %fusion.105.refs_0_, s32[2]{0:T(128)S(1)} %fusion.106.refs_1_, bf16[1,576,1024]{2,1,0:T(8,128)(2,1)} %bitcast.161, bf16[1,576,1024]{2,1,0:T(8,128)(2,1)} %copy-done.15, bf16[1,2048,512]{2,1,0:T(8,128)(2,1)} %bitcast.24.refs_4_, ...), custom_call_target="tpu_custom_call" | custom-call | flops 1 | bytes 1 | tf_op jit(solution)/shard_map/experts/pallas_call | solution.py:315
  344.9 2.9 collective-permute-done.23
  347.8 1.5 add_convert_fusion.1
  349.3 5.6 %all-to-all-start.5 = ((bf16[8,1,72,1024]{3,2,1,0:T(8,128)(2,1)}), bf16[8,1,72,1024]{3,2,1,0:T(8,128)(2,1)}, u32[]{:S(2)}, u32[]{:S(2)}) async-start(bf16[8,1,72,1024]{3,2,1,0:T(8,128)(2,1)} %bitcast.61), calls=%async_computation.5 | async-start | bytes 2359296 | tf_op jit(solution)/shard_map/all_to_all | solution.py:614
  354.9 8.8 %experts.3 = (bf16[1,576,1024]{2,1,0:T(8,128)(2,1)S(1)}, bf16[1,576,1024]{2,1,0:T(8,128)(2,1)}) custom-call(s32[2]{0:T(128)S(1)} %fusion.105.refs_0_, s32[2]{0:T(128)S(1)} %fusion.106.refs_1_, bf16[1,576,1024]{2,1,0:T(8,128)(2,1)} %bitcast.159, bf16[1,576,1024]{2,1,0:T(8,128)(2,1)} %copy-done.14, bf16[1,2048,512]{2,1,0:T(8,128)(2,1)} %bitcast.24.refs_4_, ...), custom_call_target="tpu_custom_call" | custom-call | flops 1 | bytes 1 | tf_op jit(solution)/shard_map/experts/pallas_call | solution.py:315
  364.6 2.2 collective-permute-done.24
  366.8 1.5 add_convert_fusion
  368.3 3.0 all-to-all-done.5
  371.3 2.1 fusion.18
  373.5 3.6 all-to-all-start.6
  378.0 2.1 collective-permute-start.25
  381.9 21.6 %all-to-all-done.6 = bf16[8,1,72,1024]{3,2,1,0:T(8,128)(2,1)S(1)} async-done(((bf16[8,1,72,1024]{3,2,1,0:T(8,128)(2,1)}), bf16[8,1,72,1024]{3,2,1,0:T(8,128)(2,1)S(1)}, u32[]{:S(2)}, u32[]{:S(2)}) %all-to-all-start.6) | async-done | bytes 1179680 | tf_op jit(solution)/shard_map/all_to_all | solution.py:614
  403.5 1.8 fusion.24
  (181 shorter events, 36.0 us)
Async XLA Ops:
  6.5 6.4 %copy-start.21 = (s32[128,8]{0,1:T(8,128)S(1)}, s32[128,8]{0,1:T(8,128)}, u32[]{:S(2)}) copy-start(s32[128,8]{0,1:T(8,128)} %param.29) | copy-start | bytes 12292
  6.5 11.5 %copy-start.4 = (f32[128,1024]{1,0:T(8,128)S(1)}, f32[128,1024]{1,0:T(8,128)}, u32[]{:S(2)}) copy-start(f32[128,1024]{1,0:T(8,128)} %query_ref.1) | copy-start | bytes 1572868
  6.5 11.5 %copy-start.5 = (f32[128,1024]{1,0:T(8,128)S(1)}, f32[128,1024]{1,0:T(8,128)}, u32[]{:S(2)}) copy-start(f32[128,1024]{1,0:T(8,128)} %key_ref.1) | copy-start | bytes 1572868
  6.5 11.6 %copy-start.6 = (f32[128,1024]{1,0:T(8,128)S(1)}, f32[128,1024]{1,0:T(8,128)}, u32[]{:S(2)}) copy-start(f32[128,1024]{1,0:T(8,128)} %value_ref.1) | copy-start | bytes 1572868
  9.9 29.9 %collective-permute-start = (bf16[1,128,1024]{2,1,0:T(8,128)(2,1)S(1)}, bf16[1,128,1024]{2,1,0:T(8,128)(2,1)S(1)}, u32[]{:S(2)}, u32[]{:S(2)}) collective-permute-start(bf16[1,128,1024]{2,1,0:T(8,128)(2,1)S(1)} %fusion.126), channel_id=1, source_target_pairs={{0,8},{2,10},{4,12},{6,14},{8,0},{10,2},{12,4},{14,6},{16,24},{18,... | collective-permute-start | bytes 786440 | tf_op jit(solution)/shard_map/ppermute | solution.py:31
  12.9 24.8 %collective-permute-start.1 = (s32[1,128,8]{1,2,0:T(8,128)S(1)}, s32[1,128,8]{1,2,0:T(8,128)S(1)}, u32[]{:S(2)}, u32[]{:S(2)}) collective-permute-start(s32[1,128,8]{1,2,0:T(8,128)S(1)} %bitcast.177), channel_id=1, source_target_pairs={{0,16},{2,18},{4,20},{6,22},{8,24},{10,26},{12,28},{14,30},{16,0},... | collective-permute-start | bytes 12296 | tf_op jit(solution)/shard_map/ppermute | solution.py:31
  15.7 8.3 %copy-start.16 = (f32[1024,128]{1,0:T(8,128)S(1)}, f32[1024,128]{1,0:T(8,128)}, u32[]{:S(2)}) copy-start(f32[1024,128]{1,0:T(8,128)} %param.21) | copy-start | bytes 1572868
  15.7 22.0 %collective-permute-start.6 = (bf16[64,1024]{1,0:T(8,128)(2,1)S(1)}, bf16[64,1024]{1,0:T(8,128)(2,1)S(1)}, u32[]{:S(2)}, u32[]{:S(2)}) collective-permute-start(bf16[64,1024]{1,0:T(8,128)(2,1)S(1)} %slice.160), channel_id=1, source_target_pairs={{0,16},{2,18},{4,20},{6,22},{8,24},{10,26},{12,28},{14,30},{1,17},... | collective-permute-start | bytes 393224 | tf_op jit(solution)/shard_map/ppermute | solution.py:21
  19.9 4.1 copy-start.20
  19.9 61.7 %all-to-all-start = ((bf16[16,128,384]{2,1,0:T(8,128)(2,1)}), bf16[16,128,384]{2,1,0:T(8,128)(2,1)S(1)}, u32[]{:S(2)}, u32[]{:S(2)}) async-start(bf16[16,128,384]{2,1,0:T(8,128)(2,1)} %pack_heads.1), calls=%async_computation | async-start | bytes 3145728 | tf_op jit(solution)/shard_map/all_to_all | solution.py:377
  23.9 170.9 %all-gather.2.cloned.1.call-start = ((), (), s32[]{:S(2)}) async-start(), calls=%async_computation.7 | async-start | bytes 4526080 | tf_op jit(solution)/shard_map/all_gather | solution.py:424
  37.8 13.7 %collective-permute-start.7 = (bf16[64,1024]{1,0:T(8,128)(2,1)S(1)}, bf16[64,1024]{1,0:T(8,128)(2,1)S(1)}, u32[]{:S(2)}, u32[]{:S(2)}) collective-permute-start(bf16[64,1024]{1,0:T(8,128)(2,1)S(1)} %broadcast_select_fusion), channel_id=1, source_target_pairs={{0,8},{2,10},{4,12},{6,14},{8,0},{10,2},{12,4},{14,6},{16,24},{18,... | collective-permute-start | bytes 393224 | tf_op jit(solution)/shard_map/ppermute | solution.py:31
  39.9 19.7 %collective-permute-start.2 = (bf16[2,128,512]{2,1,0:T(8,128)(2,1)S(1)}, bf16[2,128,512]{2,1,0:T(8,128)(2,1)S(1)}, u32[]{:S(2)}, u32[]{:S(2)}) collective-permute-start(bf16[2,128,512]{2,1,0:T(8,128)(2,1)S(1)} %get-tuple-element.87), channel_id=1, source_target_pairs={{0,4},{2,6},{4,0},{6,2},{8,12},{10,14},{12,8},{14,10},{16,20},{18,... | collective-permute-start | bytes 786440 | tf_op jit(solution)/shard_map/ppermute | solution.py:31
  51.5 6.9 %collective-permute-start.8 = (bf16[64,1024]{1,0:T(8,128)(2,1)S(1)}, bf16[64,1024]{1,0:T(8,128)(2,1)S(1)}, u32[]{:S(2)}, u32[]{:S(2)}) collective-permute-start(bf16[64,1024]{1,0:T(8,128)(2,1)S(1)} %fusion.125), channel_id=1, source_target_pairs={{0,4},{2,6},{4,0},{6,2},{8,12},{10,14},{12,8},{14,10},{16,20},{18,... | collective-permute-start | bytes 393224 | tf_op jit(solution)/shard_map/ppermute | solution.py:31
  53.3 9.8 %collective-permute-start.4 = (bf16[2,128,512]{2,1,0:T(8,128)(2,1)S(1)}, bf16[2,128,512]{2,1,0:T(8,128)(2,1)S(1)}, u32[]{:S(2)}, u32[]{:S(2)}) collective-permute-start(bf16[2,128,512]{2,1,0:T(8,128)(2,1)S(1)} %get-tuple-element.88), channel_id=1, source_target_pairs={{0,2},{2,0},{4,6},{6,4},{8,10},{10,8},{12,14},{14,12},{16,18},{18,... | collective-permute-start | bytes 786440 | tf_op jit(solution)/shard_map/ppermute | solution.py:31
  58.4 7.5 %collective-permute-start.9 = (bf16[64,1024]{1,0:T(8,128)(2,1)S(1)}, bf16[64,1024]{1,0:T(8,128)(2,1)S(1)}, u32[]{:S(2)}, u32[]{:S(2)}) collective-permute-start(bf16[64,1024]{1,0:T(8,128)(2,1)S(1)} %add.394), channel_id=1, source_target_pairs={{0,2},{2,0},{4,6},{6,4},{8,10},{10,8},{12,14},{14,12},{16,18},{18,... | collective-permute-start | bytes 393224 | tf_op jit(solution)/shard_map/ppermute | solution.py:31
  59.6 16.7 %collective-permute-start.3 = (bf16[4,128,512]{2,1,0:T(8,128)(2,1)S(1)}, bf16[4,128,512]{2,1,0:T(8,128)(2,1)S(1)}, u32[]{:S(2)}, u32[]{:S(2)}) collective-permute-start(bf16[4,128,512]{2,1,0:T(8,128)(2,1)S(1)} %pad_maximum_fusion.2), channel_id=1, source_target_pairs={{0,2},{2,0},{4,6},{6,4},{8,10},{10,8},{12,14},{14,12},{16,18},{18,... | collective-permute-start | bytes 1572872 | tf_op jit(solution)/shard_map/ppermute | solution.py:31
  63.1 17.0 %collective-permute-start.5 = (bf16[4,128,512]{2,1,0:T(8,128)(2,1)S(1)}, bf16[4,128,512]{2,1,0:T(8,128)(2,1)S(1)}, u32[]{:S(2)}, u32[]{:S(2)}) collective-permute-start(bf16[4,128,512]{2,1,0:T(8,128)(2,1)S(1)} %pad_maximum_fusion.3), channel_id=1, source_target_pairs={{0,4},{2,6},{4,0},{6,2},{8,12},{10,14},{12,8},{14,10},{16,20},{18,... | collective-permute-start | bytes 1572872 | tf_op jit(solution)/shard_map/ppermute | solution.py:31
  76.3 3.8 copy-start.17
  80.1 0.8 copy-start.18
  81.6 7.9 %copy-start = (bf16[16,128,384]{2,1,0:T(8,128)(2,1)}, bf16[16,128,384]{2,1,0:T(8,128)(2,1)S(1)}, u32[]{:S(2)}) copy-start(bf16[16,128,384]{2,1,0:T(8,128)(2,1)S(1)} %all-to-all-done) | copy-start | bytes 4718596
  81.6 79.6 %all-to-all-start.1 = ((bf16[16,128,512]{2,1,0:T(8,128)(2,1)}), bf16[16,128,512]{2,1,0:T(8,128)(2,1)}, u32[]{:S(2)}, u32[]{:S(2)}) async-start(bf16[16,128,512]{2,1,0:T(8,128)(2,1)} %get-tuple-element.46), calls=%async_computation.1 | async-start | bytes 4194304 | tf_op jit(solution)/shard_map/all_to_all | solution.py:417
  94.2 1.9 copy-start.23
  94.2 2.6 copy-start.22
  95.8 4.5 %collective-permute-start.10 = (bf16[1088,1024]{1,0:T(8,128)(2,1)S(1)}, bf16[1088,1024]{1,0:T(8,128)(2,1)}, u32[]{:S(2)}, u32[]{:S(2)}) collective-permute-start(bf16[1088,1024]{1,0:T(8,128)(2,1)S(1)} %pad_maximum_fusion.refs_1_), channel_id=1, source_target_pairs={{1,0},{0,1},{3,2},{2,3},{5,4},{4,5},{7,6},{6,7},{9,8},{8,9},{11,10... | collective-permute-start | bytes 6684680 | tf_op jit(solution)/shard_map/ppermute | solution.py:26
  96.7 3.6 copy-start.1
  105.8 1.1 copy-start.3
  162.4 27.3 %all-to-all-start.2 = ((bf16[16,128,128]{2,1,0:T(8,128)(2,1)}), bf16[16,128,128]{2,1,0:T(8,128)(2,1)S(1)}, u32[]{:S(2)}, u32[]{:S(2)}) async-start(bf16[16,128,128]{2,1,0:T(8,128)(2,1)} %bitcast.27), calls=%async_computation.2 | async-start | bytes 1048576 | tf_op jit(solution)/shard_map/all_to_all | solution.py:486
  189.8 83.3 %all-to-all-start.3 = ((bf16[16,128,512]{2,1,0:T(8,128)(2,1)}), bf16[16,128,512]{2,1,0:T(8,128)(2,1)}, u32[]{:S(2)}, u32[]{:S(2)}) async-start(bf16[16,128,512]{2,1,0:T(8,128)(2,1)} %get-tuple-element.58), calls=%async_computation.3 | async-start | bytes 4194304 | tf_op jit(solution)/shard_map/all_to_all | solution.py:417
  194.8 5.7 %copy-start.2 = (bf16[128,2048]{1,0:T(8,128)(2,1)S(1)}, bf16[128,2048]{1,0:T(8,128)(2,1)}, u32[]{:S(2)}) copy-start(bf16[128,2048]{1,0:T(8,128)(2,1)} %refs_2_.1) | copy-start | bytes 1572868
  194.8 5.7 %copy-start.9 = (f32[2048]{0:T(1024)S(1)}, f32[2048]{0:T(1024)}, u32[]{:S(2)}) copy-start(f32[2048]{0:T(1024)} %param.17) | copy-start | bytes 24580
  197.8 2.7 collective-permute-start.11
  201.1 1.0 copy-start.7
  202.6 47.9 %collective-permute-start.13 = (f32[1,128,16]{2,1,0:T(8,128)S(1)}, f32[1,128,16]{2,1,0:T(8,128)S(1)}, u32[]{:S(2)}, u32[]{:S(2)}) collective-permute-start(f32[1,128,16]{2,1,0:T(8,128)S(1)} %multiply_bitcast_fusion), channel_id=1, source_target_pairs={{0,16},{2,18},{4,20},{6,22},{8,24},{10,26},{12,28},{14,30},{16,0},... | collective-permute-start | bytes 24584 | tf_op jit(solution)/shard_map/ppermute | solution.py:31
  205.2 49.8 %collective-permute-start.12 = (bf16[1,128,1024]{2,1,0:T(8,128)(2,1)S(1)}, bf16[1,128,1024]{2,1,0:T(8,128)(2,1)S(1)}, u32[]{:S(2)}, u32[]{:S(2)}) collective-permute-start(bf16[1,128,1024]{2,1,0:T(8,128)(2,1)S(1)} %dynamic-slice_bitcast_fusion), channel_id=1, source_target_pairs={{0,16},{2,18},{4,20},{6,22},{8,24},{10,26},{12,28},{14,30},{16,0},... | collective-permute-start | bytes 786440 | tf_op jit(solution)/shard_map/ppermute | solution.py:31
  256.9 16.3 %collective-permute-start.14 = (bf16[2,72,1024]{2,1,0:T(8,128)(2,1)S(1)}, bf16[2,72,1024]{2,1,0:T(8,128)(2,1)S(1)}, u32[]{:S(2)}, u32[]{:S(2)}) collective-permute-start(bf16[2,72,1024]{2,1,0:T(8,128)(2,1)S(1)} %get-tuple-element.81), channel_id=1, source_target_pairs={{0,2},{2,0},{4,6},{6,4},{8,10},{10,8},{12,14},{14,12},{16,18},{18,... | collective-permute-start | bytes 884744 | tf_op jit(solution)/shard_map/ppermute | solution.py:31
  258.4 22.3 %collective-permute-start.15 = (bf16[2,72,1024]{2,1,0:T(8,128)(2,1)S(1)}, bf16[2,72,1024]{2,1,0:T(8,128)(2,1)}, u32[]{:S(2)}, u32[]{:S(2)}) collective-permute-start(bf16[2,72,1024]{2,1,0:T(8,128)(2,1)S(1)} %get-tuple-element.82), channel_id=1, source_target_pairs={{0,4},{2,6},{4,0},{6,2},{8,12},{10,14},{12,8},{14,10},{16,20},{18,... | collective-permute-start | bytes 884744 | tf_op jit(solution)/shard_map/ppermute | solution.py:31
  261.3 28.2 %collective-permute-start.18 = (bf16[2,72,1024]{2,1,0:T(8,128)(2,1)}, bf16[2,72,1024]{2,1,0:T(8,128)(2,1)}, u32[]{:S(2)}, u32[]{:S(2)}) collective-permute-start(bf16[2,72,1024]{2,1,0:T(8,128)(2,1)} %get-tuple-element.86), channel_id=1, source_target_pairs={{0,10},{2,8},{4,14},{6,12},{8,2},{10,0},{12,6},{14,4},{16,26},{18,... | collective-permute-start | bytes 884744 | tf_op jit(solution)/shard_map/ppermute | solution.py:31
  261.3 24.8 %collective-permute-start.16 = (bf16[2,72,1024]{2,1,0:T(8,128)(2,1)S(1)}, bf16[2,72,1024]{2,1,0:T(8,128)(2,1)}, u32[]{:S(2)}, u32[]{:S(2)}) collective-permute-start(bf16[2,72,1024]{2,1,0:T(8,128)(2,1)S(1)} %get-tuple-element.83), channel_id=1, source_target_pairs={{0,6},{2,4},{4,2},{6,0},{8,14},{10,12},{12,10},{14,8},{16,22},{18,... | collective-permute-start | bytes 884744 | tf_op jit(solution)/shard_map/ppermute | solution.py:31
  261.8 26.1 %collective-permute-start.17 = (bf16[2,72,1024]{2,1,0:T(8,128)(2,1)S(1)}, bf16[2,72,1024]{2,1,0:T(8,128)(2,1)}, u32[]{:S(2)}, u32[]{:S(2)}) collective-permute-start(bf16[2,72,1024]{2,1,0:T(8,128)(2,1)S(1)} %get-tuple-element.84), channel_id=1, source_target_pairs={{0,8},{2,10},{4,12},{6,14},{8,0},{10,2},{12,4},{14,6},{16,24},{18,... | collective-permute-start | bytes 884744 | tf_op jit(solution)/shard_map/ppermute | solution.py:31
  273.2 0.7 copy-start.19
  273.2 19.9 %collective-permute-start.19 = (bf16[2,72,1024]{2,1,0:T(8,128)(2,1)}, bf16[2,72,1024]{2,1,0:T(8,128)(2,1)}, u32[]{:S(2)}, u32[]{:S(2)}) collective-permute-start(bf16[2,72,1024]{2,1,0:T(8,128)(2,1)} %get-tuple-element.85), channel_id=1, source_target_pairs={{0,12},{2,14},{4,8},{6,10},{8,4},{10,6},{12,0},{14,2},{16,28},{18,... | collective-permute-start | bytes 884744 | tf_op jit(solution)/shard_map/ppermute | solution.py:31
  273.9 60.7 %all-to-all-start.4 = ((bf16[16,128,512]{2,1,0:T(8,128)(2,1)}), bf16[16,128,512]{2,1,0:T(8,128)(2,1)S(1)}, u32[]{:S(2)}, u32[]{:S(2)}) async-start(bf16[16,128,512]{2,1,0:T(8,128)(2,1)} %get-tuple-element.59), calls=%async_computation.4 | async-start | bytes 4194304 | tf_op jit(solution)/shard_map/all_to_all | solution.py:417
  280.7 44.0 %collective-permute-start.20 = (bf16[2,72,1024]{2,1,0:T(8,128)(2,1)S(1)}, bf16[2,72,1024]{2,1,0:T(8,128)(2,1)S(1)}, u32[]{:S(2)}, u32[]{:S(2)}) collective-permute-start(bf16[2,72,1024]{2,1,0:T(8,128)(2,1)S(1)} %get-tuple-element.79), channel_id=1, source_target_pairs={{0,14},{2,12},{4,10},{6,8},{8,6},{10,4},{12,2},{14,0},{16,30},{18,... | collective-permute-start | bytes 884744 | tf_op jit(solution)/shard_map/ppermute | solution.py:31
  325.4 4.1 copy-start.13
  329.9 2.9 copy-start.11
  329.9 2.9 copy-start.12
  330.0 2.9 collective-permute-start.21
  330.0 4.5 %collective-permute-start.22 = (bf16[1,576,1024]{2,1,0:T(8,128)(2,1)S(1)}, bf16[1,576,1024]{2,1,0:T(8,128)(2,1)S(1)}, u32[]{:S(2)}, u32[]{:S(2)}) collective-permute-start(bf16[1,576,1024]{2,1,0:T(8,128)(2,1)S(1)} %bitcast.158), channel_id=1, source_target_pairs={{1,0},{0,1},{3,2},{2,3},{5,4},{4,5},{7,6},{6,7},{9,8},{8,9},{11,10... | collective-permute-start | bytes 3538952 | tf_op jit(solution)/shard_map/ppermute | solution.py:26
  332.9 1.0 copy-start.15
  334.6 14.8 %copy-start.14 = (bf16[1,576,1024]{2,1,0:T(8,128)(2,1)}, bf16[1,576,1024]{2,1,0:T(8,128)(2,1)S(1)}, u32[]{:S(2)}) copy-start(bf16[1,576,1024]{2,1,0:T(8,128)(2,1)S(1)} %collective-permute-done.22.refs_3_) | copy-start | bytes 3538948
  334.6 1.4 copy-start.10
  344.8 3.1 collective-permute-start.23
  349.3 22.0 %all-to-all-start.5 = ((bf16[8,1,72,1024]{3,2,1,0:T(8,128)(2,1)}), bf16[8,1,72,1024]{3,2,1,0:T(8,128)(2,1)}, u32[]{:S(2)}, u32[]{:S(2)}) async-start(bf16[8,1,72,1024]{3,2,1,0:T(8,128)(2,1)} %bitcast.61), calls=%async_computation.5 | async-start | bytes 2359296 | tf_op jit(solution)/shard_map/all_to_all | solution.py:614
  363.7 3.1 collective-permute-start.24
  373.5 30.0 %all-to-all-start.6 = ((bf16[8,1,72,1024]{3,2,1,0:T(8,128)(2,1)}), bf16[8,1,72,1024]{3,2,1,0:T(8,128)(2,1)S(1)}, u32[]{:S(2)}, u32[]{:S(2)}) async-start(bf16[8,1,72,1024]{3,2,1,0:T(8,128)(2,1)} %bitcast.65), calls=%async_computation.6 | async-start | bytes 2359296 | tf_op jit(solution)/shard_map/all_to_all | solution.py:614
  378.0 27.4 %collective-permute-start.25 = (f32[128,1024]{1,0:T(8,128)S(1)}, f32[128,1024]{1,0:T(8,128)S(1)}, u32[]{:S(2)}, u32[]{:S(2)}) collective-permute-start(f32[128,1024]{1,0:T(8,128)S(1)} %slice_add_fusion.2), channel_id=1, source_target_pairs={{0,16},{2,18},{4,20},{6,22},{8,24},{10,26},{12,28},{14,30},{16,0},... | collective-permute-start | bytes 1572872 | tf_op jit(solution)/shard_map/ppermute | solution.py:31
  381.0 24.4 %copy-start.8 = (f32[128,2048]{1,0:T(8,128)S(1)}, f32[128,2048]{1,0:T(8,128)}, u32[]{:S(2)}) copy-start(f32[128,2048]{1,0:T(8,128)} %copy-done.7) | copy-start | bytes 3145732
Sparse Core Ops, SparseCore 0:
  27.4 137.8 all-gather.1

commit v6 on v5

--- a/solution.py
+++ b/solution.py
@@ -249,45 +249,51 @@
     )(sink, query_prompt[:, None], key_prompt[None, :], rows, rows, rows)
 
 
-def settle_body(piece_count, *refs):
+def settle_body(piece_count, width, place_ref, *refs):
     pieces = refs[:piece_count]
-    token_ref, gain_ref, router_ref, full_ref, outgoing_ref, logit_ref = refs[piece_count:]
-    full = token_ref[...].astype(jnp.float32) + sum(piece[...] for piece in pieces)
-    full_ref[...] = full
-    outgoing = rms_scale(full, gain_ref[...]).astype(jnp.bfloat16)
+    token_ref, gain_ref, router_ref, full_ref, outgoing_ref, logit_ref, router_all = refs[
+        piece_count:
+    ]
+    for place in range(full_ref.shape[1] // width):
+        here = slice(place * width, (place + 1) * width)
+        there = pl.ds(pl.multiple_of(place_ref[place] * width, width), width)
+        block = sum(piece[:, there] for piece in pieces)
+        full_ref[:, here] = token_ref[:, here].astype(jnp.float32) + block
+        router_all[:, here] = router_ref[:, there]
+    outgoing = rms_scale(full_ref[...], gain_ref[...]).astype(jnp.bfloat16)
     outgoing_ref[...] = outgoing
     logit_ref[...] = lax.dot_general(
         outgoing,
-        router_ref[...],
+        router_all[...],
         (((1,), (1,)), ((), ())),
         preferred_element_type=jnp.float32,
     )
 
 
-def settle(pieces, tokens, gain, router):
+def settle(places, pieces, tokens, gain, router, width):
     rows, columns = tokens.shape
     vmem = pl.BlockSpec(memory_space=pltpu.VMEM)
     return pl.pallas_call(
-        lambda *refs: settle_body(len(pieces), *refs),
-        in_specs=[vmem] * (len(pieces) + 3),
+        lambda *refs: settle_body(len(pieces), width, *refs),
+        in_specs=[pl.BlockSpec(memory_space=pltpu.SMEM)] + [vmem] * (len(pieces) + 3),
         out_specs=[vmem] * 3,
         out_shape=[
             jax.ShapeDtypeStruct((rows, columns), jnp.float32),
             jax.ShapeDtypeStruct((rows, columns), jnp.bfloat16),
             jax.ShapeDtypeStruct((rows, router.shape[0]), jnp.float32),
         ],
+        scratch_shapes=[pltpu.VMEM(router.shape, jnp.bfloat16)],
         compiler_params=pltpu.CompilerParams(vmem_limit_bytes=32 * 2**20),
         cost_estimate=SMALL,
         name="settle",
-    )(*pieces, tokens, gain[None, :], router)
+    )(places, *pieces, tokens, gain[None, :], router)
 
 
 def expert_body(turn_count, share, in_ref, out_ref, *refs):
-    rows, (gate_ref, up_ref, down_ref), outs = (
-        refs[:turn_count],
-        refs[turn_count : turn_count + 3],
-        refs[turn_count + 3 :],
-    )
+    rows, (gate_ref, up_ref, down_ref) = (refs[:turn_count], refs[turn_count : turn_count + 3])
+    outs = refs[turn_count + 3 : 2 * turn_count + 3]
+    sums = refs[2 * turn_count + 3 :]
+    block = pl.program_id(1)
     gate = up = 0.0
     for turn in range(turn_count):
         here = pl.ds(pl.multiple_of(in_ref[turn], share), share)
@@ -298,27 +304,36 @@
     state = (gate / (1.0 + jnp.exp(-gate)) * up).astype(jnp.bfloat16)
     for turn in range(turn_count):
         here = pl.ds(pl.multiple_of(out_ref[turn], share), share)
-        outs[turn][0] = lax.dot_general(
+        down = lax.dot_general(
             state,
             down_ref[0, here, :],
             (((1,), (1,)), ((), ())),
             preferred_element_type=jnp.float32,
-        ).astype(jnp.bfloat16)
+        )
+
+        @pl.when(block == 0)
+        def _():
+            sums[turn][...] = down
+
+        @pl.when(block > 0)
+        def _():
+            outs[turn][0] = (sums[turn][...] + down).astype(jnp.bfloat16)
 
 
 def experts(in_starts, out_starts, row_blocks, weights):
     local_experts, row_count, share = row_blocks[0].shape
-    step = row_count // 2 if row_count % 32 == 0 else row_count
-    block = pl.BlockSpec((1, step, share), lambda e, place, a, b: (e, place, 0))
-    whole = pl.BlockSpec((1, *weights[0].shape[1:]), lambda e, place, a, b: (e, 0, 0))
+    rows, width = weights[0].shape[1:]
+    block = pl.BlockSpec((1, row_count, share), lambda e, f, a, b: (e, 0, 0))
+    some = pl.BlockSpec((1, rows, width // 2), lambda e, f, a, b: (e, 0, f))
     count = len(row_blocks)
     return pl.pallas_call(
         lambda *refs: expert_body(count, share, *refs),
         grid_spec=pltpu.PrefetchScalarGridSpec(
             num_scalar_prefetch=2,
-            grid=(local_experts, row_count // step),
-            in_specs=[block] * count + [whole] * 3,
+            grid=(local_experts, 2),
+            in_specs=[block] * count + [some] * 3,
             out_specs=[block] * count,
+            scratch_shapes=[pltpu.VMEM((row_count, share), jnp.float32)] * count,
         ),
         out_shape=[jax.ShapeDtypeStruct(row_blocks[0].shape, jnp.bfloat16)] * count,
         compiler_params=pltpu.CompilerParams(vmem_limit_bytes=52 * 2**20),
@@ -388,9 +403,26 @@
     if aligned:
         edge = from_behind(share[token_count - stagger :], "seq", head_count)
         edge = jnp.where(head == head_count - 1, edge, jnp.zeros((), jnp.bfloat16))
+    out_all, _ = doubled(
+        jnp.concatenate([w_out, router.T], axis=0).astype(jnp.bfloat16), part_masks, 1
+    )
+    first_rows, first_turns = doubled(share[None], group_masks[:1], 0)
+    first_rows, all_routes, out_all, layout_map = lax.optimization_barrier(
+        (first_rows, all_routes, out_all, layout_map)
+    )
+    out_all = lax.all_gather(out_all, "seq", axis=1, tiled=True, axis_index_groups=groups)
     own_gate, own_up, own_down = order_experts(layout_map, expert_gate, expert_up, expert_down)
-    first_rows, first_turns = doubled(share[None], group_masks[:1], 0)
-    first_rows, all_routes = lax.optimization_barrier((first_rows, all_routes))
+    part_ids = (part * head_count + (head ^ turns))[:, None] * token_count + offsets[None, :]
+    part_ids = part_ids.reshape(-1)
+    if aligned:
+        edge_ids = part * part_slots - stagger + jnp.arange(stagger, dtype=jnp.int32)
+        part_ids = jnp.concatenate([part_ids, edge_ids])
+    part_positions = prompt_split(part_ids, slot_len, stagger, prompt_count)[1]
+    half_dim = HEAD // 2
+    frequency = ROPE_BASE ** (-jnp.arange(half_dim, dtype=jnp.float32) / half_dim)
+    angles = part_positions.astype(jnp.float32)[:, None] * frequency[None, :]
+    cosine = jnp.cos(angles)
+    sine_part = jnp.sin(angles)
     pieces = []
     for piece, masks in (
         (first_rows[:, :, : col_share // 2], group_masks[1:]),
@@ -399,19 +431,17 @@
         known = first_turns
         for mask in masks:
             if mask == masks[-1]:
-                piece, own_gate = lax.optimization_barrier((piece, own_gate))
+                piece, own_gate, cosine, sine_part = lax.optimization_barrier(
+                    (piece, own_gate, cosine, sine_part)
+                )
             piece = jnp.concatenate([piece, swapped(piece, "seq", mask)], axis=0)
             known = known + [turn ^ mask for turn in known]
         pieces.append(jnp.concatenate([piece[known.index(m)] for m in range(head_count)], axis=0))
     part_rows = jnp.concatenate(pieces, axis=1)
-    part_ids = (part * head_count + (head ^ turns))[:, None] * token_count + offsets[None, :]
-    part_ids = part_ids.reshape(-1)
     if aligned:
         for mask in group_masks:
             edge = edge + swapped(edge, "seq", mask)
         part_rows = jnp.concatenate([part_rows, edge], axis=0)
-        edge_ids = part * part_slots - stagger + jnp.arange(stagger, dtype=jnp.int32)
-        part_ids = jnp.concatenate([part_ids, edge_ids])
 
     def to_owner(blocks):
         taken = lax.all_to_all(blocks, "seq", split_axis=0, concat_axis=0, tiled=True)
@@ -420,10 +450,6 @@
 
     own_gate, head_weights = lax.optimization_barrier((own_gate, head_weights))
     server_gate = to_owner(own_gate)
-
-    out_all = lax.all_gather(
-        jnp.concatenate([w_out, router.T], axis=0).astype(jnp.bfloat16), "seq", axis=1, tiled=True
-    )
 
     def by_place(blocks):
         return jnp.stack(
@@ -456,12 +482,6 @@
     routings = [routing(turn, all_routes[k]) for k, turn in enumerate(part_turns)]
     chosen, valid_token, _ = routings[0]
 
-    part_positions = prompt_split(part_ids, slot_len, stagger, prompt_count)[1]
-    half_dim = HEAD // 2
-    frequency = ROPE_BASE ** (-jnp.arange(half_dim, dtype=jnp.float32) / half_dim)
-    angles = part_positions.astype(jnp.float32)[:, None] * frequency[None, :]
-    cosine = jnp.cos(angles)
-    sine_part = jnp.sin(angles)
     starts = (tp_place + jnp.arange(tp_count, dtype=jnp.int32)) % tp_count * col_share
     rows = project(starts, tp_blocks(part_rows), head_weights, cosine, sine_part)
     sink = lax.dynamic_slice_in_dim(sink_logits, head, 1, 0)
@@ -542,7 +562,27 @@
         out_pieces = [partial_out, from_turned(partial_out, "tp", 1)]
     else:
         out_pieces = [lax.psum(partial_out, "tp")]
-    full_rows, outgoing, logits = settle(out_pieces, tokens, mlp_gain, out_all[proj_width:])
+    router_rows = out_all[proj_width:]
+    slots = jnp.arange(seq_count, dtype=jnp.int32)
+    turn = part ^ (slots // head_count)
+    bits = len(part_masks)
+    turn = sum(((turn >> k) & 1) << (bits - 1 - k) for k in range(bits))
+    out_places = slots % head_count * part_count + turn
+    width = w_out.shape[1]
+    if width % 128:
+
+        def in_order(value):
+            blocks = [
+                lax.dynamic_slice_in_dim(value, out_places[place] * width, width, 1)
+                for place in range(seq_count)
+            ]
+            return jnp.concatenate(blocks, axis=1)
+
+        out_pieces, router_rows = ([in_order(piece) for piece in out_pieces], in_order(router_rows))
+        out_places, width = (jnp.zeros((1,), jnp.int32), model_width)
+    full_rows, outgoing, logits = settle(
+        out_places, out_pieces, tokens, mlp_gain, router_rows, width
+    )
     residual = lax.dynamic_slice_in_dim(full_rows, tp_place * col_share, col_share, 1)
     outgoing_share = lax.dynamic_slice_in_dim(outgoing, tp_place * col_share, col_share, 1)
 
@@ -620,7 +660,10 @@
         weighted(k, others[:, k - 1].reshape(-1, col_share)) for k in range(1, len(part_turns))
     ]
     mixes, own_rows = lax.optimization_barrier((mixes, own_rows))
-    expert_mix = sum(swapped(mix, "seq", turn) for mix, turn in zip(mixes, part_turns[1:]))
+    expert_mix = sum(
+        swapped(mix.astype(jnp.bfloat16), "seq", turn).astype(jnp.float32)
+        for mix, turn in zip(mixes, part_turns[1:])
+    )
     own_mix = weighted(0, back(own_rows)[:, 0].reshape(-1, col_share))
     return (residual + (expert_mix + own_mix)).astype(jnp.bfloat16)
 

time: 415 us -> 417 us (level)
  waiting for transfers between devices: 216 us -> 185 us
  starting transfers between devices: 76.4 us -> 97.5 us
  other arithmetic: 15.3 us -> 23.1 us
  local copies, waits for them, and re-layouts: 34.4 us -> 38.6 us
    all_to_all x3, waiting for transfers between devices: 47.7 us -> 13.6 us  [to_owner(): lax.all_to_all(blocks, 'seq', split_axis=0, concat_axis=0, tiled=True)]
    ppermute x19 -> x20, starting transfers between devices: 31.7 us -> 45.9 us  [swapped(): lax.ppermute(value, axis, [(place, place ^ mask) for place in range(count)])]
    all_to_all x3, starting transfers between devices: 15.4 us -> 24.5 us  [to_owner(): lax.all_to_all(blocks, 'seq', split_axis=0, concat_axis=0, tiled=True)]
    ppermute x19 -> x20, waiting for transfers between devices: 119 us -> 125 us  [swapped(): lax.ppermute(value, axis, [(place, place ^ mask) for place in range(count)])]
    all_to_all x2, waiting for transfers between devices: 24.6 us -> 20.2 us  [back(): lax.all_to_all(blocks, 'seq', split_axis=0, concat_axis=0, tiled=True, ax...]
    all_to_all x1, starting transfers between devices: 12.9 us -> 8.62 us  [shards(): lax.all_to_all(by_slot.reshape(seq_count, token_count, HEAD), 'seq', spli...]
    unnamed x82 -> x90, local copies, waits for them, and re-layouts: 27.1 us -> 31.4 us
  transfers between devices with their start and end apart: 34 -> 35, of which waited for: 21 -> 19; matrix products, arithmetic and copies ran while one was open for 12% -> 13% of each run, Pallas kernels for 9% -> 9%
where the time goes in v6:
time: 417 us; the launch traced here: 415 us
  waiting for transfers between devices  185 us (44%)
  starting transfers between devices  97.5 us (23%)
  Pallas kernels  47.2 us (11%)
  local copies, waits for them, and re-layouts  38.6 us (9%)
  other arithmetic  23.1 us (6%)
  between operations  14.3 us (3%)
  matrix products  9.04 us (2%)
    ppermute x20, waiting for transfers between devices, swapped(): lax.ppermute(value, axis, [(place, place ^ mask) for place in range(count)])  125 us
    ppermute x20, starting transfers between devices, swapped(): lax.ppermute(value, axis, [(place, place ^ mask) for place in range(count)])  45.9 us
    unnamed x90, local copies, waits for them, and re-layouts  31.4 us
    all_to_all x3, starting transfers between devices, to_owner(): lax.all_to_all(blocks, 'seq', split_axis=0, concat_axis=0, tiled=True)  24.5 us
    all_to_all x2, waiting for transfers between devices, back(): lax.all_to_all(blocks, 'seq', split_axis=0, concat_axis=0, tiled=True, ax...  20.2 us
    pallas_call x2, Pallas kernels, experts(): pl.pallas_call(lambda *refs: expert_body(count, share, *refs), grid_spec=...  19.1 us
    all_to_all x1, waiting for transfers between devices, shards(): lax.all_to_all(by_slot.reshape(seq_count, token_count, HEAD), 'seq', spli...  14.4 us
    all_to_all x3, waiting for transfers between devices, to_owner(): lax.all_to_all(blocks, 'seq', split_axis=0, concat_axis=0, tiled=True)  13.6 us
  transfers between devices with their start and end apart: 35, of which 19 were waited for; matrix products, arithmetic and copies ran while one was open for 13% of the time, Pallas kernels for 9%

profile of v6, /device:TPU:0, one launch (start us, length us, event | category | flops | bytes accessed | tf_op | source)
XLA Modules:
  0.0 415.1 jit_solution(7977757764085061470)
XLA Ops:
  6.5 1.3 convert_element_type.112
  7.8 1.2 multiply_reduce_fusion
  9.9 3.1 collective-permute-start
  14.1 2.7 collective-permute-start.2
  17.2 4.5 %collective-permute-start.7 = (bf16[64,1024]{1,0:T(8,128)(2,1)S(1)}, bf16[64,1024]{1,0:T(8,128)(2,1)S(1)}, u32[]{:S(2)}, u32[]{:S(2)}) collective-permute-start(bf16[64,1024]{1,0:T(8,128)(2,1)S(1)} %slice.160), channel_id=1, source_target_pairs={{0,16},{2,18},{4,20},{6,22},{8,24},{10,26},{12,28},{14,30},{1,17},... | collective-permute-start | bytes 393224 | tf_op jit(solution)/shard_map/ppermute | solution.py:21
  21.7 1.9 pack_heads.1
  23.6 3.8 all-to-all-start
  28.2 15.9 %collective-permute-start.8 = (bf16[64,1024]{1,0:T(8,128)(2,1)S(1)}, bf16[64,1024]{1,0:T(8,128)(2,1)S(1)}, u32[]{:S(2)}, u32[]{:S(2)}) collective-permute-start(bf16[64,1024]{1,0:T(8,128)(2,1)S(1)} %broadcast_select_fusion), channel_id=1, source_target_pairs={{0,8},{2,10},{4,12},{6,14},{8,0},{10,2},{12,4},{14,6},{16,24},{18,... | collective-permute-start | bytes 393224 | tf_op jit(solution)/shard_map/ppermute | solution.py:31
  44.1 1.3 pad_add_fusion.1
  45.4 9.9 %collective-permute-done.8 = bf16[64,1024]{1,0:T(8,128)(2,1)S(1)} collective-permute-done((bf16[64,1024]{1,0:T(8,128)(2,1)S(1)}, bf16[64,1024]{1,0:T(8,128)(2,1)S(1)}, u32[]{:S(2)}, u32[]{:S(2)}) %collective-permute-start.8) | collective-permute-done | bytes 131104 | tf_op jit(solution)/shard_map/ppermute | solution.py:31
  55.4 1.7 collective-permute-start.9
  58.1 1.8 pad_maximum_fusion.1
  60.4 2.2 collective-permute-done.9
  62.6 3.5 collective-permute-start.10
  66.1 3.2 multiply_sine_fusion
  69.3 12.9 %order_experts.1 = (bf16[16,128,512]{2,1,0:T(8,128)(2,1)}, bf16[16,128,512]{2,1,0:T(8,128)(2,1)}, bf16[16,128,512]{2,1,0:T(8,128)(2,1)}) custom-call(s32[16]{0:T(128)} %order_ref, f32[16,128,512]{2,1,0:T(8,128)} %gate_ref.1, f32[16,128,512]{2,1,0:T(8,128)} %up_ref.1, f32[16,128,512]{2,1,0:T(8,128)} %down_ref.1), custom_call_target="tpu_custom_call" | custom-call | flops 1 | bytes 1 | tf_op jit(solution)/shard_map/order_experts/pallas_call | solution.py:129
  82.9 2.1 collective-permute-start.4
  88.3 25.2 %collective-permute-done.4 = bf16[4,128,512]{2,1,0:T(8,128)(2,1)S(1)} collective-permute-done((bf16[4,128,512]{2,1,0:T(8,128)(2,1)S(1)}, bf16[4,128,512]{2,1,0:T(8,128)(2,1)S(1)}, u32[]{:S(2)}, u32[]{:S(2)}) %collective-permute-start.4) | collective-permute-done | bytes 524320 | tf_op jit(solution)/shard_map/ppermute | solution.py:31
  115.8 13.1 %all-to-all-start.1 = ((bf16[16,128,512]{2,1,0:T(8,128)(2,1)}), bf16[16,128,512]{2,1,0:T(8,128)(2,1)}, u32[]{:S(2)}, u32[]{:S(2)}) async-start(bf16[16,128,512]{2,1,0:T(8,128)(2,1)} %get-tuple-element.57), calls=%async_computation.1 | async-start | bytes 4194304 | tf_op jit(solution)/shard_map/all_to_all | solution.py:447
  128.9 1.6 fusion.52
  132.7 1.6 fusion.51
  134.3 1.6 fusion.50
  135.9 1.5 pad_maximum_fusion.refs_1_
  139.8 2.2 collective-permute-done.11.refs_2_
  142.0 1.4 copy-done.1
  145.5 5.4 %project.1.query_ref.key_ref.value_ref = bf16[1088,384]{1,0:T(8,128)(2,1)S(1)} custom-call(s32[2]{0:T(128)S(1)} %fusion.111.refs_0_, bf16[1088,1024]{1,0:T(8,128)(2,1)S(1)} %pad_maximum_fusion.refs_1_, bf16[1088,1024]{1,0:T(8,128)(2,1)} %collective-permute-done.11.refs_2_, bf16[2048,384]{1,0:T(8,128)(2,1)S(1)} %bitcast.150, f32[1088,64]{1,0:T(8,128)S(1)} %copy-done.4, ...), custom_call_target="tpu_custom_call" | custom-call | flops 1 | bytes 1 | tf_op jit(solution)/shard_map/project/pallas_call | solution.py:191
  152.0 6.7 %attend_once.1 = bf16[1088,128]{1,0:T(8,128)(2,1)S(1)} custom-call(f32[1]{0:T(128)} %dynamic_slice.92.sink_ref, s32[1088,1]{1,0:T(8,128)S(1)} %copy-done.5, s32[1,1088]{1,0:T(1,128)S(1)} %and_select_fusion.key_prompt_ref, bf16[1088,384]{1,0:T(8,128)(2,1)S(1)} %project.1.query_ref.key_ref.value_ref, bf16[1088,384]{1,0:T(8,128)(2,1)S(1)} %project.1.query_ref.key_ref.value_ref, ...), custom_call_target="tpu_custom_call" | custom-call | flops 1 | bytes 1 | tf_op jit(solution)/shard_map/attend_once/pallas_call | solution.py:233
  158.7 13.6 %all-to-all-done.1 = bf16[16,128,512]{2,1,0:T(8,128)(2,1)} async-done(((bf16[16,128,512]{2,1,0:T(8,128)(2,1)}), bf16[16,128,512]{2,1,0:T(8,128)(2,1)}, u32[]{:S(2)}, u32[]{:S(2)}) %all-to-all-start.1) | async-done | bytes 2097184 | tf_op jit(solution)/shard_map/all_to_all | solution.py:447
  173.5 8.6 %all-to-all-start.2 = ((bf16[16,128,128]{2,1,0:T(8,128)(2,1)}), bf16[16,128,128]{2,1,0:T(8,128)(2,1)S(1)}, u32[]{:S(2)}, u32[]{:S(2)}) async-start(bf16[16,128,128]{2,1,0:T(8,128)(2,1)} %bitcast.28), calls=%async_computation.2 | async-start | bytes 1048576 | tf_op jit(solution)/shard_map/all_to_all | solution.py:506
  182.2 14.4 %all-to-all-done.2 = bf16[16,128,128]{2,1,0:T(8,128)(2,1)S(1)} async-done(((bf16[16,128,128]{2,1,0:T(8,128)(2,1)}), bf16[16,128,128]{2,1,0:T(8,128)(2,1)S(1)}, u32[]{:S(2)}, u32[]{:S(2)}) %all-to-all-start.2) | async-done | bytes 524320 | tf_op jit(solution)/shard_map/all_to_all | solution.py:506
  196.6 6.6 %all-to-all-start.3 = ((bf16[16,128,512]{2,1,0:T(8,128)(2,1)}), bf16[16,128,512]{2,1,0:T(8,128)(2,1)}, u32[]{:S(2)}, u32[]{:S(2)}) async-start(bf16[16,128,512]{2,1,0:T(8,128)(2,1)} %get-tuple-element.70), calls=%async_computation.3 | async-start | bytes 4194304 | tf_op jit(solution)/shard_map/all_to_all | solution.py:447
  204.1 3.0 fusion.refs_1_
  208.6 1.2 collective-permute-done.12.refs_2_
  212.5 2.3 collective-permute-start.14
  215.9 42.3 %collective-permute-done.14 = f32[1,128,16]{2,1,0:T(8,128)S(1)} collective-permute-done((f32[1,128,16]{2,1,0:T(8,128)S(1)}, f32[1,128,16]{2,1,0:T(8,128)S(1)}, u32[]{:S(2)}, u32[]{:S(2)}) %collective-permute-start.14) | collective-permute-done | bytes 8224 | tf_op jit(solution)/shard_map/ppermute | solution.py:31
  258.3 4.5 %collective-permute-done.13 = bf16[1,128,1024]{2,1,0:T(8,128)(2,1)S(1)} collective-permute-done((bf16[1,128,1024]{2,1,0:T(8,128)(2,1)S(1)}, bf16[1,128,1024]{2,1,0:T(8,128)(2,1)S(1)}, u32[]{:S(2)}, u32[]{:S(2)}) %collective-permute-start.13) | collective-permute-done | bytes 262176 | tf_op jit(solution)/shard_map/ppermute | solution.py:31
  264.7 1.5 collective-permute-start.15
  266.1 1.8 collective-permute-start.16
  269.5 2.5 collective-permute-start.18
  272.0 9.0 %collective-permute-done.15 = bf16[2,72,1024]{2,1,0:T(8,128)(2,1)S(1)} collective-permute-done((bf16[2,72,1024]{2,1,0:T(8,128)(2,1)S(1)}, bf16[2,72,1024]{2,1,0:T(8,128)(2,1)S(1)}, u32[]{:S(2)}, u32[]{:S(2)}) %collective-permute-start.15) | collective-permute-done | bytes 294944 | tf_op jit(solution)/shard_map/ppermute | solution.py:31
  281.7 4.9 %all-to-all-start.4 = ((bf16[16,128,512]{2,1,0:T(8,128)(2,1)}), bf16[16,128,512]{2,1,0:T(8,128)(2,1)S(1)}, u32[]{:S(2)}, u32[]{:S(2)}) async-start(bf16[16,128,512]{2,1,0:T(8,128)(2,1)} %get-tuple-element.71), calls=%async_computation.4 | async-start | bytes 4194304 | tf_op jit(solution)/shard_map/all_to_all | solution.py:447
  286.5 1.7 bitcast_dynamic-update-slice_fusion.6
  288.3 3.7 collective-permute-start.21
  292.0 1.7 bitcast_dynamic-update-slice_fusion.5
  293.7 1.7 bitcast_dynamic-update-slice_fusion.4
  295.4 1.7 bitcast_dynamic-update-slice_fusion.3
  297.1 1.7 bitcast_dynamic-update-slice_fusion.2
  298.8 2.4 collective-permute-done.20
  301.2 1.7 bitcast_dynamic-update-slice_fusion.1
  302.9 29.6 %collective-permute-done.21 = bf16[2,72,1024]{2,1,0:T(8,128)(2,1)S(1)} collective-permute-done((bf16[2,72,1024]{2,1,0:T(8,128)(2,1)S(1)}, bf16[2,72,1024]{2,1,0:T(8,128)(2,1)S(1)}, u32[]{:S(2)}, u32[]{:S(2)}) %collective-permute-start.21) | collective-permute-done | bytes 294944 | tf_op jit(solution)/shard_map/ppermute | solution.py:31
  338.4 2.3 collective-permute-done.22.refs_3_
  342.4 1.4 copy-done.12
  343.8 9.6 %experts.2 = (bf16[1,576,1024]{2,1,0:T(8,128)(2,1)S(1)}, bf16[1,576,1024]{2,1,0:T(8,128)(2,1)}) custom-call(s32[2]{0:T(128)S(1)} %fusion.111.refs_0_, s32[2]{0:T(128)S(1)} %fusion.112.refs_1_, bf16[1,576,1024]{2,1,0:T(8,128)(2,1)} %bitcast.161, bf16[1,576,1024]{2,1,0:T(8,128)(2,1)} %copy-done.17, bf16[1,2048,512]{2,1,0:T(8,128)(2,1)} %bitcast.25.refs_4_, ...), custom_call_target="tpu_custom_call" | custom-call | flops 1 | bytes 1 | tf_op jit(solution)/shard_map/experts/pallas_call | solution.py:329
  353.5 2.9 collective-permute-done.24
  356.4 1.5 add_convert_fusion.1
  358.0 5.6 %all-to-all-start.5 = ((bf16[8,1,72,1024]{3,2,1,0:T(8,128)(2,1)}), bf16[8,1,72,1024]{3,2,1,0:T(8,128)(2,1)}, u32[]{:S(2)}, u32[]{:S(2)}) async-start(bf16[8,1,72,1024]{3,2,1,0:T(8,128)(2,1)} %bitcast.61), calls=%async_computation.5 | async-start | bytes 2359296 | tf_op jit(solution)/shard_map/all_to_all | solution.py:654
  363.6 9.6 %experts.3 = (bf16[1,576,1024]{2,1,0:T(8,128)(2,1)S(1)}, bf16[1,576,1024]{2,1,0:T(8,128)(2,1)}) custom-call(s32[2]{0:T(128)S(1)} %fusion.111.refs_0_, s32[2]{0:T(128)S(1)} %fusion.112.refs_1_, bf16[1,576,1024]{2,1,0:T(8,128)(2,1)} %bitcast.159, bf16[1,576,1024]{2,1,0:T(8,128)(2,1)} %copy-done.16, bf16[1,2048,512]{2,1,0:T(8,128)(2,1)} %bitcast.25.refs_4_, ...), custom_call_target="tpu_custom_call" | custom-call | flops 1 | bytes 1 | tf_op jit(solution)/shard_map/experts/pallas_call | solution.py:329
  374.0 2.2 collective-permute-done.25
  376.2 1.5 add_convert_fusion
  377.7 2.2 all-to-all-done.5
  380.0 2.1 fusion.18
  382.1 3.6 all-to-all-start.6
  386.6 2.0 collective-permute-start.26
  388.5 18.0 %all-to-all-done.6 = bf16[8,1,72,1024]{3,2,1,0:T(8,128)(2,1)S(1)} async-done(((bf16[8,1,72,1024]{3,2,1,0:T(8,128)(2,1)}), bf16[8,1,72,1024]{3,2,1,0:T(8,128)(2,1)S(1)}, u32[]{:S(2)}, u32[]{:S(2)}) %all-to-all-start.6) | async-done | bytes 1179680 | tf_op jit(solution)/shard_map/all_to_all | solution.py:654
  (193 shorter events, 41.2 us)
Async XLA Ops:
  6.5 7.5 %copy-start.24 = (f32[128,16]{0,1:T(8,128)S(1)}, f32[128,16]{0,1:T(8,128)}, u32[]{:S(2)}) copy-start(f32[128,16]{0,1:T(8,128)} %param.23) | copy-start | bytes 24580
  6.5 10.2 %copy-start.25 = (s32[128,8]{0,1:T(8,128)S(1)}, s32[128,8]{0,1:T(8,128)}, u32[]{:S(2)}) copy-start(s32[128,8]{0,1:T(8,128)} %param.29) | copy-start | bytes 12292
  6.5 15.2 %copy-start.6 = (f32[128,1024]{1,0:T(8,128)S(1)}, f32[128,1024]{1,0:T(8,128)}, u32[]{:S(2)}) copy-start(f32[128,1024]{1,0:T(8,128)} %query_ref.1) | copy-start | bytes 1572868
  6.5 15.2 %copy-start.7 = (f32[128,1024]{1,0:T(8,128)S(1)}, f32[128,1024]{1,0:T(8,128)}, u32[]{:S(2)}) copy-start(f32[128,1024]{1,0:T(8,128)} %key_ref.1) | copy-start | bytes 1572868
  6.5 15.2 %copy-start.8 = (f32[128,1024]{1,0:T(8,128)S(1)}, f32[128,1024]{1,0:T(8,128)}, u32[]{:S(2)}) copy-start(f32[128,1024]{1,0:T(8,128)} %value_ref.1) | copy-start | bytes 1572868
  9.9 47.2 %collective-permute-start = (bf16[1,128,1024]{2,1,0:T(8,128)(2,1)S(1)}, bf16[1,128,1024]{2,1,0:T(8,128)(2,1)}, u32[]{:S(2)}, u32[]{:S(2)}) collective-permute-start(bf16[1,128,1024]{2,1,0:T(8,128)(2,1)S(1)} %fusion.132), channel_id=1, source_target_pairs={{0,8},{2,10},{4,12},{6,14},{8,0},{10,2},{12,4},{14,6},{16,24},{18,... | collective-permute-start | bytes 786440 | tf_op jit(solution)/shard_map/ppermute | solution.py:31
  14.1 44.0 %collective-permute-start.2 = (bf16[1040,128]{1,0:T(8,128)(2,1)S(1)}, bf16[1040,128]{1,0:T(8,128)(2,1)}, u32[]{:S(2)}, u32[]{:S(2)}) collective-permute-start(bf16[1040,128]{1,0:T(8,128)(2,1)S(1)} %pad_maximum_fusion.6), channel_id=1, source_target_pairs={{0,16},{2,18},{4,20},{6,22},{8,24},{10,26},{12,28},{14,30},{16,0},... | collective-permute-start | bytes 798728 | tf_op jit(solution)/shard_map/ppermute | solution.py:31
  16.7 27.4 %collective-permute-start.1 = (s32[1,128,8]{1,2,0:T(8,128)S(1)}, s32[1,128,8]{1,2,0:T(8,128)}, u32[]{:S(2)}, u32[]{:S(2)}) collective-permute-start(s32[1,128,8]{1,2,0:T(8,128)S(1)} %bitcast.177), channel_id=1, source_target_pairs={{0,16},{2,18},{4,20},{6,22},{8,24},{10,26},{12,28},{14,30},{16,0},... | collective-permute-start | bytes 12296 | tf_op jit(solution)/shard_map/ppermute | solution.py:31
  17.2 11.0 %collective-permute-start.7 = (bf16[64,1024]{1,0:T(8,128)(2,1)S(1)}, bf16[64,1024]{1,0:T(8,128)(2,1)S(1)}, u32[]{:S(2)}, u32[]{:S(2)}) collective-permute-start(bf16[64,1024]{1,0:T(8,128)(2,1)S(1)} %slice.160), channel_id=1, source_target_pairs={{0,16},{2,18},{4,20},{6,22},{8,24},{10,26},{12,28},{14,30},{1,17},... | collective-permute-start | bytes 393224 | tf_op jit(solution)/shard_map/ppermute | solution.py:21
  23.6 92.2 %all-to-all-start = ((bf16[16,128,384]{2,1,0:T(8,128)(2,1)}), bf16[16,128,384]{2,1,0:T(8,128)(2,1)S(1)}, u32[]{:S(2)}, u32[]{:S(2)}) async-start(bf16[16,128,384]{2,1,0:T(8,128)(2,1)} %pack_heads.1), calls=%async_computation | async-start | bytes 3145728 | tf_op jit(solution)/shard_map/all_to_all | solution.py:392
  27.4 176.7 %all-gather.2.cloned.1.call-start = ((), (), s32[]{:S(2)}) async-start(), calls=%async_computation.7 | async-start | bytes 4792320 | tf_op jit(solution)/shard_map/all_gather | solution.py:413
  28.2 27.1 %collective-permute-start.8 = (bf16[64,1024]{1,0:T(8,128)(2,1)S(1)}, bf16[64,1024]{1,0:T(8,128)(2,1)S(1)}, u32[]{:S(2)}, u32[]{:S(2)}) collective-permute-start(bf16[64,1024]{1,0:T(8,128)(2,1)S(1)} %broadcast_select_fusion), channel_id=1, source_target_pairs={{0,8},{2,10},{4,12},{6,14},{8,0},{10,2},{12,4},{14,6},{16,24},{18,... | collective-permute-start | bytes 393224 | tf_op jit(solution)/shard_map/ppermute | solution.py:31
  55.4 7.2 %collective-permute-start.9 = (bf16[64,1024]{1,0:T(8,128)(2,1)S(1)}, bf16[64,1024]{1,0:T(8,128)(2,1)S(1)}, u32[]{:S(2)}, u32[]{:S(2)}) collective-permute-start(bf16[64,1024]{1,0:T(8,128)(2,1)S(1)} %fusion.131), channel_id=1, source_target_pairs={{0,4},{2,6},{4,0},{6,2},{8,12},{10,14},{12,8},{14,10},{16,20},{18,... | collective-permute-start | bytes 393224 | tf_op jit(solution)/shard_map/ppermute | solution.py:31
  59.9 22.9 %collective-permute-start.3 = (bf16[2,128,512]{2,1,0:T(8,128)(2,1)S(1)}, bf16[2,128,512]{2,1,0:T(8,128)(2,1)S(1)}, u32[]{:S(2)}, u32[]{:S(2)}) collective-permute-start(bf16[2,128,512]{2,1,0:T(8,128)(2,1)S(1)} %get-tuple-element.99), channel_id=1, source_target_pairs={{0,4},{2,6},{4,0},{6,2},{8,12},{10,14},{12,8},{14,10},{16,20},{18,... | collective-permute-start | bytes 786440 | tf_op jit(solution)/shard_map/ppermute | solution.py:31
  62.6 19.6 %collective-permute-start.10 = (bf16[64,1024]{1,0:T(8,128)(2,1)S(1)}, bf16[64,1024]{1,0:T(8,128)(2,1)S(1)}, u32[]{:S(2)}, u32[]{:S(2)}) collective-permute-start(bf16[64,1024]{1,0:T(8,128)(2,1)S(1)} %add.406), channel_id=1, source_target_pairs={{0,2},{2,0},{4,6},{6,4},{8,10},{10,8},{12,14},{14,12},{16,18},{18,... | collective-permute-start | bytes 393224 | tf_op jit(solution)/shard_map/ppermute | solution.py:31
  69.2 15.8 %collective-permute-start.5 = (bf16[2,128,512]{2,1,0:T(8,128)(2,1)S(1)}, bf16[2,128,512]{2,1,0:T(8,128)(2,1)}, u32[]{:S(2)}, u32[]{:S(2)}) collective-permute-start(bf16[2,128,512]{2,1,0:T(8,128)(2,1)S(1)} %get-tuple-element.100), channel_id=1, source_target_pairs={{0,2},{2,0},{4,6},{6,4},{8,10},{10,8},{12,14},{14,12},{16,18},{18,... | collective-permute-start | bytes 786440 | tf_op jit(solution)/shard_map/ppermute | solution.py:31
  82.9 30.6 %collective-permute-start.4 = (bf16[4,128,512]{2,1,0:T(8,128)(2,1)S(1)}, bf16[4,128,512]{2,1,0:T(8,128)(2,1)S(1)}, u32[]{:S(2)}, u32[]{:S(2)}) collective-permute-start(bf16[4,128,512]{2,1,0:T(8,128)(2,1)S(1)} %pad_maximum_fusion.3), channel_id=1, source_target_pairs={{0,2},{2,0},{4,6},{6,4},{8,10},{10,8},{12,14},{14,12},{16,18},{18,... | collective-permute-start | bytes 1572872 | tf_op jit(solution)/shard_map/ppermute | solution.py:31
  86.0 27.6 %collective-permute-start.6 = (bf16[4,128,512]{2,1,0:T(8,128)(2,1)S(1)}, bf16[4,128,512]{2,1,0:T(8,128)(2,1)S(1)}, u32[]{:S(2)}, u32[]{:S(2)}) collective-permute-start(bf16[4,128,512]{2,1,0:T(8,128)(2,1)S(1)} %pad_maximum_fusion.4), channel_id=1, source_target_pairs={{0,4},{2,6},{4,0},{6,2},{8,12},{10,14},{12,8},{14,10},{16,20},{18,... | collective-permute-start | bytes 1572872 | tf_op jit(solution)/shard_map/ppermute | solution.py:31
  113.5 0.8 copy-start.19
  114.3 0.8 copy-start.20
  115.8 15.3 %copy-start = (bf16[16,128,384]{2,1,0:T(8,128)(2,1)}, bf16[16,128,384]{2,1,0:T(8,128)(2,1)S(1)}, u32[]{:S(2)}) copy-start(bf16[16,128,384]{2,1,0:T(8,128)(2,1)S(1)} %all-to-all-done) | copy-start | bytes 4718596
  115.8 20.1 %copy-start.18 = (bf16[64,1024]{1,0:T(8,128)(2,1)S(1)}, bf16[64,1024]{1,0:T(8,128)(2,1)}, u32[]{:S(2)}) copy-start(bf16[64,1024]{1,0:T(8,128)(2,1)} %add.407) | copy-start | bytes 393220
  115.8 56.5 %all-to-all-start.1 = ((bf16[16,128,512]{2,1,0:T(8,128)(2,1)}), bf16[16,128,512]{2,1,0:T(8,128)(2,1)}, u32[]{:S(2)}, u32[]{:S(2)}) async-start(bf16[16,128,512]{2,1,0:T(8,128)(2,1)} %get-tuple-element.57), calls=%async_computation.1 | async-start | bytes 4194304 | tf_op jit(solution)/shard_map/all_to_all | solution.py:447
  135.9 2.0 copy-start.27
  135.9 2.6 copy-start.23
  135.9 2.6 copy-start.26
  137.4 4.5 %collective-permute-start.11 = (bf16[1088,1024]{1,0:T(8,128)(2,1)S(1)}, bf16[1088,1024]{1,0:T(8,128)(2,1)}, u32[]{:S(2)}, u32[]{:S(2)}) collective-permute-start(bf16[1088,1024]{1,0:T(8,128)(2,1)S(1)} %pad_maximum_fusion.refs_1_), channel_id=1, source_target_pairs={{1,0},{0,1},{3,2},{2,3},{5,4},{4,5},{7,6},{6,7},{9,8},{8,9},{11,10... | collective-permute-start | bytes 6684680 | tf_op jit(solution)/shard_map/ppermute | solution.py:26
  142.0 1.4 copy-start.1
  143.4 1.1 copy-start.3
  144.4 1.1 copy-start.4
  150.9 1.1 copy-start.5
  173.5 23.0 %all-to-all-start.2 = ((bf16[16,128,128]{2,1,0:T(8,128)(2,1)}), bf16[16,128,128]{2,1,0:T(8,128)(2,1)S(1)}, u32[]{:S(2)}, u32[]{:S(2)}) async-start(bf16[16,128,128]{2,1,0:T(8,128)(2,1)} %bitcast.28), calls=%async_computation.2 | async-start | bytes 1048576 | tf_op jit(solution)/shard_map/all_to_all | solution.py:506
  196.6 84.3 %all-to-all-start.3 = ((bf16[16,128,512]{2,1,0:T(8,128)(2,1)}), bf16[16,128,512]{2,1,0:T(8,128)(2,1)}, u32[]{:S(2)}, u32[]{:S(2)}) async-start(bf16[16,128,512]{2,1,0:T(8,128)(2,1)} %get-tuple-element.70), calls=%async_computation.3 | async-start | bytes 4194304 | tf_op jit(solution)/shard_map/all_to_all | solution.py:447
  204.1 3.1 copy-start.22
  204.1 5.7 %copy-start.2 = (bf16[128,2048]{1,0:T(8,128)(2,1)S(1)}, bf16[128,2048]{1,0:T(8,128)(2,1)}, u32[]{:S(2)}) copy-start(bf16[128,2048]{1,0:T(8,128)(2,1)} %refs_3_.1) | copy-start | bytes 1572868
  204.1 5.7 %copy-start.11 = (f32[2048]{0:T(1024)S(1)}, f32[2048]{0:T(1024)}, u32[]{:S(2)}) copy-start(f32[2048]{0:T(1024)} %param.17) | copy-start | bytes 24580
  207.1 2.7 collective-permute-start.12
  211.1 1.0 copy-start.9
  212.5 45.8 %collective-permute-start.14 = (f32[1,128,16]{2,1,0:T(8,128)S(1)}, f32[1,128,16]{2,1,0:T(8,128)S(1)}, u32[]{:S(2)}, u32[]{:S(2)}) collective-permute-start(f32[1,128,16]{2,1,0:T(8,128)S(1)} %multiply_bitcast_fusion), channel_id=1, source_target_pairs={{0,16},{2,18},{4,20},{6,22},{8,24},{10,26},{12,28},{14,30},{16,0},... | collective-permute-start | bytes 24584 | tf_op jit(solution)/shard_map/ppermute | solution.py:31
  214.8 48.0 %collective-permute-start.13 = (bf16[1,128,1024]{2,1,0:T(8,128)(2,1)S(1)}, bf16[1,128,1024]{2,1,0:T(8,128)(2,1)S(1)}, u32[]{:S(2)}, u32[]{:S(2)}) collective-permute-start(bf16[1,128,1024]{2,1,0:T(8,128)(2,1)S(1)} %dynamic-slice_bitcast_fusion), channel_id=1, source_target_pairs={{0,16},{2,18},{4,20},{6,22},{8,24},{10,26},{12,28},{14,30},{16,0},... | collective-permute-start | bytes 786440 | tf_op jit(solution)/shard_map/ppermute | solution.py:31
  264.7 16.3 %collective-permute-start.15 = (bf16[2,72,1024]{2,1,0:T(8,128)(2,1)S(1)}, bf16[2,72,1024]{2,1,0:T(8,128)(2,1)S(1)}, u32[]{:S(2)}, u32[]{:S(2)}) collective-permute-start(bf16[2,72,1024]{2,1,0:T(8,128)(2,1)S(1)} %get-tuple-element.93), channel_id=1, source_target_pairs={{0,2},{2,0},{4,6},{6,4},{8,10},{10,8},{12,14},{14,12},{16,18},{18,... | collective-permute-start | bytes 884744 | tf_op jit(solution)/shard_map/ppermute | solution.py:31
  266.1 22.1 %collective-permute-start.16 = (bf16[2,72,1024]{2,1,0:T(8,128)(2,1)S(1)}, bf16[2,72,1024]{2,1,0:T(8,128)(2,1)}, u32[]{:S(2)}, u32[]{:S(2)}) collective-permute-start(bf16[2,72,1024]{2,1,0:T(8,128)(2,1)S(1)} %get-tuple-element.94), channel_id=1, source_target_pairs={{0,4},{2,6},{4,0},{6,2},{8,12},{10,14},{12,8},{14,10},{16,20},{18,... | collective-permute-start | bytes 884744 | tf_op jit(solution)/shard_map/ppermute | solution.py:31
  268.8 28.3 %collective-permute-start.19 = (bf16[2,72,1024]{2,1,0:T(8,128)(2,1)}, bf16[2,72,1024]{2,1,0:T(8,128)(2,1)}, u32[]{:S(2)}, u32[]{:S(2)}) collective-permute-start(bf16[2,72,1024]{2,1,0:T(8,128)(2,1)} %get-tuple-element.98), channel_id=1, source_target_pairs={{0,10},{2,8},{4,14},{6,12},{8,2},{10,0},{12,6},{14,4},{16,26},{18,... | collective-permute-start | bytes 884744 | tf_op jit(solution)/shard_map/ppermute | solution.py:31
  268.9 24.9 %collective-permute-start.17 = (bf16[2,72,1024]{2,1,0:T(8,128)(2,1)S(1)}, bf16[2,72,1024]{2,1,0:T(8,128)(2,1)}, u32[]{:S(2)}, u32[]{:S(2)}) collective-permute-start(bf16[2,72,1024]{2,1,0:T(8,128)(2,1)S(1)} %get-tuple-element.95), channel_id=1, source_target_pairs={{0,6},{2,4},{4,2},{6,0},{8,14},{10,12},{12,10},{14,8},{16,22},{18,... | collective-permute-start | bytes 884744 | tf_op jit(solution)/shard_map/ppermute | solution.py:31
  269.5 25.9 %collective-permute-start.18 = (bf16[2,72,1024]{2,1,0:T(8,128)(2,1)S(1)}, bf16[2,72,1024]{2,1,0:T(8,128)(2,1)}, u32[]{:S(2)}, u32[]{:S(2)}) collective-permute-start(bf16[2,72,1024]{2,1,0:T(8,128)(2,1)S(1)} %get-tuple-element.96), channel_id=1, source_target_pairs={{0,8},{2,10},{4,12},{6,14},{8,0},{10,2},{12,4},{14,6},{16,24},{18,... | collective-permute-start | bytes 884744 | tf_op jit(solution)/shard_map/ppermute | solution.py:31
  280.9 0.7 copy-start.21
  281.0 20.2 %collective-permute-start.20 = (bf16[2,72,1024]{2,1,0:T(8,128)(2,1)}, bf16[2,72,1024]{2,1,0:T(8,128)(2,1)}, u32[]{:S(2)}, u32[]{:S(2)}) collective-permute-start(bf16[2,72,1024]{2,1,0:T(8,128)(2,1)} %get-tuple-element.97), channel_id=1, source_target_pairs={{0,12},{2,14},{4,8},{6,10},{8,4},{10,6},{12,0},{14,2},{16,28},{18,... | collective-permute-start | bytes 884744 | tf_op jit(solution)/shard_map/ppermute | solution.py:31
  281.7 60.7 %all-to-all-start.4 = ((bf16[16,128,512]{2,1,0:T(8,128)(2,1)}), bf16[16,128,512]{2,1,0:T(8,128)(2,1)S(1)}, u32[]{:S(2)}, u32[]{:S(2)}) async-start(bf16[16,128,512]{2,1,0:T(8,128)(2,1)} %get-tuple-element.71), calls=%async_computation.4 | async-start | bytes 4194304 | tf_op jit(solution)/shard_map/all_to_all | solution.py:447
  288.3 44.2 %collective-permute-start.21 = (bf16[2,72,1024]{2,1,0:T(8,128)(2,1)S(1)}, bf16[2,72,1024]{2,1,0:T(8,128)(2,1)S(1)}, u32[]{:S(2)}, u32[]{:S(2)}) collective-permute-start(bf16[2,72,1024]{2,1,0:T(8,128)(2,1)S(1)} %get-tuple-element.91), channel_id=1, source_target_pairs={{0,14},{2,12},{4,10},{6,8},{8,6},{10,4},{12,2},{14,0},{16,30},{18,... | collective-permute-start | bytes 884744 | tf_op jit(solution)/shard_map/ppermute | solution.py:31
  333.3 4.1 copy-start.15
  337.8 2.9 copy-start.13
  337.8 2.9 copy-start.14
  337.8 2.9 collective-permute-start.22
  337.9 4.5 %collective-permute-start.23 = (bf16[1,576,1024]{2,1,0:T(8,128)(2,1)S(1)}, bf16[1,576,1024]{2,1,0:T(8,128)(2,1)S(1)}, u32[]{:S(2)}, u32[]{:S(2)}) collective-permute-start(bf16[1,576,1024]{2,1,0:T(8,128)(2,1)S(1)} %bitcast.158), channel_id=1, source_target_pairs={{1,0},{0,1},{3,2},{2,3},{5,4},{4,5},{7,6},{6,7},{9,8},{8,9},{11,10... | collective-permute-start | bytes 3538952 | tf_op jit(solution)/shard_map/ppermute | solution.py:26
  340.7 1.0 copy-start.17
  342.4 15.6 %copy-start.16 = (bf16[1,576,1024]{2,1,0:T(8,128)(2,1)}, bf16[1,576,1024]{2,1,0:T(8,128)(2,1)S(1)}, u32[]{:S(2)}) copy-start(bf16[1,576,1024]{2,1,0:T(8,128)(2,1)S(1)} %collective-permute-done.23.refs_3_) | copy-start | bytes 3538948
  342.4 1.4 copy-start.12
  353.4 3.1 collective-permute-start.24
  358.0 22.0 %all-to-all-start.5 = ((bf16[8,1,72,1024]{3,2,1,0:T(8,128)(2,1)}), bf16[8,1,72,1024]{3,2,1,0:T(8,128)(2,1)}, u32[]{:S(2)}, u32[]{:S(2)}) async-start(bf16[8,1,72,1024]{3,2,1,0:T(8,128)(2,1)} %bitcast.61), calls=%async_computation.5 | async-start | bytes 2359296 | tf_op jit(solution)/shard_map/all_to_all | solution.py:654
  373.2 3.1 collective-permute-start.25
  382.1 24.4 %all-to-all-start.6 = ((bf16[8,1,72,1024]{3,2,1,0:T(8,128)(2,1)}), bf16[8,1,72,1024]{3,2,1,0:T(8,128)(2,1)S(1)}, u32[]{:S(2)}, u32[]{:S(2)}) async-start(bf16[8,1,72,1024]{3,2,1,0:T(8,128)(2,1)} %bitcast.65), calls=%async_computation.6 | async-start | bytes 2359296 | tf_op jit(solution)/shard_map/all_to_all | solution.py:654
  386.3 21.1 %copy-start.10 = (f32[128,2048]{1,0:T(8,128)S(1)}, f32[128,2048]{1,0:T(8,128)}, u32[]{:S(2)}) copy-start(f32[128,2048]{1,0:T(8,128)} %copy-done.9) | copy-start | bytes 3145732
  386.6 20.8 %collective-permute-start.26 = (bf16[128,1024]{1,0:T(8,128)(2,1)S(1)}, bf16[128,1024]{1,0:T(8,128)(2,1)S(1)}, u32[]{:S(2)}, u32[]{:S(2)}) collective-permute-start(bf16[128,1024]{1,0:T(8,128)(2,1)S(1)} %slice_add_fusion.2), channel_id=1, source_target_pairs={{0,16},{2,18},{4,20},{6,22},{8,24},{10,26},{12,28},{14,30},{16,0},... | collective-permute-start | bytes 786440 | tf_op jit(solution)/shard_map/ppermute | solution.py:31
Sparse Core Ops, SparseCore 0:
  69.4 134.6 all-gather.1

commit v7 on v6

--- a/solution.py
+++ b/solution.py
@@ -289,57 +289,71 @@
     )(places, *pieces, tokens, gain[None, :], router)
 
 
-def expert_body(turn_count, share, in_ref, out_ref, *refs):
-    rows, (gate_ref, up_ref, down_ref) = (refs[:turn_count], refs[turn_count : turn_count + 3])
-    outs = refs[turn_count + 3 : 2 * turn_count + 3]
-    sums = refs[2 * turn_count + 3 :]
-    block = pl.program_id(1)
+def hidden_body(turn_count, share, start_ref, *refs):
+    rows, (gate_ref, up_ref, out_ref) = (refs[:turn_count], refs[turn_count:])
     gate = up = 0.0
     for turn in range(turn_count):
-        here = pl.ds(pl.multiple_of(in_ref[turn], share), share)
+        here = pl.ds(pl.multiple_of(start_ref[turn], share), share)
         gate = gate + jnp.dot(
             rows[turn][0], gate_ref[0, here, :], preferred_element_type=jnp.float32
         )
         up = up + jnp.dot(rows[turn][0], up_ref[0, here, :], preferred_element_type=jnp.float32)
-    state = (gate / (1.0 + jnp.exp(-gate)) * up).astype(jnp.bfloat16)
+    out_ref[0] = (gate / (1.0 + jnp.exp(-gate)) * up).astype(jnp.bfloat16)
+
+
+def hidden_units(starts, row_blocks, gate, up):
+    local_experts, row_count, share = row_blocks[0].shape
+    rows, width = gate.shape[1:]
+    whole = pl.BlockSpec((1, rows, width), lambda e, a: (e, 0, 0))
+    count = len(row_blocks)
+    return pl.pallas_call(
+        lambda *refs: hidden_body(count, share, *refs),
+        grid_spec=pltpu.PrefetchScalarGridSpec(
+            num_scalar_prefetch=1,
+            grid=(local_experts,),
+            in_specs=[pl.BlockSpec((1, row_count, share), lambda e, a: (e, 0, 0))] * count
+            + [whole] * 2,
+            out_specs=pl.BlockSpec((1, row_count, width), lambda e, a: (e, 0, 0)),
+        ),
+        out_shape=jax.ShapeDtypeStruct((local_experts, row_count, width), jnp.bfloat16),
+        compiler_params=pltpu.CompilerParams(vmem_limit_bytes=52 * 2**20),
+        cost_estimate=SMALL,
+        name="hidden_units",
+    )(starts, *row_blocks, gate, up)
+
+
+def down_body(turn_count, share, start_ref, hidden_ref, down_ref, *outs):
     for turn in range(turn_count):
-        here = pl.ds(pl.multiple_of(out_ref[turn], share), share)
-        down = lax.dot_general(
-            state,
+        here = pl.ds(pl.multiple_of(start_ref[turn], share), share)
+        outs[turn][0] = lax.dot_general(
+            hidden_ref[0],
             down_ref[0, here, :],
             (((1,), (1,)), ((), ())),
             preferred_element_type=jnp.float32,
-        )
-
-        @pl.when(block == 0)
-        def _():
-            sums[turn][...] = down
-
-        @pl.when(block > 0)
-        def _():
-            outs[turn][0] = (sums[turn][...] + down).astype(jnp.bfloat16)
-
-
-def experts(in_starts, out_starts, row_blocks, weights):
-    local_experts, row_count, share = row_blocks[0].shape
-    rows, width = weights[0].shape[1:]
-    block = pl.BlockSpec((1, row_count, share), lambda e, f, a, b: (e, 0, 0))
-    some = pl.BlockSpec((1, rows, width // 2), lambda e, f, a, b: (e, 0, f))
-    count = len(row_blocks)
+        ).astype(jnp.bfloat16)
+
+
+def down_rows(starts, hidden, down):
+    local_experts, row_count, width = hidden.shape
+    columns, count = (down.shape[1], starts.shape[0])
+    share = columns // count
+    block = pl.BlockSpec((1, row_count, share), lambda e, a: (e, 0, 0))
     return pl.pallas_call(
-        lambda *refs: expert_body(count, share, *refs),
+        lambda *refs: down_body(count, share, *refs),
         grid_spec=pltpu.PrefetchScalarGridSpec(
-            num_scalar_prefetch=2,
-            grid=(local_experts, 2),
-            in_specs=[block] * count + [some] * 3,
+            num_scalar_prefetch=1,
+            grid=(local_experts,),
+            in_specs=[
+                pl.BlockSpec((1, row_count, width), lambda e, a: (e, 0, 0)),
+                pl.BlockSpec((1, columns, width), lambda e, a: (e, 0, 0)),
+            ],
             out_specs=[block] * count,
-            scratch_shapes=[pltpu.VMEM((row_count, share), jnp.float32)] * count,
         ),
-        out_shape=[jax.ShapeDtypeStruct(row_blocks[0].shape, jnp.bfloat16)] * count,
+        out_shape=[jax.ShapeDtypeStruct((local_experts, row_count, share), jnp.bfloat16)] * count,
         compiler_params=pltpu.CompilerParams(vmem_limit_bytes=52 * 2**20),
         cost_estimate=SMALL,
-        name="experts",
-    )(in_starts, out_starts, *row_blocks, *weights)
+        name="down_rows",
+    )(starts, hidden, down)
 
 
 def shards(
@@ -400,9 +414,6 @@
     normed = rms_scale(tokens.astype(jnp.float32), attn_gain).astype(jnp.bfloat16)
     share = lax.dynamic_slice_in_dim(normed, tp_place * col_share, col_share, 1)
     all_routes, part_turns = doubled(routes[None], part_masks, 0)
-    if aligned:
-        edge = from_behind(share[token_count - stagger :], "seq", head_count)
-        edge = jnp.where(head == head_count - 1, edge, jnp.zeros((), jnp.bfloat16))
     out_all, _ = doubled(
         jnp.concatenate([w_out, router.T], axis=0).astype(jnp.bfloat16), part_masks, 1
     )
@@ -410,13 +421,9 @@
     first_rows, all_routes, out_all, layout_map = lax.optimization_barrier(
         (first_rows, all_routes, out_all, layout_map)
     )
-    out_all = lax.all_gather(out_all, "seq", axis=1, tiled=True, axis_index_groups=groups)
     own_gate, own_up, own_down = order_experts(layout_map, expert_gate, expert_up, expert_down)
     part_ids = (part * head_count + (head ^ turns))[:, None] * token_count + offsets[None, :]
     part_ids = part_ids.reshape(-1)
-    if aligned:
-        edge_ids = part * part_slots - stagger + jnp.arange(stagger, dtype=jnp.int32)
-        part_ids = jnp.concatenate([part_ids, edge_ids])
     part_positions = prompt_split(part_ids, slot_len, stagger, prompt_count)[1]
     half_dim = HEAD // 2
     frequency = ROPE_BASE ** (-jnp.arange(half_dim, dtype=jnp.float32) / half_dim)
@@ -438,18 +445,24 @@
             known = known + [turn ^ mask for turn in known]
         pieces.append(jnp.concatenate([piece[known.index(m)] for m in range(head_count)], axis=0))
     part_rows = jnp.concatenate(pieces, axis=1)
-    if aligned:
-        for mask in group_masks:
-            edge = edge + swapped(edge, "seq", mask)
-        part_rows = jnp.concatenate([part_rows, edge], axis=0)
 
     def to_owner(blocks):
         taken = lax.all_to_all(blocks, "seq", split_axis=0, concat_axis=0, tiled=True)
         taken = taken.reshape(seq_count, local_experts, *blocks.shape[1:])
         return jnp.swapaxes(taken, 0, 1).reshape(local_experts, model_width, blocks.shape[2])
 
-    own_gate, head_weights = lax.optimization_barrier((own_gate, head_weights))
-    server_gate = to_owner(own_gate)
+    out_all, _ = doubled(out_all, group_masks[:-2], 1)
+    out_rows = out_all.shape[0] // 32 * 16
+    out_halves = [
+        (out_all[:out_rows], group_masks[-2:]),
+        (out_all[out_rows:], group_masks[-2:][::-1]),
+    ]
+    halves, head_weights, part_rows = lax.optimization_barrier(
+        ([half for half, _ in out_halves], head_weights, part_rows)
+    )
+    out_halves = [
+        (doubled(half, masks[:1], 1)[0], masks[1:]) for half, (_, masks) in zip(halves, out_halves)
+    ]
 
     def by_place(blocks):
         return jnp.stack(
@@ -494,27 +507,28 @@
         )
 
     if aligned:
-        row_prompt, row_position = prompt_split(part_ids, slot_len, stagger, prompt_count)
-        row_live = (part_ids >= 0) & (row_position < length_of(row_prompt, real_lengths))
-        mixed = attend_once(sink, row_prompt, jnp.where(row_live, row_prompt, -1), rows)
-        mixed, server_gate = lax.optimization_barrier((mixed, server_gate))
-        by_slot = by_place(mixed[:part_slots].reshape(head_count, token_count, HEAD))
-        by_slot = jnp.concatenate([mixed[part_slots:], by_slot.reshape(part_slots, HEAD)], axis=0)
-        by_slot = lax.dynamic_update_slice_in_dim(
-            jnp.zeros((stagger + total_slots, HEAD), jnp.bfloat16), by_slot, part * part_slots, 0
-        )[stagger:]
-        taken = lax.all_to_all(
-            by_slot.reshape(seq_count, token_count, HEAD),
-            "seq",
-            split_axis=0,
-            concat_axis=0,
-            tiled=True,
-        )
-        kept = lax.dynamic_slice_in_dim(taken, part * head_count, head_count, 0)
-        next_part = jnp.minimum(part + 1, part_count - 1)
-        moved = lax.dynamic_slice_in_dim(taken, next_part * head_count, head_count, 0)
-        is_moved = (head == head_count - 1) & (offsets >= token_count - stagger)
-        attention_result = jnp.where(is_moved[None, :, None], moved, kept)
+        edge_start = (head ^ (head_count - 1)) * token_count + token_count - stagger
+        edge = from_behind(
+            lax.dynamic_slice_in_dim(rows, edge_start, stagger, 0), "seq", head_count
+        )
+        edge_ids = part * part_slots - stagger + jnp.arange(stagger, dtype=jnp.int32)
+        row_ids = jnp.concatenate([part_ids, edge_ids])
+        row_prompt, row_position = prompt_split(row_ids, slot_len, stagger, prompt_count)
+        row_live = (row_ids >= 0) & (row_position < length_of(row_prompt, real_lengths))
+        halves, edge = lax.optimization_barrier(([half for half, _ in out_halves], edge))
+        out_halves = [(half, masks) for half, (_, masks) in zip(halves, out_halves)]
+        mixed = attend_once(
+            sink,
+            row_prompt,
+            jnp.where(row_live, row_prompt, -1),
+            jnp.concatenate([rows, edge], axis=0),
+        )
+        edge_back = from_behind(mixed[part_slots:], "seq", -head_count)
+        mixed = mixed[:part_slots]
+        kept = lax.dynamic_slice_in_dim(mixed, edge_start, stagger, 0)
+        mixed = lax.dynamic_update_slice_in_dim(
+            mixed, jnp.where(part < part_count - 1, edge_back, kept), edge_start, 0
+        )
     else:
         query_rows, key_rows, value_rows = (rows[:, k * HEAD : (k + 1) * HEAD] for k in range(3))
         softmax_state = attend(
@@ -540,34 +554,46 @@
             )
         _, denominator, accumulated = softmax_state
         mixed = (accumulated / denominator).astype(jnp.bfloat16)
-        mixed, server_gate = lax.optimization_barrier((mixed, server_gate))
-        attention_result = lax.all_to_all(
-            by_place(mixed.reshape(head_count, token_count, HEAD)),
-            "seq",
-            split_axis=0,
-            concat_axis=0,
-            tiled=True,
-            axis_index_groups=groups,
-        )
-    attention_result, own_up = lax.optimization_barrier((attention_result, own_up))
-    server_up = to_owner(own_up)
+    blocks = by_place(mixed.reshape(head_count, token_count, HEAD))
+    out_halves = [(half, swapped(half, "seq", masks[0])) for half, masks in out_halves]
+    blocks, out_halves = lax.optimization_barrier((blocks, out_halves))
+    attention_result = lax.all_to_all(
+        blocks, "seq", split_axis=0, concat_axis=0, tiled=True, axis_index_groups=groups
+    )
+    attention_result, own_gate = lax.optimization_barrier((attention_result, own_gate))
+    server_gate = to_owner(own_gate)
 
     proj_width = head_count * HEAD
-    partial_out = jnp.dot(
-        jnp.swapaxes(attention_result, 0, 1).reshape(token_count, proj_width),
-        out_all[:proj_width],
-        preferred_element_type=jnp.float32,
+    attention_result = jnp.swapaxes(attention_result, 0, 1).reshape(token_count, proj_width)
+
+    def joined(pieces, half):
+        if half == 0:
+            return jnp.concatenate(pieces, axis=1)
+        span = pieces[0].shape[1] // 2
+        low, high = ([piece[:, k * span : (k + 1) * span] for piece in pieces] for k in range(2))
+        return jnp.concatenate([*low, *high], axis=1)
+
+    partial_out = sum(
+        joined([jnp.dot(rows, piece, preferred_element_type=jnp.float32) for piece in pieces], half)
+        for half, (rows, pieces) in enumerate(
+            (
+                (attention_result[:, :out_rows], out_halves[0]),
+                (
+                    attention_result[:, out_rows:],
+                    [piece[: proj_width - out_rows] for piece in out_halves[1]],
+                ),
+            )
+        )
     )
     if tp_count == 2:
         out_pieces = [partial_out, from_turned(partial_out, "tp", 1)]
     else:
         out_pieces = [lax.psum(partial_out, "tp")]
-    router_rows = out_all[proj_width:]
+    router_rows = joined([piece[proj_width - out_rows :] for piece in out_halves[1]], 1)
     slots = jnp.arange(seq_count, dtype=jnp.int32)
-    turn = part ^ (slots // head_count)
-    bits = len(part_masks)
-    turn = sum(((turn >> k) & 1) << (bits - 1 - k) for k in range(bits))
-    out_places = slots % head_count * part_count + turn
+    turn = seq_place ^ slots
+    bits = len(part_masks) + len(group_masks)
+    out_places = sum(((turn >> k) & 1) << (bits - 1 - k) for k in range(bits))
     width = w_out.shape[1]
     if width % 128:
 
@@ -593,8 +619,10 @@
     route_weight = route_weight * valid_token[:, None]
     all_weights, _ = doubled(route_weight[None], part_masks, 0)
     all_rows, _ = doubled(outgoing_share[None], part_masks, 0)
-    all_rows, all_weights, own_down = lax.optimization_barrier((all_rows, all_weights, own_down))
-    server_down = to_owner(own_down)
+    all_rows, all_weights, server_gate, own_up = lax.optimization_barrier(
+        (all_rows, all_weights, server_gate, own_up)
+    )
+    server_up = to_owner(own_up)
     buffer = jnp.stack(
         [
             lax.dot_general(
@@ -613,7 +641,10 @@
         block = lax.dynamic_index_in_dim(buffer, head ^ m, 0, keepdims=False)
         return swapped(block, "seq", m) if m else block
 
-    received = by_place(jnp.stack([to_mate(m) for m in range(head_count)]))
+    received = [to_mate(m) for m in range(head_count)]
+    received[1], server_up, own_down = lax.optimization_barrier((received[1], server_up, own_down))
+    server_down = to_owner(own_down)
+    received = by_place(jnp.stack(received))
     received = received.reshape(head_count, part_count, local_experts, capacity, col_share)
     turn_ids = jnp.arange(tp_count, dtype=jnp.int32)
     in_starts = (tp_place + turn_ids) % tp_count * col_share
@@ -623,18 +654,18 @@
         tp_blocks(jnp.moveaxis(rows, 2, 0).reshape(local_experts, -1, col_share))
         for rows in (received[:, 1:], received[:, :1])
     ]
-    server = (server_gate, server_up, server_down)
-    halves, server = lax.optimization_barrier((halves, server))
-
-    def through_experts(row_blocks, parts):
-        outs = experts(in_starts, out_starts, row_blocks, server)
+    hidden = [hidden_units(in_starts, rows, server_gate, server_up) for rows in halves]
+    hidden, server_down = lax.optimization_barrier((hidden, server_down))
+
+    def through_experts(rows, parts):
+        outs = down_rows(out_starts, rows, server_down)
         outs = [outs[0]] + [from_turned(outs[k], "tp", k) for k in range(1, tp_count)]
         summed = sum(piece.astype(jnp.float32) for piece in outs).astype(jnp.bfloat16)
         summed = summed.reshape(local_experts, head_count, parts, capacity, col_share)
         return jnp.moveaxis(summed, 0, 2).reshape(head_count, parts, block_rows, col_share)
 
-    others = through_experts(halves[0], part_count - 1)
-    own_rows = through_experts(halves[1], 1)
+    others = through_experts(hidden[0], part_count - 1)
+    own_rows = through_experts(hidden[1], 1)
 
     def weighted(k, rows):
         placed = routings[k][2]

time: 417 us -> 386 us (0.926)
  starting transfers between devices: 97.5 us -> 83.7 us
  between operations: 14.3 us -> 1.08 us
  local copies, waits for them, and re-layouts: 38.6 us -> 25.8 us
  blocking collectives: 0 us -> 10 us
  other arithmetic: 23.1 us -> 17 us
    all_to_all x1 -> x0, waiting for transfers between devices: 14.4 us -> none  [shards(): lax.all_to_all(by_slot.reshape(seq_count, token_count, HEAD), 'seq', spli...]
    unnamed x90 -> x83, local copies, waits for them, and re-layouts: 31.4 us -> 19.5 us
    all_to_all x0 -> x1, blocking collectives: none -> 10 us  [shards(): lax.all_to_all(blocks, 'seq', split_axis=0, concat_axis=0, tiled=True, ax...]
    all_to_all x1 -> x0, starting transfers between devices: 8.62 us -> none  [shards(): lax.all_to_all(by_slot.reshape(seq_count, token_count, HEAD), 'seq', spli...]
    ppermute x20 -> x22, waiting for transfers between devices: 125 us -> 133 us  [swapped(): lax.ppermute(value, axis, [(place, place ^ mask) for place in range(count)])]
    ppermute x20 -> x22, starting transfers between devices: 45.9 us -> 39.5 us  [swapped(): lax.ppermute(value, axis, [(place, place ^ mask) for place in range(count)])]
    all_to_all x3, waiting for transfers between devices: 13.6 us -> 19.6 us  [to_owner(): lax.all_to_all(blocks, 'seq', split_axis=0, concat_axis=0, tiled=True)]
    ppermute x1 -> x2, waiting for transfers between devices: 0.01 us -> 4.88 us  [from_behind(): lax.ppermute(value, axis, [(source, source + steps) for source in range(f...]
  transfers between devices with their start and end apart: 35 -> 36, of which waited for: 19 -> 18; matrix products, arithmetic and copies ran while one was open for 13% -> 10% of each run, Pallas kernels for 9% -> 10%
where the time goes in v7:
time: 386 us; the launch traced here: 382 us
  waiting for transfers between devices  188 us (49%)
  starting transfers between devices  83.7 us (22%)
  Pallas kernels  49.3 us (13%)
  local copies, waits for them, and re-layouts  25.8 us (7%)
  other arithmetic  17 us (4%)
  blocking collectives  10 us (3%)
  matrix products  7.39 us (2%)
    ppermute x22, waiting for transfers between devices, swapped(): lax.ppermute(value, axis, [(place, place ^ mask) for place in range(count)])  133 us
    ppermute x22, starting transfers between devices, swapped(): lax.ppermute(value, axis, [(place, place ^ mask) for place in range(count)])  39.5 us
    all_to_all x2, waiting for transfers between devices, back(): lax.all_to_all(blocks, 'seq', split_axis=0, concat_axis=0, tiled=True, ax...  21 us
    all_to_all x3, starting transfers between devices, to_owner(): lax.all_to_all(blocks, 'seq', split_axis=0, concat_axis=0, tiled=True)  20.3 us
    all_to_all x3, waiting for transfers between devices, to_owner(): lax.all_to_all(blocks, 'seq', split_axis=0, concat_axis=0, tiled=True)  19.6 us
    unnamed x83, local copies, waits for them, and re-layouts  19.5 us
    pallas_call x1, Pallas kernels, order_experts(): pl.pallas_call(order_body, grid_spec=pltpu.PrefetchScalarGridSpec(num_sca...  12.9 us
    pallas_call x2, Pallas kernels, hidden_units(): pl.pallas_call(lambda *refs: hidden_body(count, share, *refs), grid_spec=...  11.5 us
  transfers between devices with their start and end apart: 36, of which 18 were waited for; matrix products, arithmetic and copies ran while one was open for 10% of the time, Pallas kernels for 10%

profile of v7, /device:TPU:0, one launch (start us, length us, event | category | flops | bytes accessed | tf_op | source)
XLA Modules:
  0.0 381.8 jit_solution(12880266802901886741)
XLA Ops:
  0.0 1.3 convert_element_type.112
  1.3 1.2 multiply_reduce_fusion
  3.3 3.1 collective-permute-start
  7.6 2.7 collective-permute-start.2
  10.6 1.9 pack_heads.1
  12.4 5.9 %all-to-all-start = ((bf16[16,128,384]{2,1,0:T(8,128)(2,1)}), bf16[16,128,384]{2,1,0:T(8,128)(2,1)}, u32[]{:S(2)}, u32[]{:S(2)}) async-start(bf16[16,128,384]{2,1,0:T(8,128)(2,1)} %pack_heads.1), calls=%async_computation | async-start | bytes 3145728 | tf_op jit(solution)/shard_map/all_to_all | solution.py:406
  18.5 13.9 %collective-permute-done.1 = s32[1,128,8]{1,2,0:T(8,128)S(1)} collective-permute-done((s32[1,128,8]{1,2,0:T(8,128)S(1)}, s32[1,128,8]{1,2,0:T(8,128)S(1)}, u32[]{:S(2)}, u32[]{:S(2)}) %collective-permute-start.1) | collective-permute-done | bytes 4128 | tf_op jit(solution)/shard_map/ppermute | solution.py:31
  32.7 1.9 multiply_sine_fusion
  34.6 1.6 collective-permute-start.6
  36.4 12.9 %order_experts.1 = (bf16[16,128,512]{2,1,0:T(8,128)(2,1)}, bf16[16,128,512]{2,1,0:T(8,128)(2,1)}, bf16[16,128,512]{2,1,0:T(8,128)(2,1)}) custom-call(s32[16]{0:T(128)} %order_ref, f32[16,128,512]{2,1,0:T(8,128)} %gate_ref.1, f32[16,128,512]{2,1,0:T(8,128)} %up_ref.1, f32[16,128,512]{2,1,0:T(8,128)} %down_ref.1), custom_call_target="tpu_custom_call" | custom-call | flops 1 | bytes 1 | tf_op jit(solution)/shard_map/order_experts/pallas_call | solution.py:129
  50.1 1.8 collective-permute-start.7
  51.9 6.0 %collective-permute-done.3 = bf16[1040,256]{1,0:T(8,128)(2,1)S(1)} collective-permute-done((bf16[1040,256]{1,0:T(8,128)(2,1)S(1)}, bf16[1040,256]{1,0:T(8,128)(2,1)S(1)}, u32[]{:S(2)}, u32[]{:S(2)}) %collective-permute-start.3) | collective-permute-done | bytes 532512 | tf_op jit(solution)/shard_map/ppermute | solution.py:31
  62.8 1.4 fusion.13.query_prompt_ref
  65.2 1.4 collective-permute-start.10
  66.7 12.1 %collective-permute-done.9 = bf16[512,512]{1,0:T(8,128)(2,1)S(1)} collective-permute-done((bf16[512,512]{1,0:T(8,128)(2,1)}, bf16[512,512]{1,0:T(8,128)(2,1)S(1)}, u32[]{:S(2)}, u32[]{:S(2)}) %collective-permute-start.9) | collective-permute-done | bytes 524320 | tf_op jit(solution)/shard_map/ppermute | solution.py:31
  78.8 2.2 pad_maximum_fusion.2
  80.9 5.8 %project.1 = bf16[1024,384]{1,0:T(8,128)(2,1)S(1)} custom-call(s32[2]{0:T(128)S(1)} %fusion.119.refs_0_, bf16[1024,1024]{1,0:T(8,128)(2,1)S(1)} %pad_maximum_fusion.refs_1_, bf16[1024,1024]{1,0:T(8,128)(2,1)} %collective-permute-done.8.refs_2_, bf16[2048,384]{1,0:T(8,128)(2,1)} %bitcast.8.refs_3_, f32[1024,64]{1,0:T(8,128)S(1)} %get-tuple-element.64.refs_4_, ...), custom_call_target="tpu_custom_call" | custom-call | flops 1 | bytes 1 | tf_op jit(solution)/shard_map/project/pallas_call | solution.py:191
  86.8 5.7 %collective-permute-start.11 = (bf16[64,384]{1,0:T(8,128)(2,1)S(1)}, bf16[64,384]{1,0:T(8,128)(2,1)S(1)}, u32[]{:S(2)}, u32[]{:S(2)}) collective-permute-start(bf16[64,384]{1,0:T(8,128)(2,1)S(1)} %constant_dynamic-slice_fusion.8), channel_id=1, source_target_pairs={{0,16},{2,18},{4,20},{6,22},{8,24},{10,26},{12,28},{14,30},{1,17},... | collective-permute-start | bytes 147464 | tf_op jit(solution)/shard_map/ppermute | solution.py:21
  92.6 1.5 collective-permute-done.11
  94.3 6.8 %attend_once.1 = bf16[1088,128]{1,0:T(8,128)(2,1)S(1)} custom-call(f32[1]{0:T(128)} %dynamic_slice.92.sink_ref, s32[1088,1]{1,0:T(8,128)S(1)} %fusion.13.query_prompt_ref, s32[1,1088]{1,0:T(1,128)S(1)} %and_select_fusion.key_prompt_ref, bf16[1088,384]{1,0:T(8,128)(2,1)S(1)} %pad_maximum_fusion.3.query_ref.key_ref.value_ref, ...), custom_call_target="tpu_custom_call" | custom-call | flops 1 | bytes 1 | tf_op jit(solution)/shard_map/attend_once/pallas_call | solution.py:233
  101.1 1.3 collective-permute-start.12
  102.8 1.5 collective-permute-start.13
  104.3 3.3 collective-permute-done.12
  108.8 17.8 %collective-permute-done.13 = bf16[512,1024]{1,0:T(8,128)(2,1)} collective-permute-done((bf16[512,1024]{1,0:T(8,128)(2,1)S(1)}, bf16[512,1024]{1,0:T(8,128)(2,1)}, u32[]{:S(2)}, u32[]{:S(2)}) %collective-permute-start.13) | collective-permute-done | bytes 1048608 | tf_op jit(solution)/shard_map/ppermute | solution.py:31
  127.1 10.0 %all_to_all.35 = bf16[8,128,128]{1,2,0:T(8,128)(2,1)S(1)} all-to-all(bf16[8,128,128]{1,2,0:T(8,128)(2,1)S(1)} %constant_dynamic-update-slice_fusion.2), channel_id=1, replica_groups={{0,2,4,6,8,10,12,14},{16,18,20,22,24,26,28,30},{1,3,5,7,9,11,13,15},{17..., dimensions={0} | all-to-all | bytes 524288 | tf_op jit(solution)/shard_map/all_to_all | solution.py:560
  137.1 5.0 %all-to-all-start.2 = ((bf16[16,128,512]{2,1,0:T(8,128)(2,1)}), bf16[16,128,512]{2,1,0:T(8,128)(2,1)}, u32[]{:S(2)}, u32[]{:S(2)}) async-start(bf16[16,128,512]{2,1,0:T(8,128)(2,1)} %get-tuple-element.82), calls=%async_computation.2 | async-start | bytes 4194304 | tf_op jit(solution)/shard_map/all_to_all | solution.py:450
  143.4 1.6 fusion.63
  146.2 1.7 collective-permute-done.15.refs_2_
  147.9 1.2 settle.1
  150.1 2.8 collective-permute-start.16
  153.6 46.9 %collective-permute-done.17 = f32[1,128,16]{2,1,0:T(8,128)S(1)} collective-permute-done((f32[1,128,16]{2,1,0:T(8,128)S(1)}, f32[1,128,16]{2,1,0:T(8,128)S(1)}, u32[]{:S(2)}, u32[]{:S(2)}) %collective-permute-start.17) | collective-permute-done | bytes 8224 | tf_op jit(solution)/shard_map/ppermute | solution.py:31
  200.7 4.7 %all-to-all-start.3 = ((bf16[16,128,512]{2,1,0:T(8,128)(2,1)}), bf16[16,128,512]{2,1,0:T(8,128)(2,1)S(1)}, u32[]{:S(2)}, u32[]{:S(2)}) async-start(bf16[16,128,512]{2,1,0:T(8,128)(2,1)} %get-tuple-element.86), calls=%async_computation.3 | async-start | bytes 4194304 | tf_op jit(solution)/shard_map/all_to_all | solution.py:450
  208.1 1.9 collective-permute-start.18
  210.0 1.5 collective-permute-start.19
  212.3 1.5 collective-permute-start.22
  213.8 1.5 collective-permute-start.20
  215.8 5.9 %collective-permute-done.18 = bf16[2,72,1024]{2,1,0:T(8,128)(2,1)S(1)} collective-permute-done((bf16[2,72,1024]{2,1,0:T(8,128)(2,1)S(1)}, bf16[2,72,1024]{2,1,0:T(8,128)(2,1)S(1)}, u32[]{:S(2)}, u32[]{:S(2)}) %collective-permute-start.18) | collective-permute-done | bytes 294944 | tf_op jit(solution)/shard_map/ppermute | solution.py:31
  222.4 5.2 %collective-permute-start.23 = (bf16[2,72,1024]{2,1,0:T(8,128)(2,1)}, bf16[2,72,1024]{2,1,0:T(8,128)(2,1)}, u32[]{:S(2)}, u32[]{:S(2)}) collective-permute-start(bf16[2,72,1024]{2,1,0:T(8,128)(2,1)} %get-tuple-element.113), channel_id=1, source_target_pairs={{0,12},{2,14},{4,8},{6,10},{8,4},{10,6},{12,0},{14,2},{16,28},{18,... | collective-permute-start | bytes 884744 | tf_op jit(solution)/shard_map/ppermute | solution.py:31
  227.6 19.6 %all-to-all-done.3 = bf16[16,128,512]{2,1,0:T(8,128)(2,1)S(1)} async-done(((bf16[16,128,512]{2,1,0:T(8,128)(2,1)}), bf16[16,128,512]{2,1,0:T(8,128)(2,1)S(1)}, u32[]{:S(2)}, u32[]{:S(2)}) %all-to-all-start.3) | async-done | bytes 2097184 | tf_op jit(solution)/shard_map/all_to_all | solution.py:450
  247.2 10.5 %all-to-all-start.4 = ((bf16[16,128,512]{2,1,0:T(8,128)(2,1)}), bf16[16,128,512]{2,1,0:T(8,128)(2,1)}, u32[]{:S(2)}, u32[]{:S(2)}) async-start(bf16[16,128,512]{2,1,0:T(8,128)(2,1)} %get-tuple-element.91), calls=%async_computation.4 | async-start | bytes 4194304 | tf_op jit(solution)/shard_map/all_to_all | solution.py:450
  257.8 1.7 bitcast_dynamic-update-slice_fusion.6
  259.5 3.7 collective-permute-start.24
  263.2 1.7 bitcast_dynamic-update-slice_fusion.5
  264.9 1.7 bitcast_dynamic-update-slice_fusion.4
  266.6 1.7 bitcast_dynamic-update-slice_fusion.3
  268.3 1.7 bitcast_dynamic-update-slice_fusion.2
  270.0 1.7 bitcast_dynamic-update-slice_fusion.1
  271.7 29.1 %collective-permute-done.24 = bf16[2,72,1024]{2,1,0:T(8,128)(2,1)S(1)} collective-permute-done((bf16[2,72,1024]{2,1,0:T(8,128)(2,1)S(1)}, bf16[2,72,1024]{2,1,0:T(8,128)(2,1)S(1)}, u32[]{:S(2)}, u32[]{:S(2)}) %collective-permute-start.24) | collective-permute-done | bytes 294944 | tf_op jit(solution)/shard_map/ppermute | solution.py:31
  301.5 1.1 dynamic-slice_dynamic-update-slice_fusion.7
  306.6 2.3 collective-permute-done.26.refs_2_
  308.9 1.1 copy-done.13
  310.0 5.7 %hidden_units.3.refs_1_ = bf16[1,576,512]{2,1,0:T(8,128)(2,1)S(1)} custom-call(s32[2]{0:T(128)S(1)} %fusion.119.refs_0_, bf16[1,576,1024]{2,1,0:T(8,128)(2,1)S(1)} %bitcast.155, bf16[1,576,1024]{2,1,0:T(8,128)(2,1)} %copy-done.13, bf16[1,2048,512]{2,1,0:T(8,128)(2,1)} %bitcast.34.refs_3_, bf16[1,2048,512]{2,1,0:T(8,128)(2,1)} %bitcast.157), custom_call_target="tpu_custom_call" | custom-call | flops 1 | bytes 1 | tf_op jit(solution)/shard_map/hidden_units/pallas_call | solution.py:309
  316.8 5.7 %hidden_units.2.refs_1_ = bf16[1,576,512]{2,1,0:T(8,128)(2,1)S(1)} custom-call(s32[2]{0:T(128)S(1)} %fusion.119.refs_0_, bf16[1,576,1024]{2,1,0:T(8,128)(2,1)S(1)} %bitcast.153, bf16[1,576,1024]{2,1,0:T(8,128)(2,1)} %copy-done.12, bf16[1,2048,512]{2,1,0:T(8,128)(2,1)} %bitcast.34.refs_3_, bf16[1,2048,512]{2,1,0:T(8,128)(2,1)} %bitcast.158), custom_call_target="tpu_custom_call" | custom-call | flops 1 | bytes 1 | tf_op jit(solution)/shard_map/hidden_units/pallas_call | solution.py:309
  322.6 4.6 %down_rows.2 = (bf16[1,576,1024]{2,1,0:T(8,128)(2,1)S(1)}, bf16[1,576,1024]{2,1,0:T(8,128)(2,1)}) custom-call(s32[2]{0:T(128)S(1)} %fusion.120.refs_0_, bf16[1,576,512]{2,1,0:T(8,128)(2,1)S(1)} %hidden_units.2.refs_1_, bf16[1,2048,512]{2,1,0:T(8,128)(2,1)} %bitcast.58.refs_2_), custom_call_target="tpu_custom_call" | custom-call | flops 1 | bytes 1 | tf_op jit(solution)/shard_map/down_rows/pallas_call | solution.py:341
  327.4 2.9 collective-permute-done.27
  330.3 1.6 add_convert_fusion.1
  331.8 6.6 %all-to-all-start.5 = ((bf16[8,1,72,1024]{3,2,1,0:T(8,128)(2,1)}), bf16[8,1,72,1024]{3,2,1,0:T(8,128)(2,1)S(1)}, u32[]{:S(2)}, u32[]{:S(2)}) async-start(bf16[8,1,72,1024]{3,2,1,0:T(8,128)(2,1)} %bitcast.60), calls=%async_computation.5 | async-start | bytes 2359296 | tf_op jit(solution)/shard_map/all_to_all | solution.py:685
  338.4 4.6 %down_rows.3 = (bf16[1,576,1024]{2,1,0:T(8,128)(2,1)S(1)}, bf16[1,576,1024]{2,1,0:T(8,128)(2,1)}) custom-call(s32[2]{0:T(128)S(1)} %fusion.120.refs_0_, bf16[1,576,512]{2,1,0:T(8,128)(2,1)S(1)} %hidden_units.3.refs_1_, bf16[1,2048,512]{2,1,0:T(8,128)(2,1)} %bitcast.58.refs_2_), custom_call_target="tpu_custom_call" | custom-call | flops 1 | bytes 1 | tf_op jit(solution)/shard_map/down_rows/pallas_call | solution.py:341
  343.8 2.2 collective-permute-done.28
  346.1 1.5 add_convert_fusion
  347.6 7.1 %all-to-all-done.5 = bf16[8,1,72,1024]{3,2,1,0:T(8,128)(2,1)S(1)} async-done(((bf16[8,1,72,1024]{3,2,1,0:T(8,128)(2,1)}), bf16[8,1,72,1024]{3,2,1,0:T(8,128)(2,1)S(1)}, u32[]{:S(2)}, u32[]{:S(2)}) %all-to-all-start.5) | async-done | bytes 1179680 | tf_op jit(solution)/shard_map/all_to_all | solution.py:685
  355.6 3.6 all-to-all-start.6
  360.0 6.2 %collective-permute-start.29 = (bf16[128,1024]{1,0:T(8,128)(2,1)S(1)}, bf16[128,1024]{1,0:T(8,128)(2,1)S(1)}, u32[]{:S(2)}, u32[]{:S(2)}) collective-permute-start(bf16[128,1024]{1,0:T(8,128)(2,1)S(1)} %slice_add_fusion.2), channel_id=1, source_target_pairs={{0,16},{2,18},{4,20},{6,22},{8,24},{10,26},{12,28},{14,30},{16,0},... | collective-permute-start | bytes 786440 | tf_op jit(solution)/shard_map/ppermute | solution.py:31
  366.2 13.9 %all-to-all-done.6 = bf16[8,1,72,1024]{3,2,1,0:T(8,128)(2,1)S(1)} async-done(((bf16[8,1,72,1024]{3,2,1,0:T(8,128)(2,1)}), bf16[8,1,72,1024]{3,2,1,0:T(8,128)(2,1)S(1)}, u32[]{:S(2)}, u32[]{:S(2)}) %all-to-all-start.6) | async-done | bytes 1179680 | tf_op jit(solution)/shard_map/all_to_all | solution.py:685
  (194 shorter events, 30.6 us)
Async XLA Ops:
  0.0 7.5 %copy-start.16 = (f32[128,16]{0,1:T(8,128)S(1)}, f32[128,16]{0,1:T(8,128)}, u32[]{:S(2)}) copy-start(f32[128,16]{0,1:T(8,128)} %param.23) | copy-start | bytes 24580
  0.0 10.2 %copy-start.17 = (s32[128,8]{0,1:T(8,128)S(1)}, s32[128,8]{0,1:T(8,128)}, u32[]{:S(2)}) copy-start(s32[128,8]{0,1:T(8,128)} %param.29) | copy-start | bytes 12292
  0.0 10.6 %copy-start.1 = (f32[128,1024]{1,0:T(8,128)S(1)}, f32[128,1024]{1,0:T(8,128)}, u32[]{:S(2)}) copy-start(f32[128,1024]{1,0:T(8,128)} %query_ref.1) | copy-start | bytes 1572868
  0.0 10.6 %copy-start.2 = (f32[128,1024]{1,0:T(8,128)S(1)}, f32[128,1024]{1,0:T(8,128)}, u32[]{:S(2)}) copy-start(f32[128,1024]{1,0:T(8,128)} %key_ref.1) | copy-start | bytes 1572868
  0.0 10.6 %copy-start.3 = (f32[128,1024]{1,0:T(8,128)S(1)}, f32[128,1024]{1,0:T(8,128)}, u32[]{:S(2)}) copy-start(f32[128,1024]{1,0:T(8,128)} %value_ref.1) | copy-start | bytes 1572868
  3.3 29.1 %collective-permute-start = (bf16[1,128,1024]{2,1,0:T(8,128)(2,1)S(1)}, bf16[1,128,1024]{2,1,0:T(8,128)(2,1)S(1)}, u32[]{:S(2)}, u32[]{:S(2)}) collective-permute-start(bf16[1,128,1024]{2,1,0:T(8,128)(2,1)S(1)} %fusion.48), channel_id=1, source_target_pairs={{0,8},{2,10},{4,12},{6,14},{8,0},{10,2},{12,4},{14,6},{16,24},{18,... | collective-permute-start | bytes 786440 | tf_op jit(solution)/shard_map/ppermute | solution.py:31
  7.6 24.9 %collective-permute-start.2 = (bf16[1040,128]{1,0:T(8,128)(2,1)S(1)}, bf16[1040,128]{1,0:T(8,128)(2,1)S(1)}, u32[]{:S(2)}, u32[]{:S(2)}) collective-permute-start(bf16[1040,128]{1,0:T(8,128)(2,1)S(1)} %pad_maximum_fusion.9), channel_id=1, source_target_pairs={{0,16},{2,18},{4,20},{6,22},{8,24},{10,26},{12,28},{14,30},{16,0},... | collective-permute-start | bytes 798728 | tf_op jit(solution)/shard_map/ppermute | solution.py:31
  10.2 22.2 %collective-permute-start.1 = (s32[1,128,8]{1,2,0:T(8,128)S(1)}, s32[1,128,8]{1,2,0:T(8,128)S(1)}, u32[]{:S(2)}, u32[]{:S(2)}) collective-permute-start(s32[1,128,8]{1,2,0:T(8,128)S(1)} %bitcast.173), channel_id=1, source_target_pairs={{0,16},{2,18},{4,20},{6,22},{8,24},{10,26},{12,28},{14,30},{16,0},... | collective-permute-start | bytes 12296 | tf_op jit(solution)/shard_map/ppermute | solution.py:31
  12.4 48.5 %all-to-all-start = ((bf16[16,128,384]{2,1,0:T(8,128)(2,1)}), bf16[16,128,384]{2,1,0:T(8,128)(2,1)}, u32[]{:S(2)}, u32[]{:S(2)}) async-start(bf16[16,128,384]{2,1,0:T(8,128)(2,1)} %pack_heads.1), calls=%async_computation | async-start | bytes 3145728 | tf_op jit(solution)/shard_map/all_to_all | solution.py:406
  32.6 16.7 %collective-permute-start.4 = (bf16[2,128,512]{2,1,0:T(8,128)(2,1)S(1)}, bf16[2,128,512]{2,1,0:T(8,128)(2,1)S(1)}, u32[]{:S(2)}, u32[]{:S(2)}) collective-permute-start(bf16[2,128,512]{2,1,0:T(8,128)(2,1)S(1)} %get-tuple-element.123), channel_id=1, source_target_pairs={{0,4},{2,6},{4,0},{6,2},{8,12},{10,14},{12,8},{14,10},{16,20},{18,... | collective-permute-start | bytes 786440 | tf_op jit(solution)/shard_map/ppermute | solution.py:31
  34.6 15.4 %collective-permute-start.6 = (bf16[2,128,512]{2,1,0:T(8,128)(2,1)S(1)}, bf16[2,128,512]{2,1,0:T(8,128)(2,1)S(1)}, u32[]{:S(2)}, u32[]{:S(2)}) collective-permute-start(bf16[2,128,512]{2,1,0:T(8,128)(2,1)S(1)} %get-tuple-element.124), channel_id=1, source_target_pairs={{0,2},{2,0},{4,6},{6,4},{8,10},{10,8},{12,14},{14,12},{16,18},{18,... | collective-permute-start | bytes 786440 | tf_op jit(solution)/shard_map/ppermute | solution.py:31
  36.1 21.8 %collective-permute-start.3 = (bf16[1040,256]{1,0:T(8,128)(2,1)S(1)}, bf16[1040,256]{1,0:T(8,128)(2,1)S(1)}, u32[]{:S(2)}, u32[]{:S(2)}) collective-permute-start(bf16[1040,256]{1,0:T(8,128)(2,1)S(1)} %pad_maximum_fusion.4), channel_id=1, source_target_pairs={{0,8},{2,10},{4,12},{6,14},{8,0},{10,2},{12,4},{14,6},{16,24},{18,... | collective-permute-start | bytes 1597448 | tf_op jit(solution)/shard_map/ppermute | solution.py:31
  49.4 11.0 %collective-permute-start.5 = (bf16[4,128,512]{2,1,0:T(8,128)(2,1)S(1)}, bf16[4,128,512]{2,1,0:T(8,128)(2,1)S(1)}, u32[]{:S(2)}, u32[]{:S(2)}) collective-permute-start(bf16[4,128,512]{2,1,0:T(8,128)(2,1)S(1)} %pad_maximum_fusion.6), channel_id=1, source_target_pairs={{0,2},{2,0},{4,6},{6,4},{8,10},{10,8},{12,14},{14,12},{16,18},{18,... | collective-permute-start | bytes 1572872 | tf_op jit(solution)/shard_map/ppermute | solution.py:31
  50.1 10.4 %collective-permute-start.7 = (bf16[4,128,512]{2,1,0:T(8,128)(2,1)S(1)}, bf16[4,128,512]{2,1,0:T(8,128)(2,1)S(1)}, u32[]{:S(2)}, u32[]{:S(2)}) collective-permute-start(bf16[4,128,512]{2,1,0:T(8,128)(2,1)S(1)} %pad_maximum_fusion.7), channel_id=1, source_target_pairs={{0,4},{2,6},{4,0},{6,2},{8,12},{10,14},{12,8},{14,10},{16,20},{18,... | collective-permute-start | bytes 1572872 | tf_op jit(solution)/shard_map/ppermute | solution.py:31
  60.6 1.5 copy-start.19
  60.6 4.5 %copy-start.18 = (s32[2]{0:T(128)S(1)}, s32[2]{0:T(128)}, u32[]{:S(2)}) copy-start(s32[2]{0:T(128)} %param.28) | copy-start | bytes 28
  60.9 20.0 %collective-permute-start.8 = (bf16[1024,1024]{1,0:T(8,128)(2,1)S(1)}, bf16[1024,1024]{1,0:T(8,128)(2,1)}, u32[]{:S(2)}, u32[]{:S(2)}) collective-permute-start(bf16[1024,1024]{1,0:T(8,128)(2,1)S(1)} %pad_maximum_fusion.refs_1_), channel_id=1, source_target_pairs={{1,0},{0,1},{3,2},{2,3},{5,4},{4,5},{7,6},{6,7},{9,8},{8,9},{11,10... | collective-permute-start | bytes 6291464 | tf_op jit(solution)/shard_map/ppermute | solution.py:26
  64.2 14.6 %collective-permute-start.9 = (bf16[512,512]{1,0:T(8,128)(2,1)}, bf16[512,512]{1,0:T(8,128)(2,1)S(1)}, u32[]{:S(2)}, u32[]{:S(2)}) collective-permute-start(bf16[512,512]{1,0:T(8,128)(2,1)} %slice.198), channel_id=1, source_target_pairs={{0,4},{2,6},{4,0},{6,2},{8,12},{10,14},{12,8},{14,10},{16,20},{18,... | collective-permute-start | bytes 1572872 | tf_op jit(solution)/shard_map/ppermute | solution.py:31
  65.2 27.3 %collective-permute-start.10 = (bf16[528,512]{1,0:T(8,128)(2,1)}, bf16[528,512]{1,0:T(8,128)(2,1)S(1)}, u32[]{:S(2)}, u32[]{:S(2)}) collective-permute-start(bf16[528,512]{1,0:T(8,128)(2,1)} %slice.199), channel_id=1, source_target_pairs={{0,2},{2,0},{4,6},{6,4},{8,10},{10,8},{12,14},{14,12},{16,18},{18,... | collective-permute-start | bytes 1622024 | tf_op jit(solution)/shard_map/ppermute | solution.py:31
  80.9 11.6 %copy-start.11 = (bf16[528,512]{1,0:T(8,128)(2,1)S(1)}, bf16[528,512]{1,0:T(8,128)(2,1)}, u32[]{:S(2)}) copy-start(bf16[528,512]{1,0:T(8,128)(2,1)} %slice.199) | copy-start | bytes 1622020
  86.8 7.4 %collective-permute-start.11 = (bf16[64,384]{1,0:T(8,128)(2,1)S(1)}, bf16[64,384]{1,0:T(8,128)(2,1)S(1)}, u32[]{:S(2)}, u32[]{:S(2)}) collective-permute-start(bf16[64,384]{1,0:T(8,128)(2,1)S(1)} %constant_dynamic-slice_fusion.8), channel_id=1, source_target_pairs={{0,16},{2,18},{4,20},{6,22},{8,24},{10,26},{12,28},{14,30},{1,17},... | collective-permute-start | bytes 147464 | tf_op jit(solution)/shard_map/ppermute | solution.py:21
  92.6 50.0 %copy-start.8 = (bf16[528,1024]{1,0:T(8,128)(2,1)}, bf16[528,1024]{1,0:T(8,128)(2,1)S(1)}, u32[]{:S(2)}) copy-start(bf16[528,1024]{1,0:T(8,128)(2,1)S(1)} %pad_maximum_fusion.1) | copy-start | bytes 3244036
  94.3 8.5 %copy-start.9 = (bf16[512,1024]{1,0:T(8,128)(2,1)S(1)}, bf16[512,1024]{1,0:T(8,128)(2,1)}, u32[]{:S(2)}) copy-start(bf16[512,1024]{1,0:T(8,128)(2,1)} %pad_maximum_fusion.2) | copy-start | bytes 3145732
  101.1 6.5 %collective-permute-start.12 = (bf16[64,128]{1,0:T(8,128)(2,1)S(1)}, bf16[64,128]{1,0:T(8,128)(2,1)S(1)}, u32[]{:S(2)}, u32[]{:S(2)}) collective-permute-start(bf16[64,128]{1,0:T(8,128)(2,1)S(1)} %slice.209), channel_id=1, source_target_pairs={{16,0},{18,2},{20,4},{22,6},{24,8},{26,10},{28,12},{30,14},{17,1},... | collective-permute-start | bytes 49160 | tf_op jit(solution)/shard_map/ppermute | solution.py:21
  102.5 24.7 %collective-permute-start.14 = (bf16[528,1024]{1,0:T(8,128)(2,1)S(1)}, bf16[528,1024]{1,0:T(8,128)(2,1)S(1)}, u32[]{:S(2)}, u32[]{:S(2)}) collective-permute-start(bf16[528,1024]{1,0:T(8,128)(2,1)S(1)} %pad_maximum_fusion.1), channel_id=1, source_target_pairs={{0,4},{2,6},{4,0},{6,2},{8,12},{10,14},{12,8},{14,10},{16,20},{18,... | collective-permute-start | bytes 3244040 | tf_op jit(solution)/shard_map/ppermute | solution.py:31
  102.8 23.8 %collective-permute-start.13 = (bf16[512,1024]{1,0:T(8,128)(2,1)S(1)}, bf16[512,1024]{1,0:T(8,128)(2,1)}, u32[]{:S(2)}, u32[]{:S(2)}) collective-permute-start(bf16[512,1024]{1,0:T(8,128)(2,1)S(1)} %copy-done.9), channel_id=1, source_target_pairs={{0,2},{2,0},{4,6},{6,4},{8,10},{10,8},{12,14},{14,12},{16,18},{18,... | collective-permute-start | bytes 3145736 | tf_op jit(solution)/shard_map/ppermute | solution.py:31
  127.1 15.2 %copy-start.14 = (bf16[528,1024]{1,0:T(8,128)(2,1)}, bf16[528,1024]{1,0:T(8,128)(2,1)S(1)}, u32[]{:S(2)}) copy-start(bf16[528,1024]{1,0:T(8,128)(2,1)S(1)} %collective-permute-done.14) | copy-start | bytes 3244036
  137.1 63.6 %all-to-all-start.2 = ((bf16[16,128,512]{2,1,0:T(8,128)(2,1)}), bf16[16,128,512]{2,1,0:T(8,128)(2,1)}, u32[]{:S(2)}, u32[]{:S(2)}) async-start(bf16[16,128,512]{2,1,0:T(8,128)(2,1)} %get-tuple-element.82), calls=%async_computation.2 | async-start | bytes 4194304 | tf_op jit(solution)/shard_map/all_to_all | solution.py:450
  143.4 4.5 %copy-start = (bf16[128,2048]{1,0:T(8,128)(2,1)S(1)}, bf16[128,2048]{1,0:T(8,128)(2,1)}, u32[]{:S(2)}) copy-start(bf16[128,2048]{1,0:T(8,128)(2,1)} %refs_3_.1) | copy-start | bytes 1572868
  143.4 4.5 %copy-start.6 = (f32[2048]{0:T(1024)S(1)}, f32[2048]{0:T(1024)}, u32[]{:S(2)}) copy-start(f32[2048]{0:T(1024)} %param.17) | copy-start | bytes 24580
  145.1 2.7 collective-permute-start.15
  149.1 1.0 copy-start.4
  150.1 50.5 %collective-permute-start.16 = (bf16[1,128,1024]{2,1,0:T(8,128)(2,1)S(1)}, bf16[1,128,1024]{2,1,0:T(8,128)(2,1)S(1)}, u32[]{:S(2)}, u32[]{:S(2)}) collective-permute-start(bf16[1,128,1024]{2,1,0:T(8,128)(2,1)S(1)} %dynamic-slice_bitcast_fusion), channel_id=1, source_target_pairs={{0,16},{2,18},{4,20},{6,22},{8,24},{10,26},{12,28},{14,30},{16,0},... | collective-permute-start | bytes 786440 | tf_op jit(solution)/shard_map/ppermute | solution.py:31
  153.4 47.2 %collective-permute-start.17 = (f32[1,128,16]{2,1,0:T(8,128)S(1)}, f32[1,128,16]{2,1,0:T(8,128)S(1)}, u32[]{:S(2)}, u32[]{:S(2)}) collective-permute-start(f32[1,128,16]{2,1,0:T(8,128)S(1)} %multiply_bitcast_fusion), channel_id=1, source_target_pairs={{0,16},{2,18},{4,20},{6,22},{8,24},{10,26},{12,28},{14,30},{16,0},... | collective-permute-start | bytes 24584 | tf_op jit(solution)/shard_map/ppermute | solution.py:31
  200.7 46.5 %all-to-all-start.3 = ((bf16[16,128,512]{2,1,0:T(8,128)(2,1)}), bf16[16,128,512]{2,1,0:T(8,128)(2,1)S(1)}, u32[]{:S(2)}, u32[]{:S(2)}) async-start(bf16[16,128,512]{2,1,0:T(8,128)(2,1)} %get-tuple-element.86), calls=%async_computation.3 | async-start | bytes 4194304 | tf_op jit(solution)/shard_map/all_to_all | solution.py:450
  208.1 13.6 %collective-permute-start.18 = (bf16[2,72,1024]{2,1,0:T(8,128)(2,1)S(1)}, bf16[2,72,1024]{2,1,0:T(8,128)(2,1)S(1)}, u32[]{:S(2)}, u32[]{:S(2)}) collective-permute-start(bf16[2,72,1024]{2,1,0:T(8,128)(2,1)S(1)} %get-tuple-element.109), channel_id=1, source_target_pairs={{0,2},{2,0},{4,6},{6,4},{8,10},{10,8},{12,14},{14,12},{16,18},{18,... | collective-permute-start | bytes 884744 | tf_op jit(solution)/shard_map/ppermute | solution.py:31
  210.0 49.5 %collective-permute-start.19 = (bf16[2,72,1024]{2,1,0:T(8,128)(2,1)}, bf16[2,72,1024]{2,1,0:T(8,128)(2,1)}, u32[]{:S(2)}, u32[]{:S(2)}) collective-permute-start(bf16[2,72,1024]{2,1,0:T(8,128)(2,1)} %get-tuple-element.110), channel_id=1, source_target_pairs={{0,4},{2,6},{4,0},{6,2},{8,12},{10,14},{12,8},{14,10},{16,20},{18,... | collective-permute-start | bytes 884744 | tf_op jit(solution)/shard_map/ppermute | solution.py:31
  212.3 55.9 %collective-permute-start.22 = (bf16[2,72,1024]{2,1,0:T(8,128)(2,1)}, bf16[2,72,1024]{2,1,0:T(8,128)(2,1)}, u32[]{:S(2)}, u32[]{:S(2)}) collective-permute-start(bf16[2,72,1024]{2,1,0:T(8,128)(2,1)} %get-tuple-element.114), channel_id=1, source_target_pairs={{0,10},{2,8},{4,14},{6,12},{8,2},{10,0},{12,6},{14,4},{16,26},{18,... | collective-permute-start | bytes 884744 | tf_op jit(solution)/shard_map/ppermute | solution.py:31
  213.8 51.1 %collective-permute-start.20 = (bf16[2,72,1024]{2,1,0:T(8,128)(2,1)S(1)}, bf16[2,72,1024]{2,1,0:T(8,128)(2,1)}, u32[]{:S(2)}, u32[]{:S(2)}) collective-permute-start(bf16[2,72,1024]{2,1,0:T(8,128)(2,1)S(1)} %get-tuple-element.111), channel_id=1, source_target_pairs={{0,6},{2,4},{4,2},{6,0},{8,14},{10,12},{12,10},{14,8},{16,22},{18,... | collective-permute-start | bytes 884744 | tf_op jit(solution)/shard_map/ppermute | solution.py:31
  215.3 51.3 %collective-permute-start.21 = (bf16[2,72,1024]{2,1,0:T(8,128)(2,1)S(1)}, bf16[2,72,1024]{2,1,0:T(8,128)(2,1)}, u32[]{:S(2)}, u32[]{:S(2)}) collective-permute-start(bf16[2,72,1024]{2,1,0:T(8,128)(2,1)S(1)} %get-tuple-element.112), channel_id=1, source_target_pairs={{0,8},{2,10},{4,12},{6,14},{8,0},{10,2},{12,4},{14,6},{16,24},{18,... | collective-permute-start | bytes 884744 | tf_op jit(solution)/shard_map/ppermute | solution.py:31
  221.7 0.7 copy-start.15
  222.4 47.5 %collective-permute-start.23 = (bf16[2,72,1024]{2,1,0:T(8,128)(2,1)}, bf16[2,72,1024]{2,1,0:T(8,128)(2,1)}, u32[]{:S(2)}, u32[]{:S(2)}) collective-permute-start(bf16[2,72,1024]{2,1,0:T(8,128)(2,1)} %get-tuple-element.113), channel_id=1, source_target_pairs={{0,12},{2,14},{4,8},{6,10},{8,4},{10,6},{12,0},{14,2},{16,28},{18,... | collective-permute-start | bytes 884744 | tf_op jit(solution)/shard_map/ppermute | solution.py:31
  247.2 12.3 %copy-start.7 = (bf16[16,128,512]{2,1,0:T(8,128)(2,1)}, bf16[16,128,512]{2,1,0:T(8,128)(2,1)S(1)}, u32[]{:S(2)}) copy-start(bf16[16,128,512]{2,1,0:T(8,128)(2,1)S(1)} %all-to-all-done.3) | copy-start | bytes 6291460
  247.2 75.3 %all-to-all-start.4 = ((bf16[16,128,512]{2,1,0:T(8,128)(2,1)}), bf16[16,128,512]{2,1,0:T(8,128)(2,1)}, u32[]{:S(2)}, u32[]{:S(2)}) async-start(bf16[16,128,512]{2,1,0:T(8,128)(2,1)} %get-tuple-element.91), calls=%async_computation.4 | async-start | bytes 4194304 | tf_op jit(solution)/shard_map/all_to_all | solution.py:450
  259.5 41.3 %collective-permute-start.24 = (bf16[2,72,1024]{2,1,0:T(8,128)(2,1)S(1)}, bf16[2,72,1024]{2,1,0:T(8,128)(2,1)S(1)}, u32[]{:S(2)}, u32[]{:S(2)}) collective-permute-start(bf16[2,72,1024]{2,1,0:T(8,128)(2,1)S(1)} %get-tuple-element.107), channel_id=1, source_target_pairs={{0,14},{2,12},{4,10},{6,8},{8,6},{10,4},{12,2},{14,0},{16,30},{18,... | collective-permute-start | bytes 884744 | tf_op jit(solution)/shard_map/ppermute | solution.py:31
  301.5 4.1 %copy-start.10 = (bf16[8,2,72,1024]{3,2,0,1:T(8,128)(2,1)S(1)}, bf16[8,2,72,1024]{3,2,0,1:T(8,128)(2,1)}, u32[]{:S(2)}) copy-start(bf16[8,2,72,1024]{3,2,0,1:T(8,128)(2,1)} %bitcast_dynamic-update-slice_fusion) | copy-start | bytes 7077892
  306.0 2.9 collective-permute-start.26
  306.1 9.7 %collective-permute-start.25 = (bf16[1,576,1024]{2,1,0:T(8,128)(2,1)S(1)}, bf16[1,576,1024]{2,1,0:T(8,128)(2,1)S(1)}, u32[]{:S(2)}, u32[]{:S(2)}) collective-permute-start(bf16[1,576,1024]{2,1,0:T(8,128)(2,1)S(1)} %bitcast.152), channel_id=1, source_target_pairs={{1,0},{0,1},{3,2},{2,3},{5,4},{4,5},{7,6},{6,7},{9,8},{8,9},{11,10... | collective-permute-start | bytes 3538952 | tf_op jit(solution)/shard_map/ppermute | solution.py:26
  308.9 1.1 copy-start.13
  315.7 1.1 copy-start.12
  327.2 3.1 collective-permute-start.27
  331.8 22.9 %all-to-all-start.5 = ((bf16[8,1,72,1024]{3,2,1,0:T(8,128)(2,1)}), bf16[8,1,72,1024]{3,2,1,0:T(8,128)(2,1)S(1)}, u32[]{:S(2)}, u32[]{:S(2)}) async-start(bf16[8,1,72,1024]{3,2,1,0:T(8,128)(2,1)} %bitcast.60), calls=%async_computation.5 | async-start | bytes 2359296 | tf_op jit(solution)/shard_map/all_to_all | solution.py:685
  343.0 3.1 collective-permute-start.28
  355.6 24.4 %all-to-all-start.6 = ((bf16[8,1,72,1024]{3,2,1,0:T(8,128)(2,1)}), bf16[8,1,72,1024]{3,2,1,0:T(8,128)(2,1)S(1)}, u32[]{:S(2)}, u32[]{:S(2)}) async-start(bf16[8,1,72,1024]{3,2,1,0:T(8,128)(2,1)} %bitcast.64), calls=%async_computation.6 | async-start | bytes 2359296 | tf_op jit(solution)/shard_map/all_to_all | solution.py:685
  359.7 21.1 %copy-start.5 = (f32[128,2048]{1,0:T(8,128)S(1)}, f32[128,2048]{1,0:T(8,128)}, u32[]{:S(2)}) copy-start(f32[128,2048]{1,0:T(8,128)} %copy-done.4) | copy-start | bytes 3145732
  360.0 20.8 %collective-permute-start.29 = (bf16[128,1024]{1,0:T(8,128)(2,1)S(1)}, bf16[128,1024]{1,0:T(8,128)(2,1)S(1)}, u32[]{:S(2)}, u32[]{:S(2)}) collective-permute-start(bf16[128,1024]{1,0:T(8,128)(2,1)S(1)} %slice_add_fusion.2), channel_id=1, source_target_pairs={{0,16},{2,18},{4,20},{6,22},{8,24},{10,26},{12,28},{14,30},{16,0},... | collective-permute-start | bytes 786440 | tf_op jit(solution)/shard_map/ppermute | solution.py:31

commit v8 on v7

--- a/solution.py
+++ b/solution.py
@@ -116,25 +116,30 @@
     return (new_max, denominator, accumulated)
 
 
-def order_body(order_ref, gate_ref, up_ref, down_ref, gate_out, up_out, down_out):
-    gate_out[...] = gate_ref[...].astype(jnp.bfloat16)
-    up_out[...] = up_ref[...].astype(jnp.bfloat16)
-    down_out[...] = down_ref[...].astype(jnp.bfloat16)
+def order_body(order_ref, gate_ref, up_ref, down_ref, *outs):
+    half = gate_ref.shape[2] // 2
+    outs[0][...] = gate_ref[:, :, :half].astype(jnp.bfloat16)
+    outs[1][...] = gate_ref[:, :, half:].astype(jnp.bfloat16)
+    outs[2][...] = up_ref[...].astype(jnp.bfloat16)
+    outs[3][...] = down_ref[...].astype(jnp.bfloat16)
 
 
 def order_experts(layout_map, gate, up, down):
     count, rows, width = gate.shape
     source = pl.BlockSpec((1, rows, width), lambda place, order: (order[place], 0, 0))
-    target = pl.BlockSpec((1, rows, width), lambda place, order: (place, 0, 0))
+    widths = (width // 2, width - width // 2, width, width)
     return pl.pallas_call(
         order_body,
         grid_spec=pltpu.PrefetchScalarGridSpec(
             num_scalar_prefetch=1,
             grid=(count,),
             in_specs=[source, source, source],
-            out_specs=[target, target, target],
+            out_specs=[
+                pl.BlockSpec((1, rows, some), lambda place, order: (place, 0, 0))
+                for some in widths
+            ],
         ),
-        out_shape=[jax.ShapeDtypeStruct((count, rows, width), jnp.bfloat16)] * 3,
+        out_shape=[jax.ShapeDtypeStruct((count, rows, some), jnp.bfloat16) for some in widths],
         cost_estimate=SMALL,
         name="order_experts",
     )(layout_map, gate, up, down)
@@ -290,21 +295,21 @@
 
 
 def hidden_body(turn_count, share, start_ref, *refs):
-    rows, (gate_ref, up_ref, out_ref) = (refs[:turn_count], refs[turn_count:])
-    gate = up = 0.0
+    rows, (first_ref, second_ref, up_ref, out_ref) = (refs[:turn_count], refs[turn_count:])
+    first = second = up = 0.0
     for turn in range(turn_count):
         here = pl.ds(pl.multiple_of(start_ref[turn], share), share)
-        gate = gate + jnp.dot(
-            rows[turn][0], gate_ref[0, here, :], preferred_element_type=jnp.float32
-        )
-        up = up + jnp.dot(rows[turn][0], up_ref[0, here, :], preferred_element_type=jnp.float32)
+        some = rows[turn][0]
+        first = first + jnp.dot(some, first_ref[0, here, :], preferred_element_type=jnp.float32)
+        second = second + jnp.dot(some, second_ref[0, here, :], preferred_element_type=jnp.float32)
+        up = up + jnp.dot(some, up_ref[0, here, :], preferred_element_type=jnp.float32)
+    gate = jnp.concatenate([first, second], axis=1)
     out_ref[0] = (gate / (1.0 + jnp.exp(-gate)) * up).astype(jnp.bfloat16)
 
 
-def hidden_units(starts, row_blocks, gate, up):
+def hidden_units(starts, row_blocks, weights):
     local_experts, row_count, share = row_blocks[0].shape
-    rows, width = gate.shape[1:]
-    whole = pl.BlockSpec((1, rows, width), lambda e, a: (e, 0, 0))
+    width = weights[-1].shape[2]
     count = len(row_blocks)
     return pl.pallas_call(
         lambda *refs: hidden_body(count, share, *refs),
@@ -312,14 +317,14 @@
             num_scalar_prefetch=1,
             grid=(local_experts,),
             in_specs=[pl.BlockSpec((1, row_count, share), lambda e, a: (e, 0, 0))] * count
-            + [whole] * 2,
+            + [pl.BlockSpec((1, *w.shape[1:]), lambda e, a: (e, 0, 0)) for w in weights],
             out_specs=pl.BlockSpec((1, row_count, width), lambda e, a: (e, 0, 0)),
         ),
         out_shape=jax.ShapeDtypeStruct((local_experts, row_count, width), jnp.bfloat16),
         compiler_params=pltpu.CompilerParams(vmem_limit_bytes=52 * 2**20),
         cost_estimate=SMALL,
         name="hidden_units",
-    )(starts, *row_blocks, gate, up)
+    )(starts, *row_blocks, *weights)
 
 
 def down_body(turn_count, share, start_ref, hidden_ref, down_ref, *outs):
@@ -418,10 +423,10 @@
         jnp.concatenate([w_out, router.T], axis=0).astype(jnp.bfloat16), part_masks, 1
     )
     first_rows, first_turns = doubled(share[None], group_masks[:1], 0)
-    first_rows, all_routes, out_all, layout_map = lax.optimization_barrier(
-        (first_rows, all_routes, out_all, layout_map)
-    )
-    own_gate, own_up, own_down = order_experts(layout_map, expert_gate, expert_up, expert_down)
+    first_rows, layout_map = lax.optimization_barrier((first_rows, layout_map))
+    own_first, own_second, own_up, own_down = order_experts(
+        layout_map, expert_gate, expert_up, expert_down
+    )
     part_ids = (part * head_count + (head ^ turns))[:, None] * token_count + offsets[None, :]
     part_ids = part_ids.reshape(-1)
     part_positions = prompt_split(part_ids, slot_len, stagger, prompt_count)[1]
@@ -438,8 +443,8 @@
         known = first_turns
         for mask in masks:
             if mask == masks[-1]:
-                piece, own_gate, cosine, sine_part = lax.optimization_barrier(
-                    (piece, own_gate, cosine, sine_part)
+                piece, own_first, cosine, sine_part, all_routes = lax.optimization_barrier(
+                    (piece, own_first, cosine, sine_part, all_routes)
                 )
             piece = jnp.concatenate([piece, swapped(piece, "seq", mask)], axis=0)
             known = known + [turn ^ mask for turn in known]
@@ -457,9 +462,10 @@
         (out_all[:out_rows], group_masks[-2:]),
         (out_all[out_rows:], group_masks[-2:][::-1]),
     ]
-    halves, head_weights, part_rows = lax.optimization_barrier(
-        ([half for half, _ in out_halves], head_weights, part_rows)
-    )
+    halves, head_weights, part_rows, own_first = lax.optimization_barrier(
+        ([half for half, _ in out_halves], head_weights, part_rows, own_first)
+    )
+    server_first = to_owner(own_first)
     out_halves = [
         (doubled(half, masks[:1], 1)[0], masks[1:]) for half, (_, masks) in zip(halves, out_halves)
     ]
@@ -556,12 +562,12 @@
         mixed = (accumulated / denominator).astype(jnp.bfloat16)
     blocks = by_place(mixed.reshape(head_count, token_count, HEAD))
     out_halves = [(half, swapped(half, "seq", masks[0])) for half, masks in out_halves]
-    blocks, out_halves = lax.optimization_barrier((blocks, out_halves))
+    blocks, out_halves, server_first = lax.optimization_barrier((blocks, out_halves, server_first))
     attention_result = lax.all_to_all(
         blocks, "seq", split_axis=0, concat_axis=0, tiled=True, axis_index_groups=groups
     )
-    attention_result, own_gate = lax.optimization_barrier((attention_result, own_gate))
-    server_gate = to_owner(own_gate)
+    attention_result, own_second = lax.optimization_barrier((attention_result, own_second))
+    server_second = to_owner(own_second)
 
     proj_width = head_count * HEAD
     attention_result = jnp.swapaxes(attention_result, 0, 1).reshape(token_count, proj_width)
@@ -619,8 +625,8 @@
     route_weight = route_weight * valid_token[:, None]
     all_weights, _ = doubled(route_weight[None], part_masks, 0)
     all_rows, _ = doubled(outgoing_share[None], part_masks, 0)
-    all_rows, all_weights, server_gate, own_up = lax.optimization_barrier(
-        (all_rows, all_weights, server_gate, own_up)
+    all_rows, all_weights, server_second, own_up = lax.optimization_barrier(
+        (all_rows, all_weights, server_second, own_up)
     )
     server_up = to_owner(own_up)
     buffer = jnp.stack(
@@ -642,7 +648,9 @@
         return swapped(block, "seq", m) if m else block
 
     received = [to_mate(m) for m in range(head_count)]
-    received[1], server_up, own_down = lax.optimization_barrier((received[1], server_up, own_down))
+    received[1:4], server_up, own_down = lax.optimization_barrier(
+        (received[1:4], server_up, own_down)
+    )
     server_down = to_owner(own_down)
     received = by_place(jnp.stack(received))
     received = received.reshape(head_count, part_count, local_experts, capacity, col_share)
@@ -654,7 +662,7 @@
         tp_blocks(jnp.moveaxis(rows, 2, 0).reshape(local_experts, -1, col_share))
         for rows in (received[:, 1:], received[:, :1])
     ]
-    hidden = [hidden_units(in_starts, rows, server_gate, server_up) for rows in halves]
+    hidden = [hidden_units(in_starts, rows, (server_first, server_second, server_up)) for rows in halves]
     hidden, server_down = lax.optimization_barrier((hidden, server_down))
 
     def through_experts(rows, parts):

time: 386 us -> 357 us (0.925)
  waiting for transfers between devices: 188 us -> 151 us
  blocking collectives: 10 us -> 0 us
  matrix products: 7.39 us -> 13.7 us
  other arithmetic: 17 us -> 22.9 us
  local copies, waits for them, and re-layouts: 25.8 us -> 31.2 us
    ppermute x22, waiting for transfers between devices: 133 us -> 101 us  [swapped(): lax.ppermute(value, axis, [(place, place ^ mask) for place in range(count)])]
    all_to_all x3 -> x4, waiting for transfers between devices: 19.6 us -> 3.96 us  [to_owner(): lax.all_to_all(blocks, 'seq', split_axis=0, concat_axis=0, tiled=True)]
    all_to_all x1 -> x0, blocking collectives: 10 us -> none  [shards(): lax.all_to_all(blocks, 'seq', split_axis=0, concat_axis=0, tiled=True, ax...]
    all_to_all x0 -> x1, starting transfers between devices: none -> 8.42 us  [shards(): lax.all_to_all(blocks, 'seq', split_axis=0, concat_axis=0, tiled=True, ax...]
    unnamed x83 -> x102, local copies, waits for them, and re-layouts: 19.5 us -> 26.5 us
    ppermute x22, starting transfers between devices: 39.5 us -> 32.7 us  [swapped(): lax.ppermute(value, axis, [(place, place ^ mask) for place in range(count)])]
    all_to_all x0 -> x1, waiting for transfers between devices: none -> 6.52 us  [shards(): lax.all_to_all(blocks, 'seq', split_axis=0, concat_axis=0, tiled=True, ax...]
    dot_general x4, matrix products: 2.58 us -> 7.03 us  [shards(): jnp.dot(rows, piece, preferred_element_type=jnp.float32)]
  transfers between devices with their start and end apart: 36 -> 38, of which waited for: 18 -> 20; matrix products, arithmetic and copies ran while one was open for 10% -> 14% of each run, Pallas kernels for 10% -> 13%
where the time goes in v8:
time: 357 us; the launch traced here: 355 us
  waiting for transfers between devices  151 us (42%)
  starting transfers between devices  84.3 us (24%)
  Pallas kernels  50 us (14%)
  local copies, waits for them, and re-layouts  31.2 us (9%)
  other arithmetic  22.9 us (6%)
  matrix products  13.7 us (4%)
    ppermute x22, waiting for transfers between devices, swapped(): lax.ppermute(value, axis, [(place, place ^ mask) for place in range(count)])  101 us
    ppermute x22, starting transfers between devices, swapped(): lax.ppermute(value, axis, [(place, place ^ mask) for place in range(count)])  32.7 us
    unnamed x102, local copies, waits for them, and re-layouts  26.5 us
    all_to_all x2, waiting for transfers between devices, back(): lax.all_to_all(blocks, 'seq', split_axis=0, concat_axis=0, tiled=True, ax...  25.3 us
    all_to_all x4, starting transfers between devices, to_owner(): lax.all_to_all(blocks, 'seq', split_axis=0, concat_axis=0, tiled=True)  24.4 us
    pallas_call x1, Pallas kernels, order_experts(): pl.pallas_call(order_body, grid_spec=pltpu.PrefetchScalarGridSpec(num_sca...  12.9 us
    pallas_call x2, Pallas kernels, hidden_units(): pl.pallas_call(lambda *refs: hidden_body(count, share, *refs), grid_spec=...  11.6 us
    ppermute x6, waiting for transfers between devices, from_turned(): lax.ppermute(value, axis, [((place + turn) % count, place) for place in r...  9.41 us
  transfers between devices with their start and end apart: 38, of which 20 were waited for; matrix products, arithmetic and copies ran while one was open for 14% of the time, Pallas kernels for 13%

profile of v8, /device:TPU:0, one launch (start us, length us, event | category | flops | bytes accessed | tf_op | source)
XLA Modules:
  0.0 354.6 jit_solution(14695342301574168298)
XLA Ops:
  3.3 3.1 collective-permute-start.2
  6.4 2.6 collective-permute-start.4
  10.6 1.9 pack_heads.1
  12.4 5.9 %all-to-all-start = ((bf16[16,128,384]{2,1,0:T(8,128)(2,1)}), bf16[16,128,384]{2,1,0:T(8,128)(2,1)}, u32[]{:S(2)}, u32[]{:S(2)}) async-start(bf16[16,128,384]{2,1,0:T(8,128)(2,1)} %pack_heads.1), calls=%async_computation | async-start | bytes 3145728 | tf_op jit(solution)/shard_map/all_to_all | solution.py:411
  18.5 3.1 multiply_sine_fusion
  21.7 1.9 collective-permute-start.3
  23.6 1.5 collective-permute-start.6
  25.1 12.9 %order_experts.1 = (bf16[16,128,256]{2,1,0:T(8,128)(2,1)}, bf16[16,128,256]{2,1,0:T(8,128)(2,1)}, bf16[16,128,512]{2,1,0:T(8,128)(2,1)}, bf16[16,128,512]{2,1,0:T(8,128)(2,1)}) custom-call(s32[16]{0:T(128)} %order_ref, f32[16,128,512]{2,1,0:T(8,128)} %gate_ref.1, f32[16,128,512]{2,1,0:T(8,128)} %up_ref.1, f32[16,128,512]{2,1,0:T(8,128)} %down_ref.1), custom_call_target="tpu_custom_call" | custom-call | flops 1 | bytes 1 | tf_op jit(solution)/shard_map/order_experts/pallas_call | solution.py:131
  38.0 2.5 collective-permute-done
  40.7 1.6 collective-permute-start.5
  42.5 17.6 %collective-permute-done.1 = bf16[1040,256]{1,0:T(8,128)(2,1)S(1)} collective-permute-done((bf16[1040,256]{1,0:T(8,128)(2,1)S(1)}, bf16[1040,256]{1,0:T(8,128)(2,1)S(1)}, u32[]{:S(2)}, u32[]{:S(2)}) %collective-permute-start.1) | collective-permute-done | bytes 532512 | tf_op jit(solution)/shard_map/ppermute | solution.py:31
  64.0 1.6 collective-permute-start.9
  65.6 1.4 collective-permute-start.10
  67.1 5.4 %all-to-all-start.1 = ((bf16[16,128,256]{2,1,0:T(8,128)(2,1)}), bf16[16,128,256]{2,1,0:T(8,128)(2,1)S(1)}, u32[]{:S(2)}, u32[]{:S(2)}) async-start(bf16[16,128,256]{2,1,0:T(8,128)(2,1)} %get-tuple-element.77), calls=%async_computation.1 | async-start | bytes 2097152 | tf_op jit(solution)/shard_map/all_to_all | solution.py:455
  73.1 10.8 %collective-permute-done.9 = bf16[512,512]{1,0:T(8,128)(2,1)} collective-permute-done((bf16[512,512]{1,0:T(8,128)(2,1)}, bf16[512,512]{1,0:T(8,128)(2,1)}, u32[]{:S(2)}, u32[]{:S(2)}) %collective-permute-start.9) | collective-permute-done | bytes 524320 | tf_op jit(solution)/shard_map/ppermute | solution.py:31
  83.9 2.3 pad_maximum_fusion.2
  86.2 5.8 %project.1 = bf16[1024,384]{1,0:T(8,128)(2,1)S(1)} custom-call(s32[2]{0:T(128)S(1)} %fusion.119.refs_0_, bf16[1024,1024]{1,0:T(8,128)(2,1)S(1)} %pad_maximum_fusion.refs_1_, bf16[1024,1024]{1,0:T(8,128)(2,1)} %collective-permute-done.8.refs_2_, bf16[2048,384]{1,0:T(8,128)(2,1)} %bitcast.6.refs_3_, f32[1024,64]{1,0:T(8,128)S(1)} %copy-done.3, ...), custom_call_target="tpu_custom_call" | custom-call | flops 1 | bytes 1 | tf_op jit(solution)/shard_map/project/pallas_call | solution.py:196
  92.1 3.4 collective-permute-start.11
  95.5 2.2 pad_maximum_fusion.1
  97.9 6.7 %attend_once.1 = bf16[1088,128]{1,0:T(8,128)(2,1)S(1)} custom-call(f32[1]{0:T(128)} %dynamic_slice.92.sink_ref, s32[1088,1]{1,0:T(8,128)S(1)} %copy-done.1, s32[1,1088]{1,0:T(1,128)S(1)} %and_select_fusion.key_prompt_ref, bf16[1088,384]{1,0:T(8,128)(2,1)S(1)} %pad_maximum_fusion.3.query_ref.key_ref.value_ref, ...), custom_call_target="tpu_custom_call" | custom-call | flops 1 | bytes 1 | tf_op jit(solution)/shard_map/attend_once/pallas_call | solution.py:238
  106.3 5.0 %collective-permute-done.12 = bf16[64,128]{1,0:T(8,128)(2,1)S(1)} collective-permute-done((bf16[64,128]{1,0:T(8,128)(2,1)S(1)}, bf16[64,128]{1,0:T(8,128)(2,1)S(1)}, u32[]{:S(2)}, u32[]{:S(2)}) %collective-permute-start.12) | collective-permute-done | bytes 16416 | tf_op jit(solution)/shard_map/ppermute | solution.py:21
  119.2 10.4 %collective-permute-done.13 = bf16[512,1024]{1,0:T(8,128)(2,1)} collective-permute-done((bf16[512,1024]{1,0:T(8,128)(2,1)}, bf16[512,1024]{1,0:T(8,128)(2,1)}, u32[]{:S(2)}, u32[]{:S(2)}) %collective-permute-start.13) | collective-permute-done | bytes 1048608 | tf_op jit(solution)/shard_map/ppermute | solution.py:31
  129.8 8.4 %all-to-all-start.2 = ((bf16[8,128,128]{1,2,0:T(8,128)(2,1)}), bf16[8,128,128]{1,2,0:T(8,128)(2,1)S(1)}, u32[]{:S(2)}, u32[]{:S(2)}) async-start(bf16[8,128,128]{1,2,0:T(8,128)(2,1)} %copy-done.23), calls=%async_computation.2 | async-start | bytes 524288 | tf_op jit(solution)/shard_map/all_to_all | solution.py:566
  138.4 6.5 %all-to-all-done.2 = bf16[8,128,128]{1,2,0:T(8,128)(2,1)S(1)} async-done(((bf16[8,128,128]{1,2,0:T(8,128)(2,1)}), bf16[8,128,128]{1,2,0:T(8,128)(2,1)S(1)}, u32[]{:S(2)}, u32[]{:S(2)}) %all-to-all-start.2) | async-done | bytes 262176 | tf_op jit(solution)/shard_map/all_to_all | solution.py:566
  144.9 2.4 fusion.8
  149.5 2.4 fusion.63
  151.9 5.2 %all-to-all-start.3 = ((bf16[16,128,256]{2,1,0:T(8,128)(2,1)}), bf16[16,128,256]{2,1,0:T(8,128)(2,1)}, u32[]{:S(2)}, u32[]{:S(2)}) async-start(bf16[16,128,256]{2,1,0:T(8,128)(2,1)} %get-tuple-element.89), calls=%async_computation.3 | async-start | bytes 2097152 | tf_op jit(solution)/shard_map/all_to_all | solution.py:455
  159.3 1.8 collective-permute-done.15.refs_2_
  161.1 1.9 settle.1
  164.1 2.8 collective-permute-start.16
  167.6 25.5 %collective-permute-done.17 = f32[1,128,16]{2,1,0:T(8,128)S(1)} collective-permute-done((f32[1,128,16]{2,1,0:T(8,128)S(1)}, f32[1,128,16]{2,1,0:T(8,128)S(1)}, u32[]{:S(2)}, u32[]{:S(2)}) %collective-permute-start.17) | collective-permute-done | bytes 8224 | tf_op jit(solution)/shard_map/ppermute | solution.py:31
  194.0 4.6 %all-to-all-start.4 = ((bf16[16,128,512]{2,1,0:T(8,128)(2,1)}), bf16[16,128,512]{2,1,0:T(8,128)(2,1)S(1)}, u32[]{:S(2)}, u32[]{:S(2)}) async-start(bf16[16,128,512]{2,1,0:T(8,128)(2,1)} %get-tuple-element.93), calls=%async_computation.4 | async-start | bytes 4194304 | tf_op jit(solution)/shard_map/all_to_all | solution.py:455
  203.3 1.9 collective-permute-start.18
  205.2 1.5 collective-permute-start.19
  207.7 2.8 collective-permute-start.22
  211.1 2.5 collective-permute-done.18
  213.6 5.4 %collective-permute-start.23 = (bf16[2,72,1024]{2,1,0:T(8,128)(2,1)}, bf16[2,72,1024]{2,1,0:T(8,128)(2,1)}, u32[]{:S(2)}, u32[]{:S(2)}) collective-permute-start(bf16[2,72,1024]{2,1,0:T(8,128)(2,1)} %get-tuple-element.123), channel_id=1, source_target_pairs={{0,12},{2,14},{4,8},{6,10},{8,4},{10,6},{12,0},{14,2},{16,28},{18,... | collective-permute-start | bytes 884744 | tf_op jit(solution)/shard_map/ppermute | solution.py:31
  219.0 9.2 %collective-permute-done.19 = bf16[2,72,1024]{2,1,0:T(8,128)(2,1)S(1)} collective-permute-done((bf16[2,72,1024]{2,1,0:T(8,128)(2,1)S(1)}, bf16[2,72,1024]{2,1,0:T(8,128)(2,1)S(1)}, u32[]{:S(2)}, u32[]{:S(2)}) %collective-permute-start.19) | collective-permute-done | bytes 294944 | tf_op jit(solution)/shard_map/ppermute | solution.py:31
  229.3 11.9 %collective-permute-done.20 = bf16[2,72,1024]{2,1,0:T(8,128)(2,1)} collective-permute-done((bf16[2,72,1024]{2,1,0:T(8,128)(2,1)S(1)}, bf16[2,72,1024]{2,1,0:T(8,128)(2,1)}, u32[]{:S(2)}, u32[]{:S(2)}) %collective-permute-start.20) | collective-permute-done | bytes 294944 | tf_op jit(solution)/shard_map/ppermute | solution.py:31
  241.3 9.3 %all-to-all-start.5 = ((bf16[16,128,512]{2,1,0:T(8,128)(2,1)}), bf16[16,128,512]{2,1,0:T(8,128)(2,1)}, u32[]{:S(2)}, u32[]{:S(2)}) async-start(bf16[16,128,512]{2,1,0:T(8,128)(2,1)} %get-tuple-element.101), calls=%async_computation.5 | async-start | bytes 4194304 | tf_op jit(solution)/shard_map/all_to_all | solution.py:455
  250.6 1.7 bitcast_dynamic-update-slice_fusion.6
  252.3 1.7 bitcast_dynamic-update-slice_fusion.5
  254.0 1.7 bitcast_dynamic-update-slice_fusion.4
  255.7 1.7 bitcast_dynamic-update-slice_fusion.3
  257.4 1.7 bitcast_dynamic-update-slice_fusion.2
  259.1 1.5 collective-permute-done.23
  260.6 1.7 bitcast_dynamic-update-slice_fusion.1
  262.3 9.1 %collective-permute-done.24 = bf16[2,72,1024]{2,1,0:T(8,128)(2,1)} collective-permute-done((bf16[2,72,1024]{2,1,0:T(8,128)(2,1)}, bf16[2,72,1024]{2,1,0:T(8,128)(2,1)}, u32[]{:S(2)}, u32[]{:S(2)}) %collective-permute-start.24) | collective-permute-done | bytes 294944 | tf_op jit(solution)/shard_map/ppermute | solution.py:31
  271.4 1.7 bitcast_dynamic-update-slice_fusion
  278.2 2.3 collective-permute-done.26.refs_2_
  281.6 5.8 %hidden_units.3.refs_1_ = bf16[1,576,512]{2,1,0:T(8,128)(2,1)S(1)} custom-call(s32[2]{0:T(128)S(1)} %fusion.119.refs_0_, bf16[1,576,1024]{2,1,0:T(8,128)(2,1)} %bitcast.165, bf16[1,576,1024]{2,1,0:T(8,128)(2,1)} %copy-done.22, bf16[1,2048,256]{2,1,0:T(8,128)(2,1)S(1)} %bitcast.153, bf16[1,2048,256]{2,1,0:T(8,128)(2,1)} %bitcast.35.refs_4_, ...), custom_call_target="tpu_custom_call" | custom-call | flops 1 | bytes 1 | tf_op jit(solution)/shard_map/hidden_units/pallas_call | solution.py:314
  288.5 5.8 %hidden_units.2.refs_1_ = bf16[1,576,512]{2,1,0:T(8,128)(2,1)S(1)} custom-call(s32[2]{0:T(128)S(1)} %fusion.119.refs_0_, bf16[1,576,1024]{2,1,0:T(8,128)(2,1)} %bitcast.163, bf16[1,576,1024]{2,1,0:T(8,128)(2,1)} %copy-done.21, bf16[1,2048,256]{2,1,0:T(8,128)(2,1)S(1)} %bitcast.154, bf16[1,2048,256]{2,1,0:T(8,128)(2,1)} %bitcast.35.refs_4_, ...), custom_call_target="tpu_custom_call" | custom-call | flops 1 | bytes 1 | tf_op jit(solution)/shard_map/hidden_units/pallas_call | solution.py:314
  294.4 4.0 %all-to-all-done.5 = bf16[16,128,512]{2,1,0:T(8,128)(2,1)} async-done(((bf16[16,128,512]{2,1,0:T(8,128)(2,1)}), bf16[16,128,512]{2,1,0:T(8,128)(2,1)}, u32[]{:S(2)}, u32[]{:S(2)}) %all-to-all-start.5) | async-done | bytes 2097184 | tf_op jit(solution)/shard_map/all_to_all | solution.py:455
  298.3 4.6 %down_rows.2 = (bf16[1,576,1024]{2,1,0:T(8,128)(2,1)S(1)}, bf16[1,576,1024]{2,1,0:T(8,128)(2,1)}) custom-call(s32[2]{0:T(128)S(1)} %fusion.120.refs_0_, bf16[1,576,512]{2,1,0:T(8,128)(2,1)S(1)} %hidden_units.2.refs_1_, bf16[1,2048,512]{2,1,0:T(8,128)(2,1)} %bitcast.59.refs_2_), custom_call_target="tpu_custom_call" | custom-call | flops 1 | bytes 1 | tf_op jit(solution)/shard_map/down_rows/pallas_call | solution.py:346
  302.9 3.1 collective-permute-done.27
  306.0 1.5 add_convert_fusion.1
  307.5 3.7 %all-to-all-start.6 = ((bf16[8,1,72,1024]{3,2,1,0:T(8,128)(2,1)}), bf16[8,1,72,1024]{3,2,1,0:T(8,128)(2,1)S(1)}, u32[]{:S(2)}, u32[]{:S(2)}) async-start(bf16[8,1,72,1024]{3,2,1,0:T(8,128)(2,1)} %bitcast.61), calls=%async_computation.6 | async-start | bytes 2359296 | tf_op jit(solution)/shard_map/all_to_all | solution.py:693
  311.2 4.6 %down_rows.3 = (bf16[1,576,1024]{2,1,0:T(8,128)(2,1)S(1)}, bf16[1,576,1024]{2,1,0:T(8,128)(2,1)}) custom-call(s32[2]{0:T(128)S(1)} %fusion.120.refs_0_, bf16[1,576,512]{2,1,0:T(8,128)(2,1)S(1)} %hidden_units.3.refs_1_, bf16[1,2048,512]{2,1,0:T(8,128)(2,1)} %bitcast.59.refs_2_), custom_call_target="tpu_custom_call" | custom-call | flops 1 | bytes 1 | tf_op jit(solution)/shard_map/down_rows/pallas_call | solution.py:346
  316.7 2.2 collective-permute-done.28
  318.9 1.5 add_convert_fusion
  320.4 7.2 %all-to-all-done.6 = bf16[8,1,72,1024]{3,2,1,0:T(8,128)(2,1)S(1)} async-done(((bf16[8,1,72,1024]{3,2,1,0:T(8,128)(2,1)}), bf16[8,1,72,1024]{3,2,1,0:T(8,128)(2,1)S(1)}, u32[]{:S(2)}, u32[]{:S(2)}) %all-to-all-start.6) | async-done | bytes 1179680 | tf_op jit(solution)/shard_map/all_to_all | solution.py:693
  328.5 3.6 %all-to-all-start.7 = ((bf16[8,1,72,1024]{3,2,1,0:T(8,128)(2,1)}), bf16[8,1,72,1024]{3,2,1,0:T(8,128)(2,1)S(1)}, u32[]{:S(2)}, u32[]{:S(2)}) async-start(bf16[8,1,72,1024]{3,2,1,0:T(8,128)(2,1)} %bitcast.65), calls=%async_computation.7 | async-start | bytes 2359296 | tf_op jit(solution)/shard_map/all_to_all | solution.py:693
  332.9 1.8 collective-permute-start.29
  334.7 18.1 %all-to-all-done.7 = bf16[8,1,72,1024]{3,2,1,0:T(8,128)(2,1)S(1)} async-done(((bf16[8,1,72,1024]{3,2,1,0:T(8,128)(2,1)}), bf16[8,1,72,1024]{3,2,1,0:T(8,128)(2,1)S(1)}, u32[]{:S(2)}, u32[]{:S(2)}) %all-to-all-start.7) | async-done | bytes 1179680 | tf_op jit(solution)/shard_map/all_to_all | solution.py:693
  (215 shorter events, 45.7 us)
Async XLA Ops:
  0.0 6.4 %copy-start.27 = (s32[128,8]{0,1:T(8,128)S(1)}, s32[128,8]{0,1:T(8,128)}, u32[]{:S(2)}) copy-start(s32[128,8]{0,1:T(8,128)} %param.29) | copy-start | bytes 12292
  0.0 10.1 %copy-start.26 = (f32[128,16]{0,1:T(8,128)S(1)}, f32[128,16]{0,1:T(8,128)}, u32[]{:S(2)}) copy-start(f32[128,16]{0,1:T(8,128)} %param.23) | copy-start | bytes 24580
  0.0 10.6 %copy-start.4 = (f32[128,1024]{1,0:T(8,128)S(1)}, f32[128,1024]{1,0:T(8,128)}, u32[]{:S(2)}) copy-start(f32[128,1024]{1,0:T(8,128)} %query_ref.1) | copy-start | bytes 1572868
  0.0 10.6 %copy-start.5 = (f32[128,1024]{1,0:T(8,128)S(1)}, f32[128,1024]{1,0:T(8,128)}, u32[]{:S(2)}) copy-start(f32[128,1024]{1,0:T(8,128)} %key_ref.1) | copy-start | bytes 1572868
  0.0 10.6 %copy-start.6 = (f32[128,1024]{1,0:T(8,128)S(1)}, f32[128,1024]{1,0:T(8,128)}, u32[]{:S(2)}) copy-start(f32[128,1024]{1,0:T(8,128)} %value_ref.1) | copy-start | bytes 1572868
  3.3 18.2 %collective-permute-start.2 = (bf16[1,128,1024]{2,1,0:T(8,128)(2,1)S(1)}, bf16[1,128,1024]{2,1,0:T(8,128)(2,1)S(1)}, u32[]{:S(2)}, u32[]{:S(2)}) collective-permute-start(bf16[1,128,1024]{2,1,0:T(8,128)(2,1)S(1)} %fusion.48), channel_id=1, source_target_pairs={{0,8},{2,10},{4,12},{6,14},{8,0},{10,2},{12,4},{14,6},{16,24},{18,... | collective-permute-start | bytes 786440 | tf_op jit(solution)/shard_map/ppermute | solution.py:31
  6.4 17.2 %collective-permute-start.4 = (s32[1,128,8]{1,2,0:T(8,128)S(1)}, s32[1,128,8]{1,2,0:T(8,128)S(1)}, u32[]{:S(2)}, u32[]{:S(2)}) collective-permute-start(s32[1,128,8]{1,2,0:T(8,128)S(1)} %bitcast.176), channel_id=1, source_target_pairs={{0,16},{2,18},{4,20},{6,22},{8,24},{10,26},{12,28},{14,30},{16,0},... | collective-permute-start | bytes 12296 | tf_op jit(solution)/shard_map/ppermute | solution.py:31
  10.2 30.3 %collective-permute-start = (bf16[1040,128]{1,0:T(8,128)(2,1)S(1)}, bf16[1040,128]{1,0:T(8,128)(2,1)S(1)}, u32[]{:S(2)}, u32[]{:S(2)}) collective-permute-start(bf16[1040,128]{1,0:T(8,128)(2,1)S(1)} %pad_maximum_fusion.13), channel_id=1, source_target_pairs={{0,16},{2,18},{4,20},{6,22},{8,24},{10,26},{12,28},{14,30},{16,0},... | collective-permute-start | bytes 798728 | tf_op jit(solution)/shard_map/ppermute | solution.py:31
  12.4 49.9 %all-to-all-start = ((bf16[16,128,384]{2,1,0:T(8,128)(2,1)}), bf16[16,128,384]{2,1,0:T(8,128)(2,1)}, u32[]{:S(2)}, u32[]{:S(2)}) async-start(bf16[16,128,384]{2,1,0:T(8,128)(2,1)} %pack_heads.1), calls=%async_computation | async-start | bytes 3145728 | tf_op jit(solution)/shard_map/all_to_all | solution.py:411
  21.7 19.0 %collective-permute-start.3 = (bf16[2,128,512]{2,1,0:T(8,128)(2,1)S(1)}, bf16[2,128,512]{2,1,0:T(8,128)(2,1)S(1)}, u32[]{:S(2)}, u32[]{:S(2)}) collective-permute-start(bf16[2,128,512]{2,1,0:T(8,128)(2,1)S(1)} %get-tuple-element.133), channel_id=1, source_target_pairs={{0,4},{2,6},{4,0},{6,2},{8,12},{10,14},{12,8},{14,10},{16,20},{18,... | collective-permute-start | bytes 786440 | tf_op jit(solution)/shard_map/ppermute | solution.py:31
  23.6 18.7 %collective-permute-start.6 = (bf16[2,128,512]{2,1,0:T(8,128)(2,1)S(1)}, bf16[2,128,512]{2,1,0:T(8,128)(2,1)S(1)}, u32[]{:S(2)}, u32[]{:S(2)}) collective-permute-start(bf16[2,128,512]{2,1,0:T(8,128)(2,1)S(1)} %get-tuple-element.134), channel_id=1, source_target_pairs={{0,2},{2,0},{4,6},{6,4},{8,10},{10,8},{12,14},{14,12},{16,18},{18,... | collective-permute-start | bytes 786440 | tf_op jit(solution)/shard_map/ppermute | solution.py:31
  40.6 19.5 %collective-permute-start.1 = (bf16[1040,256]{1,0:T(8,128)(2,1)S(1)}, bf16[1040,256]{1,0:T(8,128)(2,1)S(1)}, u32[]{:S(2)}, u32[]{:S(2)}) collective-permute-start(bf16[1040,256]{1,0:T(8,128)(2,1)S(1)} %pad_maximum_fusion.7), channel_id=1, source_target_pairs={{0,8},{2,10},{4,12},{6,14},{8,0},{10,2},{12,4},{14,6},{16,24},{18,... | collective-permute-start | bytes 1597448 | tf_op jit(solution)/shard_map/ppermute | solution.py:31
  40.7 21.1 %collective-permute-start.5 = (bf16[4,128,512]{2,1,0:T(8,128)(2,1)S(1)}, bf16[4,128,512]{2,1,0:T(8,128)(2,1)S(1)}, u32[]{:S(2)}, u32[]{:S(2)}) collective-permute-start(bf16[4,128,512]{2,1,0:T(8,128)(2,1)S(1)} %pad_maximum_fusion.10), channel_id=1, source_target_pairs={{0,2},{2,0},{4,6},{6,4},{8,10},{10,8},{12,14},{14,12},{16,18},{18,... | collective-permute-start | bytes 1572872 | tf_op jit(solution)/shard_map/ppermute | solution.py:31
  42.4 19.5 %collective-permute-start.7 = (bf16[4,128,512]{2,1,0:T(8,128)(2,1)S(1)}, bf16[4,128,512]{2,1,0:T(8,128)(2,1)S(1)}, u32[]{:S(2)}, u32[]{:S(2)}) collective-permute-start(bf16[4,128,512]{2,1,0:T(8,128)(2,1)S(1)} %pad_maximum_fusion.11), channel_id=1, source_target_pairs={{0,4},{2,6},{4,0},{6,2},{8,12},{10,14},{12,8},{14,10},{16,20},{18,... | collective-permute-start | bytes 1572872 | tf_op jit(solution)/shard_map/ppermute | solution.py:31
  62.1 3.5 copy-start.28
  62.3 10.2 %copy-start.29 = (f32[8]{0:T(128)S(1)}, f32[8]{0:T(128)}, u32[]{:S(2)}) copy-start(f32[8]{0:T(128)} %param.22) | copy-start | bytes 100
  62.3 23.9 %collective-permute-start.8 = (bf16[1024,1024]{1,0:T(8,128)(2,1)S(1)}, bf16[1024,1024]{1,0:T(8,128)(2,1)}, u32[]{:S(2)}, u32[]{:S(2)}) collective-permute-start(bf16[1024,1024]{1,0:T(8,128)(2,1)S(1)} %pad_maximum_fusion.refs_1_), channel_id=1, source_target_pairs={{1,0},{0,1},{3,2},{2,3},{5,4},{4,5},{7,6},{6,7},{9,8},{8,9},{11,10... | collective-permute-start | bytes 6291464 | tf_op jit(solution)/shard_map/ppermute | solution.py:26
  64.0 20.0 %collective-permute-start.9 = (bf16[512,512]{1,0:T(8,128)(2,1)}, bf16[512,512]{1,0:T(8,128)(2,1)}, u32[]{:S(2)}, u32[]{:S(2)}) collective-permute-start(bf16[512,512]{1,0:T(8,128)(2,1)} %pad_maximum_fusion.8), channel_id=1, source_target_pairs={{0,4},{2,6},{4,0},{6,2},{8,12},{10,14},{12,8},{14,10},{16,20},{18,... | collective-permute-start | bytes 1572872 | tf_op jit(solution)/shard_map/ppermute | solution.py:31
  65.6 29.9 %collective-permute-start.10 = (bf16[528,512]{1,0:T(8,128)(2,1)}, bf16[528,512]{1,0:T(8,128)(2,1)}, u32[]{:S(2)}, u32[]{:S(2)}) collective-permute-start(bf16[528,512]{1,0:T(8,128)(2,1)} %pad_maximum_fusion.4), channel_id=1, source_target_pairs={{0,2},{2,0},{4,6},{6,4},{8,10},{10,8},{12,14},{14,12},{16,18},{18,... | collective-permute-start | bytes 1622024 | tf_op jit(solution)/shard_map/ppermute | solution.py:31
  67.1 52.0 %all-to-all-start.1 = ((bf16[16,128,256]{2,1,0:T(8,128)(2,1)}), bf16[16,128,256]{2,1,0:T(8,128)(2,1)S(1)}, u32[]{:S(2)}, u32[]{:S(2)}) async-start(bf16[16,128,256]{2,1,0:T(8,128)(2,1)} %get-tuple-element.77), calls=%async_computation.1 | async-start | bytes 2097152 | tf_op jit(solution)/shard_map/all_to_all | solution.py:455
  72.5 13.7 %copy-start.2 = (f32[1024,64]{1,0:T(8,128)S(1)}, f32[1024,64]{1,0:T(8,128)}, u32[]{:S(2)}) copy-start(f32[1024,64]{1,0:T(8,128)} %get-tuple-element.71.refs_5_) | copy-start | bytes 786436
  72.5 13.7 %copy-start.3 = (f32[1024,64]{1,0:T(8,128)S(1)}, f32[1024,64]{1,0:T(8,128)}, u32[]{:S(2)}) copy-start(f32[1024,64]{1,0:T(8,128)} %get-tuple-element.70.refs_4_) | copy-start | bytes 786436
  86.2 9.3 %copy-start.16 = (bf16[528,512]{1,0:T(8,128)(2,1)S(1)}, bf16[528,512]{1,0:T(8,128)(2,1)}, u32[]{:S(2)}) copy-start(bf16[528,512]{1,0:T(8,128)(2,1)} %pad_maximum_fusion.4) | copy-start | bytes 1622020
  92.1 5.8 %copy-start.1 = (s32[1088,1]{1,0:T(8,128)S(1)}, s32[1088,1]{1,0:T(8,128)}, u32[]{:S(2)}) copy-start(s32[1088,1]{1,0:T(8,128)} %fusion.13.query_prompt_ref) | copy-start | bytes 13060
  92.1 5.7 %collective-permute-start.11 = (bf16[64,384]{1,0:T(8,128)(2,1)S(1)}, bf16[64,384]{1,0:T(8,128)(2,1)S(1)}, u32[]{:S(2)}, u32[]{:S(2)}) collective-permute-start(bf16[64,384]{1,0:T(8,128)(2,1)S(1)} %constant_dynamic-slice_fusion.8), channel_id=1, source_target_pairs={{0,16},{2,18},{4,20},{6,22},{8,24},{10,26},{12,28},{14,30},{1,17},... | collective-permute-start | bytes 147464 | tf_op jit(solution)/shard_map/ppermute | solution.py:21
  104.6 42.7 %copy-start.13 = (bf16[528,1024]{1,0:T(8,128)(2,1)S(1)}, bf16[528,1024]{1,0:T(8,128)(2,1)}, u32[]{:S(2)}) copy-start(bf16[528,1024]{1,0:T(8,128)(2,1)} %pad_maximum_fusion.1) | copy-start | bytes 3244036
  104.6 6.7 %collective-permute-start.12 = (bf16[64,128]{1,0:T(8,128)(2,1)S(1)}, bf16[64,128]{1,0:T(8,128)(2,1)S(1)}, u32[]{:S(2)}, u32[]{:S(2)}) collective-permute-start(bf16[64,128]{1,0:T(8,128)(2,1)S(1)} %slice.207), channel_id=1, source_target_pairs={{16,0},{18,2},{20,4},{22,6},{24,8},{26,10},{28,12},{30,14},{17,1},... | collective-permute-start | bytes 49160 | tf_op jit(solution)/shard_map/ppermute | solution.py:21
  106.1 23.8 %collective-permute-start.14 = (bf16[528,1024]{1,0:T(8,128)(2,1)}, bf16[528,1024]{1,0:T(8,128)(2,1)}, u32[]{:S(2)}, u32[]{:S(2)}) collective-permute-start(bf16[528,1024]{1,0:T(8,128)(2,1)} %pad_maximum_fusion.1), channel_id=1, source_target_pairs={{0,4},{2,6},{4,0},{6,2},{8,12},{10,14},{12,8},{14,10},{16,20},{18,... | collective-permute-start | bytes 3244040 | tf_op jit(solution)/shard_map/ppermute | solution.py:31
  106.3 23.2 %collective-permute-start.13 = (bf16[512,1024]{1,0:T(8,128)(2,1)}, bf16[512,1024]{1,0:T(8,128)(2,1)}, u32[]{:S(2)}, u32[]{:S(2)}) collective-permute-start(bf16[512,1024]{1,0:T(8,128)(2,1)} %pad_maximum_fusion.2), channel_id=1, source_target_pairs={{0,2},{2,0},{4,6},{6,4},{8,10},{10,8},{12,14},{14,12},{16,18},{18,... | collective-permute-start | bytes 3145736 | tf_op jit(solution)/shard_map/ppermute | solution.py:31
  114.2 34.2 %copy-start.14 = (bf16[512,1024]{1,0:T(8,128)(2,1)S(1)}, bf16[512,1024]{1,0:T(8,128)(2,1)}, u32[]{:S(2)}) copy-start(bf16[512,1024]{1,0:T(8,128)(2,1)} %pad_maximum_fusion.2) | copy-start | bytes 3145732
  119.1 10.7 %copy-start.23 = (bf16[8,128,128]{1,2,0:T(8,128)(2,1)}, bf16[8,128,128]{1,2,0:T(8,128)(2,1)S(1)}, u32[]{:S(2)}) copy-start(bf16[8,128,128]{1,2,0:T(8,128)(2,1)S(1)} %constant_dynamic-update-slice_fusion) | copy-start | bytes 786436
  129.8 15.0 %all-to-all-start.2 = ((bf16[8,128,128]{1,2,0:T(8,128)(2,1)}), bf16[8,128,128]{1,2,0:T(8,128)(2,1)S(1)}, u32[]{:S(2)}, u32[]{:S(2)}) async-start(bf16[8,128,128]{1,2,0:T(8,128)(2,1)} %copy-done.23), calls=%async_computation.2 | async-start | bytes 524288 | tf_op jit(solution)/shard_map/all_to_all | solution.py:566
  148.4 8.7 %copy-start.19 = (f32[128,1024]{1,0:T(8,128)S(1)}, f32[128,1024]{1,0:T(8,128)}, u32[]{:S(2)}) copy-start(f32[128,1024]{1,0:T(8,128)} %fusion.8) | copy-start | bytes 1572868
  149.5 7.6 %copy-start.20 = (f32[128,1024]{1,0:T(8,128)S(1)}, f32[128,1024]{1,0:T(8,128)}, u32[]{:S(2)}) copy-start(f32[128,1024]{1,0:T(8,128)} %fusion.10) | copy-start | bytes 1572868
  151.9 5.3 %copy-start.17 = (f32[128,1024]{1,0:T(8,128)S(1)}, f32[128,1024]{1,0:T(8,128)}, u32[]{:S(2)}) copy-start(f32[128,1024]{1,0:T(8,128)} %fusion.65) | copy-start | bytes 1572868
  151.9 42.1 %all-to-all-start.3 = ((bf16[16,128,256]{2,1,0:T(8,128)(2,1)}), bf16[16,128,256]{2,1,0:T(8,128)(2,1)}, u32[]{:S(2)}, u32[]{:S(2)}) async-start(bf16[16,128,256]{2,1,0:T(8,128)(2,1)} %get-tuple-element.89), calls=%async_computation.3 | async-start | bytes 2097152 | tf_op jit(solution)/shard_map/all_to_all | solution.py:455
  157.1 4.0 %copy-start = (bf16[128,2048]{1,0:T(8,128)(2,1)S(1)}, bf16[128,2048]{1,0:T(8,128)(2,1)}, u32[]{:S(2)}) copy-start(bf16[128,2048]{1,0:T(8,128)(2,1)} %refs_3_.1) | copy-start | bytes 1572868
  157.1 4.0 %copy-start.9 = (f32[2048]{0:T(1024)S(1)}, f32[2048]{0:T(1024)}, u32[]{:S(2)}) copy-start(f32[2048]{0:T(1024)} %param.17) | copy-start | bytes 24580
  158.3 2.9 collective-permute-start.15
  164.1 29.1 %collective-permute-start.16 = (bf16[1,128,1024]{2,1,0:T(8,128)(2,1)S(1)}, bf16[1,128,1024]{2,1,0:T(8,128)(2,1)S(1)}, u32[]{:S(2)}, u32[]{:S(2)}) collective-permute-start(bf16[1,128,1024]{2,1,0:T(8,128)(2,1)S(1)} %dynamic-slice_bitcast_fusion), channel_id=1, source_target_pairs={{0,16},{2,18},{4,20},{6,22},{8,24},{10,26},{12,28},{14,30},{16,0},... | collective-permute-start | bytes 786440 | tf_op jit(solution)/shard_map/ppermute | solution.py:31
  167.3 25.7 %collective-permute-start.17 = (f32[1,128,16]{2,1,0:T(8,128)S(1)}, f32[1,128,16]{2,1,0:T(8,128)S(1)}, u32[]{:S(2)}, u32[]{:S(2)}) collective-permute-start(f32[1,128,16]{2,1,0:T(8,128)S(1)} %multiply_bitcast_fusion), channel_id=1, source_target_pairs={{0,16},{2,18},{4,20},{6,22},{8,24},{10,26},{12,28},{14,30},{16,0},... | collective-permute-start | bytes 24584 | tf_op jit(solution)/shard_map/ppermute | solution.py:31
  194.0 47.2 %all-to-all-start.4 = ((bf16[16,128,512]{2,1,0:T(8,128)(2,1)}), bf16[16,128,512]{2,1,0:T(8,128)(2,1)S(1)}, u32[]{:S(2)}, u32[]{:S(2)}) async-start(bf16[16,128,512]{2,1,0:T(8,128)(2,1)} %get-tuple-element.93), calls=%async_computation.4 | async-start | bytes 4194304 | tf_op jit(solution)/shard_map/all_to_all | solution.py:455
  203.3 10.3 %collective-permute-start.18 = (bf16[2,72,1024]{2,1,0:T(8,128)(2,1)S(1)}, bf16[2,72,1024]{2,1,0:T(8,128)(2,1)S(1)}, u32[]{:S(2)}, u32[]{:S(2)}) collective-permute-start(bf16[2,72,1024]{2,1,0:T(8,128)(2,1)S(1)} %get-tuple-element.119), channel_id=1, source_target_pairs={{0,2},{2,0},{4,6},{6,4},{8,10},{10,8},{12,14},{14,12},{16,18},{18,... | collective-permute-start | bytes 884744 | tf_op jit(solution)/shard_map/ppermute | solution.py:31
  205.2 23.0 %collective-permute-start.19 = (bf16[2,72,1024]{2,1,0:T(8,128)(2,1)S(1)}, bf16[2,72,1024]{2,1,0:T(8,128)(2,1)S(1)}, u32[]{:S(2)}, u32[]{:S(2)}) collective-permute-start(bf16[2,72,1024]{2,1,0:T(8,128)(2,1)S(1)} %get-tuple-element.120), channel_id=1, source_target_pairs={{0,4},{2,6},{4,0},{6,2},{8,12},{10,14},{12,8},{14,10},{16,20},{18,... | collective-permute-start | bytes 884744 | tf_op jit(solution)/shard_map/ppermute | solution.py:31
  206.7 34.6 %collective-permute-start.20 = (bf16[2,72,1024]{2,1,0:T(8,128)(2,1)S(1)}, bf16[2,72,1024]{2,1,0:T(8,128)(2,1)}, u32[]{:S(2)}, u32[]{:S(2)}) collective-permute-start(bf16[2,72,1024]{2,1,0:T(8,128)(2,1)S(1)} %get-tuple-element.121), channel_id=1, source_target_pairs={{0,6},{2,4},{4,2},{6,0},{8,14},{10,12},{12,10},{14,8},{16,22},{18,... | collective-permute-start | bytes 884744 | tf_op jit(solution)/shard_map/ppermute | solution.py:31
  207.7 49.7 %collective-permute-start.22 = (bf16[2,72,1024]{2,1,0:T(8,128)(2,1)}, bf16[2,72,1024]{2,1,0:T(8,128)(2,1)}, u32[]{:S(2)}, u32[]{:S(2)}) collective-permute-start(bf16[2,72,1024]{2,1,0:T(8,128)(2,1)} %get-tuple-element.124), channel_id=1, source_target_pairs={{0,10},{2,8},{4,14},{6,12},{8,2},{10,0},{12,6},{14,4},{16,26},{18,... | collective-permute-start | bytes 884744 | tf_op jit(solution)/shard_map/ppermute | solution.py:31
  210.5 45.2 %collective-permute-start.21 = (bf16[2,72,1024]{2,1,0:T(8,128)(2,1)}, bf16[2,72,1024]{2,1,0:T(8,128)(2,1)}, u32[]{:S(2)}, u32[]{:S(2)}) collective-permute-start(bf16[2,72,1024]{2,1,0:T(8,128)(2,1)} %get-tuple-element.122), channel_id=1, source_target_pairs={{0,8},{2,10},{4,12},{6,14},{8,0},{10,2},{12,4},{14,6},{16,24},{18,... | collective-permute-start | bytes 884744 | tf_op jit(solution)/shard_map/ppermute | solution.py:31
  213.6 15.7 %copy-start.24 = (bf16[2,72,1024]{2,1,0:T(8,128)(2,1)}, bf16[2,72,1024]{2,1,0:T(8,128)(2,1)S(1)}, u32[]{:S(2)}) copy-start(bf16[2,72,1024]{2,1,0:T(8,128)(2,1)S(1)} %collective-permute-done.18) | copy-start | bytes 884740
  213.6 47.0 %collective-permute-start.23 = (bf16[2,72,1024]{2,1,0:T(8,128)(2,1)}, bf16[2,72,1024]{2,1,0:T(8,128)(2,1)}, u32[]{:S(2)}, u32[]{:S(2)}) collective-permute-start(bf16[2,72,1024]{2,1,0:T(8,128)(2,1)} %get-tuple-element.123), channel_id=1, source_target_pairs={{0,12},{2,14},{4,8},{6,10},{8,4},{10,6},{12,0},{14,2},{16,28},{18,... | collective-permute-start | bytes 884744 | tf_op jit(solution)/shard_map/ppermute | solution.py:31
  228.2 1.1 copy-start.25
  228.2 43.2 %collective-permute-start.24 = (bf16[2,72,1024]{2,1,0:T(8,128)(2,1)}, bf16[2,72,1024]{2,1,0:T(8,128)(2,1)}, u32[]{:S(2)}, u32[]{:S(2)}) collective-permute-start(bf16[2,72,1024]{2,1,0:T(8,128)(2,1)} %get-tuple-element.117), channel_id=1, source_target_pairs={{0,14},{2,12},{4,10},{6,8},{8,6},{10,4},{12,2},{14,0},{16,30},{18,... | collective-permute-start | bytes 884744 | tf_op jit(solution)/shard_map/ppermute | solution.py:31
  241.3 11.0 %copy-start.10 = (bf16[16,128,512]{2,1,0:T(8,128)(2,1)}, bf16[16,128,512]{2,1,0:T(8,128)(2,1)S(1)}, u32[]{:S(2)}) copy-start(bf16[16,128,512]{2,1,0:T(8,128)(2,1)S(1)} %all-to-all-done.4) | copy-start | bytes 6291460
  241.3 57.1 %all-to-all-start.5 = ((bf16[16,128,512]{2,1,0:T(8,128)(2,1)}), bf16[16,128,512]{2,1,0:T(8,128)(2,1)}, u32[]{:S(2)}, u32[]{:S(2)}) async-start(bf16[16,128,512]{2,1,0:T(8,128)(2,1)} %get-tuple-element.101), calls=%async_computation.5 | async-start | bytes 4194304 | tf_op jit(solution)/shard_map/all_to_all | solution.py:455
  273.1 4.1 %copy-start.15 = (bf16[8,2,72,1024]{3,2,0,1:T(8,128)(2,1)S(1)}, bf16[8,2,72,1024]{3,2,0,1:T(8,128)(2,1)}, u32[]{:S(2)}) copy-start(bf16[8,2,72,1024]{3,2,0,1:T(8,128)(2,1)} %bitcast_dynamic-update-slice_fusion) | copy-start | bytes 7077892
  277.6 2.9 copy-start.12
  277.6 9.8 %copy-start.11 = (bf16[8,1,1,72,1024]{4,3,0,2,1:T(8,128)(2,1)}, bf16[8,1,1,72,1024]{4,3,0,2,1:T(8,128)(2,1)S(1)}, u32[]{:S(2)}) copy-start(bf16[8,1,1,72,1024]{4,3,0,2,1:T(8,128)(2,1)S(1)} %get-tuple-element.116) | copy-start | bytes 3538948
  277.6 2.9 collective-permute-start.26
  277.7 9.7 %collective-permute-start.25 = (bf16[1,576,1024]{2,1,0:T(8,128)(2,1)S(1)}, bf16[1,576,1024]{2,1,0:T(8,128)(2,1)S(1)}, u32[]{:S(2)}, u32[]{:S(2)}) collective-permute-start(bf16[1,576,1024]{2,1,0:T(8,128)(2,1)S(1)} %bitcast.162), channel_id=1, source_target_pairs={{1,0},{0,1},{3,2},{2,3},{5,4},{4,5},{7,6},{6,7},{9,8},{8,9},{11,10... | collective-permute-start | bytes 3538952 | tf_op jit(solution)/shard_map/ppermute | solution.py:26
  302.9 3.1 collective-permute-start.27
  307.5 20.1 %all-to-all-start.6 = ((bf16[8,1,72,1024]{3,2,1,0:T(8,128)(2,1)}), bf16[8,1,72,1024]{3,2,1,0:T(8,128)(2,1)S(1)}, u32[]{:S(2)}, u32[]{:S(2)}) async-start(bf16[8,1,72,1024]{3,2,1,0:T(8,128)(2,1)} %bitcast.61), calls=%async_computation.6 | async-start | bytes 2359296 | tf_op jit(solution)/shard_map/all_to_all | solution.py:693
  315.9 3.1 collective-permute-start.28
  328.5 24.4 %all-to-all-start.7 = ((bf16[8,1,72,1024]{3,2,1,0:T(8,128)(2,1)}), bf16[8,1,72,1024]{3,2,1,0:T(8,128)(2,1)S(1)}, u32[]{:S(2)}, u32[]{:S(2)}) async-start(bf16[8,1,72,1024]{3,2,1,0:T(8,128)(2,1)} %bitcast.65), calls=%async_computation.7 | async-start | bytes 2359296 | tf_op jit(solution)/shard_map/all_to_all | solution.py:693
  332.6 21.0 %copy-start.8 = (f32[128,2048]{1,0:T(8,128)S(1)}, f32[128,2048]{1,0:T(8,128)}, u32[]{:S(2)}) copy-start(f32[128,2048]{1,0:T(8,128)} %copy-done.7) | copy-start | bytes 3145732
  332.9 20.8 %collective-permute-start.29 = (bf16[128,1024]{1,0:T(8,128)(2,1)S(1)}, bf16[128,1024]{1,0:T(8,128)(2,1)S(1)}, u32[]{:S(2)}, u32[]{:S(2)}) collective-permute-start(bf16[128,1024]{1,0:T(8,128)(2,1)S(1)} %slice_add_fusion.2), channel_id=1, source_target_pairs={{0,16},{2,18},{4,20},{6,22},{8,24},{10,26},{12,28},{14,30},{16,0},... | collective-permute-start | bytes 786440 | tf_op jit(solution)/shard_map/ppermute | solution.py:31
  (4 other events, 4.2 us)

commit v9 on v8

--- a/solution.py
+++ b/solution.py
@@ -120,14 +120,15 @@
     half = gate_ref.shape[2] // 2
     outs[0][...] = gate_ref[:, :, :half].astype(jnp.bfloat16)
     outs[1][...] = gate_ref[:, :, half:].astype(jnp.bfloat16)
-    outs[2][...] = up_ref[...].astype(jnp.bfloat16)
-    outs[3][...] = down_ref[...].astype(jnp.bfloat16)
+    outs[2][...] = up_ref[:, :, :half].astype(jnp.bfloat16)
+    outs[3][...] = up_ref[:, :, half:].astype(jnp.bfloat16)
+    outs[4][...] = down_ref[...].astype(jnp.bfloat16)
 
 
 def order_experts(layout_map, gate, up, down):
     count, rows, width = gate.shape
     source = pl.BlockSpec((1, rows, width), lambda place, order: (order[place], 0, 0))
-    widths = (width // 2, width - width // 2, width, width)
+    widths = (width // 2, width // 2, width // 2, width // 2, width)
     return pl.pallas_call(
         order_body,
         grid_spec=pltpu.PrefetchScalarGridSpec(
@@ -295,21 +296,28 @@
 
 
 def hidden_body(turn_count, share, start_ref, *refs):
-    rows, (first_ref, second_ref, up_ref, out_ref) = (refs[:turn_count], refs[turn_count:])
-    first = second = up = 0.0
-    for turn in range(turn_count):
-        here = pl.ds(pl.multiple_of(start_ref[turn], share), share)
-        some = rows[turn][0]
-        first = first + jnp.dot(some, first_ref[0, here, :], preferred_element_type=jnp.float32)
-        second = second + jnp.dot(some, second_ref[0, here, :], preferred_element_type=jnp.float32)
-        up = up + jnp.dot(some, up_ref[0, here, :], preferred_element_type=jnp.float32)
-    gate = jnp.concatenate([first, second], axis=1)
-    out_ref[0] = (gate / (1.0 + jnp.exp(-gate)) * up).astype(jnp.bfloat16)
+    rows, weights, out_ref = (refs[:turn_count], refs[turn_count:-1], refs[-1])
+    products = []
+    for weight in weights:
+        product = 0.0
+        for turn in range(turn_count):
+            here = pl.ds(pl.multiple_of(start_ref[turn], share), share)
+            product = product + jnp.dot(
+                rows[turn][0], weight[0, here, :], preferred_element_type=jnp.float32
+            )
+        products.append(product)
+    count = len(products) // 2
+    width = out_ref.shape[2] // count
+    for k in range(count):
+        gate, up = (products[k], products[count + k])
+        out_ref[0, :, k * width : (k + 1) * width] = (
+            gate / (1.0 + jnp.exp(-gate)) * up
+        ).astype(jnp.bfloat16)
 
 
 def hidden_units(starts, row_blocks, weights):
     local_experts, row_count, share = row_blocks[0].shape
-    width = weights[-1].shape[2]
+    width = sum(w.shape[2] for w in weights) // 2
     count = len(row_blocks)
     return pl.pallas_call(
         lambda *refs: hidden_body(count, share, *refs),
@@ -424,7 +432,7 @@
     )
     first_rows, first_turns = doubled(share[None], group_masks[:1], 0)
     first_rows, layout_map = lax.optimization_barrier((first_rows, layout_map))
-    own_first, own_second, own_up, own_down = order_experts(
+    own_first, own_second, own_third, own_fourth, own_down = order_experts(
         layout_map, expert_gate, expert_up, expert_down
     )
     part_ids = (part * head_count + (head ^ turns))[:, None] * token_count + offsets[None, :]
@@ -560,14 +568,18 @@
             )
         _, denominator, accumulated = softmax_state
         mixed = (accumulated / denominator).astype(jnp.bfloat16)
+    mixed, own_second, server_first = lax.optimization_barrier((mixed, own_second, server_first))
+    server_second = to_owner(own_second)
     blocks = by_place(mixed.reshape(head_count, token_count, HEAD))
     out_halves = [(half, swapped(half, "seq", masks[0])) for half, masks in out_halves]
-    blocks, out_halves, server_first = lax.optimization_barrier((blocks, out_halves, server_first))
+    blocks, out_halves, server_second = lax.optimization_barrier(
+        (blocks, out_halves, server_second)
+    )
     attention_result = lax.all_to_all(
         blocks, "seq", split_axis=0, concat_axis=0, tiled=True, axis_index_groups=groups
     )
-    attention_result, own_second = lax.optimization_barrier((attention_result, own_second))
-    server_second = to_owner(own_second)
+    attention_result, own_third = lax.optimization_barrier((attention_result, own_third))
+    server_third = to_owner(own_third)
 
     proj_width = head_count * HEAD
     attention_result = jnp.swapaxes(attention_result, 0, 1).reshape(token_count, proj_width)
@@ -625,10 +637,10 @@
     route_weight = route_weight * valid_token[:, None]
     all_weights, _ = doubled(route_weight[None], part_masks, 0)
     all_rows, _ = doubled(outgoing_share[None], part_masks, 0)
-    all_rows, all_weights, server_second, own_up = lax.optimization_barrier(
-        (all_rows, all_weights, server_second, own_up)
-    )
-    server_up = to_owner(own_up)
+    all_rows, all_weights, server_third, own_fourth = lax.optimization_barrier(
+        (all_rows, all_weights, server_third, own_fourth)
+    )
+    server_fourth = to_owner(own_fourth)
     buffer = jnp.stack(
         [
             lax.dot_general(
@@ -648,8 +660,8 @@
         return swapped(block, "seq", m) if m else block
 
     received = [to_mate(m) for m in range(head_count)]
-    received[1:4], server_up, own_down = lax.optimization_barrier(
-        (received[1:4], server_up, own_down)
+    received[1:3], server_fourth, own_down = lax.optimization_barrier(
+        (received[1:3], server_fourth, own_down)
     )
     server_down = to_owner(own_down)
     received = by_place(jnp.stack(received))
@@ -662,8 +674,11 @@
         tp_blocks(jnp.moveaxis(rows, 2, 0).reshape(local_experts, -1, col_share))
         for rows in (received[:, 1:], received[:, :1])
     ]
-    hidden = [hidden_units(in_starts, rows, (server_first, server_second, server_up)) for rows in halves]
-    hidden, server_down = lax.optimization_barrier((hidden, server_down))
+    server = (server_first, server_second, server_third, server_fourth)
+    hidden = [hidden_units(in_starts, rows, server) for rows in halves]
+    hidden[0], halves[1], server_down = lax.optimization_barrier(
+        (hidden[0], halves[1], server_down)
+    )
 
     def through_experts(rows, parts):
         outs = down_rows(out_starts, rows, server_down)

time: 357 us -> 368 us (1.031)
  waiting for transfers between devices: 151 us -> 174 us
  starting transfers between devices: 84.3 us -> 80.1 us
    ppermute x22, waiting for transfers between devices: 101 us -> 118 us  [swapped(): lax.ppermute(value, axis, [(place, place ^ mask) for place in range(count)])]
    all_to_all x4 -> x5, waiting for transfers between devices: 3.96 us -> 14 us  [to_owner(): lax.all_to_all(blocks, 'seq', split_axis=0, concat_axis=0, tiled=True)]
    all_to_all x2, waiting for transfers between devices: 25.3 us -> 19.6 us  [back(): lax.all_to_all(blocks, 'seq', split_axis=0, concat_axis=0, tiled=True, ax...]
    all_to_all x1, starting transfers between devices: 8.42 us -> 3.66 us  [shards(): lax.all_to_all(blocks, 'seq', split_axis=0, concat_axis=0, tiled=True, ax...]
    all_to_all x4 -> x5, starting transfers between devices: 24.4 us -> 23.9 us  [to_owner(): lax.all_to_all(blocks, 'seq', split_axis=0, concat_axis=0, tiled=True)]
  transfers between devices with their start and end apart: 38 -> 39, of which waited for: 20 -> 19; matrix products, arithmetic and copies ran while one was open for 14% -> 12% of each run, Pallas kernels for 13% -> 12%
where the time goes in v9:
time: 368 us; the launch traced here: 365 us
  waiting for transfers between devices  174 us (47%)
  starting transfers between devices  80.1 us (22%)
  Pallas kernels  49.9 us (14%)
  local copies, waits for them, and re-layouts  28.4 us (8%)
  other arithmetic  19.9 us (5%)
  matrix products  11.9 us (3%)
    ppermute x22, waiting for transfers between devices, swapped(): lax.ppermute(value, axis, [(place, place ^ mask) for place in range(count)])  118 us
    ppermute x22, starting transfers between devices, swapped(): lax.ppermute(value, axis, [(place, place ^ mask) for place in range(count)])  33.8 us
    all_to_all x5, starting transfers between devices, to_owner(): lax.all_to_all(blocks, 'seq', split_axis=0, concat_axis=0, tiled=True)  23.9 us
    unnamed x102, local copies, waits for them, and re-layouts  23 us
    all_to_all x2, waiting for transfers between devices, back(): lax.all_to_all(blocks, 'seq', split_axis=0, concat_axis=0, tiled=True, ax...  19.6 us
    all_to_all x5, waiting for transfers between devices, to_owner(): lax.all_to_all(blocks, 'seq', split_axis=0, concat_axis=0, tiled=True)  14 us
    pallas_call x1, Pallas kernels, order_experts(): pl.pallas_call(order_body, grid_spec=pltpu.PrefetchScalarGridSpec(num_sca...  12.9 us
    pallas_call x2, Pallas kernels, hidden_units(): pl.pallas_call(lambda *refs: hidden_body(count, share, *refs), grid_spec=...  11.5 us
  transfers between devices with their start and end apart: 39, of which 19 were waited for; matrix products, arithmetic and copies ran while one was open for 12% of the time, Pallas kernels for 12%

profile of v9, /device:TPU:0, one launch (start us, length us, event | category | flops | bytes accessed | tf_op | source)
XLA Modules:
  0.0 365.5 jit_solution(9837680011847065083)
XLA Ops:
  3.3 3.1 collective-permute-start.2
  6.4 2.6 collective-permute-start.4
  10.6 1.9 pack_heads.1
  12.4 5.9 %all-to-all-start = ((bf16[16,128,384]{2,1,0:T(8,128)(2,1)}), bf16[16,128,384]{2,1,0:T(8,128)(2,1)}, u32[]{:S(2)}, u32[]{:S(2)}) async-start(bf16[16,128,384]{2,1,0:T(8,128)(2,1)} %pack_heads.1), calls=%async_computation | async-start | bytes 3145728 | tf_op jit(solution)/shard_map/all_to_all | solution.py:419
  18.5 3.1 multiply_sine_fusion
  21.7 1.9 collective-permute-start.3
  23.6 1.5 collective-permute-start.6
  25.1 12.9 %order_experts.1 = (bf16[16,128,256]{2,1,0:T(8,128)(2,1)}, bf16[16,128,256]{2,1,0:T(8,128)(2,1)}, bf16[16,128,256]{2,1,0:T(8,128)(2,1)}, bf16[16,128,256]{2,1,0:T(8,128)(2,1)}, bf16[16,128,512]{2,1,0:T(8,128)(2,1)}) custom-call(s32[16]{0:T(128)} %order_ref, f32[16,128,512]{2,1,0:T(8,128)} %gate_ref.1, f32[16,128,512]{2,1,0:T(8,128)} %up_ref.1, ...), custom_call_target="tpu_custom_call" | custom-call | flops 1 | bytes 1 | tf_op jit(solution)/shard_map/order_experts/pallas_call | solution.py:132
  37.9 2.6 collective-permute-done
  40.7 1.6 collective-permute-start.5
  42.5 17.6 %collective-permute-done.1 = bf16[1040,256]{1,0:T(8,128)(2,1)S(1)} collective-permute-done((bf16[1040,256]{1,0:T(8,128)(2,1)S(1)}, bf16[1040,256]{1,0:T(8,128)(2,1)S(1)}, u32[]{:S(2)}, u32[]{:S(2)}) %collective-permute-start.1) | collective-permute-done | bytes 532512 | tf_op jit(solution)/shard_map/ppermute | solution.py:31
  62.5 5.6 %all-to-all-start.1 = ((bf16[16,128,256]{2,1,0:T(8,128)(2,1)}), bf16[16,128,256]{2,1,0:T(8,128)(2,1)S(1)}, u32[]{:S(2)}, u32[]{:S(2)}) async-start(bf16[16,128,256]{2,1,0:T(8,128)(2,1)} %get-tuple-element.78), calls=%async_computation.1 | async-start | bytes 2097152 | tf_op jit(solution)/shard_map/all_to_all | solution.py:463
  71.2 2.0 collective-permute-start.9
  73.3 1.5 collective-permute-start.10
  74.9 18.7 %collective-permute-done.9 = bf16[512,512]{1,0:T(8,128)(2,1)S(1)} collective-permute-done((bf16[512,512]{1,0:T(8,128)(2,1)}, bf16[512,512]{1,0:T(8,128)(2,1)S(1)}, u32[]{:S(2)}, u32[]{:S(2)}) %collective-permute-start.9) | collective-permute-done | bytes 524320 | tf_op jit(solution)/shard_map/ppermute | solution.py:31
  93.6 2.2 pad_maximum_fusion.2
  95.8 5.8 %project.1 = bf16[1024,384]{1,0:T(8,128)(2,1)S(1)} custom-call(s32[2]{0:T(128)S(1)} %fusion.119.refs_0_, bf16[1024,1024]{1,0:T(8,128)(2,1)S(1)} %pad_maximum_fusion.refs_1_, bf16[1024,1024]{1,0:T(8,128)(2,1)} %collective-permute-done.8.refs_2_, bf16[2048,384]{1,0:T(8,128)(2,1)} %bitcast.6.refs_3_, f32[1024,64]{1,0:T(8,128)S(1)} %copy-done.2, ...), custom_call_target="tpu_custom_call" | custom-call | flops 1 | bytes 1 | tf_op jit(solution)/shard_map/project/pallas_call | solution.py:197
  101.6 3.2 collective-permute-start.11
  105.0 1.5 collective-permute-done.11
  106.6 6.7 %attend_once.1 = bf16[1088,128]{1,0:T(8,128)(2,1)S(1)} custom-call(f32[1]{0:T(128)} %dynamic_slice.92.sink_ref, s32[1088,1]{1,0:T(8,128)S(1)} %fusion.13.query_prompt_ref, s32[1,1088]{1,0:T(1,128)S(1)} %and_select_fusion.key_prompt_ref, bf16[1088,384]{1,0:T(8,128)(2,1)S(1)} %pad_maximum_fusion.3.query_ref.key_ref.value_ref, ...), custom_call_target="tpu_custom_call" | custom-call | flops 1 | bytes 1 | tf_op jit(solution)/shard_map/attend_once/pallas_call | solution.py:239
  114.7 5.2 %collective-permute-done.12 = bf16[64,128]{1,0:T(8,128)(2,1)S(1)} collective-permute-done((bf16[64,128]{1,0:T(8,128)(2,1)S(1)}, bf16[64,128]{1,0:T(8,128)(2,1)S(1)}, u32[]{:S(2)}, u32[]{:S(2)}) %collective-permute-start.12) | collective-permute-done | bytes 16416 | tf_op jit(solution)/shard_map/ppermute | solution.py:21
  119.9 4.8 %all-to-all-start.2 = ((bf16[16,128,256]{2,1,0:T(8,128)(2,1)}), bf16[16,128,256]{2,1,0:T(8,128)(2,1)S(1)}, u32[]{:S(2)}, u32[]{:S(2)}) async-start(bf16[16,128,256]{2,1,0:T(8,128)(2,1)} %get-tuple-element.82), calls=%async_computation.2 | async-start | bytes 2097152 | tf_op jit(solution)/shard_map/all_to_all | solution.py:463
  124.7 1.9 collective-permute-start.14
  126.6 1.5 collective-permute-start.13
  128.7 1.5 copy.62
  130.2 1.5 copy.63
  131.7 1.5 copy.64
  133.1 1.5 copy.65
  134.6 1.5 copy.66
  141.6 17.6 %collective-permute-done.13 = bf16[512,1024]{1,0:T(8,128)(2,1)} collective-permute-done((bf16[512,1024]{1,0:T(8,128)(2,1)}, bf16[512,1024]{1,0:T(8,128)(2,1)}, u32[]{:S(2)}, u32[]{:S(2)}) %collective-permute-start.13) | collective-permute-done | bytes 1048608 | tf_op jit(solution)/shard_map/ppermute | solution.py:31
  159.9 3.7 %all-to-all-start.3 = ((bf16[8,128,128]{1,2,0:T(8,128)(2,1)}), bf16[8,128,128]{1,2,0:T(8,128)(2,1)S(1)}, u32[]{:S(2)}, u32[]{:S(2)}) async-start(bf16[8,128,128]{1,2,0:T(8,128)(2,1)} %copy-done.23), calls=%async_computation.3 | async-start | bytes 524288 | tf_op jit(solution)/shard_map/all_to_all | solution.py:578
  163.7 6.5 %all-to-all-done.3 = bf16[8,128,128]{1,2,0:T(8,128)(2,1)S(1)} async-done(((bf16[8,128,128]{1,2,0:T(8,128)(2,1)}), bf16[8,128,128]{1,2,0:T(8,128)(2,1)S(1)}, u32[]{:S(2)}, u32[]{:S(2)}) %all-to-all-start.3) | async-done | bytes 262176 | tf_op jit(solution)/shard_map/all_to_all | solution.py:578
  170.2 2.5 fusion.8
  175.0 2.4 fusion.63
  177.3 4.5 %all-to-all-start.4 = ((bf16[16,128,256]{2,1,0:T(8,128)(2,1)}), bf16[16,128,256]{2,1,0:T(8,128)(2,1)}, u32[]{:S(2)}, u32[]{:S(2)}) async-start(bf16[16,128,256]{2,1,0:T(8,128)(2,1)} %get-tuple-element.94), calls=%async_computation.4 | async-start | bytes 2097152 | tf_op jit(solution)/shard_map/all_to_all | solution.py:463
  184.0 1.8 collective-permute-done.15.refs_2_
  185.8 1.9 settle.1
  188.8 2.7 collective-permute-start.16
  192.3 27.4 %collective-permute-done.17 = f32[1,128,16]{2,1,0:T(8,128)S(1)} collective-permute-done((f32[1,128,16]{2,1,0:T(8,128)S(1)}, f32[1,128,16]{2,1,0:T(8,128)S(1)}, u32[]{:S(2)}, u32[]{:S(2)}) %collective-permute-start.17) | collective-permute-done | bytes 8224 | tf_op jit(solution)/shard_map/ppermute | solution.py:31
  219.9 4.7 %all-to-all-start.5 = ((bf16[16,128,256]{2,1,0:T(8,128)(2,1)}), bf16[16,128,256]{2,1,0:T(8,128)(2,1)}, u32[]{:S(2)}, u32[]{:S(2)}) async-start(bf16[16,128,256]{2,1,0:T(8,128)(2,1)} %get-tuple-element.98), calls=%async_computation.5 | async-start | bytes 2097152 | tf_op jit(solution)/shard_map/all_to_all | solution.py:463
  227.3 1.9 collective-permute-start.18
  229.2 1.5 collective-permute-start.19
  231.5 1.5 collective-permute-start.22
  233.0 1.5 collective-permute-start.20
  235.0 17.0 %collective-permute-done.18 = bf16[2,72,1024]{2,1,0:T(8,128)(2,1)S(1)} collective-permute-done((bf16[2,72,1024]{2,1,0:T(8,128)(2,1)S(1)}, bf16[2,72,1024]{2,1,0:T(8,128)(2,1)S(1)}, u32[]{:S(2)}, u32[]{:S(2)}) %collective-permute-start.18) | collective-permute-done | bytes 294944 | tf_op jit(solution)/shard_map/ppermute | solution.py:31
  252.0 2.7 collective-permute-start.23
  256.7 4.4 %all-to-all-start.6 = ((bf16[16,128,512]{2,1,0:T(8,128)(2,1)}), bf16[16,128,512]{2,1,0:T(8,128)(2,1)}, u32[]{:S(2)}, u32[]{:S(2)}) async-start(bf16[16,128,512]{2,1,0:T(8,128)(2,1)} %get-tuple-element.106), calls=%async_computation.6 | async-start | bytes 4194304 | tf_op jit(solution)/shard_map/all_to_all | solution.py:463
  266.2 8.9 %collective-permute-done.23 = bf16[2,72,1024]{2,1,0:T(8,128)(2,1)} collective-permute-done((bf16[2,72,1024]{2,1,0:T(8,128)(2,1)}, bf16[2,72,1024]{2,1,0:T(8,128)(2,1)}, u32[]{:S(2)}, u32[]{:S(2)}) %collective-permute-start.23) | collective-permute-done | bytes 294944 | tf_op jit(solution)/shard_map/ppermute | solution.py:31
  276.1 7.6 %collective-permute-done.24 = bf16[2,72,1024]{2,1,0:T(8,128)(2,1)} collective-permute-done((bf16[2,72,1024]{2,1,0:T(8,128)(2,1)}, bf16[2,72,1024]{2,1,0:T(8,128)(2,1)}, u32[]{:S(2)}, u32[]{:S(2)}) %collective-permute-start.24) | collective-permute-done | bytes 294944 | tf_op jit(solution)/shard_map/ppermute | solution.py:31
  285.8 2.3 collective-permute-done.25.refs_2_
  289.2 5.7 %hidden_units.2.refs_1_ = bf16[1,576,512]{2,1,0:T(8,128)(2,1)S(1)} custom-call(s32[2]{0:T(128)S(1)} %fusion.119.refs_0_, bf16[1,576,1024]{2,1,0:T(8,128)(2,1)} %bitcast.166, bf16[1,576,1024]{2,1,0:T(8,128)(2,1)} %copy-done.22, bf16[1,2048,256]{2,1,0:T(8,128)(2,1)S(1)} %bitcast.154, bf16[1,2048,256]{2,1,0:T(8,128)(2,1)} %bitcast.161, ...), custom_call_target="tpu_custom_call" | custom-call | flops 1 | bytes 1 | tf_op jit(solution)/shard_map/hidden_units/pallas_call | solution.py:322
  295.0 14.0 %all-to-all-done.6 = bf16[16,128,512]{2,1,0:T(8,128)(2,1)} async-done(((bf16[16,128,512]{2,1,0:T(8,128)(2,1)}), bf16[16,128,512]{2,1,0:T(8,128)(2,1)}, u32[]{:S(2)}, u32[]{:S(2)}) %all-to-all-start.6) | async-done | bytes 2097184 | tf_op jit(solution)/shard_map/all_to_all | solution.py:463
  308.9 4.6 %down_rows.2 = (bf16[1,576,1024]{2,1,0:T(8,128)(2,1)S(1)}, bf16[1,576,1024]{2,1,0:T(8,128)(2,1)}) custom-call(s32[2]{0:T(128)S(1)} %fusion.120.refs_0_, bf16[1,576,512]{2,1,0:T(8,128)(2,1)S(1)} %hidden_units.2.refs_1_, bf16[1,2048,512]{2,1,0:T(8,128)(2,1)} %bitcast.60.refs_2_), custom_call_target="tpu_custom_call" | custom-call | flops 1 | bytes 1 | tf_op jit(solution)/shard_map/down_rows/pallas_call | solution.py:354
  313.6 3.1 collective-permute-done.27
  316.6 1.5 add_convert_fusion.1
  318.1 3.6 all-to-all-start.7
  321.7 5.7 %hidden_units.3.refs_1_ = bf16[1,576,512]{2,1,0:T(8,128)(2,1)S(1)} custom-call(s32[2]{0:T(128)S(1)} %fusion.119.refs_0_, bf16[1,576,1024]{2,1,0:T(8,128)(2,1)} %bitcast.164, bf16[1,576,1024]{2,1,0:T(8,128)(2,1)} %copy-done.21, bf16[1,2048,256]{2,1,0:T(8,128)(2,1)S(1)} %bitcast.155, bf16[1,2048,256]{2,1,0:T(8,128)(2,1)} %bitcast.162, ...), custom_call_target="tpu_custom_call" | custom-call | flops 1 | bytes 1 | tf_op jit(solution)/shard_map/hidden_units/pallas_call | solution.py:322
  327.5 4.6 %down_rows.3 = (bf16[1,576,1024]{2,1,0:T(8,128)(2,1)S(1)}, bf16[1,576,1024]{2,1,0:T(8,128)(2,1)}) custom-call(s32[2]{0:T(128)S(1)} %fusion.120.refs_0_, bf16[1,576,512]{2,1,0:T(8,128)(2,1)S(1)} %hidden_units.3.refs_1_, bf16[1,2048,512]{2,1,0:T(8,128)(2,1)} %bitcast.60.refs_2_), custom_call_target="tpu_custom_call" | custom-call | flops 1 | bytes 1 | tf_op jit(solution)/shard_map/down_rows/pallas_call | solution.py:354
  333.1 2.1 collective-permute-done.28
  335.2 1.5 add_convert_fusion
  336.7 1.5 all-to-all-done.7
  339.1 3.9 %all-to-all-start.8 = ((bf16[8,1,72,1024]{3,2,1,0:T(8,128)(2,1)}), bf16[8,1,72,1024]{3,2,1,0:T(8,128)(2,1)S(1)}, u32[]{:S(2)}, u32[]{:S(2)}) async-start(bf16[8,1,72,1024]{3,2,1,0:T(8,128)(2,1)} %bitcast.66), calls=%async_computation.8 | async-start | bytes 2359296 | tf_op jit(solution)/shard_map/all_to_all | solution.py:708
  343.9 1.8 collective-permute-start.29
  345.7 18.1 %all-to-all-done.8 = bf16[8,1,72,1024]{3,2,1,0:T(8,128)(2,1)S(1)} async-done(((bf16[8,1,72,1024]{3,2,1,0:T(8,128)(2,1)}), bf16[8,1,72,1024]{3,2,1,0:T(8,128)(2,1)S(1)}, u32[]{:S(2)}, u32[]{:S(2)}) %all-to-all-start.8) | async-done | bytes 1179680 | tf_op jit(solution)/shard_map/all_to_all | solution.py:708
  (217 shorter events, 45.3 us)
Async XLA Ops:
  0.0 6.4 %copy-start.27 = (s32[128,8]{0,1:T(8,128)S(1)}, s32[128,8]{0,1:T(8,128)}, u32[]{:S(2)}) copy-start(s32[128,8]{0,1:T(8,128)} %param.29) | copy-start | bytes 12292
  0.0 10.1 %copy-start.26 = (f32[128,16]{0,1:T(8,128)S(1)}, f32[128,16]{0,1:T(8,128)}, u32[]{:S(2)}) copy-start(f32[128,16]{0,1:T(8,128)} %param.23) | copy-start | bytes 24580
  0.0 10.6 %copy-start.3 = (f32[128,1024]{1,0:T(8,128)S(1)}, f32[128,1024]{1,0:T(8,128)}, u32[]{:S(2)}) copy-start(f32[128,1024]{1,0:T(8,128)} %query_ref.1) | copy-start | bytes 1572868
  0.0 10.6 %copy-start.4 = (f32[128,1024]{1,0:T(8,128)S(1)}, f32[128,1024]{1,0:T(8,128)}, u32[]{:S(2)}) copy-start(f32[128,1024]{1,0:T(8,128)} %key_ref.1) | copy-start | bytes 1572868
  0.0 10.6 %copy-start.5 = (f32[128,1024]{1,0:T(8,128)S(1)}, f32[128,1024]{1,0:T(8,128)}, u32[]{:S(2)}) copy-start(f32[128,1024]{1,0:T(8,128)} %value_ref.1) | copy-start | bytes 1572868
  3.3 18.2 %collective-permute-start.2 = (bf16[1,128,1024]{2,1,0:T(8,128)(2,1)S(1)}, bf16[1,128,1024]{2,1,0:T(8,128)(2,1)S(1)}, u32[]{:S(2)}, u32[]{:S(2)}) collective-permute-start(bf16[1,128,1024]{2,1,0:T(8,128)(2,1)S(1)} %fusion.48), channel_id=1, source_target_pairs={{0,8},{2,10},{4,12},{6,14},{8,0},{10,2},{12,4},{14,6},{16,24},{18,... | collective-permute-start | bytes 786440 | tf_op jit(solution)/shard_map/ppermute | solution.py:31
  6.4 17.1 %collective-permute-start.4 = (s32[1,128,8]{1,2,0:T(8,128)S(1)}, s32[1,128,8]{1,2,0:T(8,128)S(1)}, u32[]{:S(2)}, u32[]{:S(2)}) collective-permute-start(s32[1,128,8]{1,2,0:T(8,128)S(1)} %bitcast.177), channel_id=1, source_target_pairs={{0,16},{2,18},{4,20},{6,22},{8,24},{10,26},{12,28},{14,30},{16,0},... | collective-permute-start | bytes 12296 | tf_op jit(solution)/shard_map/ppermute | solution.py:31
  10.2 30.3 %collective-permute-start = (bf16[1040,128]{1,0:T(8,128)(2,1)S(1)}, bf16[1040,128]{1,0:T(8,128)(2,1)S(1)}, u32[]{:S(2)}, u32[]{:S(2)}) collective-permute-start(bf16[1040,128]{1,0:T(8,128)(2,1)S(1)} %pad_maximum_fusion.13), channel_id=1, source_target_pairs={{0,16},{2,18},{4,20},{6,22},{8,24},{10,26},{12,28},{14,30},{16,0},... | collective-permute-start | bytes 798728 | tf_op jit(solution)/shard_map/ppermute | solution.py:31
  12.4 49.9 %all-to-all-start = ((bf16[16,128,384]{2,1,0:T(8,128)(2,1)}), bf16[16,128,384]{2,1,0:T(8,128)(2,1)}, u32[]{:S(2)}, u32[]{:S(2)}) async-start(bf16[16,128,384]{2,1,0:T(8,128)(2,1)} %pack_heads.1), calls=%async_computation | async-start | bytes 3145728 | tf_op jit(solution)/shard_map/all_to_all | solution.py:419
  21.7 19.0 %collective-permute-start.3 = (bf16[2,128,512]{2,1,0:T(8,128)(2,1)S(1)}, bf16[2,128,512]{2,1,0:T(8,128)(2,1)S(1)}, u32[]{:S(2)}, u32[]{:S(2)}) collective-permute-start(bf16[2,128,512]{2,1,0:T(8,128)(2,1)S(1)} %get-tuple-element.137), channel_id=1, source_target_pairs={{0,4},{2,6},{4,0},{6,2},{8,12},{10,14},{12,8},{14,10},{16,20},{18,... | collective-permute-start | bytes 786440 | tf_op jit(solution)/shard_map/ppermute | solution.py:31
  23.6 18.7 %collective-permute-start.6 = (bf16[2,128,512]{2,1,0:T(8,128)(2,1)S(1)}, bf16[2,128,512]{2,1,0:T(8,128)(2,1)S(1)}, u32[]{:S(2)}, u32[]{:S(2)}) collective-permute-start(bf16[2,128,512]{2,1,0:T(8,128)(2,1)S(1)} %get-tuple-element.138), channel_id=1, source_target_pairs={{0,2},{2,0},{4,6},{6,4},{8,10},{10,8},{12,14},{14,12},{16,18},{18,... | collective-permute-start | bytes 786440 | tf_op jit(solution)/shard_map/ppermute | solution.py:31
  40.5 19.6 %collective-permute-start.1 = (bf16[1040,256]{1,0:T(8,128)(2,1)S(1)}, bf16[1040,256]{1,0:T(8,128)(2,1)S(1)}, u32[]{:S(2)}, u32[]{:S(2)}) collective-permute-start(bf16[1040,256]{1,0:T(8,128)(2,1)S(1)} %pad_maximum_fusion.7), channel_id=1, source_target_pairs={{0,8},{2,10},{4,12},{6,14},{8,0},{10,2},{12,4},{14,6},{16,24},{18,... | collective-permute-start | bytes 1597448 | tf_op jit(solution)/shard_map/ppermute | solution.py:31
  40.7 21.1 %collective-permute-start.5 = (bf16[4,128,512]{2,1,0:T(8,128)(2,1)S(1)}, bf16[4,128,512]{2,1,0:T(8,128)(2,1)S(1)}, u32[]{:S(2)}, u32[]{:S(2)}) collective-permute-start(bf16[4,128,512]{2,1,0:T(8,128)(2,1)S(1)} %pad_maximum_fusion.10), channel_id=1, source_target_pairs={{0,2},{2,0},{4,6},{6,4},{8,10},{10,8},{12,14},{14,12},{16,18},{18,... | collective-permute-start | bytes 1572872 | tf_op jit(solution)/shard_map/ppermute | solution.py:31
  42.4 19.5 %collective-permute-start.7 = (bf16[4,128,512]{2,1,0:T(8,128)(2,1)S(1)}, bf16[4,128,512]{2,1,0:T(8,128)(2,1)S(1)}, u32[]{:S(2)}, u32[]{:S(2)}) collective-permute-start(bf16[4,128,512]{2,1,0:T(8,128)(2,1)S(1)} %pad_maximum_fusion.11), channel_id=1, source_target_pairs={{0,4},{2,6},{4,0},{6,2},{8,12},{10,14},{12,8},{14,10},{16,20},{18,... | collective-permute-start | bytes 1572872 | tf_op jit(solution)/shard_map/ppermute | solution.py:31
  62.3 6.9 %copy-start.29 = (f32[8]{0:T(128)S(1)}, f32[8]{0:T(128)}, u32[]{:S(2)}) copy-start(f32[8]{0:T(128)} %param.22) | copy-start | bytes 100
  62.3 10.9 %copy-start.28 = (s32[2]{0:T(128)S(1)}, s32[2]{0:T(128)}, u32[]{:S(2)}) copy-start(s32[2]{0:T(128)} %param.28) | copy-start | bytes 28
  62.3 33.4 %collective-permute-start.8 = (bf16[1024,1024]{1,0:T(8,128)(2,1)S(1)}, bf16[1024,1024]{1,0:T(8,128)(2,1)}, u32[]{:S(2)}, u32[]{:S(2)}) collective-permute-start(bf16[1024,1024]{1,0:T(8,128)(2,1)S(1)} %pad_maximum_fusion.refs_1_), channel_id=1, source_target_pairs={{1,0},{0,1},{3,2},{2,3},{5,4},{4,5},{7,6},{6,7},{9,8},{8,9},{11,10... | collective-permute-start | bytes 6291464 | tf_op jit(solution)/shard_map/ppermute | solution.py:26
  62.5 57.4 %all-to-all-start.1 = ((bf16[16,128,256]{2,1,0:T(8,128)(2,1)}), bf16[16,128,256]{2,1,0:T(8,128)(2,1)S(1)}, u32[]{:S(2)}, u32[]{:S(2)}) async-start(bf16[16,128,256]{2,1,0:T(8,128)(2,1)} %get-tuple-element.78), calls=%async_computation.1 | async-start | bytes 2097152 | tf_op jit(solution)/shard_map/all_to_all | solution.py:463
  69.2 26.5 %copy-start.1 = (f32[1024,64]{1,0:T(8,128)S(1)}, f32[1024,64]{1,0:T(8,128)}, u32[]{:S(2)}) copy-start(f32[1024,64]{1,0:T(8,128)} %get-tuple-element.73.refs_5_) | copy-start | bytes 786436
  69.2 26.5 %copy-start.2 = (f32[1024,64]{1,0:T(8,128)S(1)}, f32[1024,64]{1,0:T(8,128)}, u32[]{:S(2)}) copy-start(f32[1024,64]{1,0:T(8,128)} %get-tuple-element.72.refs_4_) | copy-start | bytes 786436
  71.2 22.3 %collective-permute-start.9 = (bf16[512,512]{1,0:T(8,128)(2,1)}, bf16[512,512]{1,0:T(8,128)(2,1)S(1)}, u32[]{:S(2)}, u32[]{:S(2)}) collective-permute-start(bf16[512,512]{1,0:T(8,128)(2,1)} %pad_maximum_fusion.8), channel_id=1, source_target_pairs={{0,4},{2,6},{4,0},{6,2},{8,12},{10,14},{12,8},{14,10},{16,20},{18,... | collective-permute-start | bytes 1572872 | tf_op jit(solution)/shard_map/ppermute | solution.py:31
  73.3 31.5 %collective-permute-start.10 = (bf16[528,512]{1,0:T(8,128)(2,1)}, bf16[528,512]{1,0:T(8,128)(2,1)S(1)}, u32[]{:S(2)}, u32[]{:S(2)}) collective-permute-start(bf16[528,512]{1,0:T(8,128)(2,1)} %pad_maximum_fusion.4), channel_id=1, source_target_pairs={{0,2},{2,0},{4,6},{6,4},{8,10},{10,8},{12,14},{14,12},{16,18},{18,... | collective-permute-start | bytes 1622024 | tf_op jit(solution)/shard_map/ppermute | solution.py:31
  95.8 9.1 %copy-start.14 = (bf16[528,512]{1,0:T(8,128)(2,1)S(1)}, bf16[528,512]{1,0:T(8,128)(2,1)}, u32[]{:S(2)}) copy-start(bf16[528,512]{1,0:T(8,128)(2,1)} %pad_maximum_fusion.4) | copy-start | bytes 1622020
  101.6 4.9 %collective-permute-start.11 = (bf16[64,384]{1,0:T(8,128)(2,1)S(1)}, bf16[64,384]{1,0:T(8,128)(2,1)S(1)}, u32[]{:S(2)}, u32[]{:S(2)}) collective-permute-start(bf16[64,384]{1,0:T(8,128)(2,1)S(1)} %constant_dynamic-slice_fusion.8), channel_id=1, source_target_pairs={{0,16},{2,18},{4,20},{6,22},{8,24},{10,26},{12,28},{14,30},{1,17},... | collective-permute-start | bytes 147464 | tf_op jit(solution)/shard_map/ppermute | solution.py:21
  105.0 67.7 %copy-start.12 = (bf16[528,1024]{1,0:T(8,128)(2,1)}, bf16[528,1024]{1,0:T(8,128)(2,1)S(1)}, u32[]{:S(2)}) copy-start(bf16[528,1024]{1,0:T(8,128)(2,1)S(1)} %pad_maximum_fusion.1) | copy-start | bytes 3244036
  113.3 6.5 %collective-permute-start.12 = (bf16[64,128]{1,0:T(8,128)(2,1)S(1)}, bf16[64,128]{1,0:T(8,128)(2,1)S(1)}, u32[]{:S(2)}, u32[]{:S(2)}) collective-permute-start(bf16[64,128]{1,0:T(8,128)(2,1)S(1)} %slice.207), channel_id=1, source_target_pairs={{16,0},{18,2},{20,4},{22,6},{24,8},{26,10},{28,12},{30,14},{17,1},... | collective-permute-start | bytes 49160 | tf_op jit(solution)/shard_map/ppermute | solution.py:21
  119.9 40.0 %all-to-all-start.2 = ((bf16[16,128,256]{2,1,0:T(8,128)(2,1)}), bf16[16,128,256]{2,1,0:T(8,128)(2,1)S(1)}, u32[]{:S(2)}, u32[]{:S(2)}) async-start(bf16[16,128,256]{2,1,0:T(8,128)(2,1)} %get-tuple-element.82), calls=%async_computation.2 | async-start | bytes 2097152 | tf_op jit(solution)/shard_map/all_to_all | solution.py:463
  124.7 35.2 %collective-permute-start.14 = (bf16[528,1024]{1,0:T(8,128)(2,1)S(1)}, bf16[528,1024]{1,0:T(8,128)(2,1)}, u32[]{:S(2)}, u32[]{:S(2)}) collective-permute-start(bf16[528,1024]{1,0:T(8,128)(2,1)S(1)} %pad_maximum_fusion.1), channel_id=1, source_target_pairs={{0,4},{2,6},{4,0},{6,2},{8,12},{10,14},{12,8},{14,10},{16,20},{18,... | collective-permute-start | bytes 3244040 | tf_op jit(solution)/shard_map/ppermute | solution.py:31
  126.6 32.7 %collective-permute-start.13 = (bf16[512,1024]{1,0:T(8,128)(2,1)}, bf16[512,1024]{1,0:T(8,128)(2,1)}, u32[]{:S(2)}, u32[]{:S(2)}) collective-permute-start(bf16[512,1024]{1,0:T(8,128)(2,1)} %pad_maximum_fusion.2), channel_id=1, source_target_pairs={{0,2},{2,0},{4,6},{6,4},{8,10},{10,8},{12,14},{14,12},{16,18},{18,... | collective-permute-start | bytes 3145736 | tf_op jit(solution)/shard_map/ppermute | solution.py:31
  141.6 18.3 %copy-start.23 = (bf16[8,128,128]{1,2,0:T(8,128)(2,1)}, bf16[8,128,128]{1,2,0:T(8,128)(2,1)S(1)}, u32[]{:S(2)}) copy-start(bf16[8,128,128]{1,2,0:T(8,128)(2,1)S(1)} %constant_dynamic-update-slice_fusion) | copy-start | bytes 786436
  159.9 15.0 %copy-start.9 = (bf16[16,128,256]{2,1,0:T(8,128)(2,1)}, bf16[16,128,256]{2,1,0:T(8,128)(2,1)S(1)}, u32[]{:S(2)}) copy-start(bf16[16,128,256]{2,1,0:T(8,128)(2,1)S(1)} %all-to-all-done.2) | copy-start | bytes 3145732
  159.9 10.3 %all-to-all-start.3 = ((bf16[8,128,128]{1,2,0:T(8,128)(2,1)}), bf16[8,128,128]{1,2,0:T(8,128)(2,1)S(1)}, u32[]{:S(2)}, u32[]{:S(2)}) async-start(bf16[8,128,128]{1,2,0:T(8,128)(2,1)} %copy-done.23), calls=%async_computation.3 | async-start | bytes 524288 | tf_op jit(solution)/shard_map/all_to_all | solution.py:578
  170.2 3.6 copy-start.13
  173.8 8.0 %copy-start.17 = (f32[128,1024]{1,0:T(8,128)S(1)}, f32[128,1024]{1,0:T(8,128)}, u32[]{:S(2)}) copy-start(f32[128,1024]{1,0:T(8,128)} %fusion.8) | copy-start | bytes 1572868
  177.3 4.5 %copy-start.18 = (f32[128,1024]{1,0:T(8,128)S(1)}, f32[128,1024]{1,0:T(8,128)}, u32[]{:S(2)}) copy-start(f32[128,1024]{1,0:T(8,128)} %fusion.10) | copy-start | bytes 1572868
  177.3 4.6 %copy-start.15 = (f32[128,1024]{1,0:T(8,128)S(1)}, f32[128,1024]{1,0:T(8,128)}, u32[]{:S(2)}) copy-start(f32[128,1024]{1,0:T(8,128)} %fusion.65) | copy-start | bytes 1572868
  177.3 42.6 %all-to-all-start.4 = ((bf16[16,128,256]{2,1,0:T(8,128)(2,1)}), bf16[16,128,256]{2,1,0:T(8,128)(2,1)}, u32[]{:S(2)}, u32[]{:S(2)}) async-start(bf16[16,128,256]{2,1,0:T(8,128)(2,1)} %get-tuple-element.94), calls=%async_computation.4 | async-start | bytes 2097152 | tf_op jit(solution)/shard_map/all_to_all | solution.py:463
  181.8 4.0 %copy-start = (bf16[128,2048]{1,0:T(8,128)(2,1)S(1)}, bf16[128,2048]{1,0:T(8,128)(2,1)}, u32[]{:S(2)}) copy-start(bf16[128,2048]{1,0:T(8,128)(2,1)} %refs_3_.1) | copy-start | bytes 1572868
  181.8 4.0 %copy-start.8 = (f32[2048]{0:T(1024)S(1)}, f32[2048]{0:T(1024)}, u32[]{:S(2)}) copy-start(f32[2048]{0:T(1024)} %param.17) | copy-start | bytes 24580
  183.0 2.9 collective-permute-start.15
  188.8 31.0 %collective-permute-start.16 = (bf16[1,128,1024]{2,1,0:T(8,128)(2,1)S(1)}, bf16[1,128,1024]{2,1,0:T(8,128)(2,1)S(1)}, u32[]{:S(2)}, u32[]{:S(2)}) collective-permute-start(bf16[1,128,1024]{2,1,0:T(8,128)(2,1)S(1)} %dynamic-slice_bitcast_fusion), channel_id=1, source_target_pairs={{0,16},{2,18},{4,20},{6,22},{8,24},{10,26},{12,28},{14,30},{16,0},... | collective-permute-start | bytes 786440 | tf_op jit(solution)/shard_map/ppermute | solution.py:31
  191.9 27.8 %collective-permute-start.17 = (f32[1,128,16]{2,1,0:T(8,128)S(1)}, f32[1,128,16]{2,1,0:T(8,128)S(1)}, u32[]{:S(2)}, u32[]{:S(2)}) collective-permute-start(f32[1,128,16]{2,1,0:T(8,128)S(1)} %multiply_bitcast_fusion), channel_id=1, source_target_pairs={{0,16},{2,18},{4,20},{6,22},{8,24},{10,26},{12,28},{14,30},{16,0},... | collective-permute-start | bytes 24584 | tf_op jit(solution)/shard_map/ppermute | solution.py:31
  219.9 36.9 %all-to-all-start.5 = ((bf16[16,128,256]{2,1,0:T(8,128)(2,1)}), bf16[16,128,256]{2,1,0:T(8,128)(2,1)}, u32[]{:S(2)}, u32[]{:S(2)}) async-start(bf16[16,128,256]{2,1,0:T(8,128)(2,1)} %get-tuple-element.98), calls=%async_computation.5 | async-start | bytes 2097152 | tf_op jit(solution)/shard_map/all_to_all | solution.py:463
  227.3 24.7 %collective-permute-start.18 = (bf16[2,72,1024]{2,1,0:T(8,128)(2,1)S(1)}, bf16[2,72,1024]{2,1,0:T(8,128)(2,1)S(1)}, u32[]{:S(2)}, u32[]{:S(2)}) collective-permute-start(bf16[2,72,1024]{2,1,0:T(8,128)(2,1)S(1)} %get-tuple-element.123), channel_id=1, source_target_pairs={{0,2},{2,0},{4,6},{6,4},{8,10},{10,8},{12,14},{14,12},{16,18},{18,... | collective-permute-start | bytes 884744 | tf_op jit(solution)/shard_map/ppermute | solution.py:31
  229.2 25.6 %collective-permute-start.19 = (bf16[2,72,1024]{2,1,0:T(8,128)(2,1)S(1)}, bf16[2,72,1024]{2,1,0:T(8,128)(2,1)S(1)}, u32[]{:S(2)}, u32[]{:S(2)}) collective-permute-start(bf16[2,72,1024]{2,1,0:T(8,128)(2,1)S(1)} %get-tuple-element.124), channel_id=1, source_target_pairs={{0,4},{2,6},{4,0},{6,2},{8,12},{10,14},{12,8},{14,10},{16,20},{18,... | collective-permute-start | bytes 884744 | tf_op jit(solution)/shard_map/ppermute | solution.py:31
  231.5 33.6 %collective-permute-start.22 = (bf16[2,72,1024]{2,1,0:T(8,128)(2,1)}, bf16[2,72,1024]{2,1,0:T(8,128)(2,1)}, u32[]{:S(2)}, u32[]{:S(2)}) collective-permute-start(bf16[2,72,1024]{2,1,0:T(8,128)(2,1)} %get-tuple-element.128), channel_id=1, source_target_pairs={{0,10},{2,8},{4,14},{6,12},{8,2},{10,0},{12,6},{14,4},{16,26},{18,... | collective-permute-start | bytes 884744 | tf_op jit(solution)/shard_map/ppermute | solution.py:31
  233.0 30.2 %collective-permute-start.20 = (bf16[2,72,1024]{2,1,0:T(8,128)(2,1)}, bf16[2,72,1024]{2,1,0:T(8,128)(2,1)}, u32[]{:S(2)}, u32[]{:S(2)}) collective-permute-start(bf16[2,72,1024]{2,1,0:T(8,128)(2,1)} %get-tuple-element.125), channel_id=1, source_target_pairs={{0,6},{2,4},{4,2},{6,0},{8,14},{10,12},{12,10},{14,8},{16,22},{18,... | collective-permute-start | bytes 884744 | tf_op jit(solution)/shard_map/ppermute | solution.py:31
  234.5 29.7 %collective-permute-start.21 = (bf16[2,72,1024]{2,1,0:T(8,128)(2,1)}, bf16[2,72,1024]{2,1,0:T(8,128)(2,1)}, u32[]{:S(2)}, u32[]{:S(2)}) collective-permute-start(bf16[2,72,1024]{2,1,0:T(8,128)(2,1)} %get-tuple-element.126), channel_id=1, source_target_pairs={{0,8},{2,10},{4,12},{6,14},{8,0},{10,2},{12,4},{14,6},{16,24},{18,... | collective-permute-start | bytes 884744 | tf_op jit(solution)/shard_map/ppermute | solution.py:31
  252.0 2.7 copy-start.24
  252.0 23.1 %collective-permute-start.23 = (bf16[2,72,1024]{2,1,0:T(8,128)(2,1)}, bf16[2,72,1024]{2,1,0:T(8,128)(2,1)}, u32[]{:S(2)}, u32[]{:S(2)}) collective-permute-start(bf16[2,72,1024]{2,1,0:T(8,128)(2,1)} %get-tuple-element.127), channel_id=1, source_target_pairs={{0,12},{2,14},{4,8},{6,10},{8,4},{10,6},{12,0},{14,2},{16,28},{18,... | collective-permute-start | bytes 884744 | tf_op jit(solution)/shard_map/ppermute | solution.py:31
  255.4 28.2 %collective-permute-start.24 = (bf16[2,72,1024]{2,1,0:T(8,128)(2,1)}, bf16[2,72,1024]{2,1,0:T(8,128)(2,1)}, u32[]{:S(2)}, u32[]{:S(2)}) collective-permute-start(bf16[2,72,1024]{2,1,0:T(8,128)(2,1)} %get-tuple-element.121), channel_id=1, source_target_pairs={{0,14},{2,12},{4,10},{6,8},{8,6},{10,4},{12,2},{14,0},{16,30},{18,... | collective-permute-start | bytes 884744 | tf_op jit(solution)/shard_map/ppermute | solution.py:31
  256.7 52.2 %all-to-all-start.6 = ((bf16[16,128,512]{2,1,0:T(8,128)(2,1)}), bf16[16,128,512]{2,1,0:T(8,128)(2,1)}, u32[]{:S(2)}, u32[]{:S(2)}) async-start(bf16[16,128,512]{2,1,0:T(8,128)(2,1)} %get-tuple-element.106), calls=%async_computation.6 | async-start | bytes 4194304 | tf_op jit(solution)/shard_map/all_to_all | solution.py:463
  285.2 2.9 copy-start.11
  285.2 9.8 %copy-start.10 = (bf16[8,1,1,72,1024]{4,3,0,2,1:T(8,128)(2,1)}, bf16[8,1,1,72,1024]{4,3,0,2,1:T(8,128)(2,1)S(1)}, u32[]{:S(2)}) copy-start(bf16[8,1,1,72,1024]{4,3,0,2,1:T(8,128)(2,1)S(1)} %get-tuple-element.119) | copy-start | bytes 3538948
  285.2 2.9 collective-permute-start.25
  285.3 9.7 %collective-permute-start.26 = (bf16[1,576,1024]{2,1,0:T(8,128)(2,1)S(1)}, bf16[1,576,1024]{2,1,0:T(8,128)(2,1)S(1)}, u32[]{:S(2)}, u32[]{:S(2)}) collective-permute-start(bf16[1,576,1024]{2,1,0:T(8,128)(2,1)S(1)} %bitcast.163), channel_id=1, source_target_pairs={{1,0},{0,1},{3,2},{2,3},{5,4},{4,5},{7,6},{6,7},{9,8},{8,9},{11,10... | collective-permute-start | bytes 3538952 | tf_op jit(solution)/shard_map/ppermute | solution.py:26
  295.0 23.2 %copy-start.21 = (bf16[1,576,1024]{2,1,0:T(8,128)(2,1)}, bf16[1,576,1024]{2,1,0:T(8,128)(2,1)S(1)}, u32[]{:S(2)}) copy-start(bf16[1,576,1024]{2,1,0:T(8,128)(2,1)S(1)} %collective-permute-done.26.refs_2_) | copy-start | bytes 3538948
  313.6 3.1 collective-permute-start.27
  318.1 20.1 %all-to-all-start.7 = ((bf16[8,1,72,1024]{3,2,1,0:T(8,128)(2,1)}), bf16[8,1,72,1024]{3,2,1,0:T(8,128)(2,1)S(1)}, u32[]{:S(2)}, u32[]{:S(2)}) async-start(bf16[8,1,72,1024]{3,2,1,0:T(8,128)(2,1)} %bitcast.62), calls=%async_computation.7 | async-start | bytes 2359296 | tf_op jit(solution)/shard_map/all_to_all | solution.py:708
  327.5 4.8 %copy-start.20 = (pred[128,576]{0,1:T(32,128)(4,1)S(1)}, pred[128,576]{0,1:T(32,128)(4,1)}, u32[]{:S(2)}) copy-start(pred[128,576]{0,1:T(32,128)(4,1)} %copy-done.19) | copy-start | bytes 221188
  332.1 3.1 collective-permute-start.28
  339.1 24.6 %all-to-all-start.8 = ((bf16[8,1,72,1024]{3,2,1,0:T(8,128)(2,1)}), bf16[8,1,72,1024]{3,2,1,0:T(8,128)(2,1)S(1)}, u32[]{:S(2)}, u32[]{:S(2)}) async-start(bf16[8,1,72,1024]{3,2,1,0:T(8,128)(2,1)} %bitcast.66), calls=%async_computation.8 | async-start | bytes 2359296 | tf_op jit(solution)/shard_map/all_to_all | solution.py:708
  343.6 21.0 %copy-start.7 = (f32[128,2048]{1,0:T(8,128)S(1)}, f32[128,2048]{1,0:T(8,128)}, u32[]{:S(2)}) copy-start(f32[128,2048]{1,0:T(8,128)} %copy-done.6) | copy-start | bytes 3145732
  343.9 20.7 %collective-permute-start.29 = (bf16[128,1024]{1,0:T(8,128)(2,1)S(1)}, bf16[128,1024]{1,0:T(8,128)(2,1)S(1)}, u32[]{:S(2)}, u32[]{:S(2)}) collective-permute-start(bf16[128,1024]{1,0:T(8,128)(2,1)S(1)} %slice_add_fusion.2), channel_id=1, source_target_pairs={{0,16},{2,18},{4,20},{6,22},{8,24},{10,26},{12,28},{14,30},{16,0},... | collective-permute-start | bytes 786440 | tf_op jit(solution)/shard_map/ppermute | solution.py:31
  (5 other events, 4.8 us)

commit v10 on v8

--- a/solution.py
+++ b/solution.py
@@ -252,6 +252,44 @@
         cost_estimate=SMALL,
         name="attend_once",
     )(sink, query_prompt[:, None], key_prompt[None, :], rows, rows, rows)
+
+
+def out_body(head_ref, first_ref, first_other_ref, second_ref, second_other_ref, out_ref):
+    heads = first_ref.shape[0] // HEAD
+    first, second = (
+        jnp.concatenate([head_ref[h] for h in place], axis=1)
+        for place in (range(heads), range(heads, head_ref.shape[0]))
+    )
+    rows = second.shape[1]
+    half = first_ref.shape[1]
+    span = half // 2
+    for k, (one, two) in enumerate(
+        ((first_ref, second_ref), (first_other_ref, second_other_ref))
+    ):
+        own = jnp.dot(first, one[...], preferred_element_type=jnp.float32)
+        other = jnp.dot(second, two[:rows, :], preferred_element_type=jnp.float32)
+        if k == 0:
+            low, high = (other[:, :span], other[:, span:])
+            out_ref[:, :span] = own[:, :span] + low
+            out_ref[:, span:half] = own[:, span:]
+            out_ref[:, half : half + span] = high
+        else:
+            out_ref[:, span:half] = out_ref[:, span:half] + other[:, :span]
+            out_ref[:, half : half + span] = out_ref[:, half : half + span] + own[:, :span]
+            out_ref[:, half + span :] = own[:, span:] + other[:, span:]
+
+
+def out_project(heads, pieces):
+    vmem = pl.BlockSpec(memory_space=pltpu.VMEM)
+    return pl.pallas_call(
+        out_body,
+        in_specs=[vmem] * 5,
+        out_specs=vmem,
+        out_shape=jax.ShapeDtypeStruct((heads.shape[1], 2 * pieces[0].shape[1]), jnp.float32),
+        compiler_params=pltpu.CompilerParams(vmem_limit_bytes=40 * 2**20),
+        cost_estimate=SMALL,
+        name="out_project",
+    )(heads, *pieces)
 
 
 def settle_body(piece_count, width, place_ref, *refs):
@@ -408,8 +446,10 @@
     groups = [[first + k for k in range(head_count)] for first in range(0, seq_count, head_count)]
     part_masks = masks_below(seq_count, head_count)
 
+    packed = pack_heads(w_query, w_key, w_value, part_count)
+    packed, tokens = lax.optimization_barrier((packed, tokens))
     head_weights = lax.all_to_all(
-        pack_heads(w_query, w_key, w_value, part_count),
+        packed,
         "seq",
         split_axis=0,
         concat_axis=0,
@@ -570,8 +610,6 @@
     server_second = to_owner(own_second)
 
     proj_width = head_count * HEAD
-    attention_result = jnp.swapaxes(attention_result, 0, 1).reshape(token_count, proj_width)
-
     def joined(pieces, half):
         if half == 0:
             return jnp.concatenate(pieces, axis=1)
@@ -579,18 +617,22 @@
         low, high = ([piece[:, k * span : (k + 1) * span] for piece in pieces] for k in range(2))
         return jnp.concatenate([*low, *high], axis=1)
 
-    partial_out = sum(
-        joined([jnp.dot(rows, piece, preferred_element_type=jnp.float32) for piece in pieces], half)
-        for half, (rows, pieces) in enumerate(
-            (
-                (attention_result[:, :out_rows], out_halves[0]),
+    if out_rows % HEAD == 0 and out_rows < proj_width:
+        partial_out = out_project(attention_result, [*out_halves[0], *out_halves[1]])
+    else:
+        attention_result = jnp.swapaxes(attention_result, 0, 1).reshape(token_count, proj_width)
+        partial_out = sum(
+            joined([jnp.dot(rows, piece, preferred_element_type=jnp.float32) for piece in pieces], half)
+            for half, (rows, pieces) in enumerate(
                 (
-                    attention_result[:, out_rows:],
-                    [piece[: proj_width - out_rows] for piece in out_halves[1]],
-                ),
+                    (attention_result[:, :out_rows], out_halves[0]),
+                    (
+                        attention_result[:, out_rows:],
+                        [piece[: proj_width - out_rows] for piece in out_halves[1]],
+                    ),
+                )
             )
         )
-    )
     if tp_count == 2:
         out_pieces = [partial_out, from_turned(partial_out, "tp", 1)]
     else:
@@ -648,8 +690,8 @@
         return swapped(block, "seq", m) if m else block
 
     received = [to_mate(m) for m in range(head_count)]
-    received[1:4], server_up, own_down = lax.optimization_barrier(
-        (received[1:4], server_up, own_down)
+    received[1:3], server_up, own_down = lax.optimization_barrier(
+        (received[1:3], server_up, own_down)
     )
     server_down = to_owner(own_down)
     received = by_place(jnp.stack(received))
@@ -662,8 +704,10 @@
         tp_blocks(jnp.moveaxis(rows, 2, 0).reshape(local_experts, -1, col_share))
         for rows in (received[:, 1:], received[:, :1])
     ]
-    hidden = [hidden_units(in_starts, rows, (server_first, server_second, server_up)) for rows in halves]
-    hidden, server_down = lax.optimization_barrier((hidden, server_down))
+    server = (server_first, server_second, server_up)
+    hidden = hidden_units(in_starts, halves[0], server)
+    hidden, own_half, server_down = lax.optimization_barrier((hidden, halves[1], server_down))
+    hidden = [hidden, hidden_units(in_starts, own_half, server)]
 
     def through_experts(rows, parts):
         outs = down_rows(out_starts, rows, server_down)

time: 357 us -> 347 us (0.972)
  matrix products: 13.7 us -> 6.69 us
  other arithmetic: 22.9 us -> 18.5 us
  waiting for transfers between devices: 151 us -> 147 us
  Pallas kernels: 50 us -> 53.7 us
    all_to_all x4, waiting for transfers between devices: 3.96 us -> 21 us  [to_owner(): lax.all_to_all(blocks, 'seq', split_axis=0, concat_axis=0, tiled=True)]
    ppermute x22, waiting for transfers between devices: 101 us -> 85.7 us  [swapped(): lax.ppermute(value, axis, [(place, place ^ mask) for place in range(count)])]
    dot_general x4 -> x0, matrix products: 7.03 us -> none  [shards(): jnp.dot(rows, piece, preferred_element_type=jnp.float32)]
    all_to_all x2, waiting for transfers between devices: 25.3 us -> 19.5 us  [back(): lax.all_to_all(blocks, 'seq', split_axis=0, concat_axis=0, tiled=True, ax...]
    all_to_all x1, starting transfers between devices: 8.42 us -> 4.59 us  [shards(): lax.all_to_all(blocks, 'seq', split_axis=0, concat_axis=0, tiled=True, ax...]
    unnamed x102 -> x90, local copies, waits for them, and re-layouts: 26.5 us -> 26.1 us
  transfers between devices with their start and end apart: 38 -> 38, of which waited for: 20 -> 20; matrix products, arithmetic and copies ran while one was open for 14% -> 13% of each run, Pallas kernels for 13% -> 14%
where the time goes in v10:
time: 347 us; the launch traced here: 345 us
  waiting for transfers between devices  147 us (42%)
  starting transfers between devices  87.7 us (25%)
  Pallas kernels  53.7 us (15%)
  local copies, waits for them, and re-layouts  30.6 us (9%)
  other arithmetic  18.5 us (5%)
  matrix products  6.69 us (2%)
    ppermute x22, waiting for transfers between devices, swapped(): lax.ppermute(value, axis, [(place, place ^ mask) for place in range(count)])  85.7 us
    ppermute x22, starting transfers between devices, swapped(): lax.ppermute(value, axis, [(place, place ^ mask) for place in range(count)])  33.8 us
    all_to_all x4, starting transfers between devices, to_owner(): lax.all_to_all(blocks, 'seq', split_axis=0, concat_axis=0, tiled=True)  27 us
    unnamed x90, local copies, waits for them, and re-layouts  26.1 us
    all_to_all x4, waiting for transfers between devices, to_owner(): lax.all_to_all(blocks, 'seq', split_axis=0, concat_axis=0, tiled=True)  21 us
    all_to_all x2, waiting for transfers between devices, back(): lax.all_to_all(blocks, 'seq', split_axis=0, concat_axis=0, tiled=True, ax...  19.5 us
    pallas_call x1, Pallas kernels, order_experts(): pl.pallas_call(order_body, grid_spec=pltpu.PrefetchScalarGridSpec(num_sca...  12.8 us
    pallas_call x2, Pallas kernels, hidden_units(): pl.pallas_call(lambda *refs: hidden_body(count, share, *refs), grid_spec=...  11.6 us
  transfers between devices with their start and end apart: 38, of which 20 were waited for; matrix products, arithmetic and copies ran while one was open for 13% of the time, Pallas kernels for 14%

profile of v10, /device:TPU:0, one launch (start us, length us, event | category | flops | bytes accessed | tf_op | source)
XLA Modules:
  0.0 345.4 jit_solution(12098137199787530726)
XLA Ops:
  3.2 1.8 pack_heads.1
  5.5 3.1 collective-permute-start.2
  8.6 2.6 collective-permute-start.4
  11.7 5.9 %all-to-all-start = ((bf16[16,128,384]{2,1,0:T(8,128)(2,1)}), bf16[16,128,384]{2,1,0:T(8,128)(2,1)}, u32[]{:S(2)}, u32[]{:S(2)}) async-start(bf16[16,128,384]{2,1,0:T(8,128)(2,1)} %pack_heads.1), calls=%async_computation | async-start | bytes 3145728 | tf_op jit(solution)/shard_map/all_to_all | solution.py:451
  17.7 3.1 multiply_sine_fusion
  20.9 1.9 collective-permute-start.3
  22.8 1.5 collective-permute-start.6
  24.2 12.8 %order_experts.1 = (bf16[16,128,256]{2,1,0:T(8,128)(2,1)}, bf16[16,128,256]{2,1,0:T(8,128)(2,1)}, bf16[16,128,512]{2,1,0:T(8,128)(2,1)}, bf16[16,128,512]{2,1,0:T(8,128)(2,1)}) custom-call(s32[16]{0:T(128)} %order_ref, f32[16,128,512]{2,1,0:T(8,128)} %gate_ref.1, f32[16,128,512]{2,1,0:T(8,128)} %up_ref.1, f32[16,128,512]{2,1,0:T(8,128)} %down_ref.1), custom_call_target="tpu_custom_call" | custom-call | flops 1 | bytes 1 | tf_op jit(solution)/shard_map/order_experts/pallas_call | solution.py:131
  37.1 6.3 %collective-permute-done = bf16[1040,128]{1,0:T(8,128)(2,1)S(1)} collective-permute-done((bf16[1040,128]{1,0:T(8,128)(2,1)S(1)}, bf16[1040,128]{1,0:T(8,128)(2,1)S(1)}, u32[]{:S(2)}, u32[]{:S(2)}) %collective-permute-start) | collective-permute-done | bytes 266272 | tf_op jit(solution)/shard_map/ppermute | solution.py:31
  43.6 1.6 collective-permute-start.5
  45.3 13.0 %collective-permute-done.1 = bf16[1040,256]{1,0:T(8,128)(2,1)S(1)} collective-permute-done((bf16[1040,256]{1,0:T(8,128)(2,1)S(1)}, bf16[1040,256]{1,0:T(8,128)(2,1)S(1)}, u32[]{:S(2)}, u32[]{:S(2)}) %collective-permute-start.1) | collective-permute-done | bytes 532512 | tf_op jit(solution)/shard_map/ppermute | solution.py:31
  62.1 1.6 collective-permute-start.9
  63.8 1.4 collective-permute-start.10
  65.3 6.0 %all-to-all-start.1 = ((bf16[16,128,256]{2,1,0:T(8,128)(2,1)}), bf16[16,128,256]{2,1,0:T(8,128)(2,1)S(1)}, u32[]{:S(2)}, u32[]{:S(2)}) async-start(bf16[16,128,256]{2,1,0:T(8,128)(2,1)} %get-tuple-element.81), calls=%async_computation.1 | async-start | bytes 2097152 | tf_op jit(solution)/shard_map/all_to_all | solution.py:495
  72.0 10.0 %collective-permute-done.9 = bf16[512,512]{1,0:T(8,128)(2,1)} collective-permute-done((bf16[512,512]{1,0:T(8,128)(2,1)}, bf16[512,512]{1,0:T(8,128)(2,1)}, u32[]{:S(2)}, u32[]{:S(2)}) %collective-permute-start.9) | collective-permute-done | bytes 524320 | tf_op jit(solution)/shard_map/ppermute | solution.py:31
  82.0 2.3 pad_maximum_fusion.2.first_ref
  84.3 5.8 %project.1 = bf16[1024,384]{1,0:T(8,128)(2,1)S(1)} custom-call(s32[2]{0:T(128)S(1)} %fusion.109.refs_0_, bf16[1024,1024]{1,0:T(8,128)(2,1)S(1)} %pad_maximum_fusion.refs_1_, bf16[1024,1024]{1,0:T(8,128)(2,1)} %collective-permute-done.8.refs_2_, bf16[2048,384]{1,0:T(8,128)(2,1)} %bitcast.6.refs_3_, f32[1024,64]{1,0:T(8,128)S(1)} %copy-done.6, ...), custom_call_target="tpu_custom_call" | custom-call | flops 1 | bytes 1 | tf_op jit(solution)/shard_map/project/pallas_call | solution.py:196
  90.2 6.6 %collective-permute-start.11 = (bf16[64,384]{1,0:T(8,128)(2,1)S(1)}, bf16[64,384]{1,0:T(8,128)(2,1)S(1)}, u32[]{:S(2)}, u32[]{:S(2)}) collective-permute-start(bf16[64,384]{1,0:T(8,128)(2,1)S(1)} %constant_dynamic-slice_fusion), channel_id=1, source_target_pairs={{0,16},{2,18},{4,20},{6,22},{8,24},{10,26},{12,28},{14,30},{1,17},... | collective-permute-start | bytes 147464 | tf_op jit(solution)/shard_map/ppermute | solution.py:21
  98.6 6.8 %attend_once.1 = bf16[1088,128]{1,0:T(8,128)(2,1)S(1)} custom-call(f32[1]{0:T(128)} %dynamic_slice.92.sink_ref, s32[1088,1]{1,0:T(8,128)S(1)} %copy-done.4, s32[1,1088]{1,0:T(1,128)S(1)} %and_select_fusion.key_prompt_ref, bf16[1088,384]{1,0:T(8,128)(2,1)S(1)} %pad_maximum_fusion.3.query_ref.key_ref.value_ref, ...), custom_call_target="tpu_custom_call" | custom-call | flops 1 | bytes 1 | tf_op jit(solution)/shard_map/attend_once/pallas_call | solution.py:238
  107.8 4.3 %collective-permute-done.12 = bf16[64,128]{1,0:T(8,128)(2,1)S(1)} collective-permute-done((bf16[64,128]{1,0:T(8,128)(2,1)S(1)}, bf16[64,128]{1,0:T(8,128)(2,1)S(1)}, u32[]{:S(2)}, u32[]{:S(2)}) %collective-permute-start.12) | collective-permute-done | bytes 16416 | tf_op jit(solution)/shard_map/ppermute | solution.py:21
  117.0 14.2 %collective-permute-done.13.first_other_ref = bf16[512,1024]{1,0:T(8,128)(2,1)} collective-permute-done((bf16[512,1024]{1,0:T(8,128)(2,1)S(1)}, bf16[512,1024]{1,0:T(8,128)(2,1)}, u32[]{:S(2)}, u32[]{:S(2)}) %collective-permute-start.13) | collective-permute-done | bytes 1048608 | tf_op jit(solution)/shard_map/ppermute | solution.py:31
  131.2 4.6 %all-to-all-start.2 = ((bf16[8,128,128]{2,1,0:T(8,128)(2,1)}), bf16[8,128,128]{2,1,0:T(8,128)(2,1)S(1)}, u32[]{:S(2)}, u32[]{:S(2)}) async-start(bf16[8,128,128]{2,1,0:T(8,128)(2,1)} %constant_dynamic-update-slice_fusion), calls=%async_computation.2 | async-start | bytes 524288 | tf_op jit(solution)/shard_map/all_to_all | solution.py:606
  135.8 6.6 %all-to-all-done.2.head_ref = bf16[8,128,128]{2,1,0:T(8,128)(2,1)S(1)} async-done(((bf16[8,128,128]{2,1,0:T(8,128)(2,1)}), bf16[8,128,128]{2,1,0:T(8,128)(2,1)S(1)}, u32[]{:S(2)}, u32[]{:S(2)}) %all-to-all-start.2) | async-done | bytes 262176 | tf_op jit(solution)/shard_map/all_to_all | solution.py:606
  142.5 5.2 %all-to-all-start.3 = ((bf16[16,128,256]{2,1,0:T(8,128)(2,1)}), bf16[16,128,256]{2,1,0:T(8,128)(2,1)}, u32[]{:S(2)}, u32[]{:S(2)}) async-start(bf16[16,128,256]{2,1,0:T(8,128)(2,1)} %get-tuple-element.93), calls=%async_computation.3 | async-start | bytes 2097152 | tf_op jit(solution)/shard_map/all_to_all | solution.py:495
  149.0 3.3 out_project.1.refs_1_
  153.2 2.1 collective-permute-done.15.refs_2_
  155.3 2.2 settle.1
  158.5 2.8 collective-permute-start.16
  162.1 21.2 %collective-permute-done.17 = f32[1,128,16]{2,1,0:T(8,128)S(1)} collective-permute-done((f32[1,128,16]{2,1,0:T(8,128)S(1)}, f32[1,128,16]{2,1,0:T(8,128)S(1)}, u32[]{:S(2)}, u32[]{:S(2)}) %collective-permute-start.17) | collective-permute-done | bytes 8224 | tf_op jit(solution)/shard_map/ppermute | solution.py:31
  184.3 4.6 %all-to-all-start.4 = ((bf16[16,128,512]{2,1,0:T(8,128)(2,1)}), bf16[16,128,512]{2,1,0:T(8,128)(2,1)S(1)}, u32[]{:S(2)}, u32[]{:S(2)}) async-start(bf16[16,128,512]{2,1,0:T(8,128)(2,1)} %get-tuple-element.97), calls=%async_computation.4 | async-start | bytes 4194304 | tf_op jit(solution)/shard_map/all_to_all | solution.py:495
  189.6 1.4 convolution_convert_fusion.1
  191.0 1.4 convolution_convert_fusion
  193.6 1.9 collective-permute-start.18
  195.5 1.5 collective-permute-start.19
  197.9 1.5 collective-permute-start.22
  199.3 1.5 collective-permute-start.20
  201.4 2.5 collective-permute-done.18
  203.9 5.5 %collective-permute-start.23 = (bf16[2,72,1024]{2,1,0:T(8,128)(2,1)}, bf16[2,72,1024]{2,1,0:T(8,128)(2,1)}, u32[]{:S(2)}, u32[]{:S(2)}) collective-permute-start(bf16[2,72,1024]{2,1,0:T(8,128)(2,1)} %get-tuple-element.127), channel_id=1, source_target_pairs={{0,12},{2,14},{4,8},{6,10},{8,4},{10,6},{12,0},{14,2},{16,28},{18,... | collective-permute-start | bytes 884744 | tf_op jit(solution)/shard_map/ppermute | solution.py:31
  209.4 8.9 %collective-permute-done.19 = bf16[2,72,1024]{2,1,0:T(8,128)(2,1)S(1)} collective-permute-done((bf16[2,72,1024]{2,1,0:T(8,128)(2,1)S(1)}, bf16[2,72,1024]{2,1,0:T(8,128)(2,1)S(1)}, u32[]{:S(2)}, u32[]{:S(2)}) %collective-permute-start.19) | collective-permute-done | bytes 294944 | tf_op jit(solution)/shard_map/ppermute | solution.py:31
  220.3 9.5 %all-to-all-done.4 = bf16[16,128,512]{2,1,0:T(8,128)(2,1)S(1)} async-done(((bf16[16,128,512]{2,1,0:T(8,128)(2,1)}), bf16[16,128,512]{2,1,0:T(8,128)(2,1)S(1)}, u32[]{:S(2)}, u32[]{:S(2)}) %all-to-all-start.4) | async-done | bytes 2097184 | tf_op jit(solution)/shard_map/all_to_all | solution.py:495
  229.7 11.3 %all-to-all-start.5 = ((bf16[16,128,512]{2,1,0:T(8,128)(2,1)}), bf16[16,128,512]{2,1,0:T(8,128)(2,1)}, u32[]{:S(2)}, u32[]{:S(2)}) async-start(bf16[16,128,512]{2,1,0:T(8,128)(2,1)} %get-tuple-element.104), calls=%async_computation.5 | async-start | bytes 4194304 | tf_op jit(solution)/shard_map/all_to_all | solution.py:495
  241.0 1.7 bitcast_dynamic-update-slice_fusion.6
  242.7 1.7 bitcast_dynamic-update-slice_fusion.5
  244.4 1.7 bitcast_dynamic-update-slice_fusion.4
  246.1 1.7 bitcast_dynamic-update-slice_fusion.3
  247.8 1.7 bitcast_dynamic-update-slice_fusion.2
  249.5 1.7 collective-permute-done.23
  251.3 1.7 bitcast_dynamic-update-slice_fusion.1
  253.0 7.8 %collective-permute-done.24 = bf16[2,72,1024]{2,1,0:T(8,128)(2,1)} collective-permute-done((bf16[2,72,1024]{2,1,0:T(8,128)(2,1)}, bf16[2,72,1024]{2,1,0:T(8,128)(2,1)}, u32[]{:S(2)}, u32[]{:S(2)}) %collective-permute-start.24) | collective-permute-done | bytes 294944 | tf_op jit(solution)/shard_map/ppermute | solution.py:31
  260.8 1.7 bitcast_dynamic-update-slice_fusion
  267.6 2.3 collective-permute-done.25.refs_2_
  271.0 5.8 %hidden_units.2.refs_1_ = bf16[1,576,512]{2,1,0:T(8,128)(2,1)S(1)} custom-call(s32[2]{0:T(128)S(1)} %fusion.109.refs_0_, bf16[1,576,1024]{2,1,0:T(8,128)(2,1)} %bitcast.160, bf16[1,576,1024]{2,1,0:T(8,128)(2,1)} %copy-done.19, bf16[1,2048,256]{2,1,0:T(8,128)(2,1)S(1)} %bitcast.148, bf16[1,2048,256]{2,1,0:T(8,128)(2,1)} %bitcast.32.refs_4_, ...), custom_call_target="tpu_custom_call" | custom-call | flops 1 | bytes 1 | tf_op jit(solution)/shard_map/hidden_units/pallas_call | solution.py:352
  276.9 11.5 %all-to-all-done.5 = bf16[16,128,512]{2,1,0:T(8,128)(2,1)} async-done(((bf16[16,128,512]{2,1,0:T(8,128)(2,1)}), bf16[16,128,512]{2,1,0:T(8,128)(2,1)}, u32[]{:S(2)}, u32[]{:S(2)}) %all-to-all-start.5) | async-done | bytes 2097184 | tf_op jit(solution)/shard_map/all_to_all | solution.py:495
  288.4 4.7 %down_rows.2 = (bf16[1,576,1024]{2,1,0:T(8,128)(2,1)S(1)}, bf16[1,576,1024]{2,1,0:T(8,128)(2,1)}) custom-call(s32[2]{0:T(128)S(1)} %fusion.110.refs_0_, bf16[1,576,512]{2,1,0:T(8,128)(2,1)S(1)} %hidden_units.2.refs_1_, bf16[1,2048,512]{2,1,0:T(8,128)(2,1)} %bitcast.56.refs_2_), custom_call_target="tpu_custom_call" | custom-call | flops 1 | bytes 1 | tf_op jit(solution)/shard_map/down_rows/pallas_call | solution.py:384
  293.0 3.1 collective-permute-done.27
  296.1 1.6 add_convert_fusion.1
  297.7 4.0 %all-to-all-start.6 = ((bf16[8,1,72,1024]{3,2,1,0:T(8,128)(2,1)}), bf16[8,1,72,1024]{3,2,1,0:T(8,128)(2,1)S(1)}, u32[]{:S(2)}, u32[]{:S(2)}) async-start(bf16[8,1,72,1024]{3,2,1,0:T(8,128)(2,1)} %bitcast.58), calls=%async_computation.6 | async-start | bytes 2359296 | tf_op jit(solution)/shard_map/all_to_all | solution.py:737
  301.7 5.8 %hidden_units.3.refs_1_ = bf16[1,576,512]{2,1,0:T(8,128)(2,1)S(1)} custom-call(s32[2]{0:T(128)S(1)} %fusion.109.refs_0_, bf16[1,576,1024]{2,1,0:T(8,128)(2,1)} %bitcast.158, bf16[1,576,1024]{2,1,0:T(8,128)(2,1)} %copy-done.18, bf16[1,2048,256]{2,1,0:T(8,128)(2,1)S(1)} %bitcast.149, bf16[1,2048,256]{2,1,0:T(8,128)(2,1)} %bitcast.32.refs_4_, ...), custom_call_target="tpu_custom_call" | custom-call | flops 1 | bytes 1 | tf_op jit(solution)/shard_map/hidden_units/pallas_call | solution.py:352
  307.5 4.6 %down_rows.3 = (bf16[1,576,1024]{2,1,0:T(8,128)(2,1)S(1)}, bf16[1,576,1024]{2,1,0:T(8,128)(2,1)}) custom-call(s32[2]{0:T(128)S(1)} %fusion.110.refs_0_, bf16[1,576,512]{2,1,0:T(8,128)(2,1)S(1)} %hidden_units.3.refs_1_, bf16[1,2048,512]{2,1,0:T(8,128)(2,1)} %bitcast.56.refs_2_), custom_call_target="tpu_custom_call" | custom-call | flops 1 | bytes 1 | tf_op jit(solution)/shard_map/down_rows/pallas_call | solution.py:384
  312.9 2.2 collective-permute-done.28
  315.1 1.5 add_convert_fusion
  318.8 3.9 %all-to-all-start.7 = ((bf16[8,1,72,1024]{3,2,1,0:T(8,128)(2,1)}), bf16[8,1,72,1024]{3,2,1,0:T(8,128)(2,1)S(1)}, u32[]{:S(2)}, u32[]{:S(2)}) async-start(bf16[8,1,72,1024]{3,2,1,0:T(8,128)(2,1)} %bitcast.62), calls=%async_computation.7 | async-start | bytes 2359296 | tf_op jit(solution)/shard_map/all_to_all | solution.py:737
  323.5 1.9 collective-permute-start.29
  325.4 18.3 %all-to-all-done.7 = bf16[8,1,72,1024]{3,2,1,0:T(8,128)(2,1)S(1)} async-done(((bf16[8,1,72,1024]{3,2,1,0:T(8,128)(2,1)}), bf16[8,1,72,1024]{3,2,1,0:T(8,128)(2,1)S(1)}, u32[]{:S(2)}, u32[]{:S(2)}) %all-to-all-start.7) | async-done | bytes 1179680 | tf_op jit(solution)/shard_map/all_to_all | solution.py:737
  (197 shorter events, 39.9 us)
Async XLA Ops:
  0.0 5.0 %copy-start = (bf16[128,2048]{1,0:T(8,128)(2,1)S(1)}, bf16[128,2048]{1,0:T(8,128)(2,1)}, u32[]{:S(2)}) copy-start(bf16[128,2048]{1,0:T(8,128)(2,1)} %refs_3_) | copy-start | bytes 1572868
  0.0 1.1 copy-start.7
  1.1 1.0 copy-start.8
  2.1 1.0 copy-start.9
  3.2 2.2 copy-start.26
  3.2 5.4 %copy-start.24 = (s32[128,8]{0,1:T(8,128)S(1)}, s32[128,8]{0,1:T(8,128)}, u32[]{:S(2)}) copy-start(s32[128,8]{0,1:T(8,128)} %param.29) | copy-start | bytes 12292
  3.2 8.0 %copy-start.20 = (f32[1024,128]{1,0:T(8,128)S(1)}, f32[1024,128]{1,0:T(8,128)}, u32[]{:S(2)}) copy-start(f32[1024,128]{1,0:T(8,128)} %param.21) | copy-start | bytes 1572868
  5.0 6.2 %copy-start.23 = (f32[128,16]{0,1:T(8,128)S(1)}, f32[128,16]{0,1:T(8,128)}, u32[]{:S(2)}) copy-start(f32[128,16]{0,1:T(8,128)} %param.23) | copy-start | bytes 24580
  5.5 15.3 %collective-permute-start.2 = (bf16[1,128,1024]{2,1,0:T(8,128)(2,1)S(1)}, bf16[1,128,1024]{2,1,0:T(8,128)(2,1)S(1)}, u32[]{:S(2)}, u32[]{:S(2)}) collective-permute-start(bf16[1,128,1024]{2,1,0:T(8,128)(2,1)S(1)} %fusion.44), channel_id=1, source_target_pairs={{0,8},{2,10},{4,12},{6,14},{8,0},{10,2},{12,4},{14,6},{16,24},{18,... | collective-permute-start | bytes 786440 | tf_op jit(solution)/shard_map/ppermute | solution.py:31
  8.6 14.2 %collective-permute-start.4 = (s32[1,128,8]{1,2,0:T(8,128)S(1)}, s32[1,128,8]{1,2,0:T(8,128)S(1)}, u32[]{:S(2)}, u32[]{:S(2)}) collective-permute-start(s32[1,128,8]{1,2,0:T(8,128)S(1)} %bitcast.174), channel_id=1, source_target_pairs={{0,16},{2,18},{4,20},{6,22},{8,24},{10,26},{12,28},{14,30},{16,0},... | collective-permute-start | bytes 12296 | tf_op jit(solution)/shard_map/ppermute | solution.py:31
  11.3 32.1 %collective-permute-start = (bf16[1040,128]{1,0:T(8,128)(2,1)S(1)}, bf16[1040,128]{1,0:T(8,128)(2,1)S(1)}, u32[]{:S(2)}, u32[]{:S(2)}) collective-permute-start(bf16[1040,128]{1,0:T(8,128)(2,1)S(1)} %pad_maximum_fusion.13), channel_id=1, source_target_pairs={{0,16},{2,18},{4,20},{6,22},{8,24},{10,26},{12,28},{14,30},{16,0},... | collective-permute-start | bytes 798728 | tf_op jit(solution)/shard_map/ppermute | solution.py:31
  11.7 48.9 %all-to-all-start = ((bf16[16,128,384]{2,1,0:T(8,128)(2,1)}), bf16[16,128,384]{2,1,0:T(8,128)(2,1)}, u32[]{:S(2)}, u32[]{:S(2)}) async-start(bf16[16,128,384]{2,1,0:T(8,128)(2,1)} %pack_heads.1), calls=%async_computation | async-start | bytes 3145728 | tf_op jit(solution)/shard_map/all_to_all | solution.py:451
  20.9 22.6 %collective-permute-start.3 = (bf16[2,128,512]{2,1,0:T(8,128)(2,1)S(1)}, bf16[2,128,512]{2,1,0:T(8,128)(2,1)S(1)}, u32[]{:S(2)}, u32[]{:S(2)}) collective-permute-start(bf16[2,128,512]{2,1,0:T(8,128)(2,1)S(1)} %get-tuple-element.133), channel_id=1, source_target_pairs={{0,4},{2,6},{4,0},{6,2},{8,12},{10,14},{12,8},{14,10},{16,20},{18,... | collective-permute-start | bytes 786440 | tf_op jit(solution)/shard_map/ppermute | solution.py:31
  22.8 22.4 %collective-permute-start.6 = (bf16[2,128,512]{2,1,0:T(8,128)(2,1)S(1)}, bf16[2,128,512]{2,1,0:T(8,128)(2,1)S(1)}, u32[]{:S(2)}, u32[]{:S(2)}) collective-permute-start(bf16[2,128,512]{2,1,0:T(8,128)(2,1)S(1)} %get-tuple-element.134), channel_id=1, source_target_pairs={{0,2},{2,0},{4,6},{6,4},{8,10},{10,8},{12,14},{14,12},{16,18},{18,... | collective-permute-start | bytes 786440 | tf_op jit(solution)/shard_map/ppermute | solution.py:31
  43.4 14.9 %collective-permute-start.1 = (bf16[1040,256]{1,0:T(8,128)(2,1)S(1)}, bf16[1040,256]{1,0:T(8,128)(2,1)S(1)}, u32[]{:S(2)}, u32[]{:S(2)}) collective-permute-start(bf16[1040,256]{1,0:T(8,128)(2,1)S(1)} %pad_maximum_fusion.7), channel_id=1, source_target_pairs={{0,8},{2,10},{4,12},{6,14},{8,0},{10,2},{12,4},{14,6},{16,24},{18,... | collective-permute-start | bytes 1597448 | tf_op jit(solution)/shard_map/ppermute | solution.py:31
  43.6 16.4 %collective-permute-start.5 = (bf16[4,128,512]{2,1,0:T(8,128)(2,1)S(1)}, bf16[4,128,512]{2,1,0:T(8,128)(2,1)S(1)}, u32[]{:S(2)}, u32[]{:S(2)}) collective-permute-start(bf16[4,128,512]{2,1,0:T(8,128)(2,1)S(1)} %pad_maximum_fusion.10), channel_id=1, source_target_pairs={{0,2},{2,0},{4,6},{6,4},{8,10},{10,8},{12,14},{14,12},{16,18},{18,... | collective-permute-start | bytes 1572872 | tf_op jit(solution)/shard_map/ppermute | solution.py:31
  45.2 14.9 %collective-permute-start.7 = (bf16[4,128,512]{2,1,0:T(8,128)(2,1)S(1)}, bf16[4,128,512]{2,1,0:T(8,128)(2,1)S(1)}, u32[]{:S(2)}, u32[]{:S(2)}) collective-permute-start(bf16[4,128,512]{2,1,0:T(8,128)(2,1)S(1)} %pad_maximum_fusion.11), channel_id=1, source_target_pairs={{0,4},{2,6},{4,0},{6,2},{8,12},{10,14},{12,8},{14,10},{16,20},{18,... | collective-permute-start | bytes 1572872 | tf_op jit(solution)/shard_map/ppermute | solution.py:31
  60.3 3.5 %copy-start.25 = (s32[2]{0:T(128)S(1)}, s32[2]{0:T(128)}, u32[]{:S(2)}) copy-start(s32[2]{0:T(128)} %param.28) | copy-start | bytes 28
  60.5 10.8 %copy-start.27 = (f32[8]{0:T(128)S(1)}, f32[8]{0:T(128)}, u32[]{:S(2)}) copy-start(f32[8]{0:T(128)} %param.22) | copy-start | bytes 100
  60.5 23.7 %collective-permute-start.8 = (bf16[1024,1024]{1,0:T(8,128)(2,1)S(1)}, bf16[1024,1024]{1,0:T(8,128)(2,1)}, u32[]{:S(2)}, u32[]{:S(2)}) collective-permute-start(bf16[1024,1024]{1,0:T(8,128)(2,1)S(1)} %pad_maximum_fusion.refs_1_), channel_id=1, source_target_pairs={{1,0},{0,1},{3,2},{2,3},{5,4},{4,5},{7,6},{6,7},{9,8},{8,9},{11,10... | collective-permute-start | bytes 6291464 | tf_op jit(solution)/shard_map/ppermute | solution.py:26
  62.1 19.8 %collective-permute-start.9 = (bf16[512,512]{1,0:T(8,128)(2,1)}, bf16[512,512]{1,0:T(8,128)(2,1)}, u32[]{:S(2)}, u32[]{:S(2)}) collective-permute-start(bf16[512,512]{1,0:T(8,128)(2,1)} %pad_maximum_fusion.8), channel_id=1, source_target_pairs={{0,4},{2,6},{4,0},{6,2},{8,12},{10,14},{12,8},{14,10},{16,20},{18,... | collective-permute-start | bytes 1572872 | tf_op jit(solution)/shard_map/ppermute | solution.py:31
  63.8 32.9 %collective-permute-start.10 = (bf16[528,512]{1,0:T(8,128)(2,1)}, bf16[528,512]{1,0:T(8,128)(2,1)}, u32[]{:S(2)}, u32[]{:S(2)}) collective-permute-start(bf16[528,512]{1,0:T(8,128)(2,1)} %pad_maximum_fusion.4), channel_id=1, source_target_pairs={{0,2},{2,0},{4,6},{6,4},{8,10},{10,8},{12,14},{14,12},{16,18},{18,... | collective-permute-start | bytes 1622024 | tf_op jit(solution)/shard_map/ppermute | solution.py:31
  65.3 51.8 %all-to-all-start.1 = ((bf16[16,128,256]{2,1,0:T(8,128)(2,1)}), bf16[16,128,256]{2,1,0:T(8,128)(2,1)S(1)}, u32[]{:S(2)}, u32[]{:S(2)}) async-start(bf16[16,128,256]{2,1,0:T(8,128)(2,1)} %get-tuple-element.81), calls=%async_computation.1 | async-start | bytes 2097152 | tf_op jit(solution)/shard_map/all_to_all | solution.py:495
  71.4 12.9 %copy-start.5 = (f32[1024,64]{1,0:T(8,128)S(1)}, f32[1024,64]{1,0:T(8,128)}, u32[]{:S(2)}) copy-start(f32[1024,64]{1,0:T(8,128)} %get-tuple-element.75.refs_5_) | copy-start | bytes 786436
  71.4 12.9 %copy-start.6 = (f32[1024,64]{1,0:T(8,128)S(1)}, f32[1024,64]{1,0:T(8,128)}, u32[]{:S(2)}) copy-start(f32[1024,64]{1,0:T(8,128)} %get-tuple-element.74.refs_4_) | copy-start | bytes 786436
  84.3 12.5 %copy-start.17 = (bf16[528,512]{1,0:T(8,128)(2,1)S(1)}, bf16[528,512]{1,0:T(8,128)(2,1)}, u32[]{:S(2)}) copy-start(bf16[528,512]{1,0:T(8,128)(2,1)} %pad_maximum_fusion.4) | copy-start | bytes 1622020
  90.1 8.4 %copy-start.4 = (s32[1088,1]{1,0:T(8,128)S(1)}, s32[1088,1]{1,0:T(8,128)}, u32[]{:S(2)}) copy-start(s32[1088,1]{1,0:T(8,128)} %fusion.9.query_prompt_ref) | copy-start | bytes 13060
  90.2 8.3 %collective-permute-start.11 = (bf16[64,384]{1,0:T(8,128)(2,1)S(1)}, bf16[64,384]{1,0:T(8,128)(2,1)S(1)}, u32[]{:S(2)}, u32[]{:S(2)}) collective-permute-start(bf16[64,384]{1,0:T(8,128)(2,1)S(1)} %constant_dynamic-slice_fusion), channel_id=1, source_target_pairs={{0,16},{2,18},{4,20},{6,22},{8,24},{10,26},{12,28},{14,30},{1,17},... | collective-permute-start | bytes 147464 | tf_op jit(solution)/shard_map/ppermute | solution.py:21
  98.6 9.2 %copy-start.2 = (bf16[512,1024]{1,0:T(8,128)(2,1)S(1)}, bf16[512,1024]{1,0:T(8,128)(2,1)}, u32[]{:S(2)}) copy-start(bf16[512,1024]{1,0:T(8,128)(2,1)} %pad_maximum_fusion.2.first_ref) | copy-start | bytes 3145732
  105.4 6.7 %collective-permute-start.12 = (bf16[64,128]{1,0:T(8,128)(2,1)S(1)}, bf16[64,128]{1,0:T(8,128)(2,1)S(1)}, u32[]{:S(2)}, u32[]{:S(2)}) collective-permute-start(bf16[64,128]{1,0:T(8,128)(2,1)S(1)} %slice.175), channel_id=1, source_target_pairs={{16,0},{18,2},{20,4},{22,6},{24,8},{26,10},{28,12},{30,14},{17,1},... | collective-permute-start | bytes 49160 | tf_op jit(solution)/shard_map/ppermute | solution.py:21
  106.7 24.5 %collective-permute-start.14 = (bf16[528,1024]{1,0:T(8,128)(2,1)S(1)}, bf16[528,1024]{1,0:T(8,128)(2,1)}, u32[]{:S(2)}, u32[]{:S(2)}) collective-permute-start(bf16[528,1024]{1,0:T(8,128)(2,1)S(1)} %pad_maximum_fusion.1.second_ref), channel_id=1, source_target_pairs={{0,4},{2,6},{4,0},{6,2},{8,12},{10,14},{12,8},{14,10},{16,20},{18,... | collective-permute-start | bytes 3244040 | tf_op jit(solution)/shard_map/ppermute | solution.py:31
  107.8 23.5 %collective-permute-start.13 = (bf16[512,1024]{1,0:T(8,128)(2,1)S(1)}, bf16[512,1024]{1,0:T(8,128)(2,1)}, u32[]{:S(2)}, u32[]{:S(2)}) collective-permute-start(bf16[512,1024]{1,0:T(8,128)(2,1)S(1)} %copy-done.2), channel_id=1, source_target_pairs={{0,2},{2,0},{4,6},{6,4},{8,10},{10,8},{12,14},{14,12},{16,18},{18,... | collective-permute-start | bytes 3145736 | tf_op jit(solution)/shard_map/ppermute | solution.py:31
  131.2 11.2 %all-to-all-start.2 = ((bf16[8,128,128]{2,1,0:T(8,128)(2,1)}), bf16[8,128,128]{2,1,0:T(8,128)(2,1)S(1)}, u32[]{:S(2)}, u32[]{:S(2)}) async-start(bf16[8,128,128]{2,1,0:T(8,128)(2,1)} %constant_dynamic-update-slice_fusion), calls=%async_computation.2 | async-start | bytes 524288 | tf_op jit(solution)/shard_map/all_to_all | solution.py:606
  142.5 41.8 %all-to-all-start.3 = ((bf16[16,128,256]{2,1,0:T(8,128)(2,1)}), bf16[16,128,256]{2,1,0:T(8,128)(2,1)}, u32[]{:S(2)}, u32[]{:S(2)}) async-start(bf16[16,128,256]{2,1,0:T(8,128)(2,1)} %get-tuple-element.93), calls=%async_computation.3 | async-start | bytes 2097152 | tf_op jit(solution)/shard_map/all_to_all | solution.py:495
  147.8 1.2 copy-start.3
  149.0 6.3 %copy-start.1 = (bf16[128,2048]{1,0:T(8,128)(2,1)S(1)}, bf16[128,2048]{1,0:T(8,128)(2,1)}, u32[]{:S(2)}) copy-start(bf16[128,2048]{1,0:T(8,128)(2,1)} %refs_3_) | copy-start | bytes 1572868
  149.0 6.3 %copy-start.12 = (f32[2048]{0:T(1024)S(1)}, f32[2048]{0:T(1024)}, u32[]{:S(2)}) copy-start(f32[2048]{0:T(1024)} %param.17) | copy-start | bytes 24580
  152.3 3.0 collective-permute-start.15
  158.5 24.8 %collective-permute-start.16 = (bf16[1,128,1024]{2,1,0:T(8,128)(2,1)S(1)}, bf16[1,128,1024]{2,1,0:T(8,128)(2,1)S(1)}, u32[]{:S(2)}, u32[]{:S(2)}) collective-permute-start(bf16[1,128,1024]{2,1,0:T(8,128)(2,1)S(1)} %dynamic-slice_bitcast_fusion), channel_id=1, source_target_pairs={{0,16},{2,18},{4,20},{6,22},{8,24},{10,26},{12,28},{14,30},{16,0},... | collective-permute-start | bytes 786440 | tf_op jit(solution)/shard_map/ppermute | solution.py:31
  161.8 21.5 %collective-permute-start.17 = (f32[1,128,16]{2,1,0:T(8,128)S(1)}, f32[1,128,16]{2,1,0:T(8,128)S(1)}, u32[]{:S(2)}, u32[]{:S(2)}) collective-permute-start(f32[1,128,16]{2,1,0:T(8,128)S(1)} %multiply_bitcast_fusion), channel_id=1, source_target_pairs={{0,16},{2,18},{4,20},{6,22},{8,24},{10,26},{12,28},{14,30},{16,0},... | collective-permute-start | bytes 24584 | tf_op jit(solution)/shard_map/ppermute | solution.py:31
  184.3 45.5 %all-to-all-start.4 = ((bf16[16,128,512]{2,1,0:T(8,128)(2,1)}), bf16[16,128,512]{2,1,0:T(8,128)(2,1)S(1)}, u32[]{:S(2)}, u32[]{:S(2)}) async-start(bf16[16,128,512]{2,1,0:T(8,128)(2,1)} %get-tuple-element.97), calls=%async_computation.4 | async-start | bytes 4194304 | tf_op jit(solution)/shard_map/all_to_all | solution.py:495
  193.6 10.2 %collective-permute-start.18 = (bf16[2,72,1024]{2,1,0:T(8,128)(2,1)S(1)}, bf16[2,72,1024]{2,1,0:T(8,128)(2,1)S(1)}, u32[]{:S(2)}, u32[]{:S(2)}) collective-permute-start(bf16[2,72,1024]{2,1,0:T(8,128)(2,1)S(1)} %get-tuple-element.123), channel_id=1, source_target_pairs={{0,2},{2,0},{4,6},{6,4},{8,10},{10,8},{12,14},{14,12},{16,18},{18,... | collective-permute-start | bytes 884744 | tf_op jit(solution)/shard_map/ppermute | solution.py:31
  195.5 22.8 %collective-permute-start.19 = (bf16[2,72,1024]{2,1,0:T(8,128)(2,1)S(1)}, bf16[2,72,1024]{2,1,0:T(8,128)(2,1)S(1)}, u32[]{:S(2)}, u32[]{:S(2)}) collective-permute-start(bf16[2,72,1024]{2,1,0:T(8,128)(2,1)S(1)} %get-tuple-element.124), channel_id=1, source_target_pairs={{0,4},{2,6},{4,0},{6,2},{8,12},{10,14},{12,8},{14,10},{16,20},{18,... | collective-permute-start | bytes 884744 | tf_op jit(solution)/shard_map/ppermute | solution.py:31
  197.9 50.0 %collective-permute-start.22 = (bf16[2,72,1024]{2,1,0:T(8,128)(2,1)}, bf16[2,72,1024]{2,1,0:T(8,128)(2,1)}, u32[]{:S(2)}, u32[]{:S(2)}) collective-permute-start(bf16[2,72,1024]{2,1,0:T(8,128)(2,1)} %get-tuple-element.128), channel_id=1, source_target_pairs={{0,10},{2,8},{4,14},{6,12},{8,2},{10,0},{12,6},{14,4},{16,26},{18,... | collective-permute-start | bytes 884744 | tf_op jit(solution)/shard_map/ppermute | solution.py:31
  199.3 45.1 %collective-permute-start.20 = (bf16[2,72,1024]{2,1,0:T(8,128)(2,1)}, bf16[2,72,1024]{2,1,0:T(8,128)(2,1)}, u32[]{:S(2)}, u32[]{:S(2)}) collective-permute-start(bf16[2,72,1024]{2,1,0:T(8,128)(2,1)} %get-tuple-element.125), channel_id=1, source_target_pairs={{0,6},{2,4},{4,2},{6,0},{8,14},{10,12},{12,10},{14,8},{16,22},{18,... | collective-permute-start | bytes 884744 | tf_op jit(solution)/shard_map/ppermute | solution.py:31
  200.8 45.3 %collective-permute-start.21 = (bf16[2,72,1024]{2,1,0:T(8,128)(2,1)}, bf16[2,72,1024]{2,1,0:T(8,128)(2,1)}, u32[]{:S(2)}, u32[]{:S(2)}) collective-permute-start(bf16[2,72,1024]{2,1,0:T(8,128)(2,1)} %get-tuple-element.126), channel_id=1, source_target_pairs={{0,8},{2,10},{4,12},{6,14},{8,0},{10,2},{12,4},{14,6},{16,24},{18,... | collective-permute-start | bytes 884744 | tf_op jit(solution)/shard_map/ppermute | solution.py:31
  203.9 14.5 %copy-start.21 = (bf16[2,72,1024]{2,1,0:T(8,128)(2,1)}, bf16[2,72,1024]{2,1,0:T(8,128)(2,1)S(1)}, u32[]{:S(2)}) copy-start(bf16[2,72,1024]{2,1,0:T(8,128)(2,1)S(1)} %collective-permute-done.18) | copy-start | bytes 884740
  203.9 47.4 %collective-permute-start.23 = (bf16[2,72,1024]{2,1,0:T(8,128)(2,1)}, bf16[2,72,1024]{2,1,0:T(8,128)(2,1)}, u32[]{:S(2)}, u32[]{:S(2)}) collective-permute-start(bf16[2,72,1024]{2,1,0:T(8,128)(2,1)} %get-tuple-element.127), channel_id=1, source_target_pairs={{0,12},{2,14},{4,8},{6,10},{8,4},{10,6},{12,0},{14,2},{16,28},{18,... | collective-permute-start | bytes 884744 | tf_op jit(solution)/shard_map/ppermute | solution.py:31
  219.0 41.8 %collective-permute-start.24 = (bf16[2,72,1024]{2,1,0:T(8,128)(2,1)}, bf16[2,72,1024]{2,1,0:T(8,128)(2,1)}, u32[]{:S(2)}, u32[]{:S(2)}) collective-permute-start(bf16[2,72,1024]{2,1,0:T(8,128)(2,1)} %get-tuple-element.121), channel_id=1, source_target_pairs={{0,14},{2,12},{4,10},{6,8},{8,6},{10,4},{12,2},{14,0},{16,30},{18,... | collective-permute-start | bytes 884744 | tf_op jit(solution)/shard_map/ppermute | solution.py:31
  229.7 13.0 %copy-start.13 = (bf16[16,128,512]{2,1,0:T(8,128)(2,1)}, bf16[16,128,512]{2,1,0:T(8,128)(2,1)S(1)}, u32[]{:S(2)}) copy-start(bf16[16,128,512]{2,1,0:T(8,128)(2,1)S(1)} %all-to-all-done.4) | copy-start | bytes 6291460
  229.7 58.6 %all-to-all-start.5 = ((bf16[16,128,512]{2,1,0:T(8,128)(2,1)}), bf16[16,128,512]{2,1,0:T(8,128)(2,1)}, u32[]{:S(2)}, u32[]{:S(2)}) async-start(bf16[16,128,512]{2,1,0:T(8,128)(2,1)} %get-tuple-element.104), calls=%async_computation.5 | async-start | bytes 4194304 | tf_op jit(solution)/shard_map/all_to_all | solution.py:495
  262.5 4.1 %copy-start.16 = (bf16[8,2,72,1024]{3,2,0,1:T(8,128)(2,1)S(1)}, bf16[8,2,72,1024]{3,2,0,1:T(8,128)(2,1)}, u32[]{:S(2)}) copy-start(bf16[8,2,72,1024]{3,2,0,1:T(8,128)(2,1)} %bitcast_dynamic-update-slice_fusion) | copy-start | bytes 7077892
  267.0 2.9 copy-start.15
  267.0 9.8 %copy-start.14 = (bf16[8,1,1,72,1024]{4,3,0,2,1:T(8,128)(2,1)}, bf16[8,1,1,72,1024]{4,3,0,2,1:T(8,128)(2,1)S(1)}, u32[]{:S(2)}) copy-start(bf16[8,1,1,72,1024]{4,3,0,2,1:T(8,128)(2,1)S(1)} %get-tuple-element.119) | copy-start | bytes 3538948
  267.1 2.9 collective-permute-start.25
  267.1 9.7 %collective-permute-start.26 = (bf16[1,576,1024]{2,1,0:T(8,128)(2,1)S(1)}, bf16[1,576,1024]{2,1,0:T(8,128)(2,1)S(1)}, u32[]{:S(2)}, u32[]{:S(2)}) collective-permute-start(bf16[1,576,1024]{2,1,0:T(8,128)(2,1)S(1)} %bitcast.157), channel_id=1, source_target_pairs={{1,0},{0,1},{3,2},{2,3},{5,4},{4,5},{7,6},{6,7},{9,8},{8,9},{11,10... | collective-permute-start | bytes 3538952 | tf_op jit(solution)/shard_map/ppermute | solution.py:26
  270.0 1.1 copy-start.19
  276.9 20.8 %copy-start.18 = (bf16[1,576,1024]{2,1,0:T(8,128)(2,1)}, bf16[1,576,1024]{2,1,0:T(8,128)(2,1)S(1)}, u32[]{:S(2)}) copy-start(bf16[1,576,1024]{2,1,0:T(8,128)(2,1)S(1)} %collective-permute-done.26.refs_2_) | copy-start | bytes 3538948
  293.0 3.1 collective-permute-start.27
  297.7 20.3 %all-to-all-start.6 = ((bf16[8,1,72,1024]{3,2,1,0:T(8,128)(2,1)}), bf16[8,1,72,1024]{3,2,1,0:T(8,128)(2,1)S(1)}, u32[]{:S(2)}, u32[]{:S(2)}) async-start(bf16[8,1,72,1024]{3,2,1,0:T(8,128)(2,1)} %bitcast.58), calls=%async_computation.6 | async-start | bytes 2359296 | tf_op jit(solution)/shard_map/all_to_all | solution.py:737
  312.1 3.1 collective-permute-start.28
  318.8 24.8 %all-to-all-start.7 = ((bf16[8,1,72,1024]{3,2,1,0:T(8,128)(2,1)}), bf16[8,1,72,1024]{3,2,1,0:T(8,128)(2,1)S(1)}, u32[]{:S(2)}, u32[]{:S(2)}) async-start(bf16[8,1,72,1024]{3,2,1,0:T(8,128)(2,1)} %bitcast.62), calls=%async_computation.7 | async-start | bytes 2359296 | tf_op jit(solution)/shard_map/all_to_all | solution.py:737
  323.2 21.2 %copy-start.11 = (f32[128,2048]{1,0:T(8,128)S(1)}, f32[128,2048]{1,0:T(8,128)}, u32[]{:S(2)}) copy-start(f32[128,2048]{1,0:T(8,128)} %copy-done.10) | copy-start | bytes 3145732
  323.5 20.9 %collective-permute-start.29 = (bf16[128,1024]{1,0:T(8,128)(2,1)S(1)}, bf16[128,1024]{1,0:T(8,128)(2,1)S(1)}, u32[]{:S(2)}, u32[]{:S(2)}) collective-permute-start(bf16[128,1024]{1,0:T(8,128)(2,1)S(1)} %slice_add_fusion.2), channel_id=1, source_target_pairs={{0,16},{2,18},{4,20},{6,22},{8,24},{10,26},{12,28},{14,30},{16,0},... | collective-permute-start | bytes 786440 | tf_op jit(solution)/shard_map/ppermute | solution.py:31
  (2 other events, 1.7 us)

commit v11 on v10

--- a/solution.py
+++ b/solution.py
@@ -458,7 +458,6 @@
 
     normed = rms_scale(tokens.astype(jnp.float32), attn_gain).astype(jnp.bfloat16)
     share = lax.dynamic_slice_in_dim(normed, tp_place * col_share, col_share, 1)
-    all_routes, part_turns = doubled(routes[None], part_masks, 0)
     out_all, _ = doubled(
         jnp.concatenate([w_out, router.T], axis=0).astype(jnp.bfloat16), part_masks, 1
     )
@@ -483,8 +482,8 @@
         known = first_turns
         for mask in masks:
             if mask == masks[-1]:
-                piece, own_first, cosine, sine_part, all_routes = lax.optimization_barrier(
-                    (piece, own_first, cosine, sine_part, all_routes)
+                piece, own_first, cosine, sine_part = lax.optimization_barrier(
+                    (piece, own_first, cosine, sine_part)
                 )
             piece = jnp.concatenate([piece, swapped(piece, "seq", mask)], axis=0)
             known = known + [turn ^ mask for turn in known]
@@ -538,11 +537,11 @@
         placed = jnp.dot(rank, spread, preferred_element_type=jnp.float32) == wanted[None, :]
         return (chosen, valid_token, placed)
 
-    routings = [routing(turn, all_routes[k]) for k, turn in enumerate(part_turns)]
-    chosen, valid_token, _ = routings[0]
 
     starts = (tp_place + jnp.arange(tp_count, dtype=jnp.int32)) % tp_count * col_share
     rows = project(starts, tp_blocks(part_rows), head_weights, cosine, sine_part)
+    rows, routes = lax.optimization_barrier((rows, routes))
+    all_routes, part_turns = doubled(routes[None], part_masks, 0)
     sink = lax.dynamic_slice_in_dim(sink_logits, head, 1, 0)
 
     def start_state(row_count):
@@ -561,7 +560,9 @@
         row_ids = jnp.concatenate([part_ids, edge_ids])
         row_prompt, row_position = prompt_split(row_ids, slot_len, stagger, prompt_count)
         row_live = (row_ids >= 0) & (row_position < length_of(row_prompt, real_lengths))
-        halves, edge = lax.optimization_barrier(([half for half, _ in out_halves], edge))
+        halves, edge, all_routes = lax.optimization_barrier(
+            ([half for half, _ in out_halves], edge, all_routes)
+        )
         out_halves = [(half, masks) for half, (_, masks) in zip(halves, out_halves)]
         mixed = attend_once(
             sink,
@@ -600,6 +601,8 @@
             )
         _, denominator, accumulated = softmax_state
         mixed = (accumulated / denominator).astype(jnp.bfloat16)
+    routings = [routing(turn, all_routes[k]) for k, turn in enumerate(part_turns)]
+    chosen, valid_token, _ = routings[0]
     blocks = by_place(mixed.reshape(head_count, token_count, HEAD))
     out_halves = [(half, swapped(half, "seq", masks[0])) for half, masks in out_halves]
     blocks, out_halves, server_first = lax.optimization_barrier((blocks, out_halves, server_first))

time: 347 us -> 350 us (level)
  starting transfers between devices: 87.7 us -> 94.5 us
  waiting for transfers between devices: 147 us -> 143 us
    ppermute x22, starting transfers between devices: 33.8 us -> 43.2 us  [swapped(): lax.ppermute(value, axis, [(place, place ^ mask) for place in range(count)])]
    ppermute x22, waiting for transfers between devices: 85.7 us -> 80.2 us  [swapped(): lax.ppermute(value, axis, [(place, place ^ mask) for place in range(count)])]
    ppermute x2, starting transfers between devices: 7.86 us -> 3.23 us  [from_behind(): lax.ppermute(value, axis, [(source, source + steps) for source in range(f...]
    unnamed x90 -> x92, local copies, waits for them, and re-layouts: 26.1 us -> 26.1 us
  transfers between devices with their start and end apart: 38 -> 38, of which waited for: 20 -> 22; matrix products, arithmetic and copies ran while one was open for 13% -> 13% of each run, Pallas kernels for 14% -> 14%
where the time goes in v11:
time: 350 us; the launch traced here: 349 us
  waiting for transfers between devices  143 us (41%)
  starting transfers between devices  94.5 us (27%)
  Pallas kernels  53.7 us (15%)
  local copies, waits for them, and re-layouts  30.5 us (9%)
  other arithmetic  19.5 us (6%)
  matrix products  6.69 us (2%)
    ppermute x22, waiting for transfers between devices, swapped(): lax.ppermute(value, axis, [(place, place ^ mask) for place in range(count)])  80.2 us
    ppermute x22, starting transfers between devices, swapped(): lax.ppermute(value, axis, [(place, place ^ mask) for place in range(count)])  43.2 us
    all_to_all x4, starting transfers between devices, to_owner(): lax.all_to_all(blocks, 'seq', split_axis=0, concat_axis=0, tiled=True)  29.1 us
    unnamed x92, local copies, waits for them, and re-layouts  26.1 us
    all_to_all x4, waiting for transfers between devices, to_owner(): lax.all_to_all(blocks, 'seq', split_axis=0, concat_axis=0, tiled=True)  21 us
    all_to_all x2, waiting for transfers between devices, back(): lax.all_to_all(blocks, 'seq', split_axis=0, concat_axis=0, tiled=True, ax...  19.6 us
    pallas_call x1, Pallas kernels, order_experts(): pl.pallas_call(order_body, grid_spec=pltpu.PrefetchScalarGridSpec(num_sca...  12.8 us
    pallas_call x2, Pallas kernels, hidden_units(): pl.pallas_call(lambda *refs: hidden_body(count, share, *refs), grid_spec=...  11.6 us
  transfers between devices with their start and end apart: 38, of which 22 were waited for; matrix products, arithmetic and copies ran while one was open for 13% of the time, Pallas kernels for 14%

profile of v11, /device:TPU:0, one launch (start us, length us, event | category | flops | bytes accessed | tf_op | source)
XLA Modules:
  0.0 348.6 jit_solution(12222662473875100394)
XLA Ops:
  3.2 1.8 pack_heads.1
  5.4 3.1 collective-permute-start.2
  8.6 2.7 collective-permute-start
  11.3 4.4 %all-to-all-start = ((bf16[16,128,384]{2,1,0:T(8,128)(2,1)}), bf16[16,128,384]{2,1,0:T(8,128)(2,1)}, u32[]{:S(2)}, u32[]{:S(2)}) async-start(bf16[16,128,384]{2,1,0:T(8,128)(2,1)} %pack_heads.1), calls=%async_computation | async-start | bytes 3145728 | tf_op jit(solution)/shard_map/all_to_all | solution.py:451
  15.8 5.2 %collective-permute-done.2 = bf16[1,128,1024]{2,1,0:T(8,128)(2,1)S(1)} collective-permute-done((bf16[1,128,1024]{2,1,0:T(8,128)(2,1)S(1)}, bf16[1,128,1024]{2,1,0:T(8,128)(2,1)S(1)}, u32[]{:S(2)}, u32[]{:S(2)}) %collective-permute-start.2) | collective-permute-done | bytes 262176 | tf_op jit(solution)/shard_map/ppermute | solution.py:31
  21.1 2.1 collective-permute-start.3
  23.2 3.0 multiply_sine_fusion
  26.2 1.5 collective-permute-start.5
  27.7 12.8 %order_experts.1 = (bf16[16,128,256]{2,1,0:T(8,128)(2,1)}, bf16[16,128,256]{2,1,0:T(8,128)(2,1)}, bf16[16,128,512]{2,1,0:T(8,128)(2,1)}, bf16[16,128,512]{2,1,0:T(8,128)(2,1)}) custom-call(s32[16]{0:T(128)} %order_ref, f32[16,128,512]{2,1,0:T(8,128)} %gate_ref.1, f32[16,128,512]{2,1,0:T(8,128)} %up_ref.1, f32[16,128,512]{2,1,0:T(8,128)} %down_ref.1), custom_call_target="tpu_custom_call" | custom-call | flops 1 | bytes 1 | tf_op jit(solution)/shard_map/order_experts/pallas_call | solution.py:131
  41.6 15.7 %collective-permute-done.1 = bf16[1040,256]{1,0:T(8,128)(2,1)S(1)} collective-permute-done((bf16[1040,256]{1,0:T(8,128)(2,1)S(1)}, bf16[1040,256]{1,0:T(8,128)(2,1)S(1)}, u32[]{:S(2)}, u32[]{:S(2)}) %collective-permute-start.1) | collective-permute-done | bytes 532512 | tf_op jit(solution)/shard_map/ppermute | solution.py:31
  61.1 2.0 collective-permute-start.8
  64.5 8.3 %all-to-all-start.1 = ((bf16[16,128,256]{2,1,0:T(8,128)(2,1)}), bf16[16,128,256]{2,1,0:T(8,128)(2,1)S(1)}, u32[]{:S(2)}, u32[]{:S(2)}) async-start(bf16[16,128,256]{2,1,0:T(8,128)(2,1)} %get-tuple-element.83), calls=%async_computation.1 | async-start | bytes 2097152 | tf_op jit(solution)/shard_map/all_to_all | solution.py:494
  73.4 2.8 collective-permute-done.8
  76.2 2.3 pad_maximum_fusion.2.first_ref
  78.6 2.1 pad_maximum_fusion.1.second_ref
  80.7 5.8 %project.1 = bf16[1024,384]{1,0:T(8,128)(2,1)S(1)} custom-call(s32[2]{0:T(128)S(1)} %fusion.109.refs_0_, bf16[1024,1024]{1,0:T(8,128)(2,1)S(1)} %pad_maximum_fusion.refs_1_, bf16[1024,1024]{1,0:T(8,128)(2,1)} %collective-permute-done.7.refs_2_, bf16[2048,384]{1,0:T(8,128)(2,1)} %bitcast.6.refs_3_, f32[1024,64]{1,0:T(8,128)S(1)} %copy-done.7, ...), custom_call_target="tpu_custom_call" | custom-call | flops 1 | bytes 1 | tf_op jit(solution)/shard_map/project/pallas_call | solution.py:196
  86.6 10.3 %collective-permute-start.11 = (s32[1,128,8]{1,2,0:T(8,128)S(1)}, s32[1,128,8]{1,2,0:T(8,128)S(1)}, u32[]{:S(2)}, u32[]{:S(2)}) collective-permute-start(s32[1,128,8]{1,2,0:T(8,128)S(1)} %bitcast.174), channel_id=1, source_target_pairs={{0,16},{2,18},{4,20},{6,22},{8,24},{10,26},{12,28},{14,30},{16,0},... | collective-permute-start | bytes 12296 | tf_op jit(solution)/shard_map/ppermute | solution.py:31
  96.8 1.9 collective-permute-start.10
  98.8 1.7 collective-permute-done.10
  100.6 6.8 %attend_once.1 = bf16[1088,128]{1,0:T(8,128)(2,1)S(1)} custom-call(f32[1]{0:T(128)} %dynamic_slice.92.sink_ref, s32[1088,1]{1,0:T(8,128)S(1)} %copy-done.5, s32[1,1088]{1,0:T(1,128)S(1)} %and_select_fusion.key_prompt_ref, bf16[1088,384]{1,0:T(8,128)(2,1)S(1)} %pad_maximum_fusion.3.query_ref.key_ref.value_ref, ...), custom_call_target="tpu_custom_call" | custom-call | flops 1 | bytes 1 | tf_op jit(solution)/shard_map/attend_once/pallas_call | solution.py:238
  110.0 4.0 %collective-permute-done.12 = bf16[64,128]{1,0:T(8,128)(2,1)S(1)} collective-permute-done((bf16[64,128]{1,0:T(8,128)(2,1)S(1)}, bf16[64,128]{1,0:T(8,128)(2,1)S(1)}, u32[]{:S(2)}, u32[]{:S(2)}) %collective-permute-start.12) | collective-permute-done | bytes 16416 | tf_op jit(solution)/shard_map/ppermute | solution.py:21
  119.0 13.7 %collective-permute-done.13.first_other_ref = bf16[512,1024]{1,0:T(8,128)(2,1)} collective-permute-done((bf16[512,1024]{1,0:T(8,128)(2,1)S(1)}, bf16[512,1024]{1,0:T(8,128)(2,1)}, u32[]{:S(2)}, u32[]{:S(2)}) %collective-permute-start.13) | collective-permute-done | bytes 1048608 | tf_op jit(solution)/shard_map/ppermute | solution.py:31
  133.2 6.1 %all-to-all-start.2 = ((bf16[8,128,128]{2,1,0:T(8,128)(2,1)}), bf16[8,128,128]{2,1,0:T(8,128)(2,1)S(1)}, u32[]{:S(2)}, u32[]{:S(2)}) async-start(bf16[8,128,128]{2,1,0:T(8,128)(2,1)} %constant_dynamic-update-slice_fusion), calls=%async_computation.2 | async-start | bytes 524288 | tf_op jit(solution)/shard_map/all_to_all | solution.py:609
  139.5 6.5 %all-to-all-done.2.head_ref = bf16[8,128,128]{2,1,0:T(8,128)(2,1)S(1)} async-done(((bf16[8,128,128]{2,1,0:T(8,128)(2,1)}), bf16[8,128,128]{2,1,0:T(8,128)(2,1)S(1)}, u32[]{:S(2)}, u32[]{:S(2)}) %all-to-all-start.2) | async-done | bytes 262176 | tf_op jit(solution)/shard_map/all_to_all | solution.py:609
  146.0 5.0 %all-to-all-start.3 = ((bf16[16,128,256]{2,1,0:T(8,128)(2,1)}), bf16[16,128,256]{2,1,0:T(8,128)(2,1)}, u32[]{:S(2)}, u32[]{:S(2)}) async-start(bf16[16,128,256]{2,1,0:T(8,128)(2,1)} %get-tuple-element.95), calls=%async_computation.3 | async-start | bytes 2097152 | tf_op jit(solution)/shard_map/all_to_all | solution.py:494
  152.3 3.3 out_project.1.refs_1_
  156.5 2.1 collective-permute-done.15.refs_2_
  158.6 2.2 settle.1
  161.8 2.8 collective-permute-start.16
  165.4 21.1 %collective-permute-done.17 = f32[1,128,16]{2,1,0:T(8,128)S(1)} collective-permute-done((f32[1,128,16]{2,1,0:T(8,128)S(1)}, f32[1,128,16]{2,1,0:T(8,128)S(1)}, u32[]{:S(2)}, u32[]{:S(2)}) %collective-permute-start.17) | collective-permute-done | bytes 8224 | tf_op jit(solution)/shard_map/ppermute | solution.py:31
  187.4 4.6 %all-to-all-start.4 = ((bf16[16,128,512]{2,1,0:T(8,128)(2,1)}), bf16[16,128,512]{2,1,0:T(8,128)(2,1)S(1)}, u32[]{:S(2)}, u32[]{:S(2)}) async-start(bf16[16,128,512]{2,1,0:T(8,128)(2,1)} %get-tuple-element.99), calls=%async_computation.4 | async-start | bytes 4194304 | tf_op jit(solution)/shard_map/all_to_all | solution.py:494
  194.2 1.4 convolution_convert_fusion
  196.8 1.9 collective-permute-start.18
  198.7 1.5 collective-permute-start.19
  201.0 1.5 collective-permute-start.22
  202.5 1.5 collective-permute-start.20
  204.5 2.5 collective-permute-done.18
  207.0 5.5 %collective-permute-start.23 = (bf16[2,72,1024]{2,1,0:T(8,128)(2,1)}, bf16[2,72,1024]{2,1,0:T(8,128)(2,1)}, u32[]{:S(2)}, u32[]{:S(2)}) collective-permute-start(bf16[2,72,1024]{2,1,0:T(8,128)(2,1)} %get-tuple-element.129), channel_id=1, source_target_pairs={{0,12},{2,14},{4,8},{6,10},{8,4},{10,6},{12,0},{14,2},{16,28},{18,... | collective-permute-start | bytes 884744 | tf_op jit(solution)/shard_map/ppermute | solution.py:31
  212.6 9.0 %collective-permute-done.19 = bf16[2,72,1024]{2,1,0:T(8,128)(2,1)S(1)} collective-permute-done((bf16[2,72,1024]{2,1,0:T(8,128)(2,1)S(1)}, bf16[2,72,1024]{2,1,0:T(8,128)(2,1)S(1)}, u32[]{:S(2)}, u32[]{:S(2)}) %collective-permute-start.19) | collective-permute-done | bytes 294944 | tf_op jit(solution)/shard_map/ppermute | solution.py:31
  223.4 9.5 %all-to-all-done.4 = bf16[16,128,512]{2,1,0:T(8,128)(2,1)S(1)} async-done(((bf16[16,128,512]{2,1,0:T(8,128)(2,1)}), bf16[16,128,512]{2,1,0:T(8,128)(2,1)S(1)}, u32[]{:S(2)}, u32[]{:S(2)}) %all-to-all-start.4) | async-done | bytes 2097184 | tf_op jit(solution)/shard_map/all_to_all | solution.py:494
  232.9 11.3 %all-to-all-start.5 = ((bf16[16,128,512]{2,1,0:T(8,128)(2,1)}), bf16[16,128,512]{2,1,0:T(8,128)(2,1)}, u32[]{:S(2)}, u32[]{:S(2)}) async-start(bf16[16,128,512]{2,1,0:T(8,128)(2,1)} %get-tuple-element.106), calls=%async_computation.5 | async-start | bytes 4194304 | tf_op jit(solution)/shard_map/all_to_all | solution.py:494
  244.2 1.7 bitcast_dynamic-update-slice_fusion.6
  245.9 1.7 bitcast_dynamic-update-slice_fusion.5
  247.6 1.7 bitcast_dynamic-update-slice_fusion.4
  249.3 1.7 bitcast_dynamic-update-slice_fusion.3
  251.0 1.7 bitcast_dynamic-update-slice_fusion.2
  252.7 1.7 collective-permute-done.23
  254.4 1.7 bitcast_dynamic-update-slice_fusion.1
  256.1 7.9 %collective-permute-done.24 = bf16[2,72,1024]{2,1,0:T(8,128)(2,1)} collective-permute-done((bf16[2,72,1024]{2,1,0:T(8,128)(2,1)}, bf16[2,72,1024]{2,1,0:T(8,128)(2,1)}, u32[]{:S(2)}, u32[]{:S(2)}) %collective-permute-start.24) | collective-permute-done | bytes 294944 | tf_op jit(solution)/shard_map/ppermute | solution.py:31
  264.0 1.7 bitcast_dynamic-update-slice_fusion
  270.8 2.3 collective-permute-done.25.refs_2_
  274.2 5.8 %hidden_units.2.refs_1_ = bf16[1,576,512]{2,1,0:T(8,128)(2,1)S(1)} custom-call(s32[2]{0:T(128)S(1)} %fusion.109.refs_0_, bf16[1,576,1024]{2,1,0:T(8,128)(2,1)} %bitcast.160, bf16[1,576,1024]{2,1,0:T(8,128)(2,1)} %copy-done.20, bf16[1,2048,256]{2,1,0:T(8,128)(2,1)S(1)} %bitcast.148, bf16[1,2048,256]{2,1,0:T(8,128)(2,1)} %bitcast.32.refs_4_, ...), custom_call_target="tpu_custom_call" | custom-call | flops 1 | bytes 1 | tf_op jit(solution)/shard_map/hidden_units/pallas_call | solution.py:352
  280.0 11.6 %all-to-all-done.5 = bf16[16,128,512]{2,1,0:T(8,128)(2,1)} async-done(((bf16[16,128,512]{2,1,0:T(8,128)(2,1)}), bf16[16,128,512]{2,1,0:T(8,128)(2,1)}, u32[]{:S(2)}, u32[]{:S(2)}) %all-to-all-start.5) | async-done | bytes 2097184 | tf_op jit(solution)/shard_map/all_to_all | solution.py:494
  291.6 4.7 %down_rows.2 = (bf16[1,576,1024]{2,1,0:T(8,128)(2,1)S(1)}, bf16[1,576,1024]{2,1,0:T(8,128)(2,1)}) custom-call(s32[2]{0:T(128)S(1)} %fusion.110.refs_0_, bf16[1,576,512]{2,1,0:T(8,128)(2,1)S(1)} %hidden_units.2.refs_1_, bf16[1,2048,512]{2,1,0:T(8,128)(2,1)} %bitcast.56.refs_2_), custom_call_target="tpu_custom_call" | custom-call | flops 1 | bytes 1 | tf_op jit(solution)/shard_map/down_rows/pallas_call | solution.py:384
  296.3 3.1 collective-permute-done.27
  299.3 1.6 add_convert_fusion.1
  300.9 4.0 %all-to-all-start.6 = ((bf16[8,1,72,1024]{3,2,1,0:T(8,128)(2,1)}), bf16[8,1,72,1024]{3,2,1,0:T(8,128)(2,1)S(1)}, u32[]{:S(2)}, u32[]{:S(2)}) async-start(bf16[8,1,72,1024]{3,2,1,0:T(8,128)(2,1)} %bitcast.58), calls=%async_computation.6 | async-start | bytes 2359296 | tf_op jit(solution)/shard_map/all_to_all | solution.py:740
  304.9 5.8 %hidden_units.3.refs_1_ = bf16[1,576,512]{2,1,0:T(8,128)(2,1)S(1)} custom-call(s32[2]{0:T(128)S(1)} %fusion.109.refs_0_, bf16[1,576,1024]{2,1,0:T(8,128)(2,1)} %bitcast.158, bf16[1,576,1024]{2,1,0:T(8,128)(2,1)} %copy-done.19, bf16[1,2048,256]{2,1,0:T(8,128)(2,1)S(1)} %bitcast.149, bf16[1,2048,256]{2,1,0:T(8,128)(2,1)} %bitcast.32.refs_4_, ...), custom_call_target="tpu_custom_call" | custom-call | flops 1 | bytes 1 | tf_op jit(solution)/shard_map/hidden_units/pallas_call | solution.py:352
  310.7 4.6 %down_rows.3 = (bf16[1,576,1024]{2,1,0:T(8,128)(2,1)S(1)}, bf16[1,576,1024]{2,1,0:T(8,128)(2,1)}) custom-call(s32[2]{0:T(128)S(1)} %fusion.110.refs_0_, bf16[1,576,512]{2,1,0:T(8,128)(2,1)S(1)} %hidden_units.3.refs_1_, bf16[1,2048,512]{2,1,0:T(8,128)(2,1)} %bitcast.56.refs_2_), custom_call_target="tpu_custom_call" | custom-call | flops 1 | bytes 1 | tf_op jit(solution)/shard_map/down_rows/pallas_call | solution.py:384
  316.1 2.2 collective-permute-done.28
  318.4 1.5 add_convert_fusion
  322.1 3.8 %all-to-all-start.7 = ((bf16[8,1,72,1024]{3,2,1,0:T(8,128)(2,1)}), bf16[8,1,72,1024]{3,2,1,0:T(8,128)(2,1)S(1)}, u32[]{:S(2)}, u32[]{:S(2)}) async-start(bf16[8,1,72,1024]{3,2,1,0:T(8,128)(2,1)} %bitcast.62), calls=%async_computation.7 | async-start | bytes 2359296 | tf_op jit(solution)/shard_map/all_to_all | solution.py:740
  326.7 1.8 collective-permute-start.29
  328.6 18.3 %all-to-all-done.7 = bf16[8,1,72,1024]{3,2,1,0:T(8,128)(2,1)S(1)} async-done(((bf16[8,1,72,1024]{3,2,1,0:T(8,128)(2,1)}), bf16[8,1,72,1024]{3,2,1,0:T(8,128)(2,1)S(1)}, u32[]{:S(2)}, u32[]{:S(2)}) %all-to-all-start.7) | async-done | bytes 1179680 | tf_op jit(solution)/shard_map/all_to_all | solution.py:740
  (199 shorter events, 41.9 us)
Async XLA Ops:
  0.0 5.0 %copy-start = (bf16[128,2048]{1,0:T(8,128)(2,1)S(1)}, bf16[128,2048]{1,0:T(8,128)(2,1)}, u32[]{:S(2)}) copy-start(bf16[128,2048]{1,0:T(8,128)(2,1)} %refs_3_) | copy-start | bytes 1572868
  0.0 1.1 copy-start.8
  1.1 1.0 copy-start.9
  3.2 2.1 copy-start.27
  3.2 5.3 %copy-start.21 = (f32[1024,128]{1,0:T(8,128)S(1)}, f32[1024,128]{1,0:T(8,128)}, u32[]{:S(2)}) copy-start(f32[1024,128]{1,0:T(8,128)} %param.21) | copy-start | bytes 1572868
  5.0 3.6 %copy-start.24 = (f32[128,16]{0,1:T(8,128)S(1)}, f32[128,16]{0,1:T(8,128)}, u32[]{:S(2)}) copy-start(f32[128,16]{0,1:T(8,128)} %param.23) | copy-start | bytes 24580
  5.4 15.6 %collective-permute-start.2 = (bf16[1,128,1024]{2,1,0:T(8,128)(2,1)S(1)}, bf16[1,128,1024]{2,1,0:T(8,128)(2,1)S(1)}, u32[]{:S(2)}, u32[]{:S(2)}) collective-permute-start(bf16[1,128,1024]{2,1,0:T(8,128)(2,1)S(1)} %fusion.44), channel_id=1, source_target_pairs={{0,8},{2,10},{4,12},{6,14},{8,0},{10,2},{12,4},{14,6},{16,24},{18,... | collective-permute-start | bytes 786440 | tf_op jit(solution)/shard_map/ppermute | solution.py:31
  8.6 31.9 %collective-permute-start = (bf16[1040,128]{1,0:T(8,128)(2,1)S(1)}, bf16[1040,128]{1,0:T(8,128)(2,1)S(1)}, u32[]{:S(2)}, u32[]{:S(2)}) collective-permute-start(bf16[1040,128]{1,0:T(8,128)(2,1)S(1)} %pad_maximum_fusion.13), channel_id=1, source_target_pairs={{0,16},{2,18},{4,20},{6,22},{8,24},{10,26},{12,28},{14,30},{16,0},... | collective-permute-start | bytes 798728 | tf_op jit(solution)/shard_map/ppermute | solution.py:31
  11.3 48.2 %all-to-all-start = ((bf16[16,128,384]{2,1,0:T(8,128)(2,1)}), bf16[16,128,384]{2,1,0:T(8,128)(2,1)}, u32[]{:S(2)}, u32[]{:S(2)}) async-start(bf16[16,128,384]{2,1,0:T(8,128)(2,1)} %pack_heads.1), calls=%async_computation | async-start | bytes 3145728 | tf_op jit(solution)/shard_map/all_to_all | solution.py:451
  21.1 19.6 %collective-permute-start.3 = (bf16[2,128,512]{2,1,0:T(8,128)(2,1)S(1)}, bf16[2,128,512]{2,1,0:T(8,128)(2,1)S(1)}, u32[]{:S(2)}, u32[]{:S(2)}) collective-permute-start(bf16[2,128,512]{2,1,0:T(8,128)(2,1)S(1)} %get-tuple-element.135), channel_id=1, source_target_pairs={{0,4},{2,6},{4,0},{6,2},{8,12},{10,14},{12,8},{14,10},{16,20},{18,... | collective-permute-start | bytes 786440 | tf_op jit(solution)/shard_map/ppermute | solution.py:31
  26.2 15.1 %collective-permute-start.5 = (bf16[2,128,512]{2,1,0:T(8,128)(2,1)S(1)}, bf16[2,128,512]{2,1,0:T(8,128)(2,1)S(1)}, u32[]{:S(2)}, u32[]{:S(2)}) collective-permute-start(bf16[2,128,512]{2,1,0:T(8,128)(2,1)S(1)} %get-tuple-element.136), channel_id=1, source_target_pairs={{0,2},{2,0},{4,6},{6,4},{8,10},{10,8},{12,14},{14,12},{16,18},{18,... | collective-permute-start | bytes 786440 | tf_op jit(solution)/shard_map/ppermute | solution.py:31
  40.6 16.6 %collective-permute-start.1 = (bf16[1040,256]{1,0:T(8,128)(2,1)S(1)}, bf16[1040,256]{1,0:T(8,128)(2,1)S(1)}, u32[]{:S(2)}, u32[]{:S(2)}) collective-permute-start(bf16[1040,256]{1,0:T(8,128)(2,1)S(1)} %pad_maximum_fusion.7), channel_id=1, source_target_pairs={{0,8},{2,10},{4,12},{6,14},{8,0},{10,2},{12,4},{14,6},{16,24},{18,... | collective-permute-start | bytes 1597448 | tf_op jit(solution)/shard_map/ppermute | solution.py:31
  40.7 18.2 %collective-permute-start.4 = (bf16[4,128,512]{2,1,0:T(8,128)(2,1)S(1)}, bf16[4,128,512]{2,1,0:T(8,128)(2,1)S(1)}, u32[]{:S(2)}, u32[]{:S(2)}) collective-permute-start(bf16[4,128,512]{2,1,0:T(8,128)(2,1)S(1)} %pad_maximum_fusion.10), channel_id=1, source_target_pairs={{0,2},{2,0},{4,6},{6,4},{8,10},{10,8},{12,14},{14,12},{16,18},{18,... | collective-permute-start | bytes 1572872 | tf_op jit(solution)/shard_map/ppermute | solution.py:31
  41.4 17.6 %collective-permute-start.6 = (bf16[4,128,512]{2,1,0:T(8,128)(2,1)S(1)}, bf16[4,128,512]{2,1,0:T(8,128)(2,1)S(1)}, u32[]{:S(2)}, u32[]{:S(2)}) collective-permute-start(bf16[4,128,512]{2,1,0:T(8,128)(2,1)S(1)} %pad_maximum_fusion.11), channel_id=1, source_target_pairs={{0,4},{2,6},{4,0},{6,2},{8,12},{10,14},{12,8},{14,10},{16,20},{18,... | collective-permute-start | bytes 1572872 | tf_op jit(solution)/shard_map/ppermute | solution.py:31
  59.2 5.2 %copy-start.26 = (s32[2]{0:T(128)S(1)}, s32[2]{0:T(128)}, u32[]{:S(2)}) copy-start(s32[2]{0:T(128)} %param.28) | copy-start | bytes 28
  59.4 13.3 %copy-start.28 = (f32[8]{0:T(128)S(1)}, f32[8]{0:T(128)}, u32[]{:S(2)}) copy-start(f32[8]{0:T(128)} %param.22) | copy-start | bytes 100
  59.5 21.3 %collective-permute-start.7 = (bf16[1024,1024]{1,0:T(8,128)(2,1)S(1)}, bf16[1024,1024]{1,0:T(8,128)(2,1)}, u32[]{:S(2)}, u32[]{:S(2)}) collective-permute-start(bf16[1024,1024]{1,0:T(8,128)(2,1)S(1)} %pad_maximum_fusion.refs_1_), channel_id=1, source_target_pairs={{1,0},{0,1},{3,2},{2,3},{5,4},{4,5},{7,6},{6,7},{9,8},{8,9},{11,10... | collective-permute-start | bytes 6291464 | tf_op jit(solution)/shard_map/ppermute | solution.py:26
  61.1 15.1 %collective-permute-start.8 = (bf16[512,512]{1,0:T(8,128)(2,1)}, bf16[512,512]{1,0:T(8,128)(2,1)}, u32[]{:S(2)}, u32[]{:S(2)}) collective-permute-start(bf16[512,512]{1,0:T(8,128)(2,1)} %pad_maximum_fusion.8), channel_id=1, source_target_pairs={{0,4},{2,6},{4,0},{6,2},{8,12},{10,14},{12,8},{14,10},{16,20},{18,... | collective-permute-start | bytes 1572872 | tf_op jit(solution)/shard_map/ppermute | solution.py:31
  63.1 15.5 %collective-permute-start.9 = (bf16[528,512]{1,0:T(8,128)(2,1)}, bf16[528,512]{1,0:T(8,128)(2,1)}, u32[]{:S(2)}, u32[]{:S(2)}) collective-permute-start(bf16[528,512]{1,0:T(8,128)(2,1)} %pad_maximum_fusion.4), channel_id=1, source_target_pairs={{0,2},{2,0},{4,6},{6,4},{8,10},{10,8},{12,14},{14,12},{16,18},{18,... | collective-permute-start | bytes 1622024 | tf_op jit(solution)/shard_map/ppermute | solution.py:31
  64.5 54.5 %all-to-all-start.1 = ((bf16[16,128,256]{2,1,0:T(8,128)(2,1)}), bf16[16,128,256]{2,1,0:T(8,128)(2,1)S(1)}, u32[]{:S(2)}, u32[]{:S(2)}) async-start(bf16[16,128,256]{2,1,0:T(8,128)(2,1)} %get-tuple-element.83), calls=%async_computation.1 | async-start | bytes 2097152 | tf_op jit(solution)/shard_map/all_to_all | solution.py:494
  72.8 5.8 %copy-start.18 = (bf16[528,512]{1,0:T(8,128)(2,1)S(1)}, bf16[528,512]{1,0:T(8,128)(2,1)}, u32[]{:S(2)}) copy-start(bf16[528,512]{1,0:T(8,128)(2,1)} %pad_maximum_fusion.4) | copy-start | bytes 1622020
  72.8 7.9 %copy-start.6 = (f32[1024,64]{1,0:T(8,128)S(1)}, f32[1024,64]{1,0:T(8,128)}, u32[]{:S(2)}) copy-start(f32[1024,64]{1,0:T(8,128)} %get-tuple-element.75.refs_5_) | copy-start | bytes 786436
  72.8 7.9 %copy-start.7 = (f32[1024,64]{1,0:T(8,128)S(1)}, f32[1024,64]{1,0:T(8,128)}, u32[]{:S(2)}) copy-start(f32[1024,64]{1,0:T(8,128)} %get-tuple-element.74.refs_4_) | copy-start | bytes 786436
  80.7 5.9 %copy-start.25 = (s32[128,8]{0,1:T(8,128)S(1)}, s32[128,8]{0,1:T(8,128)}, u32[]{:S(2)}) copy-start(s32[128,8]{0,1:T(8,128)} %param.29) | copy-start | bytes 12292
  80.7 19.9 %copy-start.5 = (s32[1088,1]{1,0:T(8,128)S(1)}, s32[1088,1]{1,0:T(8,128)}, u32[]{:S(2)}) copy-start(s32[1088,1]{1,0:T(8,128)} %fusion.9.query_prompt_ref) | copy-start | bytes 13060
  86.6 12.2 %collective-permute-start.11 = (s32[1,128,8]{1,2,0:T(8,128)S(1)}, s32[1,128,8]{1,2,0:T(8,128)S(1)}, u32[]{:S(2)}, u32[]{:S(2)}) collective-permute-start(s32[1,128,8]{1,2,0:T(8,128)S(1)} %bitcast.174), channel_id=1, source_target_pairs={{0,16},{2,18},{4,20},{6,22},{8,24},{10,26},{12,28},{14,30},{16,0},... | collective-permute-start | bytes 12296 | tf_op jit(solution)/shard_map/ppermute | solution.py:31
  96.8 3.7 %collective-permute-start.10 = (bf16[64,384]{1,0:T(8,128)(2,1)S(1)}, bf16[64,384]{1,0:T(8,128)(2,1)S(1)}, u32[]{:S(2)}, u32[]{:S(2)}) collective-permute-start(bf16[64,384]{1,0:T(8,128)(2,1)S(1)} %constant_dynamic-slice_fusion), channel_id=1, source_target_pairs={{0,16},{2,18},{4,20},{6,22},{8,24},{10,26},{12,28},{14,30},{1,17},... | collective-permute-start | bytes 147464 | tf_op jit(solution)/shard_map/ppermute | solution.py:21
  100.6 8.2 %copy-start.2 = (bf16[528,1024]{1,0:T(8,128)(2,1)S(1)}, bf16[528,1024]{1,0:T(8,128)(2,1)}, u32[]{:S(2)}) copy-start(bf16[528,1024]{1,0:T(8,128)(2,1)} %pad_maximum_fusion.1.second_ref) | copy-start | bytes 3244036
  100.6 8.7 %copy-start.3 = (bf16[512,1024]{1,0:T(8,128)(2,1)S(1)}, bf16[512,1024]{1,0:T(8,128)(2,1)}, u32[]{:S(2)}) copy-start(bf16[512,1024]{1,0:T(8,128)(2,1)} %pad_maximum_fusion.2.first_ref) | copy-start | bytes 3145732
  107.5 6.5 %collective-permute-start.12 = (bf16[64,128]{1,0:T(8,128)(2,1)S(1)}, bf16[64,128]{1,0:T(8,128)(2,1)S(1)}, u32[]{:S(2)}, u32[]{:S(2)}) collective-permute-start(bf16[64,128]{1,0:T(8,128)(2,1)S(1)} %slice.175), channel_id=1, source_target_pairs={{16,0},{18,2},{20,4},{22,6},{24,8},{26,10},{28,12},{30,14},{17,1},... | collective-permute-start | bytes 49160 | tf_op jit(solution)/shard_map/ppermute | solution.py:21
  108.9 24.4 %collective-permute-start.14 = (bf16[528,1024]{1,0:T(8,128)(2,1)S(1)}, bf16[528,1024]{1,0:T(8,128)(2,1)}, u32[]{:S(2)}, u32[]{:S(2)}) collective-permute-start(bf16[528,1024]{1,0:T(8,128)(2,1)S(1)} %copy-done.2), channel_id=1, source_target_pairs={{0,4},{2,6},{4,0},{6,2},{8,12},{10,14},{12,8},{14,10},{16,20},{18,... | collective-permute-start | bytes 3244040 | tf_op jit(solution)/shard_map/ppermute | solution.py:31
  109.3 23.3 %collective-permute-start.13 = (bf16[512,1024]{1,0:T(8,128)(2,1)S(1)}, bf16[512,1024]{1,0:T(8,128)(2,1)}, u32[]{:S(2)}, u32[]{:S(2)}) collective-permute-start(bf16[512,1024]{1,0:T(8,128)(2,1)S(1)} %copy-done.3), channel_id=1, source_target_pairs={{0,2},{2,0},{4,6},{6,4},{8,10},{10,8},{12,14},{14,12},{16,18},{18,... | collective-permute-start | bytes 3145736 | tf_op jit(solution)/shard_map/ppermute | solution.py:31
  133.2 12.7 %all-to-all-start.2 = ((bf16[8,128,128]{2,1,0:T(8,128)(2,1)}), bf16[8,128,128]{2,1,0:T(8,128)(2,1)S(1)}, u32[]{:S(2)}, u32[]{:S(2)}) async-start(bf16[8,128,128]{2,1,0:T(8,128)(2,1)} %constant_dynamic-update-slice_fusion), calls=%async_computation.2 | async-start | bytes 524288 | tf_op jit(solution)/shard_map/all_to_all | solution.py:609
  146.0 41.5 %all-to-all-start.3 = ((bf16[16,128,256]{2,1,0:T(8,128)(2,1)}), bf16[16,128,256]{2,1,0:T(8,128)(2,1)}, u32[]{:S(2)}, u32[]{:S(2)}) async-start(bf16[16,128,256]{2,1,0:T(8,128)(2,1)} %get-tuple-element.95), calls=%async_computation.3 | async-start | bytes 2097152 | tf_op jit(solution)/shard_map/all_to_all | solution.py:494
  151.1 1.2 copy-start.4
  152.3 6.3 %copy-start.1 = (bf16[128,2048]{1,0:T(8,128)(2,1)S(1)}, bf16[128,2048]{1,0:T(8,128)(2,1)}, u32[]{:S(2)}) copy-start(bf16[128,2048]{1,0:T(8,128)(2,1)} %refs_3_) | copy-start | bytes 1572868
  152.3 6.3 %copy-start.13 = (f32[2048]{0:T(1024)S(1)}, f32[2048]{0:T(1024)}, u32[]{:S(2)}) copy-start(f32[2048]{0:T(1024)} %param.17) | copy-start | bytes 24580
  155.6 3.0 collective-permute-start.15
  161.8 24.7 %collective-permute-start.16 = (bf16[1,128,1024]{2,1,0:T(8,128)(2,1)S(1)}, bf16[1,128,1024]{2,1,0:T(8,128)(2,1)S(1)}, u32[]{:S(2)}, u32[]{:S(2)}) collective-permute-start(bf16[1,128,1024]{2,1,0:T(8,128)(2,1)S(1)} %dynamic-slice_bitcast_fusion), channel_id=1, source_target_pairs={{0,16},{2,18},{4,20},{6,22},{8,24},{10,26},{12,28},{14,30},{16,0},... | collective-permute-start | bytes 786440 | tf_op jit(solution)/shard_map/ppermute | solution.py:31
  165.1 21.3 %collective-permute-start.17 = (f32[1,128,16]{2,1,0:T(8,128)S(1)}, f32[1,128,16]{2,1,0:T(8,128)S(1)}, u32[]{:S(2)}, u32[]{:S(2)}) collective-permute-start(f32[1,128,16]{2,1,0:T(8,128)S(1)} %multiply_bitcast_fusion), channel_id=1, source_target_pairs={{0,16},{2,18},{4,20},{6,22},{8,24},{10,26},{12,28},{14,30},{16,0},... | collective-permute-start | bytes 24584 | tf_op jit(solution)/shard_map/ppermute | solution.py:31
  187.4 45.5 %all-to-all-start.4 = ((bf16[16,128,512]{2,1,0:T(8,128)(2,1)}), bf16[16,128,512]{2,1,0:T(8,128)(2,1)S(1)}, u32[]{:S(2)}, u32[]{:S(2)}) async-start(bf16[16,128,512]{2,1,0:T(8,128)(2,1)} %get-tuple-element.99), calls=%async_computation.4 | async-start | bytes 4194304 | tf_op jit(solution)/shard_map/all_to_all | solution.py:494
  196.8 10.2 %collective-permute-start.18 = (bf16[2,72,1024]{2,1,0:T(8,128)(2,1)S(1)}, bf16[2,72,1024]{2,1,0:T(8,128)(2,1)S(1)}, u32[]{:S(2)}, u32[]{:S(2)}) collective-permute-start(bf16[2,72,1024]{2,1,0:T(8,128)(2,1)S(1)} %get-tuple-element.125), channel_id=1, source_target_pairs={{0,2},{2,0},{4,6},{6,4},{8,10},{10,8},{12,14},{14,12},{16,18},{18,... | collective-permute-start | bytes 884744 | tf_op jit(solution)/shard_map/ppermute | solution.py:31
  198.7 22.8 %collective-permute-start.19 = (bf16[2,72,1024]{2,1,0:T(8,128)(2,1)S(1)}, bf16[2,72,1024]{2,1,0:T(8,128)(2,1)S(1)}, u32[]{:S(2)}, u32[]{:S(2)}) collective-permute-start(bf16[2,72,1024]{2,1,0:T(8,128)(2,1)S(1)} %get-tuple-element.126), channel_id=1, source_target_pairs={{0,4},{2,6},{4,0},{6,2},{8,12},{10,14},{12,8},{14,10},{16,20},{18,... | collective-permute-start | bytes 884744 | tf_op jit(solution)/shard_map/ppermute | solution.py:31
  201.0 50.0 %collective-permute-start.22 = (bf16[2,72,1024]{2,1,0:T(8,128)(2,1)}, bf16[2,72,1024]{2,1,0:T(8,128)(2,1)}, u32[]{:S(2)}, u32[]{:S(2)}) collective-permute-start(bf16[2,72,1024]{2,1,0:T(8,128)(2,1)} %get-tuple-element.130), channel_id=1, source_target_pairs={{0,10},{2,8},{4,14},{6,12},{8,2},{10,0},{12,6},{14,4},{16,26},{18,... | collective-permute-start | bytes 884744 | tf_op jit(solution)/shard_map/ppermute | solution.py:31
  202.5 45.1 %collective-permute-start.20 = (bf16[2,72,1024]{2,1,0:T(8,128)(2,1)}, bf16[2,72,1024]{2,1,0:T(8,128)(2,1)}, u32[]{:S(2)}, u32[]{:S(2)}) collective-permute-start(bf16[2,72,1024]{2,1,0:T(8,128)(2,1)} %get-tuple-element.127), channel_id=1, source_target_pairs={{0,6},{2,4},{4,2},{6,0},{8,14},{10,12},{12,10},{14,8},{16,22},{18,... | collective-permute-start | bytes 884744 | tf_op jit(solution)/shard_map/ppermute | solution.py:31
  204.0 45.3 %collective-permute-start.21 = (bf16[2,72,1024]{2,1,0:T(8,128)(2,1)}, bf16[2,72,1024]{2,1,0:T(8,128)(2,1)}, u32[]{:S(2)}, u32[]{:S(2)}) collective-permute-start(bf16[2,72,1024]{2,1,0:T(8,128)(2,1)} %get-tuple-element.128), channel_id=1, source_target_pairs={{0,8},{2,10},{4,12},{6,14},{8,0},{10,2},{12,4},{14,6},{16,24},{18,... | collective-permute-start | bytes 884744 | tf_op jit(solution)/shard_map/ppermute | solution.py:31
  207.0 14.5 %copy-start.22 = (bf16[2,72,1024]{2,1,0:T(8,128)(2,1)}, bf16[2,72,1024]{2,1,0:T(8,128)(2,1)S(1)}, u32[]{:S(2)}) copy-start(bf16[2,72,1024]{2,1,0:T(8,128)(2,1)S(1)} %collective-permute-done.18) | copy-start | bytes 884740
  207.0 47.4 %collective-permute-start.23 = (bf16[2,72,1024]{2,1,0:T(8,128)(2,1)}, bf16[2,72,1024]{2,1,0:T(8,128)(2,1)}, u32[]{:S(2)}, u32[]{:S(2)}) collective-permute-start(bf16[2,72,1024]{2,1,0:T(8,128)(2,1)} %get-tuple-element.129), channel_id=1, source_target_pairs={{0,12},{2,14},{4,8},{6,10},{8,4},{10,6},{12,0},{14,2},{16,28},{18,... | collective-permute-start | bytes 884744 | tf_op jit(solution)/shard_map/ppermute | solution.py:31
  222.2 41.8 %collective-permute-start.24 = (bf16[2,72,1024]{2,1,0:T(8,128)(2,1)}, bf16[2,72,1024]{2,1,0:T(8,128)(2,1)}, u32[]{:S(2)}, u32[]{:S(2)}) collective-permute-start(bf16[2,72,1024]{2,1,0:T(8,128)(2,1)} %get-tuple-element.123), channel_id=1, source_target_pairs={{0,14},{2,12},{4,10},{6,8},{8,6},{10,4},{12,2},{14,0},{16,30},{18,... | collective-permute-start | bytes 884744 | tf_op jit(solution)/shard_map/ppermute | solution.py:31
  232.9 13.0 %copy-start.14 = (bf16[16,128,512]{2,1,0:T(8,128)(2,1)}, bf16[16,128,512]{2,1,0:T(8,128)(2,1)S(1)}, u32[]{:S(2)}) copy-start(bf16[16,128,512]{2,1,0:T(8,128)(2,1)S(1)} %all-to-all-done.4) | copy-start | bytes 6291460
  232.9 58.7 %all-to-all-start.5 = ((bf16[16,128,512]{2,1,0:T(8,128)(2,1)}), bf16[16,128,512]{2,1,0:T(8,128)(2,1)}, u32[]{:S(2)}, u32[]{:S(2)}) async-start(bf16[16,128,512]{2,1,0:T(8,128)(2,1)} %get-tuple-element.106), calls=%async_computation.5 | async-start | bytes 4194304 | tf_op jit(solution)/shard_map/all_to_all | solution.py:494
  265.7 4.1 %copy-start.17 = (bf16[8,2,72,1024]{3,2,0,1:T(8,128)(2,1)S(1)}, bf16[8,2,72,1024]{3,2,0,1:T(8,128)(2,1)}, u32[]{:S(2)}) copy-start(bf16[8,2,72,1024]{3,2,0,1:T(8,128)(2,1)} %bitcast_dynamic-update-slice_fusion) | copy-start | bytes 7077892
  270.2 2.9 copy-start.16
  270.2 9.8 %copy-start.15 = (bf16[8,1,1,72,1024]{4,3,0,2,1:T(8,128)(2,1)}, bf16[8,1,1,72,1024]{4,3,0,2,1:T(8,128)(2,1)S(1)}, u32[]{:S(2)}) copy-start(bf16[8,1,1,72,1024]{4,3,0,2,1:T(8,128)(2,1)S(1)} %get-tuple-element.121) | copy-start | bytes 3538948
  270.2 2.9 collective-permute-start.25
  270.3 9.7 %collective-permute-start.26 = (bf16[1,576,1024]{2,1,0:T(8,128)(2,1)S(1)}, bf16[1,576,1024]{2,1,0:T(8,128)(2,1)S(1)}, u32[]{:S(2)}, u32[]{:S(2)}) collective-permute-start(bf16[1,576,1024]{2,1,0:T(8,128)(2,1)S(1)} %bitcast.157), channel_id=1, source_target_pairs={{1,0},{0,1},{3,2},{2,3},{5,4},{4,5},{7,6},{6,7},{9,8},{8,9},{11,10... | collective-permute-start | bytes 3538952 | tf_op jit(solution)/shard_map/ppermute | solution.py:26
  273.1 1.1 copy-start.20
  280.0 20.9 %copy-start.19 = (bf16[1,576,1024]{2,1,0:T(8,128)(2,1)}, bf16[1,576,1024]{2,1,0:T(8,128)(2,1)S(1)}, u32[]{:S(2)}) copy-start(bf16[1,576,1024]{2,1,0:T(8,128)(2,1)S(1)} %collective-permute-done.26.refs_2_) | copy-start | bytes 3538948
  296.3 3.1 collective-permute-start.27
  300.9 20.3 %all-to-all-start.6 = ((bf16[8,1,72,1024]{3,2,1,0:T(8,128)(2,1)}), bf16[8,1,72,1024]{3,2,1,0:T(8,128)(2,1)S(1)}, u32[]{:S(2)}, u32[]{:S(2)}) async-start(bf16[8,1,72,1024]{3,2,1,0:T(8,128)(2,1)} %bitcast.58), calls=%async_computation.6 | async-start | bytes 2359296 | tf_op jit(solution)/shard_map/all_to_all | solution.py:740
  315.3 3.1 collective-permute-start.28
  322.1 24.8 %all-to-all-start.7 = ((bf16[8,1,72,1024]{3,2,1,0:T(8,128)(2,1)}), bf16[8,1,72,1024]{3,2,1,0:T(8,128)(2,1)S(1)}, u32[]{:S(2)}, u32[]{:S(2)}) async-start(bf16[8,1,72,1024]{3,2,1,0:T(8,128)(2,1)} %bitcast.62), calls=%async_computation.7 | async-start | bytes 2359296 | tf_op jit(solution)/shard_map/all_to_all | solution.py:740
  326.4 21.2 %copy-start.12 = (f32[128,2048]{1,0:T(8,128)S(1)}, f32[128,2048]{1,0:T(8,128)}, u32[]{:S(2)}) copy-start(f32[128,2048]{1,0:T(8,128)} %copy-done.11) | copy-start | bytes 3145732
  326.7 20.9 %collective-permute-start.29 = (bf16[128,1024]{1,0:T(8,128)(2,1)S(1)}, bf16[128,1024]{1,0:T(8,128)(2,1)S(1)}, u32[]{:S(2)}, u32[]{:S(2)}) collective-permute-start(bf16[128,1024]{1,0:T(8,128)(2,1)S(1)} %slice_add_fusion.2), channel_id=1, source_target_pairs={{0,16},{2,18},{4,20},{6,22},{8,24},{10,26},{12,28},{14,30},{16,0},... | collective-permute-start | bytes 786440 | tf_op jit(solution)/shard_map/ppermute | solution.py:31
  (3 other events, 2.7 us)

commit v12 on v10

--- a/solution.py
+++ b/solution.py
@@ -739,10 +739,10 @@
         )
 
     others = back(others)
+    others, own_rows = lax.optimization_barrier((others, own_rows))
     mixes = [
         weighted(k, others[:, k - 1].reshape(-1, col_share)) for k in range(1, len(part_turns))
     ]
-    mixes, own_rows = lax.optimization_barrier((mixes, own_rows))
     expert_mix = sum(
         swapped(mix.astype(jnp.bfloat16), "seq", turn).astype(jnp.float32)
         for mix, turn in zip(mixes, part_turns[1:])

time: 347 us -> 348 us (level)
  transfers between devices with their start and end apart: 38 -> 38, of which waited for: 20 -> 20; matrix products, arithmetic and copies ran while one was open for 13% -> 14% of each run, Pallas kernels for 14% -> 14%
where the time goes in v12:
time: 348 us; the launch traced here: 346 us
  waiting for transfers between devices  146 us (42%)
  starting transfers between devices  88.1 us (25%)
  Pallas kernels  53.7 us (15%)
  local copies, waits for them, and re-layouts  30.6 us (9%)
  other arithmetic  18.5 us (5%)
  matrix products  7.97 us (2%)
    ppermute x22, waiting for transfers between devices, swapped(): lax.ppermute(value, axis, [(place, place ^ mask) for place in range(count)])  85.7 us
    ppermute x22, starting transfers between devices, swapped(): lax.ppermute(value, axis, [(place, place ^ mask) for place in range(count)])  33.8 us
    all_to_all x4, starting transfers between devices, to_owner(): lax.all_to_all(blocks, 'seq', split_axis=0, concat_axis=0, tiled=True)  27 us
    unnamed x90, local copies, waits for them, and re-layouts  26.1 us
    all_to_all x4, waiting for transfers between devices, to_owner(): lax.all_to_all(blocks, 'seq', split_axis=0, concat_axis=0, tiled=True)  21 us
    all_to_all x2, waiting for transfers between devices, back(): lax.all_to_all(blocks, 'seq', split_axis=0, concat_axis=0, tiled=True, ax...  17.6 us
    pallas_call x1, Pallas kernels, order_experts(): pl.pallas_call(order_body, grid_spec=pltpu.PrefetchScalarGridSpec(num_sca...  12.8 us
    pallas_call x2, Pallas kernels, hidden_units(): pl.pallas_call(lambda *refs: hidden_body(count, share, *refs), grid_spec=...  11.6 us
  transfers between devices with their start and end apart: 38, of which 20 were waited for; matrix products, arithmetic and copies ran while one was open for 14% of the time, Pallas kernels for 14%

profile of v12, /device:TPU:0, one launch (start us, length us, event | category | flops | bytes accessed | tf_op | source)
XLA Modules:
  0.0 346.0 jit_solution(12594365419899472487)
XLA Ops:
  3.2 1.8 pack_heads.1
  5.5 3.1 collective-permute-start.2
  8.6 2.6 collective-permute-start.4
  11.7 5.9 %all-to-all-start = ((bf16[16,128,384]{2,1,0:T(8,128)(2,1)}), bf16[16,128,384]{2,1,0:T(8,128)(2,1)}, u32[]{:S(2)}, u32[]{:S(2)}) async-start(bf16[16,128,384]{2,1,0:T(8,128)(2,1)} %pack_heads.1), calls=%async_computation | async-start | bytes 3145728 | tf_op jit(solution)/shard_map/all_to_all | solution.py:451
  17.7 3.1 multiply_sine_fusion
  20.9 1.9 collective-permute-start.3
  22.8 1.5 collective-permute-start.6
  24.2 12.8 %order_experts.1 = (bf16[16,128,256]{2,1,0:T(8,128)(2,1)}, bf16[16,128,256]{2,1,0:T(8,128)(2,1)}, bf16[16,128,512]{2,1,0:T(8,128)(2,1)}, bf16[16,128,512]{2,1,0:T(8,128)(2,1)}) custom-call(s32[16]{0:T(128)} %order_ref, f32[16,128,512]{2,1,0:T(8,128)} %gate_ref.1, f32[16,128,512]{2,1,0:T(8,128)} %up_ref.1, f32[16,128,512]{2,1,0:T(8,128)} %down_ref.1), custom_call_target="tpu_custom_call" | custom-call | flops 1 | bytes 1 | tf_op jit(solution)/shard_map/order_experts/pallas_call | solution.py:131
  37.1 6.3 %collective-permute-done = bf16[1040,128]{1,0:T(8,128)(2,1)S(1)} collective-permute-done((bf16[1040,128]{1,0:T(8,128)(2,1)S(1)}, bf16[1040,128]{1,0:T(8,128)(2,1)S(1)}, u32[]{:S(2)}, u32[]{:S(2)}) %collective-permute-start) | collective-permute-done | bytes 266272 | tf_op jit(solution)/shard_map/ppermute | solution.py:31
  43.6 1.6 collective-permute-start.5
  45.3 13.0 %collective-permute-done.1 = bf16[1040,256]{1,0:T(8,128)(2,1)S(1)} collective-permute-done((bf16[1040,256]{1,0:T(8,128)(2,1)S(1)}, bf16[1040,256]{1,0:T(8,128)(2,1)S(1)}, u32[]{:S(2)}, u32[]{:S(2)}) %collective-permute-start.1) | collective-permute-done | bytes 532512 | tf_op jit(solution)/shard_map/ppermute | solution.py:31
  62.1 1.6 collective-permute-start.9
  63.8 1.4 collective-permute-start.10
  65.3 6.0 %all-to-all-start.1 = ((bf16[16,128,256]{2,1,0:T(8,128)(2,1)}), bf16[16,128,256]{2,1,0:T(8,128)(2,1)S(1)}, u32[]{:S(2)}, u32[]{:S(2)}) async-start(bf16[16,128,256]{2,1,0:T(8,128)(2,1)} %get-tuple-element.81), calls=%async_computation.1 | async-start | bytes 2097152 | tf_op jit(solution)/shard_map/all_to_all | solution.py:495
  72.0 10.0 %collective-permute-done.9 = bf16[512,512]{1,0:T(8,128)(2,1)} collective-permute-done((bf16[512,512]{1,0:T(8,128)(2,1)}, bf16[512,512]{1,0:T(8,128)(2,1)}, u32[]{:S(2)}, u32[]{:S(2)}) %collective-permute-start.9) | collective-permute-done | bytes 524320 | tf_op jit(solution)/shard_map/ppermute | solution.py:31
  82.0 2.3 pad_maximum_fusion.2.first_ref
  84.3 5.8 %project.1 = bf16[1024,384]{1,0:T(8,128)(2,1)S(1)} custom-call(s32[2]{0:T(128)S(1)} %fusion.110.refs_0_, bf16[1024,1024]{1,0:T(8,128)(2,1)S(1)} %pad_maximum_fusion.refs_1_, bf16[1024,1024]{1,0:T(8,128)(2,1)} %collective-permute-done.8.refs_2_, bf16[2048,384]{1,0:T(8,128)(2,1)} %bitcast.6.refs_3_, f32[1024,64]{1,0:T(8,128)S(1)} %copy-done.6, ...), custom_call_target="tpu_custom_call" | custom-call | flops 1 | bytes 1 | tf_op jit(solution)/shard_map/project/pallas_call | solution.py:196
  90.2 6.6 %collective-permute-start.11 = (bf16[64,384]{1,0:T(8,128)(2,1)S(1)}, bf16[64,384]{1,0:T(8,128)(2,1)S(1)}, u32[]{:S(2)}, u32[]{:S(2)}) collective-permute-start(bf16[64,384]{1,0:T(8,128)(2,1)S(1)} %constant_dynamic-slice_fusion), channel_id=1, source_target_pairs={{0,16},{2,18},{4,20},{6,22},{8,24},{10,26},{12,28},{14,30},{1,17},... | collective-permute-start | bytes 147464 | tf_op jit(solution)/shard_map/ppermute | solution.py:21
  98.6 6.8 %attend_once.1 = bf16[1088,128]{1,0:T(8,128)(2,1)S(1)} custom-call(f32[1]{0:T(128)} %dynamic_slice.92.sink_ref, s32[1088,1]{1,0:T(8,128)S(1)} %copy-done.4, s32[1,1088]{1,0:T(1,128)S(1)} %and_select_fusion.key_prompt_ref, bf16[1088,384]{1,0:T(8,128)(2,1)S(1)} %pad_maximum_fusion.3.query_ref.key_ref.value_ref, ...), custom_call_target="tpu_custom_call" | custom-call | flops 1 | bytes 1 | tf_op jit(solution)/shard_map/attend_once/pallas_call | solution.py:238
  107.8 4.3 %collective-permute-done.12 = bf16[64,128]{1,0:T(8,128)(2,1)S(1)} collective-permute-done((bf16[64,128]{1,0:T(8,128)(2,1)S(1)}, bf16[64,128]{1,0:T(8,128)(2,1)S(1)}, u32[]{:S(2)}, u32[]{:S(2)}) %collective-permute-start.12) | collective-permute-done | bytes 16416 | tf_op jit(solution)/shard_map/ppermute | solution.py:21
  117.0 14.2 %collective-permute-done.13.first_other_ref = bf16[512,1024]{1,0:T(8,128)(2,1)} collective-permute-done((bf16[512,1024]{1,0:T(8,128)(2,1)S(1)}, bf16[512,1024]{1,0:T(8,128)(2,1)}, u32[]{:S(2)}, u32[]{:S(2)}) %collective-permute-start.13) | collective-permute-done | bytes 1048608 | tf_op jit(solution)/shard_map/ppermute | solution.py:31
  131.2 4.6 %all-to-all-start.2 = ((bf16[8,128,128]{2,1,0:T(8,128)(2,1)}), bf16[8,128,128]{2,1,0:T(8,128)(2,1)S(1)}, u32[]{:S(2)}, u32[]{:S(2)}) async-start(bf16[8,128,128]{2,1,0:T(8,128)(2,1)} %constant_dynamic-update-slice_fusion), calls=%async_computation.2 | async-start | bytes 524288 | tf_op jit(solution)/shard_map/all_to_all | solution.py:606
  135.8 6.6 %all-to-all-done.2.head_ref = bf16[8,128,128]{2,1,0:T(8,128)(2,1)S(1)} async-done(((bf16[8,128,128]{2,1,0:T(8,128)(2,1)}), bf16[8,128,128]{2,1,0:T(8,128)(2,1)S(1)}, u32[]{:S(2)}, u32[]{:S(2)}) %all-to-all-start.2) | async-done | bytes 262176 | tf_op jit(solution)/shard_map/all_to_all | solution.py:606
  142.5 5.2 %all-to-all-start.3 = ((bf16[16,128,256]{2,1,0:T(8,128)(2,1)}), bf16[16,128,256]{2,1,0:T(8,128)(2,1)}, u32[]{:S(2)}, u32[]{:S(2)}) async-start(bf16[16,128,256]{2,1,0:T(8,128)(2,1)} %get-tuple-element.93), calls=%async_computation.3 | async-start | bytes 2097152 | tf_op jit(solution)/shard_map/all_to_all | solution.py:495
  149.0 3.3 out_project.1.refs_1_
  153.2 2.1 collective-permute-done.15.refs_2_
  155.3 2.2 settle.1
  158.5 2.8 collective-permute-start.16
  162.1 21.2 %collective-permute-done.17 = f32[1,128,16]{2,1,0:T(8,128)S(1)} collective-permute-done((f32[1,128,16]{2,1,0:T(8,128)S(1)}, f32[1,128,16]{2,1,0:T(8,128)S(1)}, u32[]{:S(2)}, u32[]{:S(2)}) %collective-permute-start.17) | collective-permute-done | bytes 8224 | tf_op jit(solution)/shard_map/ppermute | solution.py:31
  184.3 4.6 %all-to-all-start.4 = ((bf16[16,128,512]{2,1,0:T(8,128)(2,1)}), bf16[16,128,512]{2,1,0:T(8,128)(2,1)S(1)}, u32[]{:S(2)}, u32[]{:S(2)}) async-start(bf16[16,128,512]{2,1,0:T(8,128)(2,1)} %get-tuple-element.97), calls=%async_computation.4 | async-start | bytes 4194304 | tf_op jit(solution)/shard_map/all_to_all | solution.py:495
  189.6 1.4 convolution_convert_fusion.1
  193.6 1.9 collective-permute-start.18
  195.5 1.5 collective-permute-start.19
  197.9 1.5 collective-permute-start.22
  199.3 1.5 collective-permute-start.20
  201.4 2.5 collective-permute-done.18
  203.9 5.5 %collective-permute-start.23 = (bf16[2,72,1024]{2,1,0:T(8,128)(2,1)}, bf16[2,72,1024]{2,1,0:T(8,128)(2,1)}, u32[]{:S(2)}, u32[]{:S(2)}) collective-permute-start(bf16[2,72,1024]{2,1,0:T(8,128)(2,1)} %get-tuple-element.127), channel_id=1, source_target_pairs={{0,12},{2,14},{4,8},{6,10},{8,4},{10,6},{12,0},{14,2},{16,28},{18,... | collective-permute-start | bytes 884744 | tf_op jit(solution)/shard_map/ppermute | solution.py:31
  209.4 8.9 %collective-permute-done.19 = bf16[2,72,1024]{2,1,0:T(8,128)(2,1)S(1)} collective-permute-done((bf16[2,72,1024]{2,1,0:T(8,128)(2,1)S(1)}, bf16[2,72,1024]{2,1,0:T(8,128)(2,1)S(1)}, u32[]{:S(2)}, u32[]{:S(2)}) %collective-permute-start.19) | collective-permute-done | bytes 294944 | tf_op jit(solution)/shard_map/ppermute | solution.py:31
  220.3 9.5 %all-to-all-done.4 = bf16[16,128,512]{2,1,0:T(8,128)(2,1)S(1)} async-done(((bf16[16,128,512]{2,1,0:T(8,128)(2,1)}), bf16[16,128,512]{2,1,0:T(8,128)(2,1)S(1)}, u32[]{:S(2)}, u32[]{:S(2)}) %all-to-all-start.4) | async-done | bytes 2097184 | tf_op jit(solution)/shard_map/all_to_all | solution.py:495
  229.7 11.3 %all-to-all-start.5 = ((bf16[16,128,512]{2,1,0:T(8,128)(2,1)}), bf16[16,128,512]{2,1,0:T(8,128)(2,1)}, u32[]{:S(2)}, u32[]{:S(2)}) async-start(bf16[16,128,512]{2,1,0:T(8,128)(2,1)} %get-tuple-element.104), calls=%async_computation.5 | async-start | bytes 4194304 | tf_op jit(solution)/shard_map/all_to_all | solution.py:495
  241.0 1.7 bitcast_dynamic-update-slice_fusion.6
  242.7 1.7 bitcast_dynamic-update-slice_fusion.5
  244.4 1.7 bitcast_dynamic-update-slice_fusion.4
  246.1 1.7 bitcast_dynamic-update-slice_fusion.3
  247.8 1.7 bitcast_dynamic-update-slice_fusion.2
  249.5 1.7 collective-permute-done.23
  251.3 1.7 bitcast_dynamic-update-slice_fusion.1
  253.0 7.8 %collective-permute-done.24 = bf16[2,72,1024]{2,1,0:T(8,128)(2,1)} collective-permute-done((bf16[2,72,1024]{2,1,0:T(8,128)(2,1)}, bf16[2,72,1024]{2,1,0:T(8,128)(2,1)}, u32[]{:S(2)}, u32[]{:S(2)}) %collective-permute-start.24) | collective-permute-done | bytes 294944 | tf_op jit(solution)/shard_map/ppermute | solution.py:31
  260.8 1.7 bitcast_dynamic-update-slice_fusion
  267.6 2.3 collective-permute-done.25.refs_2_
  271.0 5.8 %hidden_units.2.refs_1_ = bf16[1,576,512]{2,1,0:T(8,128)(2,1)S(1)} custom-call(s32[2]{0:T(128)S(1)} %fusion.110.refs_0_, bf16[1,576,1024]{2,1,0:T(8,128)(2,1)} %bitcast.160, bf16[1,576,1024]{2,1,0:T(8,128)(2,1)} %copy-done.19, bf16[1,2048,256]{2,1,0:T(8,128)(2,1)S(1)} %bitcast.148, bf16[1,2048,256]{2,1,0:T(8,128)(2,1)} %bitcast.32.refs_4_, ...), custom_call_target="tpu_custom_call" | custom-call | flops 1 | bytes 1 | tf_op jit(solution)/shard_map/hidden_units/pallas_call | solution.py:352
  276.9 11.5 %all-to-all-done.5 = bf16[16,128,512]{2,1,0:T(8,128)(2,1)} async-done(((bf16[16,128,512]{2,1,0:T(8,128)(2,1)}), bf16[16,128,512]{2,1,0:T(8,128)(2,1)}, u32[]{:S(2)}, u32[]{:S(2)}) %all-to-all-start.5) | async-done | bytes 2097184 | tf_op jit(solution)/shard_map/all_to_all | solution.py:495
  288.4 4.7 %down_rows.2 = (bf16[1,576,1024]{2,1,0:T(8,128)(2,1)S(1)}, bf16[1,576,1024]{2,1,0:T(8,128)(2,1)}) custom-call(s32[2]{0:T(128)S(1)} %fusion.111.refs_0_, bf16[1,576,512]{2,1,0:T(8,128)(2,1)S(1)} %hidden_units.2.refs_1_, bf16[1,2048,512]{2,1,0:T(8,128)(2,1)} %bitcast.56.refs_2_), custom_call_target="tpu_custom_call" | custom-call | flops 1 | bytes 1 | tf_op jit(solution)/shard_map/down_rows/pallas_call | solution.py:384
  293.0 3.1 collective-permute-done.27
  296.1 1.6 add_convert_fusion.1
  297.7 4.0 %all-to-all-start.6 = ((bf16[8,1,72,1024]{3,2,1,0:T(8,128)(2,1)}), bf16[8,1,72,1024]{3,2,1,0:T(8,128)(2,1)S(1)}, u32[]{:S(2)}, u32[]{:S(2)}) async-start(bf16[8,1,72,1024]{3,2,1,0:T(8,128)(2,1)} %bitcast.58), calls=%async_computation.6 | async-start | bytes 2359296 | tf_op jit(solution)/shard_map/all_to_all | solution.py:737
  301.7 5.8 %hidden_units.3.refs_1_ = bf16[1,576,512]{2,1,0:T(8,128)(2,1)S(1)} custom-call(s32[2]{0:T(128)S(1)} %fusion.110.refs_0_, bf16[1,576,1024]{2,1,0:T(8,128)(2,1)} %bitcast.158, bf16[1,576,1024]{2,1,0:T(8,128)(2,1)} %copy-done.18, bf16[1,2048,256]{2,1,0:T(8,128)(2,1)S(1)} %bitcast.149, bf16[1,2048,256]{2,1,0:T(8,128)(2,1)} %bitcast.32.refs_4_, ...), custom_call_target="tpu_custom_call" | custom-call | flops 1 | bytes 1 | tf_op jit(solution)/shard_map/hidden_units/pallas_call | solution.py:352
  307.5 4.6 %down_rows.3 = (bf16[1,576,1024]{2,1,0:T(8,128)(2,1)S(1)}, bf16[1,576,1024]{2,1,0:T(8,128)(2,1)}) custom-call(s32[2]{0:T(128)S(1)} %fusion.111.refs_0_, bf16[1,576,512]{2,1,0:T(8,128)(2,1)S(1)} %hidden_units.3.refs_1_, bf16[1,2048,512]{2,1,0:T(8,128)(2,1)} %bitcast.56.refs_2_), custom_call_target="tpu_custom_call" | custom-call | flops 1 | bytes 1 | tf_op jit(solution)/shard_map/down_rows/pallas_call | solution.py:384
  312.1 3.1 collective-permute-done.28
  315.1 1.5 add_convert_fusion
  317.9 4.3 %all-to-all-start.7 = ((bf16[8,1,72,1024]{3,2,1,0:T(8,128)(2,1)}), bf16[8,1,72,1024]{3,2,1,0:T(8,128)(2,1)}, u32[]{:S(2)}, u32[]{:S(2)}) async-start(bf16[8,1,72,1024]{3,2,1,0:T(8,128)(2,1)} %bitcast.62), calls=%async_computation.7 | async-start | bytes 2359296 | tf_op jit(solution)/shard_map/all_to_all | solution.py:737
  324.8 1.9 collective-permute-start.29
  326.6 16.4 %all-to-all-done.7 = bf16[8,1,72,1024]{3,2,1,0:T(8,128)(2,1)} async-done(((bf16[8,1,72,1024]{3,2,1,0:T(8,128)(2,1)}), bf16[8,1,72,1024]{3,2,1,0:T(8,128)(2,1)}, u32[]{:S(2)}, u32[]{:S(2)}) %all-to-all-start.7) | async-done | bytes 1179680 | tf_op jit(solution)/shard_map/all_to_all | solution.py:737
  343.0 2.1 fusion.23
  (197 shorter events, 40.6 us)
Async XLA Ops:
  0.0 5.0 %copy-start = (bf16[128,2048]{1,0:T(8,128)(2,1)S(1)}, bf16[128,2048]{1,0:T(8,128)(2,1)}, u32[]{:S(2)}) copy-start(bf16[128,2048]{1,0:T(8,128)(2,1)} %refs_3_) | copy-start | bytes 1572868
  0.0 1.1 copy-start.7
  1.1 1.0 copy-start.8
  2.1 1.0 copy-start.9
  3.2 2.2 copy-start.26
  3.2 5.4 %copy-start.24 = (s32[128,8]{0,1:T(8,128)S(1)}, s32[128,8]{0,1:T(8,128)}, u32[]{:S(2)}) copy-start(s32[128,8]{0,1:T(8,128)} %param.29) | copy-start | bytes 12292
  3.2 8.0 %copy-start.20 = (f32[1024,128]{1,0:T(8,128)S(1)}, f32[1024,128]{1,0:T(8,128)}, u32[]{:S(2)}) copy-start(f32[1024,128]{1,0:T(8,128)} %param.21) | copy-start | bytes 1572868
  5.0 6.2 %copy-start.23 = (f32[128,16]{0,1:T(8,128)S(1)}, f32[128,16]{0,1:T(8,128)}, u32[]{:S(2)}) copy-start(f32[128,16]{0,1:T(8,128)} %param.23) | copy-start | bytes 24580
  5.5 15.3 %collective-permute-start.2 = (bf16[1,128,1024]{2,1,0:T(8,128)(2,1)S(1)}, bf16[1,128,1024]{2,1,0:T(8,128)(2,1)S(1)}, u32[]{:S(2)}, u32[]{:S(2)}) collective-permute-start(bf16[1,128,1024]{2,1,0:T(8,128)(2,1)S(1)} %fusion.45), channel_id=1, source_target_pairs={{0,8},{2,10},{4,12},{6,14},{8,0},{10,2},{12,4},{14,6},{16,24},{18,... | collective-permute-start | bytes 786440 | tf_op jit(solution)/shard_map/ppermute | solution.py:31
  8.6 14.2 %collective-permute-start.4 = (s32[1,128,8]{1,2,0:T(8,128)S(1)}, s32[1,128,8]{1,2,0:T(8,128)S(1)}, u32[]{:S(2)}, u32[]{:S(2)}) collective-permute-start(s32[1,128,8]{1,2,0:T(8,128)S(1)} %bitcast.173), channel_id=1, source_target_pairs={{0,16},{2,18},{4,20},{6,22},{8,24},{10,26},{12,28},{14,30},{16,0},... | collective-permute-start | bytes 12296 | tf_op jit(solution)/shard_map/ppermute | solution.py:31
  11.3 32.1 %collective-permute-start = (bf16[1040,128]{1,0:T(8,128)(2,1)S(1)}, bf16[1040,128]{1,0:T(8,128)(2,1)S(1)}, u32[]{:S(2)}, u32[]{:S(2)}) collective-permute-start(bf16[1040,128]{1,0:T(8,128)(2,1)S(1)} %pad_maximum_fusion.13), channel_id=1, source_target_pairs={{0,16},{2,18},{4,20},{6,22},{8,24},{10,26},{12,28},{14,30},{16,0},... | collective-permute-start | bytes 798728 | tf_op jit(solution)/shard_map/ppermute | solution.py:31
  11.7 48.9 %all-to-all-start = ((bf16[16,128,384]{2,1,0:T(8,128)(2,1)}), bf16[16,128,384]{2,1,0:T(8,128)(2,1)}, u32[]{:S(2)}, u32[]{:S(2)}) async-start(bf16[16,128,384]{2,1,0:T(8,128)(2,1)} %pack_heads.1), calls=%async_computation | async-start | bytes 3145728 | tf_op jit(solution)/shard_map/all_to_all | solution.py:451
  20.9 22.6 %collective-permute-start.3 = (bf16[2,128,512]{2,1,0:T(8,128)(2,1)S(1)}, bf16[2,128,512]{2,1,0:T(8,128)(2,1)S(1)}, u32[]{:S(2)}, u32[]{:S(2)}) collective-permute-start(bf16[2,128,512]{2,1,0:T(8,128)(2,1)S(1)} %get-tuple-element.133), channel_id=1, source_target_pairs={{0,4},{2,6},{4,0},{6,2},{8,12},{10,14},{12,8},{14,10},{16,20},{18,... | collective-permute-start | bytes 786440 | tf_op jit(solution)/shard_map/ppermute | solution.py:31
  22.8 22.4 %collective-permute-start.6 = (bf16[2,128,512]{2,1,0:T(8,128)(2,1)S(1)}, bf16[2,128,512]{2,1,0:T(8,128)(2,1)S(1)}, u32[]{:S(2)}, u32[]{:S(2)}) collective-permute-start(bf16[2,128,512]{2,1,0:T(8,128)(2,1)S(1)} %get-tuple-element.134), channel_id=1, source_target_pairs={{0,2},{2,0},{4,6},{6,4},{8,10},{10,8},{12,14},{14,12},{16,18},{18,... | collective-permute-start | bytes 786440 | tf_op jit(solution)/shard_map/ppermute | solution.py:31
  43.4 14.9 %collective-permute-start.1 = (bf16[1040,256]{1,0:T(8,128)(2,1)S(1)}, bf16[1040,256]{1,0:T(8,128)(2,1)S(1)}, u32[]{:S(2)}, u32[]{:S(2)}) collective-permute-start(bf16[1040,256]{1,0:T(8,128)(2,1)S(1)} %pad_maximum_fusion.7), channel_id=1, source_target_pairs={{0,8},{2,10},{4,12},{6,14},{8,0},{10,2},{12,4},{14,6},{16,24},{18,... | collective-permute-start | bytes 1597448 | tf_op jit(solution)/shard_map/ppermute | solution.py:31
  43.6 16.4 %collective-permute-start.5 = (bf16[4,128,512]{2,1,0:T(8,128)(2,1)S(1)}, bf16[4,128,512]{2,1,0:T(8,128)(2,1)S(1)}, u32[]{:S(2)}, u32[]{:S(2)}) collective-permute-start(bf16[4,128,512]{2,1,0:T(8,128)(2,1)S(1)} %pad_maximum_fusion.10), channel_id=1, source_target_pairs={{0,2},{2,0},{4,6},{6,4},{8,10},{10,8},{12,14},{14,12},{16,18},{18,... | collective-permute-start | bytes 1572872 | tf_op jit(solution)/shard_map/ppermute | solution.py:31
  45.2 14.9 %collective-permute-start.7 = (bf16[4,128,512]{2,1,0:T(8,128)(2,1)S(1)}, bf16[4,128,512]{2,1,0:T(8,128)(2,1)S(1)}, u32[]{:S(2)}, u32[]{:S(2)}) collective-permute-start(bf16[4,128,512]{2,1,0:T(8,128)(2,1)S(1)} %pad_maximum_fusion.11), channel_id=1, source_target_pairs={{0,4},{2,6},{4,0},{6,2},{8,12},{10,14},{12,8},{14,10},{16,20},{18,... | collective-permute-start | bytes 1572872 | tf_op jit(solution)/shard_map/ppermute | solution.py:31
  60.3 3.5 %copy-start.25 = (s32[2]{0:T(128)S(1)}, s32[2]{0:T(128)}, u32[]{:S(2)}) copy-start(s32[2]{0:T(128)} %param.28) | copy-start | bytes 28
  60.5 10.8 %copy-start.27 = (f32[8]{0:T(128)S(1)}, f32[8]{0:T(128)}, u32[]{:S(2)}) copy-start(f32[8]{0:T(128)} %param.22) | copy-start | bytes 100
  60.5 23.7 %collective-permute-start.8 = (bf16[1024,1024]{1,0:T(8,128)(2,1)S(1)}, bf16[1024,1024]{1,0:T(8,128)(2,1)}, u32[]{:S(2)}, u32[]{:S(2)}) collective-permute-start(bf16[1024,1024]{1,0:T(8,128)(2,1)S(1)} %pad_maximum_fusion.refs_1_), channel_id=1, source_target_pairs={{1,0},{0,1},{3,2},{2,3},{5,4},{4,5},{7,6},{6,7},{9,8},{8,9},{11,10... | collective-permute-start | bytes 6291464 | tf_op jit(solution)/shard_map/ppermute | solution.py:26
  62.1 19.8 %collective-permute-start.9 = (bf16[512,512]{1,0:T(8,128)(2,1)}, bf16[512,512]{1,0:T(8,128)(2,1)}, u32[]{:S(2)}, u32[]{:S(2)}) collective-permute-start(bf16[512,512]{1,0:T(8,128)(2,1)} %pad_maximum_fusion.8), channel_id=1, source_target_pairs={{0,4},{2,6},{4,0},{6,2},{8,12},{10,14},{12,8},{14,10},{16,20},{18,... | collective-permute-start | bytes 1572872 | tf_op jit(solution)/shard_map/ppermute | solution.py:31
  63.8 32.9 %collective-permute-start.10 = (bf16[528,512]{1,0:T(8,128)(2,1)}, bf16[528,512]{1,0:T(8,128)(2,1)}, u32[]{:S(2)}, u32[]{:S(2)}) collective-permute-start(bf16[528,512]{1,0:T(8,128)(2,1)} %pad_maximum_fusion.4), channel_id=1, source_target_pairs={{0,2},{2,0},{4,6},{6,4},{8,10},{10,8},{12,14},{14,12},{16,18},{18,... | collective-permute-start | bytes 1622024 | tf_op jit(solution)/shard_map/ppermute | solution.py:31
  65.3 51.8 %all-to-all-start.1 = ((bf16[16,128,256]{2,1,0:T(8,128)(2,1)}), bf16[16,128,256]{2,1,0:T(8,128)(2,1)S(1)}, u32[]{:S(2)}, u32[]{:S(2)}) async-start(bf16[16,128,256]{2,1,0:T(8,128)(2,1)} %get-tuple-element.81), calls=%async_computation.1 | async-start | bytes 2097152 | tf_op jit(solution)/shard_map/all_to_all | solution.py:495
  71.4 12.9 %copy-start.5 = (f32[1024,64]{1,0:T(8,128)S(1)}, f32[1024,64]{1,0:T(8,128)}, u32[]{:S(2)}) copy-start(f32[1024,64]{1,0:T(8,128)} %get-tuple-element.75.refs_5_) | copy-start | bytes 786436
  71.4 12.9 %copy-start.6 = (f32[1024,64]{1,0:T(8,128)S(1)}, f32[1024,64]{1,0:T(8,128)}, u32[]{:S(2)}) copy-start(f32[1024,64]{1,0:T(8,128)} %get-tuple-element.74.refs_4_) | copy-start | bytes 786436
  84.3 12.5 %copy-start.17 = (bf16[528,512]{1,0:T(8,128)(2,1)S(1)}, bf16[528,512]{1,0:T(8,128)(2,1)}, u32[]{:S(2)}) copy-start(bf16[528,512]{1,0:T(8,128)(2,1)} %pad_maximum_fusion.4) | copy-start | bytes 1622020
  90.1 8.4 %copy-start.4 = (s32[1088,1]{1,0:T(8,128)S(1)}, s32[1088,1]{1,0:T(8,128)}, u32[]{:S(2)}) copy-start(s32[1088,1]{1,0:T(8,128)} %fusion.9.query_prompt_ref) | copy-start | bytes 13060
  90.2 8.3 %collective-permute-start.11 = (bf16[64,384]{1,0:T(8,128)(2,1)S(1)}, bf16[64,384]{1,0:T(8,128)(2,1)S(1)}, u32[]{:S(2)}, u32[]{:S(2)}) collective-permute-start(bf16[64,384]{1,0:T(8,128)(2,1)S(1)} %constant_dynamic-slice_fusion), channel_id=1, source_target_pairs={{0,16},{2,18},{4,20},{6,22},{8,24},{10,26},{12,28},{14,30},{1,17},... | collective-permute-start | bytes 147464 | tf_op jit(solution)/shard_map/ppermute | solution.py:21
  98.6 9.2 %copy-start.2 = (bf16[512,1024]{1,0:T(8,128)(2,1)S(1)}, bf16[512,1024]{1,0:T(8,128)(2,1)}, u32[]{:S(2)}) copy-start(bf16[512,1024]{1,0:T(8,128)(2,1)} %pad_maximum_fusion.2.first_ref) | copy-start | bytes 3145732
  105.4 6.7 %collective-permute-start.12 = (bf16[64,128]{1,0:T(8,128)(2,1)S(1)}, bf16[64,128]{1,0:T(8,128)(2,1)S(1)}, u32[]{:S(2)}, u32[]{:S(2)}) collective-permute-start(bf16[64,128]{1,0:T(8,128)(2,1)S(1)} %slice.175), channel_id=1, source_target_pairs={{16,0},{18,2},{20,4},{22,6},{24,8},{26,10},{28,12},{30,14},{17,1},... | collective-permute-start | bytes 49160 | tf_op jit(solution)/shard_map/ppermute | solution.py:21
  106.7 24.5 %collective-permute-start.14 = (bf16[528,1024]{1,0:T(8,128)(2,1)S(1)}, bf16[528,1024]{1,0:T(8,128)(2,1)}, u32[]{:S(2)}, u32[]{:S(2)}) collective-permute-start(bf16[528,1024]{1,0:T(8,128)(2,1)S(1)} %pad_maximum_fusion.1.second_ref), channel_id=1, source_target_pairs={{0,4},{2,6},{4,0},{6,2},{8,12},{10,14},{12,8},{14,10},{16,20},{18,... | collective-permute-start | bytes 3244040 | tf_op jit(solution)/shard_map/ppermute | solution.py:31
  107.8 23.5 %collective-permute-start.13 = (bf16[512,1024]{1,0:T(8,128)(2,1)S(1)}, bf16[512,1024]{1,0:T(8,128)(2,1)}, u32[]{:S(2)}, u32[]{:S(2)}) collective-permute-start(bf16[512,1024]{1,0:T(8,128)(2,1)S(1)} %copy-done.2), channel_id=1, source_target_pairs={{0,2},{2,0},{4,6},{6,4},{8,10},{10,8},{12,14},{14,12},{16,18},{18,... | collective-permute-start | bytes 3145736 | tf_op jit(solution)/shard_map/ppermute | solution.py:31
  131.2 11.2 %all-to-all-start.2 = ((bf16[8,128,128]{2,1,0:T(8,128)(2,1)}), bf16[8,128,128]{2,1,0:T(8,128)(2,1)S(1)}, u32[]{:S(2)}, u32[]{:S(2)}) async-start(bf16[8,128,128]{2,1,0:T(8,128)(2,1)} %constant_dynamic-update-slice_fusion), calls=%async_computation.2 | async-start | bytes 524288 | tf_op jit(solution)/shard_map/all_to_all | solution.py:606
  142.5 41.8 %all-to-all-start.3 = ((bf16[16,128,256]{2,1,0:T(8,128)(2,1)}), bf16[16,128,256]{2,1,0:T(8,128)(2,1)}, u32[]{:S(2)}, u32[]{:S(2)}) async-start(bf16[16,128,256]{2,1,0:T(8,128)(2,1)} %get-tuple-element.93), calls=%async_computation.3 | async-start | bytes 2097152 | tf_op jit(solution)/shard_map/all_to_all | solution.py:495
  147.8 1.2 copy-start.3
  149.0 6.3 %copy-start.1 = (bf16[128,2048]{1,0:T(8,128)(2,1)S(1)}, bf16[128,2048]{1,0:T(8,128)(2,1)}, u32[]{:S(2)}) copy-start(bf16[128,2048]{1,0:T(8,128)(2,1)} %refs_3_) | copy-start | bytes 1572868
  149.0 6.3 %copy-start.12 = (f32[2048]{0:T(1024)S(1)}, f32[2048]{0:T(1024)}, u32[]{:S(2)}) copy-start(f32[2048]{0:T(1024)} %param.17) | copy-start | bytes 24580
  152.3 3.0 collective-permute-start.15
  158.5 24.8 %collective-permute-start.16 = (bf16[1,128,1024]{2,1,0:T(8,128)(2,1)S(1)}, bf16[1,128,1024]{2,1,0:T(8,128)(2,1)S(1)}, u32[]{:S(2)}, u32[]{:S(2)}) collective-permute-start(bf16[1,128,1024]{2,1,0:T(8,128)(2,1)S(1)} %dynamic-slice_bitcast_fusion), channel_id=1, source_target_pairs={{0,16},{2,18},{4,20},{6,22},{8,24},{10,26},{12,28},{14,30},{16,0},... | collective-permute-start | bytes 786440 | tf_op jit(solution)/shard_map/ppermute | solution.py:31
  161.8 21.5 %collective-permute-start.17 = (f32[1,128,16]{2,1,0:T(8,128)S(1)}, f32[1,128,16]{2,1,0:T(8,128)S(1)}, u32[]{:S(2)}, u32[]{:S(2)}) collective-permute-start(f32[1,128,16]{2,1,0:T(8,128)S(1)} %multiply_bitcast_fusion), channel_id=1, source_target_pairs={{0,16},{2,18},{4,20},{6,22},{8,24},{10,26},{12,28},{14,30},{16,0},... | collective-permute-start | bytes 24584 | tf_op jit(solution)/shard_map/ppermute | solution.py:31
  184.3 45.5 %all-to-all-start.4 = ((bf16[16,128,512]{2,1,0:T(8,128)(2,1)}), bf16[16,128,512]{2,1,0:T(8,128)(2,1)S(1)}, u32[]{:S(2)}, u32[]{:S(2)}) async-start(bf16[16,128,512]{2,1,0:T(8,128)(2,1)} %get-tuple-element.97), calls=%async_computation.4 | async-start | bytes 4194304 | tf_op jit(solution)/shard_map/all_to_all | solution.py:495
  193.6 10.2 %collective-permute-start.18 = (bf16[2,72,1024]{2,1,0:T(8,128)(2,1)S(1)}, bf16[2,72,1024]{2,1,0:T(8,128)(2,1)S(1)}, u32[]{:S(2)}, u32[]{:S(2)}) collective-permute-start(bf16[2,72,1024]{2,1,0:T(8,128)(2,1)S(1)} %get-tuple-element.123), channel_id=1, source_target_pairs={{0,2},{2,0},{4,6},{6,4},{8,10},{10,8},{12,14},{14,12},{16,18},{18,... | collective-permute-start | bytes 884744 | tf_op jit(solution)/shard_map/ppermute | solution.py:31
  195.5 22.8 %collective-permute-start.19 = (bf16[2,72,1024]{2,1,0:T(8,128)(2,1)S(1)}, bf16[2,72,1024]{2,1,0:T(8,128)(2,1)S(1)}, u32[]{:S(2)}, u32[]{:S(2)}) collective-permute-start(bf16[2,72,1024]{2,1,0:T(8,128)(2,1)S(1)} %get-tuple-element.124), channel_id=1, source_target_pairs={{0,4},{2,6},{4,0},{6,2},{8,12},{10,14},{12,8},{14,10},{16,20},{18,... | collective-permute-start | bytes 884744 | tf_op jit(solution)/shard_map/ppermute | solution.py:31
  197.9 50.0 %collective-permute-start.22 = (bf16[2,72,1024]{2,1,0:T(8,128)(2,1)}, bf16[2,72,1024]{2,1,0:T(8,128)(2,1)}, u32[]{:S(2)}, u32[]{:S(2)}) collective-permute-start(bf16[2,72,1024]{2,1,0:T(8,128)(2,1)} %get-tuple-element.128), channel_id=1, source_target_pairs={{0,10},{2,8},{4,14},{6,12},{8,2},{10,0},{12,6},{14,4},{16,26},{18,... | collective-permute-start | bytes 884744 | tf_op jit(solution)/shard_map/ppermute | solution.py:31
  199.3 45.1 %collective-permute-start.20 = (bf16[2,72,1024]{2,1,0:T(8,128)(2,1)}, bf16[2,72,1024]{2,1,0:T(8,128)(2,1)}, u32[]{:S(2)}, u32[]{:S(2)}) collective-permute-start(bf16[2,72,1024]{2,1,0:T(8,128)(2,1)} %get-tuple-element.125), channel_id=1, source_target_pairs={{0,6},{2,4},{4,2},{6,0},{8,14},{10,12},{12,10},{14,8},{16,22},{18,... | collective-permute-start | bytes 884744 | tf_op jit(solution)/shard_map/ppermute | solution.py:31
  200.8 45.3 %collective-permute-start.21 = (bf16[2,72,1024]{2,1,0:T(8,128)(2,1)}, bf16[2,72,1024]{2,1,0:T(8,128)(2,1)}, u32[]{:S(2)}, u32[]{:S(2)}) collective-permute-start(bf16[2,72,1024]{2,1,0:T(8,128)(2,1)} %get-tuple-element.126), channel_id=1, source_target_pairs={{0,8},{2,10},{4,12},{6,14},{8,0},{10,2},{12,4},{14,6},{16,24},{18,... | collective-permute-start | bytes 884744 | tf_op jit(solution)/shard_map/ppermute | solution.py:31
  203.9 14.5 %copy-start.21 = (bf16[2,72,1024]{2,1,0:T(8,128)(2,1)}, bf16[2,72,1024]{2,1,0:T(8,128)(2,1)S(1)}, u32[]{:S(2)}) copy-start(bf16[2,72,1024]{2,1,0:T(8,128)(2,1)S(1)} %collective-permute-done.18) | copy-start | bytes 884740
  203.9 47.4 %collective-permute-start.23 = (bf16[2,72,1024]{2,1,0:T(8,128)(2,1)}, bf16[2,72,1024]{2,1,0:T(8,128)(2,1)}, u32[]{:S(2)}, u32[]{:S(2)}) collective-permute-start(bf16[2,72,1024]{2,1,0:T(8,128)(2,1)} %get-tuple-element.127), channel_id=1, source_target_pairs={{0,12},{2,14},{4,8},{6,10},{8,4},{10,6},{12,0},{14,2},{16,28},{18,... | collective-permute-start | bytes 884744 | tf_op jit(solution)/shard_map/ppermute | solution.py:31
  219.0 41.8 %collective-permute-start.24 = (bf16[2,72,1024]{2,1,0:T(8,128)(2,1)}, bf16[2,72,1024]{2,1,0:T(8,128)(2,1)}, u32[]{:S(2)}, u32[]{:S(2)}) collective-permute-start(bf16[2,72,1024]{2,1,0:T(8,128)(2,1)} %get-tuple-element.121), channel_id=1, source_target_pairs={{0,14},{2,12},{4,10},{6,8},{8,6},{10,4},{12,2},{14,0},{16,30},{18,... | collective-permute-start | bytes 884744 | tf_op jit(solution)/shard_map/ppermute | solution.py:31
  229.7 13.0 %copy-start.13 = (bf16[16,128,512]{2,1,0:T(8,128)(2,1)}, bf16[16,128,512]{2,1,0:T(8,128)(2,1)S(1)}, u32[]{:S(2)}) copy-start(bf16[16,128,512]{2,1,0:T(8,128)(2,1)S(1)} %all-to-all-done.4) | copy-start | bytes 6291460
  229.7 58.6 %all-to-all-start.5 = ((bf16[16,128,512]{2,1,0:T(8,128)(2,1)}), bf16[16,128,512]{2,1,0:T(8,128)(2,1)}, u32[]{:S(2)}, u32[]{:S(2)}) async-start(bf16[16,128,512]{2,1,0:T(8,128)(2,1)} %get-tuple-element.104), calls=%async_computation.5 | async-start | bytes 4194304 | tf_op jit(solution)/shard_map/all_to_all | solution.py:495
  262.5 4.1 %copy-start.16 = (bf16[8,2,72,1024]{3,2,0,1:T(8,128)(2,1)S(1)}, bf16[8,2,72,1024]{3,2,0,1:T(8,128)(2,1)}, u32[]{:S(2)}) copy-start(bf16[8,2,72,1024]{3,2,0,1:T(8,128)(2,1)} %bitcast_dynamic-update-slice_fusion) | copy-start | bytes 7077892
  267.0 2.9 copy-start.15
  267.0 9.8 %copy-start.14 = (bf16[8,1,1,72,1024]{4,3,0,2,1:T(8,128)(2,1)}, bf16[8,1,1,72,1024]{4,3,0,2,1:T(8,128)(2,1)S(1)}, u32[]{:S(2)}) copy-start(bf16[8,1,1,72,1024]{4,3,0,2,1:T(8,128)(2,1)S(1)} %get-tuple-element.119) | copy-start | bytes 3538948
  267.1 2.9 collective-permute-start.25
  267.1 9.7 %collective-permute-start.26 = (bf16[1,576,1024]{2,1,0:T(8,128)(2,1)S(1)}, bf16[1,576,1024]{2,1,0:T(8,128)(2,1)S(1)}, u32[]{:S(2)}, u32[]{:S(2)}) collective-permute-start(bf16[1,576,1024]{2,1,0:T(8,128)(2,1)S(1)} %bitcast.157), channel_id=1, source_target_pairs={{1,0},{0,1},{3,2},{2,3},{5,4},{4,5},{7,6},{6,7},{9,8},{8,9},{11,10... | collective-permute-start | bytes 3538952 | tf_op jit(solution)/shard_map/ppermute | solution.py:26
  270.0 1.1 copy-start.19
  276.9 20.8 %copy-start.18 = (bf16[1,576,1024]{2,1,0:T(8,128)(2,1)}, bf16[1,576,1024]{2,1,0:T(8,128)(2,1)S(1)}, u32[]{:S(2)}) copy-start(bf16[1,576,1024]{2,1,0:T(8,128)(2,1)S(1)} %collective-permute-done.26.refs_2_) | copy-start | bytes 3538948
  293.0 3.1 collective-permute-start.27
  297.7 20.3 %all-to-all-start.6 = ((bf16[8,1,72,1024]{3,2,1,0:T(8,128)(2,1)}), bf16[8,1,72,1024]{3,2,1,0:T(8,128)(2,1)S(1)}, u32[]{:S(2)}, u32[]{:S(2)}) async-start(bf16[8,1,72,1024]{3,2,1,0:T(8,128)(2,1)} %bitcast.58), calls=%async_computation.6 | async-start | bytes 2359296 | tf_op jit(solution)/shard_map/all_to_all | solution.py:737
  312.1 3.1 collective-permute-start.28
  317.9 25.0 %all-to-all-start.7 = ((bf16[8,1,72,1024]{3,2,1,0:T(8,128)(2,1)}), bf16[8,1,72,1024]{3,2,1,0:T(8,128)(2,1)}, u32[]{:S(2)}, u32[]{:S(2)}) async-start(bf16[8,1,72,1024]{3,2,1,0:T(8,128)(2,1)} %bitcast.62), calls=%async_computation.7 | async-start | bytes 2359296 | tf_op jit(solution)/shard_map/all_to_all | solution.py:737
  324.8 20.3 %copy-start.11 = (f32[128,2048]{1,0:T(8,128)S(1)}, f32[128,2048]{1,0:T(8,128)}, u32[]{:S(2)}) copy-start(f32[128,2048]{1,0:T(8,128)} %copy-done.10) | copy-start | bytes 3145732
  324.8 20.3 %collective-permute-start.29 = (bf16[128,1024]{1,0:T(8,128)(2,1)S(1)}, bf16[128,1024]{1,0:T(8,128)(2,1)S(1)}, u32[]{:S(2)}, u32[]{:S(2)}) collective-permute-start(bf16[128,1024]{1,0:T(8,128)(2,1)S(1)} %fusion.14), channel_id=1, source_target_pairs={{0,16},{2,18},{4,20},{6,22},{8,24},{10,26},{12,28},{14,30},{16,0},... | collective-permute-start | bytes 786440 | tf_op jit(solution)/shard_map/ppermute | solution.py:31
  (2 other events, 1.7 us)
